TPU v7x, 32 devices: a whole 2x2x4 slice. The times are simulated.
32 devices in a mesh: groups: 2 (over y), seq: 4 (over z), head: 2 (over x), rep: 2 (over core).
Axes of the slice: x: 2, y: 2, z: 4, core: 2. Of those that a mesh axis runs over, the one named last changes fastest.
Arguments:
- queries: bfloat16 [2048, 4096], P(('groups', 'seq'), ('head', 'rep')), parts along dimension 0, may hold values from -5 to 5
- keys: bfloat16 [2048, 4096], P(('groups', 'seq'), ('head', 'rep')), parts along dimension 0, may hold values from -5 to 5
- values: bfloat16 [2048, 4096], P(('groups', 'seq'), ('head', 'rep')), parts along dimension 0, may hold values from -10 to 10
- out_weight: bfloat16 [4096, 4096], P(None, ('head', 'rep')), may hold values from -0.125 to 0.125
- level_mask: int32 [16, 5], P(('groups', 'seq')), parts along dimension 0, may hold values 0 or 1
- cotangent: bfloat16 [2048, 4096], P(('groups', 'seq'), ('head', 'rep')), parts along dimension 0, may hold values from -6 to 6
Outputs:
- attended: bfloat16 [2048, 4096], P(('groups', 'seq'), ('head', 'rep')), parts along dimension 0
- q_grad: bfloat16 [2048, 4096], P(('groups', 'seq'), ('head', 'rep')), parts along dimension 0
- k_grad: bfloat16 [2048, 4096], P(('groups', 'seq'), ('head', 'rep')), parts along dimension 0
- v_grad: bfloat16 [2048, 4096], P(('groups', 'seq'), ('head', 'rep')), parts along dimension 0
- weight_grad: bfloat16 [8192, 4096], P(('groups', 'seq'), ('head', 'rep')), parts along dimension 0
There are 2 independent parts, one for each index of `groups`. A program takes and returns all parts, laid end to end along the dimension named above; an argument that names none is the same for every part. Nothing has to cross between parts.
All inputs are finite; a program needn't handle non-finite values. No bound on the sum of `level_mask` on one device may be relied on, other than what follows from the above.
Results may differ from a plain program's by a relative error of at most 0.0095.
Values may be sent and summed in bfloat16 or wider, within the bound.
No kernel may reach another device: no remote copies, remote signals or barrier semaphores. Data moves between devices by JAX's collectives and lax.ppermute only.
A program may use at most 128 MiB of HBM per device.

v0:
```python
import jax
import jax.numpy as jnp
from jax import lax
from jax.sharding import PartitionSpec as P

HEAD_DIM = 128
BLOCK = 128
LEVELS = 5


masked_score = -1e30


def passed_along(value, axis, by):
    peers = lax.axis_size(axis)
    pairs = [(i, i + by) for i in range(peers) if 0 <= i + by < peers]
    return lax.ppermute(value, axis, pairs)


def per_device(queries, keys, values, out_weight, level_mask, cotangent):
    rows_here, columns = queries.shape
    heads_here = columns // HEAD_DIM
    blocks_here = rows_here // BLOCK
    seq_count = lax.axis_size("seq")
    seq_place = lax.axis_index("seq")
    score_scale = HEAD_DIM ** (-0.5)
    key_value = jnp.stack([keys, values])
    block_ids = seq_place * blocks_here + jnp.arange(blocks_here, dtype=jnp.int32)
    level_blocks = []
    gathered = lax.all_gather(key_value, "seq", axis=1, tiled=True)
    margin = 2 ** (LEVELS - 1) * BLOCK
    padded = jnp.concatenate([jnp.zeros((2, margin, columns), key_value.dtype), gathered], axis=1)
    for level_index in range(LEVELS):
        first_row = seq_place * rows_here + margin - 2**level_index * BLOCK
        level_blocks.append(lax.dynamic_slice_in_dim(padded, first_row, rows_here, axis=1))
    usable = jnp.stack(
        [
            (block_ids >= 2**level_index) & (level_mask[:, level_index] == 1)
            for level_index in range(LEVELS)
        ],
        axis=1,
    )
    causal = jnp.arange(BLOCK)[:, None] >= jnp.arange(BLOCK)[None, :]
    own_mask = jnp.broadcast_to(causal[None], (blocks_here, BLOCK, BLOCK))
    far_mask = jnp.broadcast_to(
        jnp.repeat(usable, BLOCK, axis=1)[:, None, :], (blocks_here, BLOCK, LEVELS * BLOCK)
    )
    allowed = jnp.concatenate([own_mask, far_mask], axis=2)
    kv_all = jnp.concatenate(
        [blocks.reshape(2, blocks_here, BLOCK, columns) for blocks in [key_value] + level_blocks],
        axis=2,
    )
    kv_all = kv_all.reshape(2, blocks_here, (LEVELS + 1) * BLOCK, heads_here, HEAD_DIM)
    key_all = kv_all[0]
    value_all = kv_all[1]
    query_blocks = queries.reshape(blocks_here, BLOCK, heads_here, HEAD_DIM)
    scores = (
        jnp.einsum("nqhd,nkhd->nhqk", query_blocks, key_all, preferred_element_type=jnp.float32)
        * score_scale
    )
    scores = jnp.where(allowed[:, None], scores, masked_score)
    row_max = jnp.max(scores, -1, keepdims=True)
    exponent = jnp.exp(scores - row_max)
    attn_prob = exponent / jnp.sum(exponent, -1, keepdims=True)
    attn_low = attn_prob.astype(jnp.bfloat16)
    mixed_heads = jnp.einsum(
        "nhqk,nkhd->nqhd", attn_low, value_all, preferred_element_type=jnp.float32
    )
    mixed_heads = mixed_heads.astype(jnp.bfloat16).reshape(rows_here, columns)
    partial_value = lax.dot_general(
        mixed_heads, out_weight, (((1,), (1,)), ((), ())), preferred_element_type=jnp.float32
    )
    attended = lax.psum_scatter(
        partial_value.astype(jnp.bfloat16), ("head", "rep"), scatter_dimension=1, tiled=True
    )
    full_cotangent = lax.all_gather(cotangent, ("head", "rep"), axis=1, tiled=True)
    mixed_grad = jnp.dot(full_cotangent, out_weight, preferred_element_type=jnp.float32).astype(
        jnp.bfloat16
    )
    weight_grad = lax.psum_scatter(
        lax.dot_general(
            full_cotangent,
            mixed_heads,
            (((0,), (0,)), ((), ())),
            preferred_element_type=jnp.float32,
        ).astype(jnp.bfloat16),
        "seq",
        scatter_dimension=0,
        tiled=True,
    ).astype(jnp.float32)
    weight_grad = weight_grad.astype(jnp.bfloat16)
    grad_blocks = mixed_grad.reshape(blocks_here, BLOCK, heads_here, HEAD_DIM)
    prob_grad = jnp.einsum(
        "nqhd,nkhd->nhqk", grad_blocks, value_all, preferred_element_type=jnp.float32
    )
    row_dot = jnp.sum(attn_prob * prob_grad, -1, keepdims=True)
    score_grad = (attn_prob * (prob_grad - row_dot) * score_scale).astype(jnp.bfloat16)
    q_grad = jnp.einsum("nhqk,nkhd->nqhd", score_grad, key_all, preferred_element_type=jnp.float32)
    q_grad = q_grad.astype(jnp.bfloat16).reshape(rows_here, columns)
    key_part = jnp.einsum(
        "nhqk,nqhd->nkhd", score_grad, query_blocks, preferred_element_type=jnp.float32
    )
    value_part = jnp.einsum(
        "nhqk,nqhd->nkhd", attn_low, grad_blocks, preferred_element_type=jnp.float32
    )
    both_parts = jnp.stack([key_part, value_part]).reshape(
        2, blocks_here, LEVELS + 1, BLOCK, columns
    )
    own_total = both_parts[:, :, 0].reshape(2, rows_here, columns)
    near_sum = jnp.zeros((2, 2 * rows_here, columns), jnp.float32)
    outgoing = []
    for level_index in range(LEVELS):
        offset = 2**level_index
        contrib = both_parts[:, :, level_index + 1].reshape(2, rows_here, columns)
        if offset <= blocks_here:
            near_sum = near_sum + jnp.pad(
                contrib, ((0, 0), ((blocks_here - offset) * BLOCK, offset * BLOCK), (0, 0))
            )
        elif offset // blocks_here < seq_count:
            outgoing.append((offset // blocks_here, contrib))
    own_total = own_total + near_sum[:, rows_here:]
    outgoing = [(1, near_sum[:, :rows_here])] + outgoing
    for distance, contrib in outgoing:
        own_total = own_total + passed_along(contrib.astype(jnp.bfloat16), "seq", -distance).astype(
            contrib.dtype
        )
    k_grad = own_total[0].astype(jnp.bfloat16)
    v_grad = own_total[1].astype(jnp.bfloat16)
    return (attended, q_grad, k_grad, v_grad, weight_grad)


def solution(mesh):
    placed = (
        P(("groups", "seq"), ("head", "rep")),
        P(("groups", "seq"), ("head", "rep")),
        P(("groups", "seq"), ("head", "rep")),
        P(None, ("head", "rep")),
        P(("groups", "seq"), None),
        P(("groups", "seq"), ("head", "rep")),
    )
    return jax.shard_map(
        per_device,
        mesh=mesh,
        in_specs=placed,
        out_specs=(
            P(("groups", "seq"), ("head", "rep")),
            P(("groups", "seq"), ("head", "rep")),
            P(("groups", "seq"), ("head", "rep")),
            P(("groups", "seq"), ("head", "rep")),
            P(("groups", "seq"), ("head", "rep")),
        ),
        check_vma=False,
    )
```

profile of v0, /device:TPU:0, one launch (start us, length us, event | category | flops | bytes accessed | tf_op | source)
XLA Modules:
  0.0 361.4 jit_solution(5043464017296899892)
XLA Ops:
  16.0 77.7 %all-gather.3.cloned.1.call-done = bf16[2,1024,1024]{2,1,0:T(8,128)(2,1)} async-done(((bf16[2,256,1024]{2,1,0:T(8,128)(2,1)}), bf16[2,1024,1024]{2,1,0:T(8,128)(2,1)}) %all-gather.3.cloned.1.call-update) | async-done | bytes 4194320 | tf_op jit(solution)/shard_map/all_gather | solution.py:30
  93.7 2.9 pad_dynamic-slice_fusion
  97.0 3.4 fusion.56
  100.4 3.2 copy.30
  103.6 5.5 %copy.29 = bf16[1,2,768,1024]{2,3,1,0:T(8,128)(2,1)} copy(bf16[1,2,768,1024]{3,2,1,0:T(8,128)(2,1)} %get-tuple-element.19) | data formatting | bytes 6291456 | tf_op jit(solution)/shard_map/slice | solution.py:55
  111.2 3.0 fusion.57
  114.3 2.7 copy-done.7
  118.3 7.2 %convert_bitcast_fusion = bf16[4096,1024]{0,1:T(8,128)(2,1)} fusion(bf16[256,4096]{1,0:T(8,128)(2,1)} %all-gather.5.cloned.1.call-done, bf16[32,8,8,128]{3,2,1,0:T(8,128)(2,1)S(1)} %bitcast.102), kind=kOutput, calls=%fused_computation.7 | convolution fusion | flops 2151677952 | bytes 11010048 | tf_op jit(solution)/shard_map/dot_general | solution.py:81
  127.1 5.7 %fusion.35 = bf16[32,8,8,128]{3,1,2,0:T(8,128)(2,1)S(1)} fusion(bf16[256,4096]{1,0:T(8,128)(2,1)S(1)} %copy-done.6, bf16[4096,1024]{1,0:T(8,128)(2,1)} %param.9), kind=kOutput, calls=%fused_computation.41 | convolution fusion | flops 2147745792 | bytes 11010048 | tf_op jit(solution)/shard_map/dot_general | solution.py:77
  133.3 7.3 %convolution_convert_fusion = bf16[256,4096]{1,0:T(8,128)(2,1)} fusion(bf16[4096,1024]{1,0:T(8,128)(2,1)} %param.9, bf16[32,8,8,128]{3,2,1,0:T(8,128)(2,1)S(1)} %bitcast.103), kind=kOutput, calls=%fused_computation.13 | convolution fusion | flops 2148532224 | bytes 11010048 | tf_op jit(solution)/shard_map/dot_general | solution.py:70
  140.7 6.4 %convolution_bitcast_fusion = f32[2,768,8,128]{1,3,2,0:T(8,128)} fusion(bf16[2,128,8,128]{1,3,2,0:T(8,128)(2,1)S(1)} %copy.43, f32[2,8,128,768]{2,3,1,0:T(8,128)} %copy-done.7, f32[2,8,128]{2,1,0:T(8,128)S(1)} %get-tuple-element.32), kind=kOutput, calls=%fused_computation.26 | convolution fusion | flops 405798912 | bytes 13115392 | tf_op jit(solution)/shard_map/nhqk,nqhd->nkhd/dot_general | solution.py:103
  147.1 6.6 %copy.45 = f32[2,768,8,128]{3,2,1,0:T(8,128)} copy(f32[2,768,8,128]{1,3,2,0:T(8,128)} %convolution_bitcast_fusion) | data formatting | bytes 12582912 | tf_op jit(solution)/shard_map/nhqk,nqhd->nkhd/transpose | solution.py:103
  153.7 7.3 %stack.40 = f32[1,2,6,128,1024]{4,3,2,1,0:T(8,128)} reshape(f32[2,768,8,128]{3,2,1,0:T(8,128)} %copy.45) | data formatting | bytes 12582912 | tf_op jit(solution)/shard_map/stack | solution.py:106
  161.0 4.7 %fusion.58 = f32[2,8,128,768]{2,3,1,0:T(8,128)} fusion(bf16[2,128,8,128]{1,3,2,0:T(8,128)(2,1)} %copy-done.5, bf16[2,768,8,128]{1,3,2,0:T(8,128)(2,1)S(1)} %bitcast.88), kind=kOutput, calls=%fused_computation.82 | convolution fusion | flops 402653184 | bytes 9961472 | tf_op jit(solution)/shard_map/nqhd,nkhd->nhqk/dot_general | solution.py:93
  165.7 12.9 %fusion.17 = f32[2,768,8,128]{3,1,2,0:T(8,128)} fusion(f32[2,8,128,768]{2,3,1,0:T(8,128)} %fusion.58, bf16[2,128,8,128]{3,2,1,0:T(8,128)(2,1)} %bitcast.95, f32[2,8,128,768]{2,3,1,0:T(8,128)} %copy-done.7, f32[2,8,128]{2,1,0:T(8,128)S(1)} %get-tuple-element.32), kind=kOutput, calls=%fused_computation.25 | convolution fusion | flops 413666048 | bytes 19406848 | tf_op jit(solution)/shard_map/nhqk,nqhd->nkhd/dot_general | solution.py:100
  178.6 9.0 %copy.42 = f32[2,768,8,128]{3,2,1,0:T(8,128)} copy(f32[2,768,8,128]{3,1,2,0:T(8,128)} %fusion.17) | data formatting | bytes 12582912 | tf_op jit(solution)/shard_map/nhqk,nqhd->nkhd/transpose | solution.py:100
  187.6 7.3 %stack.39 = f32[1,2,6,128,1024]{4,3,2,1,0:T(8,128)} reshape(f32[2,768,8,128]{3,2,1,0:T(8,128)} %copy.42) | data formatting | bytes 12582912 | tf_op jit(solution)/shard_map/stack | solution.py:106
  194.9 3.8 %constant_dynamic-update-slice_fusion.6 = f32[2,2,6,128,1024]{4,3,2,1,0:T(8,128)S(1)} fusion(f32[1,2,6,128,1024]{4,3,2,1,0:T(8,128)} %stack.39), kind=kLoop, calls=%fused_computation.64 | loop fusion | bytes 12582912
  208.3 11.5 %fusion.36 = bf16[2,128,8,128]{1,3,2,0:T(8,128)(2,1)S(1)} fusion(bf16[2,768,8,128]{1,3,2,0:T(8,128)(2,1)} %bitcast.86, f32[2,8,128,768]{2,3,1,0:T(8,128)} %fusion.58, f32[2,8,128,768]{2,3,1,0:T(8,128)} %copy-done.7, f32[2,8,128]{2,1,0:T(8,128)S(1)} %get-tuple-element.32), kind=kOutput, calls=%fused_computation.42 | convolution fusion | flops 413928192 | bytes 16261120 | tf_op jit(solution)/shard_map/nhqk,nkhd->nqhd/dot_general | solution.py:98
  221.0 49.7 %collective-permute-done = bf16[2,256,1024]{2,1,0:T(8,128)(2,1)} collective-permute-done((bf16[2,256,1024]{2,1,0:T(8,128)(2,1)}, bf16[2,256,1024]{2,1,0:T(8,128)(2,1)}, u32[]{:S(2)}, u32[]{:S(2)}) %collective-permute-start) | collective-permute-done | bytes 1048608 | tf_op jit(solution)/shard_map/ppermute | solution.py:17
  270.7 65.8 %collective-permute-done.1 = bf16[2,256,1024]{2,1,0:T(8,128)(2,1)} collective-permute-done((bf16[2,256,1024]{2,1,0:T(8,128)(2,1)}, bf16[2,256,1024]{2,1,0:T(8,128)(2,1)}, u32[]{:S(2)}, u32[]{:S(2)}) %collective-permute-start.1) | collective-permute-done | bytes 1048608 | tf_op jit(solution)/shard_map/ppermute | solution.py:17
  336.5 3.1 fusion.24
  340.7 3.9 %copy.46 = bf16[1024,1024]{1,0:T(8,128)(2,1)} copy(bf16[1024,1024]{0,1:T(8,128)(2,1)} %reduce-scatter.5.cloned.1.call-done) | data formatting | bytes 4194304
  344.6 10.3 %reduce-scatter.3.cloned.1.call-done = bf16[256,1024]{1,0:T(8,128)(2,1)} async-done(((bf16[256,4096]{1,0:T(8,128)(2,1)}), bf16[256,1024]{1,0:T(8,128)(2,1)}) %reduce-scatter.3.cloned.1.call-update) | async-done | bytes 524304 | tf_op jit(solution)/shard_map/reduce_scatter | solution.py:73
  (60 shorter events, 26.4 us)
Async XLA Ops:
  7.2 86.5 %all-gather.3.cloned.1.call-start = ((), (), s32[]{:S(2)}) async-start(), calls=%async_computation.2 | async-start | bytes 5242880 | tf_op jit(solution)/shard_map/all_gather | solution.py:30
  9.5 108.8 %all-gather.5.cloned.1.call-start = ((), (), s32[]{:S(2)}) async-start(), calls=%async_computation.4 | async-start | bytes 2621440 | tf_op jit(solution)/shard_map/all_gather | solution.py:76
  10.3 330.4 %reduce-scatter.5.cloned.1.call-start = ((), (), s32[]{:S(2)}) async-start(), calls=%async_computation.5 | async-start | bytes 10485760 | tf_op jit(solution)/shard_map/reduce_scatter | solution.py:80
  93.7 2.9 copy-start.4
  103.6 7.6 %copy-start.1 = (bf16[1,2,768,1024]{2,3,1,0:T(8,128)(2,1)}, bf16[1,2,768,1024]{2,3,1,0:T(8,128)(2,1)S(1)}, u32[]{:S(2)}) copy-start(bf16[1,2,768,1024]{2,3,1,0:T(8,128)(2,1)S(1)} %copy.30) | copy-start | bytes 9437188
  111.2 5.7 %copy-start.2 = (bf16[1,2,768,1024]{2,3,1,0:T(8,128)(2,1)S(1)}, bf16[1,2,768,1024]{2,3,1,0:T(8,128)(2,1)}, u32[]{:S(2)}) copy-start(bf16[1,2,768,1024]{2,3,1,0:T(8,128)(2,1)} %copy.29) | copy-start | bytes 9437188
  114.3 2.7 copy-start.7
  125.5 1.6 copy-start.6
  125.5 229.3 %reduce-scatter.3.cloned.1.call-start = ((), (), s32[]{:S(2)}) async-start(), calls=%async_computation.3 | async-start | bytes 2621440 | tf_op jit(solution)/shard_map/reduce_scatter | solution.py:73
  133.3 7.4 %copy-start.5 = (bf16[2,128,8,128]{1,3,2,0:T(8,128)(2,1)}, bf16[2,128,8,128]{1,3,2,0:T(8,128)(2,1)S(1)}, u32[]{:S(2)}) copy-start(bf16[2,128,8,128]{1,3,2,0:T(8,128)(2,1)S(1)} %copy.43) | copy-start | bytes 1572868
  153.7 7.3 %copy-start.3 = (bf16[1,2,768,1024]{2,3,1,0:T(8,128)(2,1)S(1)}, bf16[1,2,768,1024]{2,3,1,0:T(8,128)(2,1)}, u32[]{:S(2)}) copy-start(bf16[1,2,768,1024]{2,3,1,0:T(8,128)(2,1)} %copy.29) | copy-start | bytes 9437188
  187.6 11.1 %slice-start = ((s8[6291456]{0:T(1024)(128)(4,1)}), s8[2097152]{0:T(1024)(128)(4,1)S(1)}, s32[]{:S(2)}) async-start(s8[6291456]{0:T(1024)(128)(4,1)} %bitcast.79), calls=%async_computation.6 | async-start | bytes 4194304
  194.9 4.3 %slice-start.1 = ((s8[6291456]{0:T(1024)(128)(4,1)}), s8[4194304]{0:T(1024)(128)(4,1)S(1)}, s32[]{:S(2)}) async-start(s8[6291456]{0:T(1024)(128)(4,1)} %bitcast.79), calls=%async_computation.7 | async-start | bytes 8388608
  202.9 1.3 copy-start
  205.5 65.2 %collective-permute-start = (bf16[2,256,1024]{2,1,0:T(8,128)(2,1)}, bf16[2,256,1024]{2,1,0:T(8,128)(2,1)}, u32[]{:S(2)}, u32[]{:S(2)}) collective-permute-start(bf16[2,256,1024]{2,1,0:T(8,128)(2,1)} %fusion.25), channel_id=1, source_target_pairs={{4,0},{8,4},{12,8},{5,1},{9,5},{13,9},{6,2},{10,6},{14,10},{7,3},{... | collective-permute-start | bytes 3145736 | tf_op jit(solution)/shard_map/ppermute | solution.py:17
  206.7 129.7 %collective-permute-start.1 = (bf16[2,256,1024]{2,1,0:T(8,128)(2,1)}, bf16[2,256,1024]{2,1,0:T(8,128)(2,1)}, u32[]{:S(2)}, u32[]{:S(2)}) collective-permute-start(bf16[2,256,1024]{2,1,0:T(8,128)(2,1)} %bitcast.19), channel_id=1, source_target_pairs={{8,0},{12,4},{9,1},{13,5},{10,2},{14,6},{11,3},{15,7},{24,16},{28,... | collective-permute-start | bytes 3145736 | tf_op jit(solution)/shard_map/ppermute | solution.py:17
Sparse Core Ops, SparseCore 0:
  10.1 83.4 all-gather.2
  95.2 21.1 all-gather.4
  125.6 188.6 reduce-scatter.4
  317.3 37.5 reduce-scatter.2
where the time goes:
time: 362 us; the launch traced here: 361 us
  waiting for transfers between devices  204 us (56%)
  local copies, waits for them, and re-layouts  68.3 us (19%)
  matrix products  58.9 us (16%)
  between operations  14 us (4%)
  other arithmetic  12.9 us (4%)
    ppermute x2, waiting for transfers between devices, passed_along(): return lax.ppermute(value, axis, pairs)  115 us
    all_gather x1, waiting for transfers between devices, per_device(): gathered = lax.all_gather(key_value, 'seq', axis=1, tiled=True)  77.7 us
    unnamed x31, local copies, waits for them, and re-layouts  16.9 us
    another operation x3, local copies, waits for them, and re-layouts, per_device(): jnp.stack([key_part, value_part])  15.1 us
    dot_general x1, matrix products, per_device(): jnp.einsum('nhqk,nqhd->nkhd', score_grad, query_blocks, preferred_element...  12.9 us
    dot_general x1, matrix products, per_device(): jnp.einsum('nhqk,nkhd->nqhd', score_grad, key_all, preferred_element_type...  11.5 us
    reduce_scatter x1, waiting for transfers between devices, per_device(): lax.psum_scatter(partial_value.astype(jnp.bfloat16), ('head', 'rep'), sca...  10.3 us
    transpose x1, local copies, waits for them, and re-layouts, per_device(): jnp.einsum('nhqk,nqhd->nkhd', score_grad, query_blocks, preferred_element...  9.03 us
  transfers between devices with their start and end apart: 6, of which 4 were waited for; matrix products, arithmetic and copies ran while one was open for 34% of the time, Pallas kernels for 0%

commit v1 on v0

v1 whole, which is shorter than its diff:
```python
import functools
import math

import jax
import jax.numpy as jnp
from jax import lax
from jax.experimental import pallas as pl
from jax.experimental.pallas import tpu as pltpu
from jax.sharding import PartitionSpec as P

HEAD_DIM = 128
BLOCK = 128
LEVELS = 5
SCALE = HEAD_DIM ** (-0.5)
LOG2_SCALE = SCALE * math.log2(math.e)
MASKED = -1e30

F32 = jnp.float32
BF16 = jnp.bfloat16
NT = (((1,), (1,)), ((), ()))


def shift(value, by):
    peers = lax.axis_size("seq")
    return lax.ppermute(
        value, "seq", [(i, i + by) for i in range(peers) if 0 <= i + by < peers]
    )


def cyclic(value, by):
    peers = lax.axis_size("seq")
    return lax.ppermute(value, "seq", [(i, (i + by) % peers) for i in range(peers)])


def swap(value, axis):
    return lax.ppermute(value, axis, [(0, 1), (1, 0)])


def dot(a, b):
    return jnp.dot(a, b, preferred_element_type=F32)


def dot_nt(a, b):
    return lax.dot_general(a, b, NT, preferred_element_type=F32)


def seen_tiles(blocks, peers):
    tiles = []
    for n in range(blocks):
        mine = [(0, n, None)]
        for level in range(LEVELS):
            target = n - 2**level
            distance = -(target // blocks)
            if distance < peers:
                mine.append((distance, target % blocks, level))
        tiles.append(mine)
    return tiles


def whole(shape):
    return pl.BlockSpec(shape, lambda h, *_: (0,) * len(shape))


def head_cols(rows):
    return pl.BlockSpec((rows, HEAD_DIM), lambda h, *_: (0, h))


def block_rows(n):
    return pl.ds(n * BLOCK, BLOCK)


def cat(parts, axis=0):
    return parts[0] if len(parts) == 1 else jnp.concatenate(parts, axis)


def causal_tile(transposed):
    rows = lax.broadcasted_iota(jnp.int32, (BLOCK, BLOCK), 0)
    cols = lax.broadcasted_iota(jnp.int32, (BLOCK, BLOCK), 1)
    return rows <= cols if transposed else rows >= cols


def forward_kernel(tiles, count, use_ref, q_ref, *refs):
    k_refs, v_refs = refs[:count], refs[count : 2 * count]
    mixed_ref, lse_ref = refs[2 * count :]
    head = pl.program_id(0)
    lane = lax.broadcasted_iota(jnp.int32, (BLOCK, HEAD_DIM), 1)
    causal = causal_tile(False)
    for n, mine in enumerate(tiles):
        keys = cat([k_refs[d][block_rows(b), :] for d, b, _ in mine])
        vals = cat([v_refs[d][block_rows(b), :] for d, b, _ in mine])
        raw = dot_nt(q_ref[block_rows(n), :], keys)
        parts = []
        for i, (_, _, level) in enumerate(mine):
            part = raw[:, i * BLOCK : (i + 1) * BLOCK]
            if level is None:
                part = jnp.where(causal, part, MASKED)
            else:
                part = jnp.where(use_ref[n * LEVELS + level] == 1, part, MASKED)
            parts.append(part)
        raw = cat(parts, 1)
        top = jnp.max(raw, 1, keepdims=True)
        grown = jnp.exp2((raw - top) * LOG2_SCALE)
        total = jnp.sum(grown, 1, keepdims=True)
        prob = grown * (1.0 / total)
        mixed_ref[block_rows(n), :] = dot(prob.astype(BF16), vals).astype(BF16)
        lse = top * LOG2_SCALE + jnp.log2(total)
        old = jnp.where(head == 0, 0.0, lse_ref[block_rows(n), :])
        lse_ref[block_rows(n), :] = jnp.where(lane == head, lse, old)


def query_kernel(tiles, count, heads_up, use_ref, q_ref, g_ref, lse_ref, *refs):
    k_refs, v_refs = refs[:count], refs[count : 2 * count]
    dq_ref, stats_ref, delta_ref = refs[2 * count :]
    head = pl.program_id(0)
    lane = lax.broadcasted_iota(jnp.int32, (BLOCK, HEAD_DIM), 1)
    causal = causal_tile(False)
    for n, mine in enumerate(tiles):
        rows = block_rows(n)
        keys = cat([k_refs[d][block_rows(b), :] for d, b, _ in mine])
        vals = cat([v_refs[d][block_rows(b), :] for d, b, _ in mine])
        lse = jnp.sum(jnp.where(lane == head, lse_ref[rows, :], 0.0), 1, keepdims=True)
        logits = dot_nt(q_ref[rows, :], keys) * LOG2_SCALE - lse
        parts = []
        for i, (_, _, level) in enumerate(mine):
            part = logits[:, i * BLOCK : (i + 1) * BLOCK]
            if level is None:
                part = jnp.where(causal, part, MASKED)
            else:
                part = jnp.where(use_ref[n * LEVELS + level] == 1, part, MASKED)
            parts.append(part)
        prob = jnp.exp2(cat(parts, 1))
        prob_grad = dot_nt(g_ref[rows, :], vals)
        delta = jnp.sum(prob * prob_grad, 1, keepdims=True)
        score_grad = (prob * (prob_grad - delta) * SCALE).astype(BF16)
        dq_ref[rows, :] = dot(score_grad, keys).astype(BF16)
        old = jnp.where(head == 0, 0.0, delta_ref[rows, :])
        delta_ref[rows, :] = jnp.where(lane == head, delta, old)

    @pl.when(head == pl.num_programs(0) - 1)
    def _():
        stats_ref[:heads_up, :] = lse_ref[...].T[:heads_up, :]
        stats_ref[heads_up : 2 * heads_up, :] = delta_ref[...].T[:heads_up, :]
        level_row = lax.broadcasted_iota(jnp.int32, (8, BLOCK), 0)
        for n in range(len(tiles)):
            rows = jnp.zeros((8, BLOCK), F32)
            for level in range(LEVELS):
                flag = jnp.where(use_ref[n * LEVELS + level] == 1, 1.0, 0.0)
                rows = jnp.where(level_row == level, flag, rows)
            stats_ref[2 * heads_up :, n * BLOCK : (n + 1) * BLOCK] = rows


def key_kernel(tiles, count, heads_up, k_ref, v_ref, *refs):
    q_refs, g_refs, s_refs = refs[:count], refs[count : 2 * count], refs[2 * count : 3 * count]
    dk_ref, dv_ref = refs[3 * count :]
    head = pl.program_id(0)
    causal = causal_tile(True)
    head_row = lax.broadcasted_iota(jnp.int32, (heads_up, BLOCK), 0)

    def of_head(stat):
        return jnp.sum(jnp.where(head_row == head, stat, 0.0), 0, keepdims=True)

    for b in range(len(tiles)):
        rows = block_rows(b)
        seers = [
            (d, n, level)
            for n, mine in enumerate(tiles)
            for d, block, level in mine
            if block == b
        ]
        ques = cat([q_refs[d][block_rows(n), :] for d, n, _ in seers])
        grads = cat([g_refs[d][block_rows(n), :] for d, n, _ in seers])
        raw = dot_nt(k_ref[rows, :], ques)
        prob_grad = dot_nt(v_ref[rows, :], grads)
        probs, score_grads = [], []
        for i, (d, n, level) in enumerate(seers):
            cols = slice(i * BLOCK, (i + 1) * BLOCK)
            here = slice(n * BLOCK, (n + 1) * BLOCK)
            lse = of_head(s_refs[d][:heads_up, here])
            delta = of_head(s_refs[d][heads_up : 2 * heads_up, here])
            if level is None:
                logits = jnp.where(causal, raw[:, cols] * LOG2_SCALE - lse, MASKED)
            else:
                row = 2 * heads_up + level
                off = lse + (1.0 - s_refs[d][row : row + 1, here]) * (-MASKED)
                logits = raw[:, cols] * LOG2_SCALE - off
            prob = jnp.exp2(logits)
            probs.append(prob.astype(BF16))
            score_grads.append((prob * (prob_grad[:, cols] - delta) * SCALE).astype(BF16))
        dv_ref[rows, :] = dot(cat(probs, 1), grads).astype(BF16)
        dk_ref[rows, :] = dot(cat(score_grads, 1), ques).astype(BF16)


def mixed_grad_kernel(count, place_ref, *refs):
    c_refs, w_ref, out_ref, acc_ref = refs[:count], refs[count], refs[count + 1], refs[count + 2]
    step = pl.program_id(0)
    for i in range(count):

        @pl.when(step == i)
        def _(i=i):
            part = dot(c_refs[i][...], w_ref[...])
            acc_ref[...] = part if i == 0 else acc_ref[...] + part

    @pl.when(step == count - 1)
    def _():
        out_ref[...] = acc_ref[...].astype(BF16)


def weight_grad_kernel(count, place_ref, c_ref, *refs):
    m_refs, out_ref = refs[:count], refs[count]
    total = None
    for p in range(count):
        part = dot(c_ref[place_ref[p]], m_refs[p][...])
        total = part if total is None else total + part
    out_ref[...] = total.astype(BF16)


VMEM_LIMIT = 48 * 1024 * 1024


def params():
    return pltpu.CompilerParams(
        dimension_semantics=("arbitrary",), vmem_limit_bytes=VMEM_LIMIT
    )


def cost(flops, bytes_accessed, exps=0):
    return pl.CostEstimate(
        flops=int(flops), bytes_accessed=int(bytes_accessed), transcendentals=int(exps)
    )


def features_here(value):
    heads, reps = lax.axis_size("head"), lax.axis_size("rep")
    if heads == 2 and reps == 2:
        h, r = lax.axis_index("head"), lax.axis_index("rep")
        across = swap(value, "head")
        blocks = [value, swap(value, "rep"), across, swap(across, "rep")]
        places = [2 * h + r, 2 * h + 1 - r, 2 * (1 - h) + r, 2 * (1 - h) + 1 - r]
        return blocks, jnp.stack(places).astype(jnp.int32)
    gathered = lax.all_gather(value, ("head", "rep"), axis=0)
    count = heads * reps
    return [gathered[i] for i in range(count)], jnp.arange(count, dtype=jnp.int32)


def summed_share(partial_value):
    heads, reps = lax.axis_size("head"), lax.axis_size("rep")
    if heads == 2 and reps == 2:
        rows, features = partial_value.shape
        h, r = lax.axis_index("head"), lax.axis_index("rep")
        parts = partial_value.reshape(rows, 2, 2, features // 4)
        give = lax.dynamic_index_in_dim(parts, 1 - r, 2, False).astype(BF16)
        keep = lax.dynamic_index_in_dim(parts, r, 2, False).astype(F32)
        keep = keep + swap(give, "rep").astype(F32)
        give = lax.dynamic_index_in_dim(keep, 1 - h, 1, False).astype(BF16)
        keep = lax.dynamic_index_in_dim(keep, h, 1, False)
        return (keep + swap(give, "head").astype(F32)).astype(BF16)
    return lax.psum_scatter(
        partial_value.astype(BF16), ("head", "rep"), scatter_dimension=1, tiled=True
    )


def per_device(queries, keys, values, out_weight, level_mask, cotangent):
    rows, columns = queries.shape
    features = out_weight.shape[0]
    heads = columns // HEAD_DIM
    heads_up = -(-heads // 8) * 8
    blocks = rows // BLOCK
    peers = lax.axis_size("seq")
    place = lax.axis_index("seq")
    tiles = seen_tiles(blocks, peers)
    distances = sorted({d for mine in tiles for d, _, _ in mine})
    count = len(distances)
    slot = {d: i for i, d in enumerate(distances)}
    tiles = [[(slot[d], b, level) for d, b, level in mine] for mine in tiles]
    pairs = sum(len(mine) for mine in tiles)

    def reached(value, sign):
        got = [value]
        for near, far in zip(distances, distances[1:]):
            got.append(shift(got[-1], sign * (far - near)))
        return got

    block_ids = place * blocks + jnp.arange(blocks, dtype=jnp.int32)
    offsets = 2 ** jnp.arange(LEVELS, dtype=jnp.int32)
    use = ((block_ids[:, None] >= offsets[None]) & (level_mask == 1)).astype(jnp.int32)
    use = use.reshape(-1)

    key_all = reached(keys, 1)
    value_all = reached(values, 1)
    query_all = reached(queries, -1)

    c_blocks, c_places = features_here(cotangent)
    group_count = len(c_blocks)
    part_cols = cotangent.shape[1]
    mixed_grad = pl.pallas_call(
        functools.partial(mixed_grad_kernel, group_count),
        grid_spec=pltpu.PrefetchScalarGridSpec(
            num_scalar_prefetch=1,
            grid=(group_count,),
            in_specs=[whole((rows, part_cols))] * group_count
            + [pl.BlockSpec((part_cols, columns), lambda i, at: (at[i], 0))],
            out_specs=whole((rows, columns)),
            scratch_shapes=[pltpu.VMEM((rows, columns), F32)],
        ),
        out_shape=jax.ShapeDtypeStruct((rows, columns), BF16),
        compiler_params=params(),
        cost_estimate=cost(2 * rows * columns * features, 2 * columns * features),
        name="mixed_grad",
    )(c_places, *c_blocks, out_weight)
    grad_all = reached(mixed_grad, -1)

    attention_flops = 2 * heads * pairs * BLOCK * BLOCK * HEAD_DIM
    array_bytes = 2 * rows * columns
    exps = heads * pairs * BLOCK * BLOCK
    smem = pl.BlockSpec(memory_space=pltpu.SMEM)
    cols = head_cols(rows)
    mixed_heads, lse = pl.pallas_call(
        functools.partial(forward_kernel, tiles, count),
        grid=(heads,),
        in_specs=[smem, cols] + [cols] * (2 * count),
        out_specs=[cols, whole((rows, HEAD_DIM))],
        out_shape=[
            jax.ShapeDtypeStruct((rows, columns), BF16),
            jax.ShapeDtypeStruct((rows, HEAD_DIM), F32),
        ],
        compiler_params=params(),
        cost_estimate=cost(2 * attention_flops, (2 * count + 2) * array_bytes, exps),
        name="attention_forward",
    )(use, queries, *key_all, *value_all)

    if peers <= 4:
        mixed_all = [mixed_heads] + [cyclic(mixed_heads, k) for k in range(1, peers)]
    else:
        gathered = lax.all_gather(mixed_heads, "seq", axis=0)
        mixed_all = [
            lax.dynamic_index_in_dim(gathered, (place - k) % peers, 0, False)
            for k in range(peers)
        ]

    partial_value = lax.dot_general(
        mixed_heads, out_weight, NT, preferred_element_type=F32
    ).astype(BF16)
    attended = summed_share(partial_value)

    stats_shape = (2 * heads_up + 8, rows)
    q_grad, stats = pl.pallas_call(
        functools.partial(query_kernel, tiles, count, heads_up),
        grid=(heads,),
        in_specs=[smem, cols, cols, whole((rows, HEAD_DIM))] + [cols] * (2 * count),
        out_specs=[cols, whole(stats_shape)],
        out_shape=[
            jax.ShapeDtypeStruct((rows, columns), BF16),
            jax.ShapeDtypeStruct(stats_shape, F32),
        ],
        scratch_shapes=[pltpu.VMEM((rows, HEAD_DIM), F32)],
        compiler_params=params(),
        cost_estimate=cost(3 * attention_flops, (2 * count + 3) * array_bytes, exps),
        name="attention_query_grad",
    )(use, queries, mixed_grad, lse, *key_all, *value_all)

    stats_all = [stats] + [shift(stats, -d) for d in distances[1:]]
    k_grad, v_grad = pl.pallas_call(
        functools.partial(key_kernel, tiles, count, heads_up),
        grid=(heads,),
        in_specs=[cols] * (2 + 2 * count) + [whole(stats_shape)] * count,
        out_specs=[cols, cols],
        out_shape=[jax.ShapeDtypeStruct((rows, columns), BF16)] * 2,
        compiler_params=params(),
        cost_estimate=cost(4 * attention_flops, (2 * count + 4) * array_bytes, exps),
        name="attention_key_grad",
    )(keys, values, *query_all, *grad_all, *stats_all)

    h, r = lax.axis_index("head"), lax.axis_index("rep")
    n_head, n_rep = lax.axis_size("head"), lax.axis_size("rep")
    step_of = lambda i: (i // n_rep) + n_head * (i % n_rep)
    mine = h * n_rep + r
    wanted = (place + step_of(mine)) % peers
    out_block = sum(
        jnp.where(c_places[i] == wanted, c_blocks[i], 0) for i in range(group_count)
    )
    links = []
    for s in range(peers):
        for q in range(group_count):
            links.append((s * group_count + q, ((s + step_of(q)) % peers) * group_count + q))
    got = lax.ppermute(out_block, ("seq", "head", "rep"), links)
    ct_blocks, ct_places = features_here(got)
    ct = jnp.stack([block.T for block in ct_blocks])
    steps = step_of(ct_places)
    ct_at = jnp.sum(
        jnp.where(steps[None] == jnp.arange(peers)[:, None], jnp.arange(group_count)[None], 0), 1
    ).astype(jnp.int32)
    f_rows = min(256, part_cols)
    weight_grad = pl.pallas_call(
        functools.partial(weight_grad_kernel, peers),
        grid_spec=pltpu.PrefetchScalarGridSpec(
            num_scalar_prefetch=1,
            grid=(part_cols // f_rows,),
            in_specs=[pl.BlockSpec((group_count, f_rows, rows), lambda i, at: (0, i, 0))]
            + [whole((rows, columns))] * peers,
            out_specs=pl.BlockSpec((f_rows, columns), lambda i, at: (i, 0)),
        ),
        out_shape=jax.ShapeDtypeStruct((part_cols, columns), BF16),
        compiler_params=params(),
        cost_estimate=cost(
            2 * part_cols * columns * rows * peers, 2 * array_bytes * peers + 2 * part_cols * columns
        ),
        name="weight_grad",
    )(ct_at, ct, *mixed_all)
    return (attended, q_grad, k_grad, v_grad, weight_grad)


def solution(mesh):
    shared = P(("groups", "seq"), ("head", "rep"))
    return jax.shard_map(
        per_device,
        mesh=mesh,
        in_specs=(shared, shared, shared, P(None, ("head", "rep")), P(("groups", "seq"), None), shared),
        out_specs=(shared,) * 5,
        check_vma=False,
    )
```

time: 362 us -> 199 us (0.55)
  the two profiles are of different devices: /device:TPU:0 before, /device:TPU:9 now
where the time goes in v1:
time: 199 us; the launch traced here: 198 us
  waiting for transfers between devices  79.8 us (40%)
  starting transfers between devices  43 us (22%)
  Pallas kernels  36.9 us (19%)
  local copies, waits for them, and re-layouts  21 us (11%)
  other arithmetic  8.61 us (4%)
  matrix products  7.26 us (4%)
    ppermute x10, waiting for transfers between devices, shift(): lax.ppermute(value, 'seq', [(i, i + by) for i in range(peers) if 0 <= i +...  45.8 us
    ppermute x3, waiting for transfers between devices, cyclic(): lax.ppermute(value, 'seq', [(i, (i + by) % peers) for i in range(peers)])  34 us
    ppermute x10, starting transfers between devices, shift(): lax.ppermute(value, 'seq', [(i, i + by) for i in range(peers) if 0 <= i +...  25.2 us
    ppermute x8, starting transfers between devices, swap(): return lax.ppermute(value, axis, [(0, 1), (1, 0)])  9.55 us
    pallas_call x1, Pallas kernels, per_device(): pl.pallas_call(functools.partial(forward_kernel, tiles, count), grid=(hea...  8.97 us
    pallas_call x1, Pallas kernels, per_device(): pl.pallas_call(functools.partial(query_kernel, tiles, count, heads_up), g...  8.63 us
    pallas_call x1, Pallas kernels, per_device(): pl.pallas_call(functools.partial(key_kernel, tiles, count, heads_up), gri...  7.77 us
    dot_general x1, matrix products, per_device(): lax.dot_general(mixed_heads, out_weight, NT, preferred_element_type=F32)  7.26 us
  transfers between devices with their start and end apart: 22, of which 10 were waited for; matrix products, arithmetic and copies ran while one was open for 16% of the time, Pallas kernels for 16%

profile of v1, /device:TPU:9, one launch (start us, length us, event | category | flops | bytes accessed | tf_op | source)
XLA Modules:
  0.0 197.5 jit_solution(17271203961386089438)
XLA Ops:
  0.6 3.2 %collective-permute-start = (bf16[256,1024]{1,0:T(8,128)(2,1)}, bf16[256,1024]{1,0:T(8,128)(2,1)S(1)}, u32[]{:S(2)}, u32[]{:S(2)}) collective-permute-start(bf16[256,1024]{1,0:T(8,128)(2,1)} %k_ref.1), channel_id=1, source_target_pairs={{0,4},{4,8},{8,12},{1,5},{5,9},{9,13},{2,6},{6,10},{10,14},{3,7},{... | collective-permute-start | bytes 1572872 | tf_op jit(solution)/shard_map/ppermute | solution.py:25
  3.8 3.2 %collective-permute-start.2 = (bf16[256,1024]{1,0:T(8,128)(2,1)}, bf16[256,1024]{1,0:T(8,128)(2,1)S(1)}, u32[]{:S(2)}, u32[]{:S(2)}) collective-permute-start(bf16[256,1024]{1,0:T(8,128)(2,1)} %v_ref.1), channel_id=1, source_target_pairs={{0,4},{4,8},{8,12},{1,5},{5,9},{9,13},{2,6},{6,10},{10,14},{3,7},{... | collective-permute-start | bytes 1572872 | tf_op jit(solution)/shard_map/ppermute | solution.py:25
  10.3 5.2 %collective-permute-done.refs_1_ = bf16[256,1024]{1,0:T(8,128)(2,1)S(1)} collective-permute-done((bf16[256,1024]{1,0:T(8,128)(2,1)}, bf16[256,1024]{1,0:T(8,128)(2,1)S(1)}, u32[]{:S(2)}, u32[]{:S(2)}) %collective-permute-start) | collective-permute-done | bytes 524320 | tf_op jit(solution)/shard_map/ppermute | solution.py:25
  15.5 3.2 %collective-permute-start.1 = (bf16[256,1024]{1,0:T(8,128)(2,1)S(1)}, bf16[256,1024]{1,0:T(8,128)(2,1)S(1)}, u32[]{:S(2)}, u32[]{:S(2)}) collective-permute-start(bf16[256,1024]{1,0:T(8,128)(2,1)S(1)} %collective-permute-done.refs_1_), channel_id=1, source_target_pairs={{0,4},{4,8},{8,12},{1,5},{5,9},{9,13},{2,6},{6,10},{10,14},{3,7},{... | collective-permute-start | bytes 1572872 | tf_op jit(solution)/shard_map/ppermute | solution.py:25
  18.7 8.0 %collective-permute-done.2.refs_4_ = bf16[256,1024]{1,0:T(8,128)(2,1)S(1)} collective-permute-done((bf16[256,1024]{1,0:T(8,128)(2,1)}, bf16[256,1024]{1,0:T(8,128)(2,1)S(1)}, u32[]{:S(2)}, u32[]{:S(2)}) %collective-permute-start.2) | collective-permute-done | bytes 524320 | tf_op jit(solution)/shard_map/ppermute | solution.py:25
  26.8 3.2 %collective-permute-start.3 = (bf16[256,1024]{1,0:T(8,128)(2,1)S(1)}, bf16[256,1024]{1,0:T(8,128)(2,1)S(1)}, u32[]{:S(2)}, u32[]{:S(2)}) collective-permute-start(bf16[256,1024]{1,0:T(8,128)(2,1)S(1)} %collective-permute-done.2.refs_4_), channel_id=1, source_target_pairs={{0,4},{4,8},{8,12},{1,5},{5,9},{9,13},{2,6},{6,10},{10,14},{3,7},{... | collective-permute-start | bytes 1572872 | tf_op jit(solution)/shard_map/ppermute | solution.py:25
  30.0 3.0 %collective-permute-start.6 = (bf16[256,1024]{0,1:T(8,128)(2,1)}, bf16[256,1024]{0,1:T(8,128)(2,1)S(1)}, u32[]{:S(2)}, u32[]{:S(2)}) collective-permute-start(bf16[256,1024]{0,1:T(8,128)(2,1)} %copy.21), channel_id=1, source_target_pairs={{0,1},{1,0},{2,3},{3,2},{4,5},{5,4},{6,7},{7,6},{8,9},{9,8},{10,11... | collective-permute-start | bytes 1572872 | tf_op jit(solution)/shard_map/ppermute | solution.py:36
  33.9 4.1 %collective-permute-done.1.refs_2_ = bf16[256,1024]{1,0:T(8,128)(2,1)S(1)} collective-permute-done((bf16[256,1024]{1,0:T(8,128)(2,1)S(1)}, bf16[256,1024]{1,0:T(8,128)(2,1)S(1)}, u32[]{:S(2)}, u32[]{:S(2)}) %collective-permute-start.1) | collective-permute-done | bytes 524320 | tf_op jit(solution)/shard_map/ppermute | solution.py:25
  38.0 11.2 %collective-permute-done.3.refs_5_ = bf16[256,1024]{1,0:T(8,128)(2,1)S(1)} collective-permute-done((bf16[256,1024]{1,0:T(8,128)(2,1)S(1)}, bf16[256,1024]{1,0:T(8,128)(2,1)S(1)}, u32[]{:S(2)}, u32[]{:S(2)}) %collective-permute-start.3) | collective-permute-done | bytes 524320 | tf_op jit(solution)/shard_map/ppermute | solution.py:25
  52.4 9.0 %attention_forward.1 = (bf16[256,1024]{1,0:T(8,128)(2,1)}, f32[256,128]{1,0:T(8,128)S(1)}) custom-call(s32[10]{0:T(128)S(1)} %reshape.264.use_ref, bf16[256,1024]{1,0:T(8,128)(2,1)S(1)} %copy-done, bf16[256,1024]{1,0:T(8,128)(2,1)S(1)} %copy-done.2, bf16[256,1024]{1,0:T(8,128)(2,1)S(1)} %collective-permute-done.refs_1_, ...), custom_call_target="tpu_custom_call" | custom-call | flops 536870912 | bytes 4194304 | tf_op jit(solution)/shard_map/attention_forward/pallas_call | solution.py:317
  61.3 7.3 %convolution_convert_fusion = bf16[256,4096]{1,0:T(8,128)(2,1)} fusion(bf16[256,1024]{1,0:T(8,128)(2,1)} %get-tuple-element.11.refs_0_, bf16[4096,1024]{1,0:T(8,128)(2,1)} %refs_4_.1), kind=kOutput, calls=%fused_computation | convolution fusion | flops 2148532224 | bytes 11010048 | tf_op jit(solution)/shard_map/dot_general | solution.py:340
  68.6 4.5 %reshape.262 = bf16[256,2,2,1024]{3,2,1,0:T(2,128)(2,1)} reshape(bf16[256,4096]{1,0:T(8,128)(2,1)} %convolution_convert_fusion) | data formatting | bytes 4194304 | tf_op jit(solution)/shard_map/reshape | solution.py:250
  74.1 5.5 %collective-permute-start.15 = (bf16[256,1024]{0,1:T(8,128)(2,1)}, bf16[256,1024]{0,1:T(8,128)(2,1)}, u32[]{:S(2)}, u32[]{:S(2)}) collective-permute-start(bf16[256,1024]{0,1:T(8,128)(2,1)} %select_add_fusion), channel_id=1, source_target_pairs={{0,0},{1,9},{2,6},{3,15},{4,4},{5,13},{6,10},{7,3},{8,8},{9,1},{10... | collective-permute-start | bytes 1572872 | tf_op jit(solution)/shard_map/ppermute | solution.py:385
  79.5 5.6 %constant_dynamic-slice_fusion.1 = (bf16[256,2,1,1024]{3,2,1,0:T(2,128)(2,1)}, bf16[256,2,1,1024]{3,2,1,0:T(2,128)(2,1)S(1)}) fusion(bf16[256,2,2,1024]{3,2,1,0:T(2,128)(2,1)S(1)} %copy-done.15, s32[]{:T(128)S(6)} %select_n.130, s32[]{:T(128)S(6)} %select_n.131), kind=kLoop, calls=%fused_computation.25 | loop fusion | bytes 4194312 | tf_op jit(solution)/shard_map/jit(dynamic_index_in_dim)/dynamic_slice | solution.py:252
  93.6 6.1 %mixed_grad.1.g_ref.refs_3_ = bf16[256,1024]{1,0:T(8,128)(2,1)S(1)} custom-call(s32[4]{0:T(128)S(1)} %get-tuple-element.18.place_ref, bf16[256,1024]{1,0:T(8,128)(2,1)S(1)} %copy-done.6, bf16[256,1024]{1,0:T(8,128)(2,1)S(1)} %copy.23.refs_1_, bf16[256,1024]{1,0:T(8,128)(2,1)S(1)} %copy.24.refs_2_, bf16[256,1024]{1,0:T(8,128)(2,1)S(1)} %copy.25.refs_3_, ...), custom_call_target="tpu_custom_call" | custom-call | flops 2147483648 | bytes 8388608 | tf_op jit(solution)/shard_map/mixed_grad/pallas_call | solution.py:295
  107.4 7.4 %collective-permute-done.11.refs_4_ = bf16[256,1024]{1,0:T(8,128)(2,1)S(1)} collective-permute-done((bf16[256,1024]{1,0:T(8,128)(2,1)S(1)}, bf16[256,1024]{1,0:T(8,128)(2,1)S(1)}, u32[]{:S(2)}, u32[]{:S(2)}) %collective-permute-start.11) | collective-permute-done | bytes 524320 | tf_op jit(solution)/shard_map/ppermute | solution.py:25
  123.1 8.6 %attention_query_grad.1 = (bf16[256,1024]{1,0:T(8,128)(2,1)}, f32[24,256]{1,0:T(8,128)S(1)}) custom-call(s32[10]{0:T(128)S(1)} %reshape.264.use_ref, bf16[256,1024]{1,0:T(8,128)(2,1)S(1)} %copy-done.1, bf16[256,1024]{1,0:T(8,128)(2,1)S(1)} %mixed_grad.1.g_ref.refs_3_, f32[256,128]{1,0:T(8,128)S(1)} %get-tuple-element.12.lse_ref, ...), custom_call_target="tpu_custom_call" | custom-call | flops 805306368 | bytes 4718592 | tf_op jit(solution)/shard_map/attention_query_grad/pallas_call | solution.py:346
  133.6 4.1 %collective-permute-done.13.refs_7_ = f32[24,256]{1,0:T(8,128)S(1)} collective-permute-done((f32[24,256]{1,0:T(8,128)S(1)}, f32[24,256]{1,0:T(8,128)S(1)}, u32[]{:S(2)}, u32[]{:S(2)}) %collective-permute-start.13) | collective-permute-done | bytes 24608 | tf_op jit(solution)/shard_map/ppermute | solution.py:25
  139.2 4.1 %collective-permute-done.14.refs_8_ = f32[24,256]{1,0:T(8,128)S(1)} collective-permute-done((f32[24,256]{1,0:T(8,128)S(1)}, f32[24,256]{1,0:T(8,128)S(1)}, u32[]{:S(2)}, u32[]{:S(2)}) %collective-permute-start.14) | collective-permute-done | bytes 24608 | tf_op jit(solution)/shard_map/ppermute | solution.py:25
  143.2 2.8 %collective-permute-start.20 = (bf16[256,1024]{1,0:T(8,128)(2,1)}, bf16[256,1024]{1,0:T(8,128)(2,1)S(1)}, u32[]{:S(2)}, u32[]{:S(2)}) collective-permute-start(bf16[256,1024]{1,0:T(8,128)(2,1)} %get-tuple-element.11.refs_0_), channel_id=1, source_target_pairs={{0,8},{4,12},{8,0},{12,4},{1,9},{5,13},{9,1},{13,5},{2,10},{6,14},... | collective-permute-start | bytes 1572872 | tf_op jit(solution)/shard_map/ppermute | solution.py:32
  146.1 7.8 %attention_key_grad.1 = (bf16[256,1024]{1,0:T(8,128)(2,1)}, bf16[256,1024]{1,0:T(8,128)(2,1)}) custom-call(bf16[256,1024]{1,0:T(8,128)(2,1)S(1)} %copy-done.3, bf16[256,1024]{1,0:T(8,128)(2,1)S(1)} %copy-done.5, bf16[256,1024]{1,0:T(8,128)(2,1)S(1)} %copy-done.1, bf16[256,1024]{1,0:T(8,128)(2,1)} %collective-permute-done.9.refs_1_, ...), custom_call_target="tpu_custom_call" | custom-call | flops 1073741824 | bytes 5242880 | tf_op jit(solution)/shard_map/attention_key_grad/pallas_call | solution.py:362
  158.1 28.4 %collective-permute-done.20.refs_2_ = bf16[256,1024]{1,0:T(8,128)(2,1)S(1)} collective-permute-done((bf16[256,1024]{1,0:T(8,128)(2,1)}, bf16[256,1024]{1,0:T(8,128)(2,1)S(1)}, u32[]{:S(2)}, u32[]{:S(2)}) %collective-permute-start.20) | collective-permute-done | bytes 524320 | tf_op jit(solution)/shard_map/ppermute | solution.py:32
  186.4 5.6 %collective-permute-done.21.refs_3_ = bf16[256,1024]{1,0:T(8,128)(2,1)S(1)} collective-permute-done((bf16[256,1024]{1,0:T(8,128)(2,1)}, bf16[256,1024]{1,0:T(8,128)(2,1)S(1)}, u32[]{:S(2)}, u32[]{:S(2)}) %collective-permute-start.21) | collective-permute-done | bytes 524320 | tf_op jit(solution)/shard_map/ppermute | solution.py:32
  192.1 5.5 %weight_grad.1 = bf16[1024,1024]{1,0:T(8,128)(2,1)} custom-call(s32[4]{0:T(128)S(1)} %select_reduce_fusion.place_ref, bf16[4,1024,256]{2,1,0:T(8,128)(2,1)S(1)} %pad_maximum_fusion.c_ref, bf16[256,1024]{1,0:T(8,128)(2,1)} %get-tuple-element.11.refs_0_, bf16[256,1024]{1,0:T(8,128)(2,1)S(1)} %collective-permute-done.19.refs_1_, ...), custom_call_target="tpu_custom_call" | custom-call | flops 2147483648 | bytes 6291456 | tf_op jit(solution)/shard_map/weight_grad/pallas_call | solution.py:393
  (86 shorter events, 40.1 us)
Async XLA Ops:
  0.6 14.9 %collective-permute-start = (bf16[256,1024]{1,0:T(8,128)(2,1)}, bf16[256,1024]{1,0:T(8,128)(2,1)S(1)}, u32[]{:S(2)}, u32[]{:S(2)}) collective-permute-start(bf16[256,1024]{1,0:T(8,128)(2,1)} %k_ref.1), channel_id=1, source_target_pairs={{0,4},{4,8},{8,12},{1,5},{5,9},{9,13},{2,6},{6,10},{10,14},{3,7},{... | collective-permute-start | bytes 1572872 | tf_op jit(solution)/shard_map/ppermute | solution.py:25
  3.8 22.9 %collective-permute-start.2 = (bf16[256,1024]{1,0:T(8,128)(2,1)}, bf16[256,1024]{1,0:T(8,128)(2,1)S(1)}, u32[]{:S(2)}, u32[]{:S(2)}) collective-permute-start(bf16[256,1024]{1,0:T(8,128)(2,1)} %v_ref.1), channel_id=1, source_target_pairs={{0,4},{4,8},{8,12},{1,5},{5,9},{9,13},{2,6},{6,10},{10,14},{3,7},{... | collective-permute-start | bytes 1572872 | tf_op jit(solution)/shard_map/ppermute | solution.py:25
  9.1 24.8 %collective-permute-start.7 = (bf16[256,1024]{0,1:T(8,128)(2,1)}, bf16[256,1024]{0,1:T(8,128)(2,1)S(1)}, u32[]{:S(2)}, u32[]{:S(2)}) collective-permute-start(bf16[256,1024]{0,1:T(8,128)(2,1)} %copy.21), channel_id=1, source_target_pairs={{0,2},{2,0},{1,3},{3,1},{4,6},{6,4},{5,7},{7,5},{8,10},{10,8},{9,1... | collective-permute-start | bytes 1572872 | tf_op jit(solution)/shard_map/ppermute | solution.py:36
  15.5 53.1 %copy-start.7 = (bf16[256,1024]{1,0:T(8,128)(2,1)}, bf16[256,1024]{1,0:T(8,128)(2,1)S(1)}, u32[]{:S(2)}) copy-start(bf16[256,1024]{1,0:T(8,128)(2,1)S(1)} %collective-permute-done.refs_1_) | copy-start | bytes 1572868
  15.5 22.5 %collective-permute-start.1 = (bf16[256,1024]{1,0:T(8,128)(2,1)S(1)}, bf16[256,1024]{1,0:T(8,128)(2,1)S(1)}, u32[]{:S(2)}, u32[]{:S(2)}) collective-permute-start(bf16[256,1024]{1,0:T(8,128)(2,1)S(1)} %collective-permute-done.refs_1_), channel_id=1, source_target_pairs={{0,4},{4,8},{8,12},{1,5},{5,9},{9,13},{2,6},{6,10},{10,14},{3,7},{... | collective-permute-start | bytes 1572872 | tf_op jit(solution)/shard_map/ppermute | solution.py:25
  26.8 41.8 %copy-start.9 = (bf16[256,1024]{1,0:T(8,128)(2,1)}, bf16[256,1024]{1,0:T(8,128)(2,1)S(1)}, u32[]{:S(2)}) copy-start(bf16[256,1024]{1,0:T(8,128)(2,1)S(1)} %collective-permute-done.2.refs_4_) | copy-start | bytes 1572868
  26.8 22.5 %collective-permute-start.3 = (bf16[256,1024]{1,0:T(8,128)(2,1)S(1)}, bf16[256,1024]{1,0:T(8,128)(2,1)S(1)}, u32[]{:S(2)}, u32[]{:S(2)}) collective-permute-start(bf16[256,1024]{1,0:T(8,128)(2,1)S(1)} %collective-permute-done.2.refs_4_), channel_id=1, source_target_pairs={{0,4},{4,8},{8,12},{1,5},{5,9},{9,13},{2,6},{6,10},{10,14},{3,7},{... | collective-permute-start | bytes 1572872 | tf_op jit(solution)/shard_map/ppermute | solution.py:25
  30.0 43.1 %collective-permute-start.6 = (bf16[256,1024]{0,1:T(8,128)(2,1)}, bf16[256,1024]{0,1:T(8,128)(2,1)S(1)}, u32[]{:S(2)}, u32[]{:S(2)}) collective-permute-start(bf16[256,1024]{0,1:T(8,128)(2,1)} %copy.21), channel_id=1, source_target_pairs={{0,1},{1,0},{2,3},{3,2},{4,5},{5,4},{6,7},{7,6},{8,9},{9,8},{10,11... | collective-permute-start | bytes 1572872 | tf_op jit(solution)/shard_map/ppermute | solution.py:36
  33.9 39.2 %collective-permute-start.8 = (bf16[256,1024]{0,1:T(8,128)(2,1)S(1)}, bf16[256,1024]{0,1:T(8,128)(2,1)}, u32[]{:S(2)}, u32[]{:S(2)}) collective-permute-start(bf16[256,1024]{0,1:T(8,128)(2,1)S(1)} %collective-permute-done.7), channel_id=1, source_target_pairs={{0,1},{1,0},{2,3},{3,2},{4,5},{5,4},{6,7},{7,6},{8,9},{9,8},{10,11... | collective-permute-start | bytes 1572872 | tf_op jit(solution)/shard_map/ppermute | solution.py:36
  74.1 27.6 %collective-permute-start.15 = (bf16[256,1024]{0,1:T(8,128)(2,1)}, bf16[256,1024]{0,1:T(8,128)(2,1)}, u32[]{:S(2)}, u32[]{:S(2)}) collective-permute-start(bf16[256,1024]{0,1:T(8,128)(2,1)} %select_add_fusion), channel_id=1, source_target_pairs={{0,0},{1,9},{2,6},{3,15},{4,4},{5,13},{6,10},{7,3},{8,8},{9,1},{10... | collective-permute-start | bytes 1572872 | tf_op jit(solution)/shard_map/ppermute | solution.py:385
  86.8 32.1 %collective-permute-start.4 = (bf16[256,2,1024]{2,0,1:T(8,128)(2,1)}, bf16[256,2,1024]{2,0,1:T(8,128)(2,1)}, u32[]{:S(2)}, u32[]{:S(2)}) collective-permute-start(bf16[256,2,1024]{2,0,1:T(8,128)(2,1)} %bitcast.31), channel_id=1, source_target_pairs={{0,1},{1,0},{2,3},{3,2},{4,5},{5,4},{6,7},{7,6},{8,9},{9,8},{10,11... | collective-permute-start | bytes 3145736 | tf_op jit(solution)/shard_map/ppermute | solution.py:36
  88.3 15.4 %collective-permute-start.9 = (bf16[256,1024]{1,0:T(8,128)(2,1)S(1)}, bf16[256,1024]{1,0:T(8,128)(2,1)}, u32[]{:S(2)}, u32[]{:S(2)}) collective-permute-start(bf16[256,1024]{1,0:T(8,128)(2,1)S(1)} %copy-done.1), channel_id=1, source_target_pairs={{4,0},{8,4},{12,8},{5,1},{9,5},{13,9},{6,2},{10,6},{14,10},{7,3},{... | collective-permute-start | bytes 1572872 | tf_op jit(solution)/shard_map/ppermute | solution.py:25
  99.7 15.1 %collective-permute-start.11 = (bf16[256,1024]{1,0:T(8,128)(2,1)S(1)}, bf16[256,1024]{1,0:T(8,128)(2,1)S(1)}, u32[]{:S(2)}, u32[]{:S(2)}) collective-permute-start(bf16[256,1024]{1,0:T(8,128)(2,1)S(1)} %mixed_grad.1.g_ref.refs_3_), channel_id=1, source_target_pairs={{4,0},{8,4},{12,8},{5,1},{9,5},{13,9},{6,2},{10,6},{14,10},{7,3},{... | collective-permute-start | bytes 1572872 | tf_op jit(solution)/shard_map/ppermute | solution.py:25
  101.7 15.7 %collective-permute-start.17 = (bf16[256,1024]{0,1:T(8,128)(2,1)}, bf16[256,1024]{0,1:T(8,128)(2,1)}, u32[]{:S(2)}, u32[]{:S(2)}) collective-permute-start(bf16[256,1024]{0,1:T(8,128)(2,1)} %collective-permute-done.15), channel_id=1, source_target_pairs={{0,2},{2,0},{1,3},{3,1},{4,6},{6,4},{5,7},{7,5},{8,10},{10,8},{9,1... | collective-permute-start | bytes 1572872 | tf_op jit(solution)/shard_map/ppermute | solution.py:36
  103.7 28.0 %collective-permute-start.10 = (bf16[256,1024]{1,0:T(8,128)(2,1)}, bf16[256,1024]{1,0:T(8,128)(2,1)S(1)}, u32[]{:S(2)}, u32[]{:S(2)}) collective-permute-start(bf16[256,1024]{1,0:T(8,128)(2,1)} %collective-permute-done.9.refs_1_), channel_id=1, source_target_pairs={{4,0},{8,4},{12,8},{5,1},{9,5},{13,9},{6,2},{10,6},{14,10},{7,3},{... | collective-permute-start | bytes 1572872 | tf_op jit(solution)/shard_map/ppermute | solution.py:25
  106.0 40.1 %collective-permute-start.16 = (bf16[256,1024]{0,1:T(8,128)(2,1)}, bf16[256,1024]{0,1:T(8,128)(2,1)}, u32[]{:S(2)}, u32[]{:S(2)}) collective-permute-start(bf16[256,1024]{0,1:T(8,128)(2,1)} %collective-permute-done.15), channel_id=1, source_target_pairs={{0,1},{1,0},{2,3},{3,2},{4,5},{5,4},{6,7},{7,6},{8,9},{9,8},{10,11... | collective-permute-start | bytes 1572872 | tf_op jit(solution)/shard_map/ppermute | solution.py:36
  114.8 28.5 %collective-permute-start.12 = (bf16[256,1024]{1,0:T(8,128)(2,1)S(1)}, bf16[256,1024]{1,0:T(8,128)(2,1)}, u32[]{:S(2)}, u32[]{:S(2)}) collective-permute-start(bf16[256,1024]{1,0:T(8,128)(2,1)S(1)} %collective-permute-done.11.refs_4_), channel_id=1, source_target_pairs={{4,0},{8,4},{12,8},{5,1},{9,5},{13,9},{6,2},{10,6},{14,10},{7,3},{... | collective-permute-start | bytes 1572872 | tf_op jit(solution)/shard_map/ppermute | solution.py:25
  117.3 36.5 %collective-permute-start.18 = (bf16[256,1024]{0,1:T(8,128)(2,1)}, bf16[256,1024]{0,1:T(8,128)(2,1)}, u32[]{:S(2)}, u32[]{:S(2)}) collective-permute-start(bf16[256,1024]{0,1:T(8,128)(2,1)} %collective-permute-done.17), channel_id=1, source_target_pairs={{0,1},{1,0},{2,3},{3,2},{4,5},{5,4},{6,7},{7,6},{8,9},{9,8},{10,11... | collective-permute-start | bytes 1572872 | tf_op jit(solution)/shard_map/ppermute | solution.py:36
  122.6 33.1 %collective-permute-start.5 = (bf16[256,1024]{1,0:T(8,128)(2,1)}, bf16[256,1024]{1,0:T(8,128)(2,1)}, u32[]{:S(2)}, u32[]{:S(2)}) collective-permute-start(bf16[256,1024]{1,0:T(8,128)(2,1)} %fusion.1), channel_id=1, source_target_pairs={{0,2},{2,0},{1,3},{3,1},{4,6},{6,4},{5,7},{7,5},{8,10},{10,8},{9,1... | collective-permute-start | bytes 1572872 | tf_op jit(solution)/shard_map/ppermute | solution.py:36
  131.7 6.0 %collective-permute-start.13 = (f32[24,256]{1,0:T(8,128)S(1)}, f32[24,256]{1,0:T(8,128)S(1)}, u32[]{:S(2)}, u32[]{:S(2)}) collective-permute-start(f32[24,256]{1,0:T(8,128)S(1)} %get-tuple-element.14.refs_6_), channel_id=1, source_target_pairs={{4,0},{8,4},{12,8},{5,1},{9,5},{13,9},{6,2},{10,6},{14,10},{7,3},{... | collective-permute-start | bytes 73736 | tf_op jit(solution)/shard_map/ppermute | solution.py:25
  137.8 5.5 %collective-permute-start.14 = (f32[24,256]{1,0:T(8,128)S(1)}, f32[24,256]{1,0:T(8,128)S(1)}, u32[]{:S(2)}, u32[]{:S(2)}) collective-permute-start(f32[24,256]{1,0:T(8,128)S(1)} %get-tuple-element.14.refs_6_), channel_id=1, source_target_pairs={{8,0},{12,4},{9,1},{13,5},{10,2},{14,6},{11,3},{15,7},{24,16},{28,... | collective-permute-start | bytes 73736 | tf_op jit(solution)/shard_map/ppermute | solution.py:25
  143.2 14.8 %collective-permute-start.19 = (bf16[256,1024]{1,0:T(8,128)(2,1)}, bf16[256,1024]{1,0:T(8,128)(2,1)S(1)}, u32[]{:S(2)}, u32[]{:S(2)}) collective-permute-start(bf16[256,1024]{1,0:T(8,128)(2,1)} %get-tuple-element.11.refs_0_), channel_id=1, source_target_pairs={{0,4},{4,8},{8,12},{12,0},{1,5},{5,9},{9,13},{13,1},{2,6},{6,10},{... | collective-permute-start | bytes 1572872 | tf_op jit(solution)/shard_map/ppermute | solution.py:32
  143.2 43.2 %collective-permute-start.20 = (bf16[256,1024]{1,0:T(8,128)(2,1)}, bf16[256,1024]{1,0:T(8,128)(2,1)S(1)}, u32[]{:S(2)}, u32[]{:S(2)}) collective-permute-start(bf16[256,1024]{1,0:T(8,128)(2,1)} %get-tuple-element.11.refs_0_), channel_id=1, source_target_pairs={{0,8},{4,12},{8,0},{12,4},{1,9},{5,13},{9,1},{13,5},{2,10},{6,14},... | collective-permute-start | bytes 1572872 | tf_op jit(solution)/shard_map/ppermute | solution.py:32
  146.1 46.0 %collective-permute-start.21 = (bf16[256,1024]{1,0:T(8,128)(2,1)}, bf16[256,1024]{1,0:T(8,128)(2,1)S(1)}, u32[]{:S(2)}, u32[]{:S(2)}) collective-permute-start(bf16[256,1024]{1,0:T(8,128)(2,1)} %get-tuple-element.11.refs_0_), channel_id=1, source_target_pairs={{0,12},{4,0},{8,4},{12,8},{1,13},{5,1},{9,5},{13,9},{2,14},{6,2},{... | collective-permute-start | bytes 1572872 | tf_op jit(solution)/shard_map/ppermute | solution.py:32
  (19 other events, 151.3 us)

commit v2 on v1

v2 whole, which is shorter than its diff:
```python
import functools
import math

import jax
import jax.numpy as jnp
from jax import lax
from jax.experimental import pallas as pl
from jax.experimental.pallas import tpu as pltpu
from jax.sharding import PartitionSpec as P

HEAD_DIM = 128
BLOCK = 128
LEVELS = 5
SCALE = HEAD_DIM ** (-0.5)
LOG2_SCALE = SCALE * math.log2(math.e)
MASKED = -1e30

F32 = jnp.float32
BF16 = jnp.bfloat16
NT = (((1,), (1,)), ((), ()))
TN = (((0,), (0,)), ((), ()))


def shift(value, by):
    peers = lax.axis_size("seq")
    return lax.ppermute(
        value, "seq", [(i, i + by) for i in range(peers) if 0 <= i + by < peers]
    )


def cyclic(value, by):
    peers = lax.axis_size("seq")
    return lax.ppermute(value, "seq", [(i, (i + by) % peers) for i in range(peers)])


def swap(value, axis):
    return lax.ppermute(value, axis, [(0, 1), (1, 0)])


def dot(a, b):
    return jnp.dot(a, b, preferred_element_type=F32)


def dot_nt(a, b):
    return lax.dot_general(a, b, NT, preferred_element_type=F32)


def dot_tn(a, b):
    return lax.dot_general(a, b, TN, preferred_element_type=F32)


def after(value, *others):
    return lax.optimization_barrier((value, others))[0]


def seen_tiles(blocks, peers):
    tiles = []
    for n in range(blocks):
        mine = [(0, n, None)]
        for level in range(LEVELS):
            target = n - 2**level
            distance = -(target // blocks)
            if distance < peers:
                mine.append((distance, target % blocks, level))
        tiles.append(mine)
    return tiles


def block_rows(n):
    return pl.ds(n * BLOCK, BLOCK)


def head_cols(j):
    return slice(j * HEAD_DIM, (j + 1) * HEAD_DIM)


def cat(parts, axis=0):
    return parts[0] if len(parts) == 1 else jnp.concatenate(parts, axis)


def causal_tile():
    rows = lax.broadcasted_iota(jnp.int32, (BLOCK, BLOCK), 0)
    cols = lax.broadcasted_iota(jnp.int32, (BLOCK, BLOCK), 1)
    return rows <= cols


def forward_kernel(tiles, count, heads, use_ref, q_ref, *refs):
    k_refs, v_refs = refs[:count], refs[count : 2 * count]
    mixed_ref, lse_ref = refs[2 * count :]
    causal = causal_tile()
    for n, mine in enumerate(tiles):
        rows = block_rows(n)
        for j in range(heads):
            cols = head_cols(j)
            keys = cat([k_refs[d][block_rows(b), cols] for d, b, _ in mine])
            vals = cat([v_refs[d][block_rows(b), cols] for d, b, _ in mine])
            raw = dot_nt(keys, q_ref[rows, cols])
            parts = []
            for i, (_, _, level) in enumerate(mine):
                part = raw[i * BLOCK : (i + 1) * BLOCK]
                if level is None:
                    part = jnp.where(causal, part, MASKED)
                else:
                    part = part + jnp.where(use_ref[n * LEVELS + level] == 1, 0.0, MASKED)
                parts.append(part)
            top = jnp.max(functools.reduce(jnp.maximum, parts), 0, keepdims=True) * LOG2_SCALE
            grown = [jnp.exp2(part * LOG2_SCALE - top) for part in parts]
            total = jnp.sum(functools.reduce(jnp.add, grown), 0, keepdims=True)
            share = 1.0 / total
            prob = cat([(part * share).astype(BF16) for part in grown])
            mixed_ref[rows, cols] = dot_tn(prob, vals).astype(BF16)
            lse_ref[j : j + 1, rows] = top + jnp.log2(total)


def query_kernel(tiles, count, heads, heads_up, use_ref, q_ref, g_ref, lse_ref, *refs):
    k_refs, v_refs = refs[:count], refs[count : 2 * count]
    dq_ref, stats_ref = refs[2 * count :]
    causal = causal_tile()
    for n, mine in enumerate(tiles):
        rows = block_rows(n)
        for j in range(heads):
            cols = head_cols(j)
            keys = cat([k_refs[d][block_rows(b), cols] for d, b, _ in mine])
            vals = cat([v_refs[d][block_rows(b), cols] for d, b, _ in mine])
            lse = lse_ref[j : j + 1, rows]
            raw = dot_nt(keys, q_ref[rows, cols])
            prob_grad = dot_nt(vals, g_ref[rows, cols])
            probs, weighted = [], None
            for i, (_, _, level) in enumerate(mine):
                here = slice(i * BLOCK, (i + 1) * BLOCK)
                if level is None:
                    logits = jnp.where(causal, raw[here] * LOG2_SCALE - lse, MASKED)
                else:
                    off = lse + jnp.where(use_ref[n * LEVELS + level] == 1, 0.0, -MASKED)
                    logits = raw[here] * LOG2_SCALE - off
                prob = jnp.exp2(logits)
                probs.append(prob)
                part = prob * prob_grad[here]
                weighted = part if weighted is None else weighted + part
            delta = jnp.sum(weighted, 0, keepdims=True)
            score_grad = [
                (prob * SCALE * (prob_grad[i * BLOCK : (i + 1) * BLOCK] - delta)).astype(BF16)
                for i, prob in enumerate(probs)
            ]
            dq_ref[rows, cols] = dot_tn(cat(score_grad), keys).astype(BF16)
            stats_ref[j : j + 1, rows] = lse
            stats_ref[heads_up + j : heads_up + j + 1, rows] = delta
        flags = jnp.zeros((8, BLOCK), F32)
        level_row = lax.broadcasted_iota(jnp.int32, (8, BLOCK), 0)
        for level in range(LEVELS):
            flag = jnp.where(use_ref[n * LEVELS + level] == 1, 1.0, 0.0)
            flags = jnp.where(level_row == level, flag, flags)
        stats_ref[2 * heads_up :, rows] = flags
    for row in range(heads, heads_up):
        for first in (0, heads_up):
            stats_ref[first + row : first + row + 1, :] = jnp.zeros((1, stats_ref.shape[1]), F32)


def key_kernel(tiles, count, heads, heads_up, k_ref, v_ref, *refs):
    q_refs, g_refs, s_refs = refs[:count], refs[count : 2 * count], refs[2 * count : 3 * count]
    dk_ref, dv_ref = refs[3 * count :]
    causal = causal_tile()
    for b in range(len(tiles)):
        rows = block_rows(b)
        seers = [
            (d, n, level)
            for n, mine in enumerate(tiles)
            for d, block, level in mine
            if block == b
        ]
        for j in range(heads):
            cols = head_cols(j)
            ques = cat([q_refs[d][block_rows(n), cols] for d, n, _ in seers])
            grads = cat([g_refs[d][block_rows(n), cols] for d, n, _ in seers])
            raw = dot_nt(k_ref[rows, cols], ques)
            prob_grad = dot_nt(v_ref[rows, cols], grads)
            probs, score_grads = [], []
            for i, (d, n, level) in enumerate(seers):
                here = slice(i * BLOCK, (i + 1) * BLOCK)
                lse = s_refs[d][j : j + 1, block_rows(n)]
                delta = s_refs[d][heads_up + j : heads_up + j + 1, block_rows(n)]
                if level is None:
                    logits = jnp.where(causal, raw[:, here] * LOG2_SCALE - lse, MASKED)
                else:
                    row = 2 * heads_up + level
                    off = lse + (1.0 - s_refs[d][row : row + 1, block_rows(n)]) * (-MASKED)
                    logits = raw[:, here] * LOG2_SCALE - off
                prob = jnp.exp2(logits)
                probs.append(prob.astype(BF16))
                score_grads.append((prob * SCALE * (prob_grad[:, here] - delta)).astype(BF16))
            dv_ref[rows, cols] = dot(cat(probs, 1), grads).astype(BF16)
            dk_ref[rows, cols] = dot(cat(score_grads, 1), ques).astype(BF16)


def mixed_grad_kernel(count, place_ref, *refs):
    c_refs, w_ref, out_ref = refs[:count], refs[count], refs[count + 1]
    depth = c_refs[0].shape[1]
    columns = out_ref.shape[1]
    width = min(512, columns)
    for first in range(0, columns, width):
        total = None
        for i in range(count):
            rows = pl.ds(pl.multiple_of(place_ref[i] * depth, depth), depth)
            part = dot(c_refs[i][...], w_ref[rows, first : first + width])
            total = part if total is None else total + part
        out_ref[:, first : first + width] = total.astype(BF16)


def partial_kernel(place_ref, m_ref, w_ref, keep_ref, give_ref):
    depth = keep_ref.shape[2]
    half = depth // 2
    for out_ref, base in ((give_ref, 2), (keep_ref, 0)):
        for i in range(2):
            for part in range(2):
                first = pl.multiple_of(place_ref[base + i] * depth + part * half, half)
                out_ref[i, :, part * half : (part + 1) * half] = dot_nt(
                    m_ref[...], w_ref[pl.ds(first, half), :]
                ).astype(BF16)


def weight_grad_kernel(count, place_ref, c_ref, *refs):
    m_refs, out_ref = refs[:count], refs[count]
    features = out_ref.shape[0]
    height = min(512, features)
    for first in range(0, features, height):
        total = None
        for p in range(count):
            part = dot_tn(c_ref[place_ref[p], :, first : first + height], m_refs[p][...])
            total = part if total is None else total + part
        out_ref[first : first + height, :] = total.astype(BF16)


def cost(flops, bytes_accessed, exps=0):
    return pl.CostEstimate(
        flops=int(flops), bytes_accessed=int(bytes_accessed), transcendentals=int(exps)
    )


def kernel_call(body, name, scalars, arrays, out_shape, estimate):
    smem = pl.BlockSpec(memory_space=pltpu.SMEM)
    vmem = pl.BlockSpec(memory_space=pltpu.VMEM)
    return pl.pallas_call(
        body,
        in_specs=[smem] * len(scalars) + [vmem] * len(arrays),
        out_specs=jax.tree.map(lambda _: vmem, out_shape),
        out_shape=out_shape,
        compiler_params=pltpu.CompilerParams(vmem_limit_bytes=VMEM_LIMIT),
        cost_estimate=estimate,
        name=name,
    )(*scalars, *arrays)


VMEM_LIMIT = 16 * 1024 * 1024


def features_here(value):
    heads, reps = lax.axis_size("head"), lax.axis_size("rep")
    if heads == 2 and reps == 2:
        h, r = lax.axis_index("head"), lax.axis_index("rep")
        across = swap(value, "head")
        blocks = [value, swap(value, "rep"), across, swap(across, "rep")]
        places = [2 * h + r, 2 * h + 1 - r, 2 * (1 - h) + r, 2 * (1 - h) + 1 - r]
        return blocks, jnp.stack(places).astype(jnp.int32)
    gathered = lax.all_gather(value, ("head", "rep"), axis=0)
    count = heads * reps
    return [gathered[i] for i in range(count)], jnp.arange(count, dtype=jnp.int32)


def attended_share(mixed_heads, out_weight, places, estimate):
    heads, reps = lax.axis_size("head"), lax.axis_size("rep")
    rows = mixed_heads.shape[0]
    if heads == 2 and reps == 2:
        share = out_weight.shape[0] // 4
        order = jnp.stack([places[0], places[2], places[1], places[3]])
        keep, give = kernel_call(
            partial_kernel,
            "attended_partial",
            [order],
            [mixed_heads, out_weight],
            [jax.ShapeDtypeStruct((2, rows, share), BF16)] * 2,
            estimate,
        )
        got = swap(give, "rep")
        across = (keep[1].astype(F32) + got[1].astype(F32)).astype(BF16)
        across = swap(across, "head")
        return (keep[0].astype(F32) + got[0].astype(F32) + across.astype(F32)).astype(BF16)
    partial_value = lax.dot_general(mixed_heads, out_weight, NT, preferred_element_type=F32)
    return lax.psum_scatter(
        partial_value.astype(BF16), ("head", "rep"), scatter_dimension=1, tiled=True
    )


def per_device(queries, keys, values, out_weight, level_mask, cotangent):
    rows, columns = queries.shape
    features = out_weight.shape[0]
    heads = columns // HEAD_DIM
    heads_up = -(-heads // 8) * 8
    blocks = rows // BLOCK
    peers = lax.axis_size("seq")
    place = lax.axis_index("seq")
    tiles = seen_tiles(blocks, peers)
    distances = sorted({d for mine in tiles for d, _, _ in mine})
    count = len(distances)
    slot = {d: i for i, d in enumerate(distances)}
    tiles = [[(slot[d], b, level) for d, b, level in mine] for mine in tiles]
    pairs = sum(len(mine) for mine in tiles)
    attention_flops = 2 * heads * pairs * BLOCK * BLOCK * HEAD_DIM
    array_bytes = 2 * rows * columns
    exps = heads * pairs * BLOCK * BLOCK
    like_queries = jax.ShapeDtypeStruct((rows, columns), BF16)

    def further(got, sign, *others):
        near, far = distances[len(got) - 1], distances[len(got)]
        return got + [shift(after(got[-1], *others), sign * (far - near))]

    block_ids = place * blocks + jnp.arange(blocks, dtype=jnp.int32)
    offsets = 2 ** jnp.arange(LEVELS, dtype=jnp.int32)
    use = ((block_ids[:, None] >= offsets[None]) & (level_mask == 1)).astype(jnp.int32)
    use = use.reshape(-1)

    key_all, value_all, query_all = [keys], [values], [queries]
    key_all = further(key_all, 1)
    value_all = further(value_all, 1)
    query_all = further(query_all, -1)
    c_blocks, c_places = features_here(cotangent)
    group_count = len(c_blocks)
    part_cols = cotangent.shape[1]
    key_all = further(key_all, 1)
    value_all = further(value_all, 1, query_all[1])
    query_all = further(query_all, -1)

    mixed_grad = kernel_call(
        functools.partial(mixed_grad_kernel, group_count),
        "mixed_grad",
        [c_places],
        [*c_blocks, out_weight],
        like_queries,
        cost(2 * rows * columns * features, 2 * columns * features),
    )
    grad_all = further([mixed_grad], -1)

    h, r = lax.axis_index("head"), lax.axis_index("rep")
    n_head, n_rep = lax.axis_size("head"), lax.axis_size("rep")
    step_of = lambda i: (i // n_rep) + n_head * (i % n_rep)
    wanted = (place + step_of(h * n_rep + r)) % peers
    out_block = c_blocks[0]
    for i in range(1, group_count):
        out_block = jnp.where(c_places[i] == wanted, c_blocks[i], out_block)
    links = []
    for s in range(peers):
        for q in range(group_count):
            links.append((s * group_count + q, ((s + step_of(q)) % peers) * group_count + q))
    arrived = lax.ppermute(out_block, ("seq", "head", "rep"), links)

    while len(key_all) < count:
        key_all = further(key_all, 1)
        value_all = further(value_all, 1)
        query_all = further(query_all, -1)
    held_queries = after(queries, query_all[-1], grad_all[1], arrived)
    mixed_heads, lse = kernel_call(
        functools.partial(forward_kernel, tiles, count, heads),
        "attention_forward",
        [use],
        [held_queries, *key_all, *value_all],
        [like_queries, jax.ShapeDtypeStruct((heads_up, rows), F32)],
        cost(2 * attention_flops, (2 * count + 2) * array_bytes, exps),
    )
    while len(grad_all) < count:
        grad_all = further(grad_all, -1)

    if peers <= 4:
        mixed_all = [mixed_heads] + [cyclic(mixed_heads, k) for k in range(1, peers)]
    else:
        gathered = lax.all_gather(mixed_heads, "seq", axis=0)
        mixed_all = [
            lax.dynamic_index_in_dim(gathered, (place - k) % peers, 0, False)
            for k in range(peers)
        ]

    attended = attended_share(
        mixed_heads, out_weight, c_places, cost(2 * rows * columns * features, 2 * rows * features)
    )

    stats_shape = jax.ShapeDtypeStruct((2 * heads_up + 8, rows), F32)
    q_grad, stats = kernel_call(
        functools.partial(query_kernel, tiles, count, heads, heads_up),
        "attention_query_grad",
        [use],
        [queries, mixed_grad, lse, *key_all, *value_all],
        [like_queries, stats_shape],
        cost(3 * attention_flops, (2 * count + 3) * array_bytes, exps),
    )
    stats_all = [stats] + [shift(stats, -d) for d in distances[1:]]
    k_grad, v_grad = kernel_call(
        functools.partial(key_kernel, tiles, count, heads, heads_up),
        "attention_key_grad",
        [],
        [keys, values, *query_all, *grad_all, *stats_all],
        [like_queries] * 2,
        cost(4 * attention_flops, (2 * count + 4) * array_bytes, exps),
    )

    ct_blocks, ct_places = features_here(arrived)
    steps = step_of(ct_places)
    ct_at = jnp.sum(
        jnp.where(steps[None] == jnp.arange(peers)[:, None], jnp.arange(group_count)[None], 0), 1
    ).astype(jnp.int32)
    weight_grad = kernel_call(
        functools.partial(weight_grad_kernel, peers),
        "weight_grad",
        [ct_at],
        [jnp.stack(ct_blocks), *mixed_all],
        jax.ShapeDtypeStruct((part_cols, columns), BF16),
        cost(2 * part_cols * columns * rows * peers, 2 * array_bytes * peers),
    )
    return (attended, q_grad, k_grad, v_grad, weight_grad)


def solution(mesh):
    shared = P(("groups", "seq"), ("head", "rep"))
    return jax.shard_map(
        per_device,
        mesh=mesh,
        in_specs=(shared, shared, shared, P(None, ("head", "rep")), P(("groups", "seq"), None), shared),
        out_specs=(shared,) * 5,
        check_vma=False,
    )
```

time: 199 us -> 159 us (0.80)
  the two profiles are of different devices: /device:TPU:9 before, /device:TPU:0 now
where the time goes in v2:
time: 159 us; the launch traced here: 158 us
  waiting for transfers between devices  65.6 us (41%)
  starting transfers between devices  50.4 us (32%)
  Pallas kernels  27.1 us (17%)
  local copies, waits for them, and re-layouts  10.3 us (6%)
  other arithmetic  3.83 us (2%)
    ppermute x3, waiting for transfers between devices, cyclic(): lax.ppermute(value, 'seq', [(i, (i + by) % peers) for i in range(peers)])  34.8 us
    pallas_call x6, Pallas kernels, kernel_call(): pl.pallas_call(body, in_specs=[smem] * len(scalars) + [vmem] * len(arrays...  27.1 us
    ppermute x10, starting transfers between devices, shift(): lax.ppermute(value, 'seq', [(i, i + by) for i in range(peers) if 0 <= i +...  25 us
    ppermute x10, waiting for transfers between devices, shift(): lax.ppermute(value, 'seq', [(i, i + by) for i in range(peers) if 0 <= i +...  24 us
    ppermute x8, starting transfers between devices, swap(): return lax.ppermute(value, axis, [(0, 1), (1, 0)])  16.5 us
    unnamed x20, local copies, waits for them, and re-layouts  10.2 us
    ppermute x8, waiting for transfers between devices, swap(): return lax.ppermute(value, axis, [(0, 1), (1, 0)])  6.74 us
    ppermute x1, starting transfers between devices, per_device(): arrived = lax.ppermute(out_block, ('seq', 'head', 'rep'), links)  5.36 us
  transfers between devices with their start and end apart: 22, of which 9 were waited for; matrix products, arithmetic and copies ran while one was open for 2% of the time, Pallas kernels for 13%

profile of v2, /device:TPU:0, one launch (start us, length us, event | category | flops | bytes accessed | tf_op | source)
XLA Modules:
  0.0 158.0 jit_solution(2396579813151030857)
XLA Ops:
  0.6 3.0 %collective-permute-start.3 = (bf16[256,1024]{1,0:T(8,128)(2,1)}, bf16[256,1024]{1,0:T(8,128)(2,1)S(1)}, u32[]{:S(2)}, u32[]{:S(2)}) collective-permute-start(bf16[256,1024]{1,0:T(8,128)(2,1)} %refs_0_.4), channel_id=1, source_target_pairs={{0,2},{2,0},{1,3},{3,1},{4,6},{6,4},{5,7},{7,5},{8,10},{10,8},{9,1... | collective-permute-start | bytes 1572872 | tf_op jit(solution)/shard_map/ppermute | solution.py:37
  3.6 3.5 %collective-permute-start.7 = (bf16[256,1024]{1,0:T(8,128)(2,1)}, bf16[256,1024]{1,0:T(8,128)(2,1)S(1)}, u32[]{:S(2)}, u32[]{:S(2)}) collective-permute-start(bf16[256,1024]{1,0:T(8,128)(2,1)} %k_ref.1), channel_id=1, source_target_pairs={{0,4},{4,8},{8,12},{1,5},{5,9},{9,13},{2,6},{6,10},{10,14},{3,7},{... | collective-permute-start | bytes 1572872 | tf_op jit(solution)/shard_map/ppermute | solution.py:26
  7.1 3.5 %collective-permute-start.9 = (bf16[256,1024]{1,0:T(8,128)(2,1)}, bf16[256,1024]{1,0:T(8,128)(2,1)S(1)}, u32[]{:S(2)}, u32[]{:S(2)}) collective-permute-start(bf16[256,1024]{1,0:T(8,128)(2,1)} %v_ref.1), channel_id=1, source_target_pairs={{0,4},{4,8},{8,12},{1,5},{5,9},{9,13},{2,6},{6,10},{10,14},{3,7},{... | collective-permute-start | bytes 1572872 | tf_op jit(solution)/shard_map/ppermute | solution.py:26
  12.0 3.7 %collective-permute-done.3.refs_2_ = bf16[256,1024]{1,0:T(8,128)(2,1)S(1)} collective-permute-done((bf16[256,1024]{1,0:T(8,128)(2,1)}, bf16[256,1024]{1,0:T(8,128)(2,1)S(1)}, u32[]{:S(2)}, u32[]{:S(2)}) %collective-permute-start.3) | collective-permute-done | bytes 524320 | tf_op jit(solution)/shard_map/ppermute | solution.py:37
  15.9 3.9 %collective-permute-done.7.refs_1_ = bf16[256,1024]{1,0:T(8,128)(2,1)S(1)} collective-permute-done((bf16[256,1024]{1,0:T(8,128)(2,1)}, bf16[256,1024]{1,0:T(8,128)(2,1)S(1)}, u32[]{:S(2)}, u32[]{:S(2)}) %collective-permute-start.7) | collective-permute-done | bytes 524320 | tf_op jit(solution)/shard_map/ppermute | solution.py:26
  19.8 5.1 %collective-permute-start.8 = (bf16[256,1024]{1,0:T(8,128)(2,1)S(1)}, bf16[256,1024]{1,0:T(8,128)(2,1)}, u32[]{:S(2)}, u32[]{:S(2)}) collective-permute-start(bf16[256,1024]{1,0:T(8,128)(2,1)S(1)} %collective-permute-done.7.refs_1_), channel_id=1, source_target_pairs={{0,4},{4,8},{8,12},{1,5},{5,9},{9,13},{2,6},{6,10},{10,14},{3,7},{... | collective-permute-start | bytes 1572872 | tf_op jit(solution)/shard_map/ppermute | solution.py:26
  24.9 6.2 %collective-permute-done.9.refs_4_ = bf16[256,1024]{1,0:T(8,128)(2,1)S(1)} collective-permute-done((bf16[256,1024]{1,0:T(8,128)(2,1)}, bf16[256,1024]{1,0:T(8,128)(2,1)S(1)}, u32[]{:S(2)}, u32[]{:S(2)}) %collective-permute-start.9) | collective-permute-done | bytes 524320 | tf_op jit(solution)/shard_map/ppermute | solution.py:26
  31.0 5.1 %collective-permute-start.10 = (bf16[256,1024]{1,0:T(8,128)(2,1)S(1)}, bf16[256,1024]{1,0:T(8,128)(2,1)}, u32[]{:S(2)}, u32[]{:S(2)}) collective-permute-start(bf16[256,1024]{1,0:T(8,128)(2,1)S(1)} %collective-permute-done.9.refs_4_), channel_id=1, source_target_pairs={{0,4},{4,8},{8,12},{1,5},{5,9},{9,13},{2,6},{6,10},{10,14},{3,7},{... | collective-permute-start | bytes 1572872 | tf_op jit(solution)/shard_map/ppermute | solution.py:26
  37.4 3.4 %copy-done = bf16[4096,1024]{1,0:T(8,128)(2,1)S(1)} copy-done((bf16[4096,1024]{1,0:T(8,128)(2,1)S(1)}, bf16[4096,1024]{1,0:T(8,128)(2,1)}, u32[]{:S(2)}) %copy-start) | copy-done | bytes 8388632
  41.8 2.9 %mixed_grad.1.g_ref.refs_3_ = bf16[256,1024]{1,0:T(8,128)(2,1)S(1)} custom-call(s32[4]{0:T(128)S(1)} %get-tuple-element.26.place_ref, bf16[256,1024]{1,0:T(8,128)(2,1)S(1)} %copy-done.5, bf16[256,1024]{1,0:T(8,128)(2,1)S(1)} %collective-permute-done.2.refs_1_, bf16[256,1024]{1,0:T(8,128)(2,1)S(1)} %collective-permute-done.3.refs_2_, ...), custom_call_target="tpu_custom_call" | custom-call | flops 2147483648 | bytes 8388608 | tf_op jit(solution)/shard_map/mixed_grad/pallas_call | solution.py:242
  49.4 5.4 %collective-permute-start.6 = (bf16[256,1024]{1,0:T(8,128)(2,1)}, bf16[256,1024]{1,0:T(8,128)(2,1)}, u32[]{:S(2)}, u32[]{:S(2)}) collective-permute-start(bf16[256,1024]{1,0:T(8,128)(2,1)} %select_select_fusion), channel_id=1, source_target_pairs={{0,0},{1,9},{2,6},{3,15},{4,4},{5,13},{6,10},{7,3},{8,8},{9,1},{10... | collective-permute-start | bytes 1572872 | tf_op jit(solution)/shard_map/ppermute | solution.py:353
  55.1 6.7 %collective-permute-done.5.refs_4_ = bf16[256,1024]{1,0:T(8,128)(2,1)} collective-permute-done((bf16[256,1024]{1,0:T(8,128)(2,1)S(1)}, bf16[256,1024]{1,0:T(8,128)(2,1)}, u32[]{:S(2)}, u32[]{:S(2)}) %collective-permute-start.5) | collective-permute-done | bytes 524320 | tf_op jit(solution)/shard_map/ppermute | solution.py:26
  61.8 3.7 %attention_forward.1 = (bf16[256,1024]{1,0:T(8,128)(2,1)S(1)}, f32[8,256]{1,0:T(8,128)S(1)}) custom-call(s32[10]{0:T(128)S(1)} %reshape.264.use_ref, bf16[256,1024]{1,0:T(8,128)(2,1)S(1)} %copy-done.2, bf16[256,1024]{1,0:T(8,128)(2,1)S(1)} %copy-done.3, bf16[256,1024]{1,0:T(8,128)(2,1)S(1)} %collective-permute-done.7.refs_1_, ...), custom_call_target="tpu_custom_call" | custom-call | flops 536870912 | bytes 4194304 | tf_op jit(solution)/shard_map/attention_forward/pallas_call | solution.py:242
  65.5 3.4 %copy-done.1 = bf16[4096,1024]{1,0:T(8,128)(2,1)S(1)} copy-done((bf16[4096,1024]{1,0:T(8,128)(2,1)S(1)}, bf16[4096,1024]{1,0:T(8,128)(2,1)}, u32[]{:S(2)}) %copy-start.1) | copy-done | bytes 8388632
  68.8 2.9 %attended_partial.1 = (bf16[2,256,1024]{2,1,0:T(8,128)(2,1)S(1)}, bf16[2,256,1024]{2,1,0:T(8,128)(2,1)S(1)}) custom-call(s32[4]{0:T(128)S(1)} %add_add_fusion.place_ref, bf16[256,1024]{1,0:T(8,128)(2,1)S(1)} %get-tuple-element.17.m_ref.refs_0_, bf16[4096,1024]{1,0:T(8,128)(2,1)S(1)} %copy-done.1), custom_call_target="tpu_custom_call" | custom-call | flops 2147483648 | bytes 2097152 | tf_op jit(solution)/shard_map/attended_partial/pallas_call | solution.py:242
  71.8 11.1 %collective-permute-start.11 = (bf16[2,256,1024]{2,1,0:T(8,128)(2,1)S(1)}, bf16[2,256,1024]{2,1,0:T(8,128)(2,1)S(1)}, u32[]{:S(2)}, u32[]{:S(2)}) collective-permute-start(bf16[2,256,1024]{2,1,0:T(8,128)(2,1)S(1)} %get-tuple-element.19), channel_id=1, source_target_pairs={{0,1},{1,0},{2,3},{3,2},{4,5},{5,4},{6,7},{7,6},{8,9},{9,8},{10,11... | collective-permute-start | bytes 3145736 | tf_op jit(solution)/shard_map/ppermute | solution.py:37
  85.4 7.3 %attention_query_grad.1 = (bf16[256,1024]{1,0:T(8,128)(2,1)}, f32[24,256]{1,0:T(8,128)S(1)}) custom-call(s32[10]{0:T(128)S(1)} %reshape.264.use_ref, bf16[256,1024]{1,0:T(8,128)(2,1)S(1)} %copy-done.2, bf16[256,1024]{1,0:T(8,128)(2,1)S(1)} %mixed_grad.1.g_ref.refs_3_, f32[8,256]{1,0:T(8,128)S(1)} %get-tuple-element.20.lse_ref, ...), custom_call_target="tpu_custom_call" | custom-call | flops 805306368 | bytes 4718592 | tf_op jit(solution)/shard_map/attention_query_grad/pallas_call | solution.py:242
  94.0 3.0 %collective-permute-done.17 = bf16[256,1024]{1,0:T(8,128)(2,1)S(1)} collective-permute-done((bf16[256,1024]{1,0:T(8,128)(2,1)}, bf16[256,1024]{1,0:T(8,128)(2,1)S(1)}, u32[]{:S(2)}, u32[]{:S(2)}) %collective-permute-start.17) | collective-permute-done | bytes 524320 | tf_op jit(solution)/shard_map/ppermute | solution.py:37
  97.0 2.4 %collective-permute-done.15.refs_8_ = f32[24,256]{1,0:T(8,128)S(1)} collective-permute-done((f32[24,256]{1,0:T(8,128)S(1)}, f32[24,256]{1,0:T(8,128)S(1)}, u32[]{:S(2)}, u32[]{:S(2)}) %collective-permute-start.15) | collective-permute-done | bytes 24608 | tf_op jit(solution)/shard_map/ppermute | solution.py:26
  100.7 4.9 %collective-permute-done.14.refs_7_ = f32[24,256]{1,0:T(8,128)S(1)} collective-permute-done((f32[24,256]{1,0:T(8,128)S(1)}, f32[24,256]{1,0:T(8,128)S(1)}, u32[]{:S(2)}, u32[]{:S(2)}) %collective-permute-start.14) | collective-permute-done | bytes 24608 | tf_op jit(solution)/shard_map/ppermute | solution.py:26
  105.5 3.5 %collective-permute-start.20 = (bf16[256,1024]{1,0:T(8,128)(2,1)S(1)}, bf16[256,1024]{1,0:T(8,128)(2,1)S(1)}, u32[]{:S(2)}, u32[]{:S(2)}) collective-permute-start(bf16[256,1024]{1,0:T(8,128)(2,1)S(1)} %get-tuple-element.17.m_ref.refs_0_), channel_id=1, source_target_pairs={{0,8},{4,12},{8,0},{12,4},{1,9},{5,13},{9,1},{13,5},{2,10},{6,14},... | collective-permute-start | bytes 1572872 | tf_op jit(solution)/shard_map/ppermute | solution.py:33
  110.4 6.2 %attention_key_grad.1 = (bf16[256,1024]{1,0:T(8,128)(2,1)}, bf16[256,1024]{1,0:T(8,128)(2,1)}) custom-call(bf16[256,1024]{1,0:T(8,128)(2,1)S(1)} %copy-done.3, bf16[256,1024]{1,0:T(8,128)(2,1)S(1)} %copy-done.4, bf16[256,1024]{1,0:T(8,128)(2,1)S(1)} %copy-done.2, bf16[256,1024]{1,0:T(8,128)(2,1)} %collective-permute-done.refs_1_, ...), custom_call_target="tpu_custom_call" | custom-call | flops 1073741824 | bytes 5242880 | tf_op jit(solution)/shard_map/attention_key_grad/pallas_call | solution.py:242
  118.3 34.4 %collective-permute-done.20.refs_2_ = bf16[256,1024]{1,0:T(8,128)(2,1)S(1)} collective-permute-done((bf16[256,1024]{1,0:T(8,128)(2,1)S(1)}, bf16[256,1024]{1,0:T(8,128)(2,1)S(1)}, u32[]{:S(2)}, u32[]{:S(2)}) %collective-permute-start.20) | collective-permute-done | bytes 524320 | tf_op jit(solution)/shard_map/ppermute | solution.py:33
  152.7 4.2 %weight_grad.1 = bf16[1024,1024]{1,0:T(8,128)(2,1)} custom-call(s32[4]{0:T(128)S(1)} %select_reduce_fusion.place_ref, bf16[4,256,1024]{2,1,0:T(8,128)(2,1)S(1)} %pad_maximum_fusion.c_ref, bf16[256,1024]{1,0:T(8,128)(2,1)S(1)} %get-tuple-element.17.m_ref.refs_0_, bf16[256,1024]{1,0:T(8,128)(2,1)S(1)} %collective-permute-done.19.refs_1_, ...), custom_call_target="tpu_custom_call" | custom-call | flops 2147483648 | bytes 4194304 | tf_op jit(solution)/shard_map/weight_grad/pallas_call | solution.py:242
  (57 shorter events, 18.1 us)
Async XLA Ops:
  0.6 15.1 %collective-permute-start.3 = (bf16[256,1024]{1,0:T(8,128)(2,1)}, bf16[256,1024]{1,0:T(8,128)(2,1)S(1)}, u32[]{:S(2)}, u32[]{:S(2)}) collective-permute-start(bf16[256,1024]{1,0:T(8,128)(2,1)} %refs_0_.4), channel_id=1, source_target_pairs={{0,2},{2,0},{1,3},{3,1},{4,6},{6,4},{5,7},{7,5},{8,10},{10,8},{9,1... | collective-permute-start | bytes 1572872 | tf_op jit(solution)/shard_map/ppermute | solution.py:37
  3.6 16.1 %collective-permute-start.7 = (bf16[256,1024]{1,0:T(8,128)(2,1)}, bf16[256,1024]{1,0:T(8,128)(2,1)S(1)}, u32[]{:S(2)}, u32[]{:S(2)}) collective-permute-start(bf16[256,1024]{1,0:T(8,128)(2,1)} %k_ref.1), channel_id=1, source_target_pairs={{0,4},{4,8},{8,12},{1,5},{5,9},{9,13},{2,6},{6,10},{10,14},{3,7},{... | collective-permute-start | bytes 1572872 | tf_op jit(solution)/shard_map/ppermute | solution.py:26
  7.1 23.9 %collective-permute-start.9 = (bf16[256,1024]{1,0:T(8,128)(2,1)}, bf16[256,1024]{1,0:T(8,128)(2,1)S(1)}, u32[]{:S(2)}, u32[]{:S(2)}) collective-permute-start(bf16[256,1024]{1,0:T(8,128)(2,1)} %v_ref.1), channel_id=1, source_target_pairs={{0,4},{4,8},{8,12},{1,5},{5,9},{9,13},{2,6},{6,10},{10,14},{3,7},{... | collective-permute-start | bytes 1572872 | tf_op jit(solution)/shard_map/ppermute | solution.py:26
  10.6 20.4 %collective-permute-start = (bf16[256,1024]{1,0:T(8,128)(2,1)}, bf16[256,1024]{1,0:T(8,128)(2,1)}, u32[]{:S(2)}, u32[]{:S(2)}) collective-permute-start(bf16[256,1024]{1,0:T(8,128)(2,1)} %refs_0_.7), channel_id=1, source_target_pairs={{4,0},{8,4},{12,8},{5,1},{9,5},{13,9},{6,2},{10,6},{14,10},{7,3},{... | collective-permute-start | bytes 1572872 | tf_op jit(solution)/shard_map/ppermute | solution.py:26
  11.9 25.4 %collective-permute-start.2 = (bf16[256,1024]{1,0:T(8,128)(2,1)}, bf16[256,1024]{1,0:T(8,128)(2,1)S(1)}, u32[]{:S(2)}, u32[]{:S(2)}) collective-permute-start(bf16[256,1024]{1,0:T(8,128)(2,1)} %refs_0_.4), channel_id=1, source_target_pairs={{0,1},{1,0},{2,3},{3,2},{4,5},{5,4},{6,7},{7,6},{8,9},{9,8},{10,11... | collective-permute-start | bytes 1572872 | tf_op jit(solution)/shard_map/ppermute | solution.py:37
  15.8 21.6 %collective-permute-start.4 = (bf16[256,1024]{1,0:T(8,128)(2,1)S(1)}, bf16[256,1024]{1,0:T(8,128)(2,1)S(1)}, u32[]{:S(2)}, u32[]{:S(2)}) collective-permute-start(bf16[256,1024]{1,0:T(8,128)(2,1)S(1)} %collective-permute-done.3.refs_2_), channel_id=1, source_target_pairs={{0,1},{1,0},{2,3},{3,2},{4,5},{5,4},{6,7},{7,6},{8,9},{9,8},{10,11... | collective-permute-start | bytes 1572872 | tf_op jit(solution)/shard_map/ppermute | solution.py:37
  19.8 42.0 %collective-permute-start.8 = (bf16[256,1024]{1,0:T(8,128)(2,1)S(1)}, bf16[256,1024]{1,0:T(8,128)(2,1)}, u32[]{:S(2)}, u32[]{:S(2)}) collective-permute-start(bf16[256,1024]{1,0:T(8,128)(2,1)S(1)} %collective-permute-done.7.refs_1_), channel_id=1, source_target_pairs={{0,4},{4,8},{8,12},{1,5},{5,9},{9,13},{2,6},{6,10},{10,14},{3,7},{... | collective-permute-start | bytes 1572872 | tf_op jit(solution)/shard_map/ppermute | solution.py:26
  31.0 30.7 %collective-permute-start.10 = (bf16[256,1024]{1,0:T(8,128)(2,1)S(1)}, bf16[256,1024]{1,0:T(8,128)(2,1)}, u32[]{:S(2)}, u32[]{:S(2)}) collective-permute-start(bf16[256,1024]{1,0:T(8,128)(2,1)S(1)} %collective-permute-done.9.refs_4_), channel_id=1, source_target_pairs={{0,4},{4,8},{8,12},{1,5},{5,9},{9,13},{2,6},{6,10},{10,14},{3,7},{... | collective-permute-start | bytes 1572872 | tf_op jit(solution)/shard_map/ppermute | solution.py:26
  36.1 19.0 %collective-permute-start.1 = (bf16[256,1024]{1,0:T(8,128)(2,1)}, bf16[256,1024]{1,0:T(8,128)(2,1)}, u32[]{:S(2)}, u32[]{:S(2)}) collective-permute-start(bf16[256,1024]{1,0:T(8,128)(2,1)} %collective-permute-done.refs_1_), channel_id=1, source_target_pairs={{4,0},{8,4},{12,8},{5,1},{9,5},{13,9},{6,2},{10,6},{14,10},{7,3},{... | collective-permute-start | bytes 1572872 | tf_op jit(solution)/shard_map/ppermute | solution.py:26
  47.1 14.7 %copy-start.3 = (bf16[256,1024]{1,0:T(8,128)(2,1)S(1)}, bf16[256,1024]{1,0:T(8,128)(2,1)}, u32[]{:S(2)}) copy-start(bf16[256,1024]{1,0:T(8,128)(2,1)} %k_ref.1) | copy-start | bytes 1572868
  47.1 14.7 %copy-start.4 = (bf16[256,1024]{1,0:T(8,128)(2,1)S(1)}, bf16[256,1024]{1,0:T(8,128)(2,1)}, u32[]{:S(2)}) copy-start(bf16[256,1024]{1,0:T(8,128)(2,1)} %v_ref.1) | copy-start | bytes 1572868
  47.1 14.6 %collective-permute-start.5 = (bf16[256,1024]{1,0:T(8,128)(2,1)S(1)}, bf16[256,1024]{1,0:T(8,128)(2,1)}, u32[]{:S(2)}, u32[]{:S(2)}) collective-permute-start(bf16[256,1024]{1,0:T(8,128)(2,1)S(1)} %mixed_grad.1.g_ref.refs_3_), channel_id=1, source_target_pairs={{4,0},{8,4},{12,8},{5,1},{9,5},{13,9},{6,2},{10,6},{14,10},{7,3},{... | collective-permute-start | bytes 1572872 | tf_op jit(solution)/shard_map/ppermute | solution.py:26
  49.4 12.3 %collective-permute-start.6 = (bf16[256,1024]{1,0:T(8,128)(2,1)}, bf16[256,1024]{1,0:T(8,128)(2,1)}, u32[]{:S(2)}, u32[]{:S(2)}) collective-permute-start(bf16[256,1024]{1,0:T(8,128)(2,1)} %select_select_fusion), channel_id=1, source_target_pairs={{0,0},{1,9},{2,6},{3,15},{4,4},{5,13},{6,10},{7,3},{8,8},{9,1},{10... | collective-permute-start | bytes 1572872 | tf_op jit(solution)/shard_map/ppermute | solution.py:353
  71.8 37.3 %collective-permute-start.11 = (bf16[2,256,1024]{2,1,0:T(8,128)(2,1)S(1)}, bf16[2,256,1024]{2,1,0:T(8,128)(2,1)S(1)}, u32[]{:S(2)}, u32[]{:S(2)}) collective-permute-start(bf16[2,256,1024]{2,1,0:T(8,128)(2,1)S(1)} %get-tuple-element.19), channel_id=1, source_target_pairs={{0,1},{1,0},{2,3},{3,2},{4,5},{5,4},{6,7},{7,6},{8,9},{9,8},{10,11... | collective-permute-start | bytes 3145736 | tf_op jit(solution)/shard_map/ppermute | solution.py:37
  82.9 14.1 %collective-permute-start.17 = (bf16[256,1024]{1,0:T(8,128)(2,1)}, bf16[256,1024]{1,0:T(8,128)(2,1)S(1)}, u32[]{:S(2)}, u32[]{:S(2)}) collective-permute-start(bf16[256,1024]{1,0:T(8,128)(2,1)} %collective-permute-done.6), channel_id=1, source_target_pairs={{0,2},{2,0},{1,3},{3,1},{4,6},{6,4},{5,7},{7,5},{8,10},{10,8},{9,1... | collective-permute-start | bytes 1572872 | tf_op jit(solution)/shard_map/ppermute | solution.py:37
  83.9 21.6 %collective-permute-start.13 = (bf16[256,1024]{1,0:T(8,128)(2,1)}, bf16[256,1024]{1,0:T(8,128)(2,1)S(1)}, u32[]{:S(2)}, u32[]{:S(2)}) collective-permute-start(bf16[256,1024]{1,0:T(8,128)(2,1)} %collective-permute-done.5.refs_4_), channel_id=1, source_target_pairs={{4,0},{8,4},{12,8},{5,1},{9,5},{13,9},{6,2},{10,6},{14,10},{7,3},{... | collective-permute-start | bytes 1572872 | tf_op jit(solution)/shard_map/ppermute | solution.py:26
  85.2 24.0 %collective-permute-start.16 = (bf16[256,1024]{1,0:T(8,128)(2,1)}, bf16[256,1024]{1,0:T(8,128)(2,1)S(1)}, u32[]{:S(2)}, u32[]{:S(2)}) collective-permute-start(bf16[256,1024]{1,0:T(8,128)(2,1)} %collective-permute-done.6), channel_id=1, source_target_pairs={{0,1},{1,0},{2,3},{3,2},{4,5},{5,4},{6,7},{7,6},{8,9},{9,8},{10,11... | collective-permute-start | bytes 1572872 | tf_op jit(solution)/shard_map/ppermute | solution.py:37
  92.7 6.6 %collective-permute-start.15 = (f32[24,256]{1,0:T(8,128)S(1)}, f32[24,256]{1,0:T(8,128)S(1)}, u32[]{:S(2)}, u32[]{:S(2)}) collective-permute-start(f32[24,256]{1,0:T(8,128)S(1)} %get-tuple-element.22.refs_6_), channel_id=1, source_target_pairs={{8,0},{12,4},{9,1},{13,5},{10,2},{14,6},{11,3},{15,7},{24,16},{28,... | collective-permute-start | bytes 73736 | tf_op jit(solution)/shard_map/ppermute | solution.py:26
  97.0 19.6 %collective-permute-start.18 = (bf16[256,1024]{1,0:T(8,128)(2,1)S(1)}, bf16[256,1024]{1,0:T(8,128)(2,1)S(1)}, u32[]{:S(2)}, u32[]{:S(2)}) collective-permute-start(bf16[256,1024]{1,0:T(8,128)(2,1)S(1)} %collective-permute-done.17), channel_id=1, source_target_pairs={{0,1},{1,0},{2,3},{3,2},{4,5},{5,4},{6,7},{7,6},{8,9},{9,8},{10,11... | collective-permute-start | bytes 1572872 | tf_op jit(solution)/shard_map/ppermute | solution.py:37
  99.4 6.2 %collective-permute-start.14 = (f32[24,256]{1,0:T(8,128)S(1)}, f32[24,256]{1,0:T(8,128)S(1)}, u32[]{:S(2)}, u32[]{:S(2)}) collective-permute-start(f32[24,256]{1,0:T(8,128)S(1)} %get-tuple-element.22.refs_6_), channel_id=1, source_target_pairs={{4,0},{8,4},{12,8},{5,1},{9,5},{13,9},{6,2},{10,6},{14,10},{7,3},{... | collective-permute-start | bytes 73736 | tf_op jit(solution)/shard_map/ppermute | solution.py:26
  105.5 12.8 %collective-permute-start.21 = (bf16[256,1024]{1,0:T(8,128)(2,1)S(1)}, bf16[256,1024]{1,0:T(8,128)(2,1)S(1)}, u32[]{:S(2)}, u32[]{:S(2)}) collective-permute-start(bf16[256,1024]{1,0:T(8,128)(2,1)S(1)} %get-tuple-element.17.m_ref.refs_0_), channel_id=1, source_target_pairs={{0,12},{4,0},{8,4},{12,8},{1,13},{5,1},{9,5},{13,9},{2,14},{6,2},{... | collective-permute-start | bytes 1572872 | tf_op jit(solution)/shard_map/ppermute | solution.py:33
  105.5 47.2 %collective-permute-start.20 = (bf16[256,1024]{1,0:T(8,128)(2,1)S(1)}, bf16[256,1024]{1,0:T(8,128)(2,1)S(1)}, u32[]{:S(2)}, u32[]{:S(2)}) collective-permute-start(bf16[256,1024]{1,0:T(8,128)(2,1)S(1)} %get-tuple-element.17.m_ref.refs_0_), channel_id=1, source_target_pairs={{0,8},{4,12},{8,0},{12,4},{1,9},{5,13},{9,1},{13,5},{2,10},{6,14},... | collective-permute-start | bytes 1572872 | tf_op jit(solution)/shard_map/ppermute | solution.py:33
  109.0 43.7 %collective-permute-start.19 = (bf16[256,1024]{1,0:T(8,128)(2,1)S(1)}, bf16[256,1024]{1,0:T(8,128)(2,1)S(1)}, u32[]{:S(2)}, u32[]{:S(2)}) collective-permute-start(bf16[256,1024]{1,0:T(8,128)(2,1)S(1)} %get-tuple-element.17.m_ref.refs_0_), channel_id=1, source_target_pairs={{0,4},{4,8},{8,12},{12,0},{1,5},{5,9},{9,13},{13,1},{2,6},{6,10},{... | collective-permute-start | bytes 1572872 | tf_op jit(solution)/shard_map/ppermute | solution.py:33
  109.2 47.7 %collective-permute-start.12 = (bf16[256,1024]{1,0:T(8,128)(2,1)S(1)}, bf16[256,1024]{1,0:T(8,128)(2,1)S(1)}, u32[]{:S(2)}, u32[]{:S(2)}) collective-permute-start(bf16[256,1024]{1,0:T(8,128)(2,1)S(1)} %fusion.1), channel_id=1, source_target_pairs={{0,2},{2,0},{1,3},{3,1},{4,6},{6,4},{5,7},{7,5},{8,10},{10,8},{9,1... | collective-permute-start | bytes 1572872 | tf_op jit(solution)/shard_map/ppermute | solution.py:37
  (8 other events, 32.6 us)

commit v3 on v2

--- a/solution.py
+++ b/solution.py
@@ -193,29 +193,35 @@
 
 
 def mixed_grad_kernel(count, place_ref, *refs):
-    c_refs, w_ref, out_ref = refs[:count], refs[count], refs[count + 1]
+    c_refs, w_ref, out_ref, held, sems = refs[:count], refs[count], *refs[count + 1 :]
     depth = c_refs[0].shape[1]
-    columns = out_ref.shape[1]
-    width = min(512, columns)
-    for first in range(0, columns, width):
-        total = None
-        for i in range(count):
-            rows = pl.ds(pl.multiple_of(place_ref[i] * depth, depth), depth)
-            part = dot(c_refs[i][...], w_ref[rows, first : first + width])
-            total = part if total is None else total + part
-        out_ref[:, first : first + width] = total.astype(BF16)
-
-
-def partial_kernel(place_ref, m_ref, w_ref, keep_ref, give_ref):
+    copies = []
+    for i in range(count):
+        rows = pl.ds(pl.multiple_of(place_ref[i] * depth, depth), depth)
+        copies.append(pltpu.make_async_copy(w_ref.at[rows, :], held.at[i], sems.at[i]))
+    for copy in copies:
+        copy.start()
+    total = None
+    for i, copy in enumerate(copies):
+        copy.wait()
+        part = dot(c_refs[i][...], held[i])
+        total = part if total is None else total + part
+    out_ref[...] = total.astype(BF16)
+
+
+def partial_kernel(place_ref, m_ref, w_ref, keep_ref, give_ref, held, sems):
     depth = keep_ref.shape[2]
-    half = depth // 2
-    for out_ref, base in ((give_ref, 2), (keep_ref, 0)):
-        for i in range(2):
-            for part in range(2):
-                first = pl.multiple_of(place_ref[base + i] * depth + part * half, half)
-                out_ref[i, :, part * half : (part + 1) * half] = dot_nt(
-                    m_ref[...], w_ref[pl.ds(first, half), :]
-                ).astype(BF16)
+    copies = []
+    for i in range(4):
+        rows = pl.ds(pl.multiple_of(place_ref[i] * depth, depth), depth)
+        copies.append(pltpu.make_async_copy(w_ref.at[rows, :], held.at[i], sems.at[i]))
+    for copy in copies:
+        copy.start()
+    outs = [(give_ref, 0), (give_ref, 1), (keep_ref, 0), (keep_ref, 1)]
+    for i, copy in enumerate(copies):
+        copy.wait()
+        out_ref, at = outs[i]
+        out_ref[at] = dot_nt(m_ref[...], held[i]).astype(BF16)
 
 
 def weight_grad_kernel(count, place_ref, c_ref, *refs):
@@ -232,33 +238,48 @@
 
 def cost(flops, bytes_accessed, exps=0):
     return pl.CostEstimate(
-        flops=int(flops), bytes_accessed=int(bytes_accessed), transcendentals=int(exps)
-    )
-
-
-def kernel_call(body, name, scalars, arrays, out_shape, estimate):
+        flops=int(flops * ORDER_WEIGHT),
+        bytes_accessed=int(bytes_accessed * ORDER_WEIGHT),
+        transcendentals=int(exps),
+    )
+
+
+def kernel_call(body, name, scalars, arrays, out_shape, estimate, outside=(), scratch=()):
     smem = pl.BlockSpec(memory_space=pltpu.SMEM)
     vmem = pl.BlockSpec(memory_space=pltpu.VMEM)
     return pl.pallas_call(
         body,
-        in_specs=[smem] * len(scalars) + [vmem] * len(arrays),
+        in_specs=[smem] * len(scalars)
+        + [vmem] * len(arrays)
+        + [pl.BlockSpec(memory_space=pltpu.HBM)] * len(outside),
         out_specs=jax.tree.map(lambda _: vmem, out_shape),
         out_shape=out_shape,
-        compiler_params=pltpu.CompilerParams(vmem_limit_bytes=VMEM_LIMIT),
+        scratch_shapes=list(scratch),
+        compiler_params=pltpu.CompilerParams(
+            vmem_limit_bytes=STREAM_LIMIT if outside else VMEM_LIMIT
+        ),
         cost_estimate=estimate,
         name=name,
-    )(*scalars, *arrays)
-
-
-VMEM_LIMIT = 16 * 1024 * 1024
-
-
-def features_here(value):
+    )(*scalars, *arrays, *outside)
+
+
+def weight_scratch(count, depth, columns):
+    return [pltpu.VMEM((count, depth, columns), BF16), pltpu.SemaphoreType.DMA((count,))]
+
+
+VMEM_LIMIT = 20 * 1024 * 1024
+ORDER_WEIGHT = 100
+STREAM_LIMIT = 54 * 1024 * 1024
+
+
+def features_here(value, *others, serial=False):
     heads, reps = lax.axis_size("head"), lax.axis_size("rep")
     if heads == 2 and reps == 2:
         h, r = lax.axis_index("head"), lax.axis_index("rep")
-        across = swap(value, "head")
-        blocks = [value, swap(value, "rep"), across, swap(across, "rep")]
+        across = swap(after(value, *others), "head")
+        beside = swap(after(value, across) if serial else value, "rep")
+        corner = swap(after(across, beside) if serial else across, "rep")
+        blocks = [value, beside, across, corner]
         places = [2 * h + r, 2 * h + 1 - r, 2 * (1 - h) + r, 2 * (1 - h) + 1 - r]
         return blocks, jnp.stack(places).astype(jnp.int32)
     gathered = lax.all_gather(value, ("head", "rep"), axis=0)
@@ -266,21 +287,23 @@
     return [gathered[i] for i in range(count)], jnp.arange(count, dtype=jnp.int32)
 
 
-def attended_share(mixed_heads, out_weight, places, estimate):
+def attended_share(mixed_heads, out_weight, places, estimate, *others):
     heads, reps = lax.axis_size("head"), lax.axis_size("rep")
     rows = mixed_heads.shape[0]
     if heads == 2 and reps == 2:
         share = out_weight.shape[0] // 4
-        order = jnp.stack([places[0], places[2], places[1], places[3]])
+        order = jnp.stack([places[1], places[3], places[0], places[2]])
         keep, give = kernel_call(
             partial_kernel,
             "attended_partial",
             [order],
-            [mixed_heads, out_weight],
+            [mixed_heads],
             [jax.ShapeDtypeStruct((2, rows, share), BF16)] * 2,
             estimate,
+            [out_weight],
+            weight_scratch(4, share, mixed_heads.shape[1]),
         )
-        got = swap(give, "rep")
+        got = swap(after(give, *others), "rep")
         across = (keep[1].astype(F32) + got[1].astype(F32)).astype(BF16)
         across = swap(across, "head")
         return (keep[0].astype(F32) + got[0].astype(F32) + across.astype(F32)).astype(BF16)
@@ -326,16 +349,18 @@
     group_count = len(c_blocks)
     part_cols = cotangent.shape[1]
     key_all = further(key_all, 1)
-    value_all = further(value_all, 1, query_all[1])
+    value_all = further(value_all, 1, key_all[-1])
     query_all = further(query_all, -1)
 
     mixed_grad = kernel_call(
         functools.partial(mixed_grad_kernel, group_count),
         "mixed_grad",
         [c_places],
-        [*c_blocks, out_weight],
+        c_blocks,
         like_queries,
         cost(2 * rows * columns * features, 2 * columns * features),
+        [out_weight],
+        weight_scratch(group_count, part_cols, columns),
     )
     grad_all = further([mixed_grad], -1)
 
@@ -354,7 +379,7 @@
 
     while len(key_all) < count:
         key_all = further(key_all, 1)
-        value_all = further(value_all, 1)
+        value_all = further(value_all, 1, key_all[-1])
         query_all = further(query_all, -1)
     held_queries = after(queries, query_all[-1], grad_all[1], arrived)
     mixed_heads, lse = kernel_call(
@@ -377,9 +402,9 @@
             for k in range(peers)
         ]
 
-    attended = attended_share(
-        mixed_heads, out_weight, c_places, cost(2 * rows * columns * features, 2 * rows * features)
-    )
+    estimate = cost(2 * rows * columns * features, 2 * rows * features)
+    attended = attended_share(mixed_heads, out_weight, c_places, estimate, grad_all[-1])
+    ct_blocks, ct_places = features_here(arrived, mixed_heads, serial=True)
 
     stats_shape = jax.ShapeDtypeStruct((2 * heads_up + 8, rows), F32)
     q_grad, stats = kernel_call(
@@ -390,7 +415,9 @@
         [like_queries, stats_shape],
         cost(3 * attention_flops, (2 * count + 3) * array_bytes, exps),
     )
-    stats_all = [stats] + [shift(stats, -d) for d in distances[1:]]
+    stats_all = [after(stats, ct_blocks[-1])]
+    while len(stats_all) < count:
+        stats_all = further(stats_all, -1)
     k_grad, v_grad = kernel_call(
         functools.partial(key_kernel, tiles, count, heads, heads_up),
         "attention_key_grad",
@@ -400,7 +427,6 @@
         cost(4 * attention_flops, (2 * count + 4) * array_bytes, exps),
     )
 
-    ct_blocks, ct_places = features_here(arrived)
     steps = step_of(ct_places)
     ct_at = jnp.sum(
         jnp.where(steps[None] == jnp.arange(peers)[:, None], jnp.arange(group_count)[None], 0), 1
@@ -409,7 +435,7 @@
         functools.partial(weight_grad_kernel, peers),
         "weight_grad",
         [ct_at],
-        [jnp.stack(ct_blocks), *mixed_all],
+        [jnp.stack(ct_blocks), after(mixed_all[0], attended, k_grad), *mixed_all[1:]],
         jax.ShapeDtypeStruct((part_cols, columns), BF16),
         cost(2 * part_cols * columns * rows * peers, 2 * array_bytes * peers),
     )

time: 159 us -> 164 us (1.031)
  Pallas kernels: 27.1 us -> 37.7 us
  local copies, waits for them, and re-layouts: 10.3 us -> 0.14 us
  starting transfers between devices: 50.4 us -> 54.5 us
  other arithmetic: 3.83 us -> 6.48 us
  waiting for transfers between devices: 65.6 us -> 63.6 us
    ppermute x3, waiting for transfers between devices: 34.8 us -> 0.01 us  [cyclic(): lax.ppermute(value, 'seq', [(i, (i + by) % peers) for i in range(peers)])]
    ppermute x10, waiting for transfers between devices: 24 us -> 54.6 us  [shift(): lax.ppermute(value, 'seq', [(i, i + by) for i in range(peers) if 0 <= i +...]
    pallas_call x6, Pallas kernels: 27.1 us -> 37.7 us  [kernel_call(): pl.pallas_call(body, in_specs=[smem] * len(scalars) + [vmem] * len(arrays...]
    unnamed x20 -> x24, local copies, waits for them, and re-layouts: 10.2 us -> 0.05 us
    ppermute x10, starting transfers between devices: 25 us -> 31.8 us  [shift(): lax.ppermute(value, 'seq', [(i, i + by) for i in range(peers) if 0 <= i +...]
    ppermute x8, starting transfers between devices: 16.5 us -> 11 us  [swap(): return lax.ppermute(value, axis, [(0, 1), (1, 0)])]
    ppermute x3, starting transfers between devices: 3.48 us -> 6.37 us  [cyclic(): lax.ppermute(value, 'seq', [(i, (i + by) % peers) for i in range(peers)])]
    ppermute x8, waiting for transfers between devices: 6.74 us -> 8.98 us  [swap(): return lax.ppermute(value, axis, [(0, 1), (1, 0)])]
  transfers between devices with their start and end apart: 22 -> 22, of which waited for: 9 -> 7; matrix products, arithmetic and copies ran while one was open for 2% -> 4% of each run, Pallas kernels for 13% -> 17%
where the time goes in v3:
time: 164 us; the launch traced here: 163 us
  waiting for transfers between devices  63.6 us (39%)
  starting transfers between devices  54.5 us (33%)
  Pallas kernels  37.7 us (23%)
  other arithmetic  6.48 us (4%)
    ppermute x10, waiting for transfers between devices, shift(): lax.ppermute(value, 'seq', [(i, i + by) for i in range(peers) if 0 <= i +...  54.6 us
    pallas_call x6, Pallas kernels, kernel_call(): pl.pallas_call(body, in_specs=[smem] * len(scalars) + [vmem] * len(arrays...  37.7 us
    ppermute x10, starting transfers between devices, shift(): lax.ppermute(value, 'seq', [(i, i + by) for i in range(peers) if 0 <= i +...  31.8 us
    ppermute x8, starting transfers between devices, swap(): return lax.ppermute(value, axis, [(0, 1), (1, 0)])  11 us
    ppermute x8, waiting for transfers between devices, swap(): return lax.ppermute(value, axis, [(0, 1), (1, 0)])  8.98 us
    ppermute x3, starting transfers between devices, cyclic(): lax.ppermute(value, 'seq', [(i, (i + by) % peers) for i in range(peers)])  6.37 us
    ppermute x1, starting transfers between devices, per_device(): arrived = lax.ppermute(out_block, ('seq', 'head', 'rep'), links)  5.37 us
  transfers between devices with their start and end apart: 22, of which 7 were waited for; matrix products, arithmetic and copies ran while one was open for 4% of the time, Pallas kernels for 17%

profile of v3, /device:TPU:0, one launch (start us, length us, event | category | flops | bytes accessed | tf_op | source)
XLA Modules:
  0.0 163.3 jit_solution(3605001171000065976)
XLA Ops:
  0.6 3.0 %collective-permute-start.3 = (bf16[256,1024]{1,0:T(8,128)(2,1)}, bf16[256,1024]{1,0:T(8,128)(2,1)S(1)}, u32[]{:S(2)}, u32[]{:S(2)}) collective-permute-start(bf16[256,1024]{1,0:T(8,128)(2,1)} %refs_0_.4), channel_id=1, source_target_pairs={{0,2},{2,0},{1,3},{3,1},{4,6},{6,4},{5,7},{7,5},{8,10},{10,8},{9,1... | collective-permute-start | bytes 1572872 | tf_op jit(solution)/shard_map/ppermute | solution.py:37
  4.9 5.4 %collective-permute-start.7 = (bf16[256,1024]{1,0:T(8,128)(2,1)}, bf16[256,1024]{1,0:T(8,128)(2,1)}, u32[]{:S(2)}, u32[]{:S(2)}) collective-permute-start(bf16[256,1024]{1,0:T(8,128)(2,1)} %k_ref.1), channel_id=1, source_target_pairs={{0,4},{4,8},{8,12},{1,5},{5,9},{9,13},{2,6},{6,10},{10,14},{3,7},{... | collective-permute-start | bytes 1572872 | tf_op jit(solution)/shard_map/ppermute | solution.py:26
  10.3 5.5 %collective-permute-done.3.refs_2_ = bf16[256,1024]{1,0:T(8,128)(2,1)S(1)} collective-permute-done((bf16[256,1024]{1,0:T(8,128)(2,1)}, bf16[256,1024]{1,0:T(8,128)(2,1)S(1)}, u32[]{:S(2)}, u32[]{:S(2)}) %collective-permute-start.3) | collective-permute-done | bytes 524320 | tf_op jit(solution)/shard_map/ppermute | solution.py:37
  15.8 4.5 %collective-permute-start.9 = (bf16[256,1024]{1,0:T(8,128)(2,1)}, bf16[256,1024]{1,0:T(8,128)(2,1)}, u32[]{:S(2)}, u32[]{:S(2)}) collective-permute-start(bf16[256,1024]{1,0:T(8,128)(2,1)} %v_ref.1), channel_id=1, source_target_pairs={{0,4},{4,8},{8,12},{1,5},{5,9},{9,13},{2,6},{6,10},{10,14},{3,7},{... | collective-permute-start | bytes 1572872 | tf_op jit(solution)/shard_map/ppermute | solution.py:26
  22.3 5.4 %collective-permute-start.8 = (bf16[256,1024]{1,0:T(8,128)(2,1)}, bf16[256,1024]{1,0:T(8,128)(2,1)}, u32[]{:S(2)}, u32[]{:S(2)}) collective-permute-start(bf16[256,1024]{1,0:T(8,128)(2,1)} %collective-permute-done.7.refs_1_), channel_id=1, source_target_pairs={{0,4},{4,8},{8,12},{1,5},{5,9},{9,13},{2,6},{6,10},{10,14},{3,7},{... | collective-permute-start | bytes 1572872 | tf_op jit(solution)/shard_map/ppermute | solution.py:26
  27.7 2.3 %select_select_fusion = bf16[256,1024]{1,0:T(8,128)(2,1)} fusion(bf16[256,1024]{1,0:T(8,128)(2,1)S(1)} %collective-permute-done.4.refs_3_, bf16[256,1024]{1,0:T(8,128)(2,1)S(1)} %collective-permute-done.3.refs_2_, bf16[256,1024]{1,0:T(8,128)(2,1)S(1)} %collective-permute-done.2.refs_1_, bf16[256,1024]{1,0:T(8,128)(2,1)} %refs_0_.4, pred[]{:T(512)S(6)} %eq.33, ...), kind=kLoop, calls=%fused_computation.5 | loop fusion | flops 786432 | bytes 2621443 | tf_op jit(solution)/shard_map/jit(_where)/select_n | solution.py:373
  30.0 5.4 %collective-permute-start.6 = (bf16[256,1024]{1,0:T(8,128)(2,1)}, bf16[256,1024]{1,0:T(8,128)(2,1)}, u32[]{:S(2)}, u32[]{:S(2)}) collective-permute-start(bf16[256,1024]{1,0:T(8,128)(2,1)} %select_select_fusion), channel_id=1, source_target_pairs={{0,0},{1,9},{2,6},{3,15},{4,4},{5,13},{6,10},{7,3},{8,8},{9,1},{10... | collective-permute-start | bytes 1572872 | tf_op jit(solution)/shard_map/ppermute | solution.py:378
  35.4 7.1 %mixed_grad.1.g_ref.refs_3_ = bf16[256,1024]{1,0:T(8,128)(2,1)} custom-call(s32[4]{0:T(128)} %get-tuple-element.38.place_ref, bf16[256,1024]{1,0:T(8,128)(2,1)} %refs_0_.4, bf16[256,1024]{1,0:T(8,128)(2,1)} %copy-done.6, bf16[256,1024]{1,0:T(8,128)(2,1)} %copy-done.5, bf16[256,1024]{1,0:T(8,128)(2,1)} %copy-done.7, bf16[4096,1024]{1,0:T(8,128)(2,1)} %w_ref.1), custom_call_target="tpu_custom_call" | custom-call | flops 214748364800 | bytes 838860800 | tf_op jit(solution)/shard_map/mixed_grad/pallas_call | solution.py:250
  43.9 8.4 %collective-permute-start.10 = (bf16[256,1024]{1,0:T(8,128)(2,1)}, bf16[256,1024]{1,0:T(8,128)(2,1)S(1)}, u32[]{:S(2)}, u32[]{:S(2)}) collective-permute-start(bf16[256,1024]{1,0:T(8,128)(2,1)} %collective-permute-done.9.refs_4_), channel_id=1, source_target_pairs={{0,4},{4,8},{8,12},{1,5},{5,9},{9,13},{2,6},{6,10},{10,14},{3,7},{... | collective-permute-start | bytes 1572872 | tf_op jit(solution)/shard_map/ppermute | solution.py:26
  52.5 7.1 %collective-permute-done.5.refs_4_ = bf16[256,1024]{1,0:T(8,128)(2,1)} collective-permute-done((bf16[256,1024]{1,0:T(8,128)(2,1)}, bf16[256,1024]{1,0:T(8,128)(2,1)}, u32[]{:S(2)}, u32[]{:S(2)}) %collective-permute-start.5) | collective-permute-done | bytes 524320 | tf_op jit(solution)/shard_map/ppermute | solution.py:26
  59.8 4.6 %attention_forward.1 = (bf16[256,1024]{1,0:T(8,128)(2,1)}, f32[8,256]{1,0:T(8,128)S(1)}) custom-call(s32[10]{0:T(128)S(1)} %reshape.264.use_ref, bf16[256,1024]{1,0:T(8,128)(2,1)S(1)} %copy-done, bf16[256,1024]{1,0:T(8,128)(2,1)S(1)} %copy-done.1, bf16[256,1024]{1,0:T(8,128)(2,1)} %collective-permute-done.7.refs_1_, ...), custom_call_target="tpu_custom_call" | custom-call | flops 53687091200 | bytes 419430400 | tf_op jit(solution)/shard_map/attention_forward/pallas_call | solution.py:250
  64.4 7.1 %collective-permute-start.14 = (bf16[256,1024]{1,0:T(8,128)(2,1)}, bf16[256,1024]{1,0:T(8,128)(2,1)S(1)}, u32[]{:S(2)}, u32[]{:S(2)}) collective-permute-start(bf16[256,1024]{1,0:T(8,128)(2,1)} %collective-permute-done.6), channel_id=1, source_target_pairs={{0,2},{2,0},{1,3},{3,1},{4,6},{6,4},{5,7},{7,5},{8,10},{10,8},{9,1... | collective-permute-start | bytes 1572872 | tf_op jit(solution)/shard_map/ppermute | solution.py:37
  72.2 2.4 %collective-permute-start.19 = (bf16[256,1024]{1,0:T(8,128)(2,1)}, bf16[256,1024]{1,0:T(8,128)(2,1)}, u32[]{:S(2)}, u32[]{:S(2)}) collective-permute-start(bf16[256,1024]{1,0:T(8,128)(2,1)} %get-tuple-element.36.m_ref.refs_0_), channel_id=1, source_target_pairs={{0,4},{4,8},{8,12},{12,0},{1,5},{5,9},{9,13},{13,1},{2,6},{6,10},{... | collective-permute-start | bytes 1572872 | tf_op jit(solution)/shard_map/ppermute | solution.py:33
  74.6 2.6 %collective-permute-start.20 = (bf16[256,1024]{1,0:T(8,128)(2,1)}, bf16[256,1024]{1,0:T(8,128)(2,1)}, u32[]{:S(2)}, u32[]{:S(2)}) collective-permute-start(bf16[256,1024]{1,0:T(8,128)(2,1)} %get-tuple-element.36.m_ref.refs_0_), channel_id=1, source_target_pairs={{0,8},{4,12},{8,0},{12,4},{1,9},{5,13},{9,1},{13,5},{2,10},{6,14},... | collective-permute-start | bytes 1572872 | tf_op jit(solution)/shard_map/ppermute | solution.py:33
  80.0 3.5 %collective-permute-done.14 = bf16[256,1024]{1,0:T(8,128)(2,1)S(1)} collective-permute-done((bf16[256,1024]{1,0:T(8,128)(2,1)}, bf16[256,1024]{1,0:T(8,128)(2,1)S(1)}, u32[]{:S(2)}, u32[]{:S(2)}) %collective-permute-start.14) | collective-permute-done | bytes 524320 | tf_op jit(solution)/shard_map/ppermute | solution.py:37
  83.5 6.8 %attended_partial.1 = (bf16[2,256,1024]{2,1,0:T(8,128)(2,1)}, bf16[2,256,1024]{2,1,0:T(8,128)(2,1)}) custom-call(s32[4]{0:T(128)} %pad_add_fusion.place_ref, bf16[256,1024]{1,0:T(8,128)(2,1)} %get-tuple-element.36.m_ref.refs_0_, bf16[4096,1024]{1,0:T(8,128)(2,1)} %w_ref.1), custom_call_target="tpu_custom_call" | custom-call | flops 214748364800 | bytes 209715200 | tf_op jit(solution)/shard_map/attended_partial/pallas_call | solution.py:250
  90.4 31.0 %collective-permute-done.11.refs_5_ = bf16[256,1024]{1,0:T(8,128)(2,1)} collective-permute-done((bf16[256,1024]{1,0:T(8,128)(2,1)}, bf16[256,1024]{1,0:T(8,128)(2,1)}, u32[]{:S(2)}, u32[]{:S(2)}) %collective-permute-start.11) | collective-permute-done | bytes 524320 | tf_op jit(solution)/shard_map/ppermute | solution.py:26
  121.8 7.6 %attention_query_grad.1 = (bf16[256,1024]{1,0:T(8,128)(2,1)}, f32[24,256]{1,0:T(8,128)S(1)}) custom-call(s32[10]{0:T(128)S(1)} %reshape.264.use_ref, bf16[256,1024]{1,0:T(8,128)(2,1)S(1)} %copy-done, bf16[256,1024]{1,0:T(8,128)(2,1)S(1)} %copy-done.3, f32[8,256]{1,0:T(8,128)S(1)} %get-tuple-element.27.lse_ref, bf16[256,1024]{1,0:T(8,128)(2,1)S(1)} %copy-done.1, ...), custom_call_target="tpu_custom_call" | custom-call | flops 80530636800 | bytes 471859200 | tf_op jit(solution)/shard_map/attention_query_grad/pallas_call | solution.py:250
  131.4 13.6 %collective-permute-done.17.refs_7_ = f32[24,256]{1,0:T(8,128)S(1)} collective-permute-done((f32[24,256]{1,0:T(8,128)S(1)}, f32[24,256]{1,0:T(8,128)S(1)}, u32[]{:S(2)}, u32[]{:S(2)}) %collective-permute-start.17) | collective-permute-done | bytes 24608 | tf_op jit(solution)/shard_map/ppermute | solution.py:26
  145.0 1.5 collective-permute-start.18
  146.5 1.5 pad_maximum_fusion.c_ref
  148.0 2.7 %collective-permute-done.18.refs_8_ = f32[24,256]{1,0:T(8,128)S(1)} collective-permute-done((f32[24,256]{1,0:T(8,128)S(1)}, f32[24,256]{1,0:T(8,128)S(1)}, u32[]{:S(2)}, u32[]{:S(2)}) %collective-permute-start.18) | collective-permute-done | bytes 24608 | tf_op jit(solution)/shard_map/ppermute | solution.py:26
  150.7 6.3 %attention_key_grad.1 = (bf16[256,1024]{1,0:T(8,128)(2,1)}, bf16[256,1024]{1,0:T(8,128)(2,1)}) custom-call(bf16[256,1024]{1,0:T(8,128)(2,1)S(1)} %copy-done.1, bf16[256,1024]{1,0:T(8,128)(2,1)S(1)} %copy-done.2, bf16[256,1024]{1,0:T(8,128)(2,1)S(1)} %copy-done, bf16[256,1024]{1,0:T(8,128)(2,1)} %collective-permute-done.refs_1_, ...), custom_call_target="tpu_custom_call" | custom-call | flops 107374182400 | bytes 524288000 | tf_op jit(solution)/shard_map/attention_key_grad/pallas_call | solution.py:250
  158.1 5.2 %weight_grad.1 = bf16[1024,1024]{1,0:T(8,128)(2,1)} custom-call(s32[4]{0:T(128)S(1)} %select_reduce_fusion.place_ref, bf16[4,256,1024]{2,1,0:T(8,128)(2,1)S(1)} %pad_maximum_fusion.c_ref, bf16[256,1024]{1,0:T(8,128)(2,1)} %get-tuple-element.36.m_ref.refs_0_, bf16[256,1024]{1,0:T(8,128)(2,1)} %collective-permute-done.19.refs_1_, ...), custom_call_target="tpu_custom_call" | custom-call | flops 214748364800 | bytes 419430400 | tf_op jit(solution)/shard_map/weight_grad/pallas_call | solution.py:250
  (61 shorter events, 12.1 us)
Async XLA Ops:
  0.6 15.1 %collective-permute-start.3 = (bf16[256,1024]{1,0:T(8,128)(2,1)}, bf16[256,1024]{1,0:T(8,128)(2,1)S(1)}, u32[]{:S(2)}, u32[]{:S(2)}) collective-permute-start(bf16[256,1024]{1,0:T(8,128)(2,1)} %refs_0_.4), channel_id=1, source_target_pairs={{0,2},{2,0},{1,3},{3,1},{4,6},{6,4},{5,7},{7,5},{8,10},{10,8},{9,1... | collective-permute-start | bytes 1572872 | tf_op jit(solution)/shard_map/ppermute | solution.py:37
  3.6 17.3 %collective-permute-start = (bf16[256,1024]{1,0:T(8,128)(2,1)}, bf16[256,1024]{1,0:T(8,128)(2,1)}, u32[]{:S(2)}, u32[]{:S(2)}) collective-permute-start(bf16[256,1024]{1,0:T(8,128)(2,1)} %refs_0_.7), channel_id=1, source_target_pairs={{4,0},{8,4},{12,8},{5,1},{9,5},{13,9},{6,2},{10,6},{14,10},{7,3},{... | collective-permute-start | bytes 1572872 | tf_op jit(solution)/shard_map/ppermute | solution.py:26
  4.9 17.3 %collective-permute-start.7 = (bf16[256,1024]{1,0:T(8,128)(2,1)}, bf16[256,1024]{1,0:T(8,128)(2,1)}, u32[]{:S(2)}, u32[]{:S(2)}) collective-permute-start(bf16[256,1024]{1,0:T(8,128)(2,1)} %k_ref.1), channel_id=1, source_target_pairs={{0,4},{4,8},{8,12},{1,5},{5,9},{9,13},{2,6},{6,10},{10,14},{3,7},{... | collective-permute-start | bytes 1572872 | tf_op jit(solution)/shard_map/ppermute | solution.py:26
  10.3 17.4 %collective-permute-start.2 = (bf16[256,1024]{1,0:T(8,128)(2,1)}, bf16[256,1024]{1,0:T(8,128)(2,1)S(1)}, u32[]{:S(2)}, u32[]{:S(2)}) collective-permute-start(bf16[256,1024]{1,0:T(8,128)(2,1)} %refs_0_.4), channel_id=1, source_target_pairs={{0,1},{1,0},{2,3},{3,2},{4,5},{5,4},{6,7},{7,6},{8,9},{9,8},{10,11... | collective-permute-start | bytes 1572872 | tf_op jit(solution)/shard_map/ppermute | solution.py:37
  15.8 11.9 %collective-permute-start.4 = (bf16[256,1024]{1,0:T(8,128)(2,1)S(1)}, bf16[256,1024]{1,0:T(8,128)(2,1)S(1)}, u32[]{:S(2)}, u32[]{:S(2)}) collective-permute-start(bf16[256,1024]{1,0:T(8,128)(2,1)S(1)} %collective-permute-done.3.refs_2_), channel_id=1, source_target_pairs={{0,1},{1,0},{2,3},{3,2},{4,5},{5,4},{6,7},{7,6},{8,9},{9,8},{10,11... | collective-permute-start | bytes 1572872 | tf_op jit(solution)/shard_map/ppermute | solution.py:37
  15.8 28.1 %collective-permute-start.9 = (bf16[256,1024]{1,0:T(8,128)(2,1)}, bf16[256,1024]{1,0:T(8,128)(2,1)}, u32[]{:S(2)}, u32[]{:S(2)}) collective-permute-start(bf16[256,1024]{1,0:T(8,128)(2,1)} %v_ref.1), channel_id=1, source_target_pairs={{0,4},{4,8},{8,12},{1,5},{5,9},{9,13},{2,6},{6,10},{10,14},{3,7},{... | collective-permute-start | bytes 1572872 | tf_op jit(solution)/shard_map/ppermute | solution.py:26
  21.0 31.5 %collective-permute-start.1 = (bf16[256,1024]{1,0:T(8,128)(2,1)}, bf16[256,1024]{1,0:T(8,128)(2,1)}, u32[]{:S(2)}, u32[]{:S(2)}) collective-permute-start(bf16[256,1024]{1,0:T(8,128)(2,1)} %collective-permute-done.refs_1_), channel_id=1, source_target_pairs={{4,0},{8,4},{12,8},{5,1},{9,5},{13,9},{6,2},{10,6},{14,10},{7,3},{... | collective-permute-start | bytes 1572872 | tf_op jit(solution)/shard_map/ppermute | solution.py:26
  22.3 21.6 %collective-permute-start.8 = (bf16[256,1024]{1,0:T(8,128)(2,1)}, bf16[256,1024]{1,0:T(8,128)(2,1)}, u32[]{:S(2)}, u32[]{:S(2)}) collective-permute-start(bf16[256,1024]{1,0:T(8,128)(2,1)} %collective-permute-done.7.refs_1_), channel_id=1, source_target_pairs={{0,4},{4,8},{8,12},{1,5},{5,9},{9,13},{2,6},{6,10},{10,14},{3,7},{... | collective-permute-start | bytes 1572872 | tf_op jit(solution)/shard_map/ppermute | solution.py:26
  30.0 22.5 %collective-permute-start.6 = (bf16[256,1024]{1,0:T(8,128)(2,1)}, bf16[256,1024]{1,0:T(8,128)(2,1)}, u32[]{:S(2)}, u32[]{:S(2)}) collective-permute-start(bf16[256,1024]{1,0:T(8,128)(2,1)} %select_select_fusion), channel_id=1, source_target_pairs={{0,0},{1,9},{2,6},{3,15},{4,4},{5,13},{6,10},{7,3},{8,8},{9,1},{10... | collective-permute-start | bytes 1572872 | tf_op jit(solution)/shard_map/ppermute | solution.py:378
  42.5 17.0 %collective-permute-start.5 = (bf16[256,1024]{1,0:T(8,128)(2,1)}, bf16[256,1024]{1,0:T(8,128)(2,1)}, u32[]{:S(2)}, u32[]{:S(2)}) collective-permute-start(bf16[256,1024]{1,0:T(8,128)(2,1)} %mixed_grad.1.g_ref.refs_3_), channel_id=1, source_target_pairs={{4,0},{8,4},{12,8},{5,1},{9,5},{13,9},{6,2},{10,6},{14,10},{7,3},{... | collective-permute-start | bytes 1572872 | tf_op jit(solution)/shard_map/ppermute | solution.py:26
  43.9 15.9 %collective-permute-start.10 = (bf16[256,1024]{1,0:T(8,128)(2,1)}, bf16[256,1024]{1,0:T(8,128)(2,1)S(1)}, u32[]{:S(2)}, u32[]{:S(2)}) collective-permute-start(bf16[256,1024]{1,0:T(8,128)(2,1)} %collective-permute-done.9.refs_4_), channel_id=1, source_target_pairs={{0,4},{4,8},{8,12},{1,5},{5,9},{9,13},{2,6},{6,10},{10,14},{3,7},{... | collective-permute-start | bytes 1572872 | tf_op jit(solution)/shard_map/ppermute | solution.py:26
  64.4 19.1 %collective-permute-start.14 = (bf16[256,1024]{1,0:T(8,128)(2,1)}, bf16[256,1024]{1,0:T(8,128)(2,1)S(1)}, u32[]{:S(2)}, u32[]{:S(2)}) collective-permute-start(bf16[256,1024]{1,0:T(8,128)(2,1)} %collective-permute-done.6), channel_id=1, source_target_pairs={{0,2},{2,0},{1,3},{3,1},{4,6},{6,4},{5,7},{7,5},{8,10},{10,8},{9,1... | collective-permute-start | bytes 1572872 | tf_op jit(solution)/shard_map/ppermute | solution.py:37
  72.2 85.9 %collective-permute-start.19 = (bf16[256,1024]{1,0:T(8,128)(2,1)}, bf16[256,1024]{1,0:T(8,128)(2,1)}, u32[]{:S(2)}, u32[]{:S(2)}) collective-permute-start(bf16[256,1024]{1,0:T(8,128)(2,1)} %get-tuple-element.36.m_ref.refs_0_), channel_id=1, source_target_pairs={{0,4},{4,8},{8,12},{12,0},{1,5},{5,9},{9,13},{13,1},{2,6},{6,10},{... | collective-permute-start | bytes 1572872 | tf_op jit(solution)/shard_map/ppermute | solution.py:33
  74.6 83.5 %collective-permute-start.20 = (bf16[256,1024]{1,0:T(8,128)(2,1)}, bf16[256,1024]{1,0:T(8,128)(2,1)}, u32[]{:S(2)}, u32[]{:S(2)}) collective-permute-start(bf16[256,1024]{1,0:T(8,128)(2,1)} %get-tuple-element.36.m_ref.refs_0_), channel_id=1, source_target_pairs={{0,8},{4,12},{8,0},{12,4},{1,9},{5,13},{9,1},{13,5},{2,10},{6,14},... | collective-permute-start | bytes 1572872 | tf_op jit(solution)/shard_map/ppermute | solution.py:33
  77.2 80.9 %collective-permute-start.21 = (bf16[256,1024]{1,0:T(8,128)(2,1)}, bf16[256,1024]{1,0:T(8,128)(2,1)}, u32[]{:S(2)}, u32[]{:S(2)}) collective-permute-start(bf16[256,1024]{1,0:T(8,128)(2,1)} %get-tuple-element.36.m_ref.refs_0_), channel_id=1, source_target_pairs={{0,12},{4,0},{8,4},{12,8},{1,13},{5,1},{9,5},{13,9},{2,14},{6,2},{... | collective-permute-start | bytes 1572872 | tf_op jit(solution)/shard_map/ppermute | solution.py:33
  78.5 42.8 %collective-permute-start.11 = (bf16[256,1024]{1,0:T(8,128)(2,1)}, bf16[256,1024]{1,0:T(8,128)(2,1)}, u32[]{:S(2)}, u32[]{:S(2)}) collective-permute-start(bf16[256,1024]{1,0:T(8,128)(2,1)} %collective-permute-done.5.refs_4_), channel_id=1, source_target_pairs={{4,0},{8,4},{12,8},{5,1},{9,5},{13,9},{6,2},{10,6},{14,10},{7,3},{... | collective-permute-start | bytes 1572872 | tf_op jit(solution)/shard_map/ppermute | solution.py:26
  83.5 37.8 %collective-permute-start.15 = (bf16[256,1024]{1,0:T(8,128)(2,1)}, bf16[256,1024]{1,0:T(8,128)(2,1)}, u32[]{:S(2)}, u32[]{:S(2)}) collective-permute-start(bf16[256,1024]{1,0:T(8,128)(2,1)} %collective-permute-done.6), channel_id=1, source_target_pairs={{0,1},{1,0},{2,3},{3,2},{4,5},{5,4},{6,7},{7,6},{8,9},{9,8},{10,11... | collective-permute-start | bytes 1572872 | tf_op jit(solution)/shard_map/ppermute | solution.py:37
  83.5 38.3 %copy-start.3 = (bf16[256,1024]{1,0:T(8,128)(2,1)S(1)}, bf16[256,1024]{1,0:T(8,128)(2,1)}, u32[]{:S(2)}) copy-start(bf16[256,1024]{1,0:T(8,128)(2,1)} %mixed_grad.1.g_ref.refs_3_) | copy-start | bytes 1572868
  121.3 9.4 %collective-permute-start.12 = (bf16[2,256,1024]{2,1,0:T(8,128)(2,1)}, bf16[2,256,1024]{2,1,0:T(8,128)(2,1)S(1)}, u32[]{:S(2)}, u32[]{:S(2)}) collective-permute-start(bf16[2,256,1024]{2,1,0:T(8,128)(2,1)} %get-tuple-element.26), channel_id=1, source_target_pairs={{0,1},{1,0},{2,3},{3,2},{4,5},{5,4},{6,7},{7,6},{8,9},{9,8},{10,11... | collective-permute-start | bytes 3145736 | tf_op jit(solution)/shard_map/ppermute | solution.py:37
  121.3 8.1 %collective-permute-start.16 = (bf16[256,1024]{1,0:T(8,128)(2,1)}, bf16[256,1024]{1,0:T(8,128)(2,1)S(1)}, u32[]{:S(2)}, u32[]{:S(2)}) collective-permute-start(bf16[256,1024]{1,0:T(8,128)(2,1)} %copy-done.8), channel_id=1, source_target_pairs={{0,1},{1,0},{2,3},{3,2},{4,5},{5,4},{6,7},{7,6},{8,9},{9,8},{10,11... | collective-permute-start | bytes 1572872 | tf_op jit(solution)/shard_map/ppermute | solution.py:37
  121.8 24.7 %copy-start.9 = (bf16[256,1024]{1,0:T(8,128)(2,1)S(1)}, bf16[256,1024]{1,0:T(8,128)(2,1)}, u32[]{:S(2)}) copy-start(bf16[256,1024]{1,0:T(8,128)(2,1)} %copy-done.8) | copy-start | bytes 1572868
  129.4 15.6 %collective-permute-start.17 = (f32[24,256]{1,0:T(8,128)S(1)}, f32[24,256]{1,0:T(8,128)S(1)}, u32[]{:S(2)}, u32[]{:S(2)}) collective-permute-start(f32[24,256]{1,0:T(8,128)S(1)} %get-tuple-element.33.refs_6_), channel_id=1, source_target_pairs={{4,0},{8,4},{12,8},{5,1},{9,5},{13,9},{6,2},{10,6},{14,10},{7,3},{... | collective-permute-start | bytes 73736 | tf_op jit(solution)/shard_map/ppermute | solution.py:26
  130.9 26.1 %collective-permute-start.13 = (bf16[256,1024]{1,0:T(8,128)(2,1)S(1)}, bf16[256,1024]{1,0:T(8,128)(2,1)S(1)}, u32[]{:S(2)}, u32[]{:S(2)}) collective-permute-start(bf16[256,1024]{1,0:T(8,128)(2,1)S(1)} %fusion.1), channel_id=1, source_target_pairs={{0,2},{2,0},{1,3},{3,1},{4,6},{6,4},{5,7},{7,5},{8,10},{10,8},{9,1... | collective-permute-start | bytes 1572872 | tf_op jit(solution)/shard_map/ppermute | solution.py:37
  145.0 5.7 %collective-permute-start.18 = (f32[24,256]{1,0:T(8,128)S(1)}, f32[24,256]{1,0:T(8,128)S(1)}, u32[]{:S(2)}, u32[]{:S(2)}) collective-permute-start(f32[24,256]{1,0:T(8,128)S(1)} %collective-permute-done.17.refs_7_), channel_id=1, source_target_pairs={{4,0},{8,4},{12,8},{5,1},{9,5},{13,9},{6,2},{10,6},{14,10},{7,3},{... | collective-permute-start | bytes 73736 | tf_op jit(solution)/shard_map/ppermute | solution.py:26
  (10 other events, 160.5 us)

commit v4 on v3

--- a/solution.py
+++ b/solution.py
@@ -192,36 +192,54 @@
             dk_ref[rows, cols] = dot(cat(score_grads, 1), ques).astype(BF16)
 
 
-def mixed_grad_kernel(count, place_ref, *refs):
+class Stream:
+    def __init__(self, w_ref, held, sems, firsts, height):
+        self.held = held
+        self.height = height
+        self.copies = [
+            pltpu.make_async_copy(
+                w_ref.at[pl.ds(pl.multiple_of(first, height), height), :],
+                held.at[i],
+                sems.at[i],
+            )
+            for i, first in enumerate(firsts)
+        ]
+        for copy in self.copies[:2]:
+            copy.start()
+
+    def piece(self, i):
+        self.copies[i].wait()
+        if i + 2 < len(self.copies):
+            self.copies[i + 2].start()
+        return self.held[i]
+
+
+def mixed_grad_kernel(count, split, place_ref, *refs):
     c_refs, w_ref, out_ref, held, sems = refs[:count], refs[count], *refs[count + 1 :]
     depth = c_refs[0].shape[1]
-    copies = []
+    height = depth // split
+    firsts = [place_ref[i] * depth + part * height for i in range(count) for part in range(split)]
+    stream = Stream(w_ref, held, sems, firsts, height)
+    total = None
     for i in range(count):
-        rows = pl.ds(pl.multiple_of(place_ref[i] * depth, depth), depth)
-        copies.append(pltpu.make_async_copy(w_ref.at[rows, :], held.at[i], sems.at[i]))
-    for copy in copies:
-        copy.start()
-    total = None
-    for i, copy in enumerate(copies):
-        copy.wait()
-        part = dot(c_refs[i][...], held[i])
-        total = part if total is None else total + part
+        for part in range(split):
+            piece = stream.piece(i * split + part)
+            step = dot(c_refs[i][:, part * height : (part + 1) * height], piece)
+            total = step if total is None else total + step
     out_ref[...] = total.astype(BF16)
 
 
-def partial_kernel(place_ref, m_ref, w_ref, keep_ref, give_ref, held, sems):
+def partial_kernel(split, place_ref, m_ref, w_ref, keep_ref, give_ref, held, sems):
     depth = keep_ref.shape[2]
-    copies = []
-    for i in range(4):
-        rows = pl.ds(pl.multiple_of(place_ref[i] * depth, depth), depth)
-        copies.append(pltpu.make_async_copy(w_ref.at[rows, :], held.at[i], sems.at[i]))
-    for copy in copies:
-        copy.start()
+    height = depth // split
+    firsts = [place_ref[i] * depth + part * height for i in range(4) for part in range(split)]
+    stream = Stream(w_ref, held, sems, firsts, height)
     outs = [(give_ref, 0), (give_ref, 1), (keep_ref, 0), (keep_ref, 1)]
-    for i, copy in enumerate(copies):
-        copy.wait()
-        out_ref, at = outs[i]
-        out_ref[at] = dot_nt(m_ref[...], held[i]).astype(BF16)
+    for i, (out_ref, at) in enumerate(outs):
+        for part in range(split):
+            piece = stream.piece(i * split + part)
+            cols = slice(part * height, (part + 1) * height)
+            out_ref[at, :, cols] = dot_nt(m_ref[...], piece).astype(BF16)
 
 
 def weight_grad_kernel(count, place_ref, c_ref, *refs):
@@ -236,11 +254,11 @@
         out_ref[first : first + height, :] = total.astype(BF16)
 
 
-def cost(flops, bytes_accessed, exps=0):
+def cost(flops, bytes_accessed, exps=0, weight=1.0):
     return pl.CostEstimate(
-        flops=int(flops * ORDER_WEIGHT),
-        bytes_accessed=int(bytes_accessed * ORDER_WEIGHT),
-        transcendentals=int(exps),
+        flops=int(flops * weight),
+        bytes_accessed=int(bytes_accessed * weight),
+        transcendentals=int(exps * weight),
     )
 
 
@@ -268,7 +286,7 @@
 
 
 VMEM_LIMIT = 20 * 1024 * 1024
-ORDER_WEIGHT = 100
+WEIGHTS = dict(mixed_grad=100.0, forward=100.0, partial=0.0, query=100.0, key=0.0)
 STREAM_LIMIT = 54 * 1024 * 1024
 
 
@@ -287,30 +305,36 @@
     return [gathered[i] for i in range(count)], jnp.arange(count, dtype=jnp.int32)
 
 
-def attended_share(mixed_heads, out_weight, places, estimate, *others):
+def attended_partial(mixed_heads, out_weight, places, estimate):
     heads, reps = lax.axis_size("head"), lax.axis_size("rep")
-    rows = mixed_heads.shape[0]
     if heads == 2 and reps == 2:
+        rows = mixed_heads.shape[0]
         share = out_weight.shape[0] // 4
         order = jnp.stack([places[1], places[3], places[0], places[2]])
-        keep, give = kernel_call(
-            partial_kernel,
+        return kernel_call(
+            functools.partial(partial_kernel, 2),
             "attended_partial",
             [order],
             [mixed_heads],
             [jax.ShapeDtypeStruct((2, rows, share), BF16)] * 2,
             estimate,
             [out_weight],
-            weight_scratch(4, share, mixed_heads.shape[1]),
+            weight_scratch(8, share // 2, mixed_heads.shape[1]),
         )
-        got = swap(after(give, *others), "rep")
-        across = (keep[1].astype(F32) + got[1].astype(F32)).astype(BF16)
-        across = swap(across, "head")
-        return (keep[0].astype(F32) + got[0].astype(F32) + across.astype(F32)).astype(BF16)
     partial_value = lax.dot_general(mixed_heads, out_weight, NT, preferred_element_type=F32)
-    return lax.psum_scatter(
-        partial_value.astype(BF16), ("head", "rep"), scatter_dimension=1, tiled=True
-    )
+    return [partial_value.astype(BF16)]
+
+
+def attended_share(partial_products, *others):
+    if len(partial_products) == 1:
+        return lax.psum_scatter(
+            partial_products[0], ("head", "rep"), scatter_dimension=1, tiled=True
+        )
+    keep, give = partial_products
+    got = swap(after(give, *others), "rep")
+    across = (keep[1].astype(F32) + got[1].astype(F32)).astype(BF16)
+    across = swap(across, "head")
+    return (keep[0].astype(F32) + got[0].astype(F32) + across.astype(F32)).astype(BF16)
 
 
 def per_device(queries, keys, values, out_weight, level_mask, cotangent):
@@ -341,28 +365,34 @@
     use = ((block_ids[:, None] >= offsets[None]) & (level_mask == 1)).astype(jnp.int32)
     use = use.reshape(-1)
 
-    key_all, value_all, query_all = [keys], [values], [queries]
-    key_all = further(key_all, 1)
-    value_all = further(value_all, 1)
-    query_all = further(query_all, -1)
+    key_all = further([keys], 1)
+    value_all = further([values], 1)
+    query_all = further([queries], -1)
+    first_ones = (key_all[-1], value_all[-1], query_all[-1])
     c_blocks, c_places = features_here(cotangent)
     group_count = len(c_blocks)
     part_cols = cotangent.shape[1]
-    key_all = further(key_all, 1)
-    value_all = further(value_all, 1, key_all[-1])
-    query_all = further(query_all, -1)
-
+    while len(query_all) < count:
+        query_all = further(query_all, -1)
     mixed_grad = kernel_call(
-        functools.partial(mixed_grad_kernel, group_count),
+        functools.partial(mixed_grad_kernel, group_count, 2),
         "mixed_grad",
         [c_places],
         c_blocks,
         like_queries,
-        cost(2 * rows * columns * features, 2 * columns * features),
+        cost(2 * rows * columns * features, 2 * columns * features, 0, WEIGHTS["mixed_grad"]),
         [out_weight],
-        weight_scratch(group_count, part_cols, columns),
-    )
-    grad_all = further([mixed_grad], -1)
+        weight_scratch(2 * group_count, part_cols // 2, columns),
+    )
+    key_all = further(key_all, 1, *first_ones)
+    grad_all = further([mixed_grad], -1, query_all[-1])
+    while len(key_all) < count:
+        key_all = further(key_all, 1)
+    relayed = (key_all[-1], grad_all[-1])
+    while len(value_all) < count:
+        value_all = further(value_all, 1, *relayed)
+    while len(grad_all) < count:
+        grad_all = further(grad_all, -1, *relayed)
 
     h, r = lax.axis_index("head"), lax.axis_index("rep")
     n_head, n_rep = lax.axis_size("head"), lax.axis_size("rep")
@@ -375,56 +405,60 @@
     for s in range(peers):
         for q in range(group_count):
             links.append((s * group_count + q, ((s + step_of(q)) % peers) * group_count + q))
-    arrived = lax.ppermute(out_block, ("seq", "head", "rep"), links)
-
-    while len(key_all) < count:
-        key_all = further(key_all, 1)
-        value_all = further(value_all, 1, key_all[-1])
-        query_all = further(query_all, -1)
-    held_queries = after(queries, query_all[-1], grad_all[1], arrived)
+    arrived = lax.ppermute(after(out_block, *relayed), ("seq", "head", "rep"), links)
+
     mixed_heads, lse = kernel_call(
         functools.partial(forward_kernel, tiles, count, heads),
         "attention_forward",
         [use],
-        [held_queries, *key_all, *value_all],
+        [after(queries, query_all[-1]), *key_all, *value_all],
         [like_queries, jax.ShapeDtypeStruct((heads_up, rows), F32)],
-        cost(2 * attention_flops, (2 * count + 2) * array_bytes, exps),
-    )
-    while len(grad_all) < count:
-        grad_all = further(grad_all, -1)
-
+        cost(2 * attention_flops, (2 * count + 2) * array_bytes, exps, WEIGHTS["forward"]),
+    )
+    mixed_heads = after(mixed_heads, arrived, grad_all[-1])
+
+    near = {}
     if peers <= 4:
-        mixed_all = [mixed_heads] + [cyclic(mixed_heads, k) for k in range(1, peers)]
+        near = {k: cyclic(mixed_heads, k) for k in sorted({1, peers - 1}) if 0 < k < peers}
+    stats_shape = jax.ShapeDtypeStruct((2 * heads_up + 8, rows), F32)
+    q_grad, stats = kernel_call(
+        functools.partial(query_kernel, tiles, count, heads, heads_up),
+        "attention_query_grad",
+        [use],
+        [after(queries, mixed_heads), mixed_grad, lse, *key_all, *value_all],
+        [like_queries, stats_shape],
+        cost(3 * attention_flops, (2 * count + 3) * array_bytes, exps, WEIGHTS["query"]),
+    )
+    stats_all = [stats] + [shift(stats, -d) for d in distances[1:]]
+    partial_products = attended_partial(
+        mixed_heads, out_weight, c_places, cost(2 * rows * columns * features, 2 * rows * features, 0, WEIGHTS["partial"])
+    )
+    ct_across = swap(after(arrived, mixed_heads), "head") if n_head == 2 and n_rep == 2 else arrived
+    held = after(mixed_heads, ct_across, *near.values(), *stats_all[1:], *partial_products)
+    if peers <= 4:
+        mixed_all = [mixed_heads] + [
+            near[k] if k in near else cyclic(held, k) for k in range(1, peers)
+        ]
     else:
         gathered = lax.all_gather(mixed_heads, "seq", axis=0)
         mixed_all = [
             lax.dynamic_index_in_dim(gathered, (place - k) % peers, 0, False)
             for k in range(peers)
         ]
-
-    estimate = cost(2 * rows * columns * features, 2 * rows * features)
-    attended = attended_share(mixed_heads, out_weight, c_places, estimate, grad_all[-1])
-    ct_blocks, ct_places = features_here(arrived, mixed_heads, serial=True)
-
-    stats_shape = jax.ShapeDtypeStruct((2 * heads_up + 8, rows), F32)
-    q_grad, stats = kernel_call(
-        functools.partial(query_kernel, tiles, count, heads, heads_up),
-        "attention_query_grad",
-        [use],
-        [queries, mixed_grad, lse, *key_all, *value_all],
-        [like_queries, stats_shape],
-        cost(3 * attention_flops, (2 * count + 3) * array_bytes, exps),
-    )
-    stats_all = [after(stats, ct_blocks[-1])]
-    while len(stats_all) < count:
-        stats_all = further(stats_all, -1)
+    attended = attended_share(partial_products, held)
+    if n_head == 2 and n_rep == 2:
+        ct_blocks = [arrived, swap(after(arrived, held), "rep"), ct_across, swap(after(ct_across, held), "rep")]
+        ct_places = c_places
+    else:
+        ct_blocks, ct_places = features_here(arrived)
+    ct = jnp.stack(ct_blocks)
     k_grad, v_grad = kernel_call(
         functools.partial(key_kernel, tiles, count, heads, heads_up),
         "attention_key_grad",
         [],
-        [keys, values, *query_all, *grad_all, *stats_all],
+        [after(keys, held), values, *query_all, *grad_all, *stats_all],
         [like_queries] * 2,
-        cost(4 * attention_flops, (2 * count + 4) * array_bytes, exps),
+        cost(4 * attention_flops, (2 * count + 4) * array_bytes, exps, WEIGHTS["key"]),
     )
 
     steps = step_of(ct_places)
@@ -435,7 +469,7 @@
         functools.partial(weight_grad_kernel, peers),
         "weight_grad",
         [ct_at],
-        [jnp.stack(ct_blocks), after(mixed_all[0], attended, k_grad), *mixed_all[1:]],
+        [ct, after(mixed_all[0], attended, k_grad), *mixed_all[1:]],
         jax.ShapeDtypeStruct((part_cols, columns), BF16),
         cost(2 * part_cols * columns * rows * peers, 2 * array_bytes * peers),
     )

time: 164 us -> 161 us (0.982)
  waiting for transfers between devices: 63.6 us -> 61.2 us
  starting transfers between devices: 54.5 us -> 52.8 us
    ppermute x10, waiting for transfers between devices: 54.6 us -> 40.3 us  [shift(): lax.ppermute(value, 'seq', [(i, i + by) for i in range(peers) if 0 <= i +...]
    ppermute x3, waiting for transfers between devices: 0.01 us -> 13.6 us  [cyclic(): lax.ppermute(value, 'seq', [(i, (i + by) % peers) for i in range(peers)])]
    ppermute x8, starting transfers between devices: 11 us -> 19.3 us  [swap(): return lax.ppermute(value, axis, [(0, 1), (1, 0)])]
    ppermute x10, starting transfers between devices: 31.8 us -> 25.4 us  [shift(): lax.ppermute(value, 'seq', [(i, i + by) for i in range(peers) if 0 <= i +...]
    ppermute x1, starting transfers between devices: 5.37 us -> 0.83 us  [per_device(): lax.ppermute(after(out_block, *relayed), ('seq', 'head', 'rep'), links)]
    ppermute x8, waiting for transfers between devices: 8.98 us -> 7.26 us  [swap(): return lax.ppermute(value, axis, [(0, 1), (1, 0)])]
  transfers between devices with their start and end apart: 22 -> 22, of which waited for: 7 -> 10; matrix products, arithmetic and copies ran while one was open for 4% -> 3% of each run, Pallas kernels for 17% -> 21%
where the time goes in v4:
time: 161 us; the launch traced here: 160 us
  waiting for transfers between devices  61.2 us (38%)
  starting transfers between devices  52.8 us (33%)
  Pallas kernels  38.9 us (24%)
  other arithmetic  5.3 us (3%)
    ppermute x10, waiting for transfers between devices, shift(): lax.ppermute(value, 'seq', [(i, i + by) for i in range(peers) if 0 <= i +...  40.3 us
    pallas_call x6, Pallas kernels, kernel_call(): pl.pallas_call(body, in_specs=[smem] * len(scalars) + [vmem] * len(arrays...  38.9 us
    ppermute x10, starting transfers between devices, shift(): lax.ppermute(value, 'seq', [(i, i + by) for i in range(peers) if 0 <= i +...  25.4 us
    ppermute x8, starting transfers between devices, swap(): return lax.ppermute(value, axis, [(0, 1), (1, 0)])  19.3 us
    ppermute x3, waiting for transfers between devices, cyclic(): lax.ppermute(value, 'seq', [(i, (i + by) % peers) for i in range(peers)])  13.6 us
    ppermute x3, starting transfers between devices, cyclic(): lax.ppermute(value, 'seq', [(i, (i + by) % peers) for i in range(peers)])  7.37 us
    ppermute x8, waiting for transfers between devices, swap(): return lax.ppermute(value, axis, [(0, 1), (1, 0)])  7.26 us
  transfers between devices with their start and end apart: 22, of which 10 were waited for; matrix products, arithmetic and copies ran while one was open for 3% of the time, Pallas kernels for 21%

profile of v4, /device:TPU:0, one launch (start us, length us, event | category | flops | bytes accessed | tf_op | source)
XLA Modules:
  0.0 160.3 jit_solution(16334504979082220135)
XLA Ops:
  0.6 3.0 %collective-permute-start.6 = (bf16[256,1024]{1,0:T(8,128)(2,1)}, bf16[256,1024]{1,0:T(8,128)(2,1)S(1)}, u32[]{:S(2)}, u32[]{:S(2)}) collective-permute-start(bf16[256,1024]{1,0:T(8,128)(2,1)} %refs_0_.4), channel_id=1, source_target_pairs={{0,2},{2,0},{1,3},{3,1},{4,6},{6,4},{5,7},{7,5},{8,10},{10,8},{9,1... | collective-permute-start | bytes 1572872 | tf_op jit(solution)/shard_map/ppermute | solution.py:37
  4.9 4.6 %collective-permute-start.3 = (bf16[256,1024]{1,0:T(8,128)(2,1)}, bf16[256,1024]{1,0:T(8,128)(2,1)S(1)}, u32[]{:S(2)}, u32[]{:S(2)}) collective-permute-start(bf16[256,1024]{1,0:T(8,128)(2,1)} %v_ref.1), channel_id=1, source_target_pairs={{0,4},{4,8},{8,12},{1,5},{5,9},{9,13},{2,6},{6,10},{10,14},{3,7},{... | collective-permute-start | bytes 1572872 | tf_op jit(solution)/shard_map/ppermute | solution.py:26
  9.5 4.3 %collective-permute-start.2 = (bf16[256,1024]{1,0:T(8,128)(2,1)}, bf16[256,1024]{1,0:T(8,128)(2,1)}, u32[]{:S(2)}, u32[]{:S(2)}) collective-permute-start(bf16[256,1024]{1,0:T(8,128)(2,1)} %k_ref), channel_id=1, source_target_pairs={{0,4},{4,8},{8,12},{1,5},{5,9},{9,13},{2,6},{6,10},{10,14},{3,7},{... | collective-permute-start | bytes 1572872 | tf_op jit(solution)/shard_map/ppermute | solution.py:26
  13.8 2.0 %collective-permute-done.6.refs_2_ = bf16[256,1024]{1,0:T(8,128)(2,1)S(1)} collective-permute-done((bf16[256,1024]{1,0:T(8,128)(2,1)}, bf16[256,1024]{1,0:T(8,128)(2,1)S(1)}, u32[]{:S(2)}, u32[]{:S(2)}) %collective-permute-start.6) | collective-permute-done | bytes 524320 | tf_op jit(solution)/shard_map/ppermute | solution.py:37
  16.6 2.6 %collective-permute-done.refs_1_ = bf16[256,1024]{1,0:T(8,128)(2,1)} collective-permute-done((bf16[256,1024]{1,0:T(8,128)(2,1)}, bf16[256,1024]{1,0:T(8,128)(2,1)}, u32[]{:S(2)}, u32[]{:S(2)}) %collective-permute-start) | collective-permute-done | bytes 524320 | tf_op jit(solution)/shard_map/ppermute | solution.py:26
  22.2 9.5 %collective-permute-done.2.refs_1_ = bf16[256,1024]{1,0:T(8,128)(2,1)} collective-permute-done((bf16[256,1024]{1,0:T(8,128)(2,1)}, bf16[256,1024]{1,0:T(8,128)(2,1)}, u32[]{:S(2)}, u32[]{:S(2)}) %collective-permute-start.2) | collective-permute-done | bytes 524320 | tf_op jit(solution)/shard_map/ppermute | solution.py:26
  31.6 5.2 %collective-permute-start.4 = (bf16[256,1024]{1,0:T(8,128)(2,1)}, bf16[256,1024]{1,0:T(8,128)(2,1)}, u32[]{:S(2)}, u32[]{:S(2)}) collective-permute-start(bf16[256,1024]{1,0:T(8,128)(2,1)} %collective-permute-done.2.refs_1_), channel_id=1, source_target_pairs={{0,4},{4,8},{8,12},{1,5},{5,9},{9,13},{2,6},{6,10},{10,14},{3,7},{... | collective-permute-start | bytes 1572872 | tf_op jit(solution)/shard_map/ppermute | solution.py:26
  37.8 8.3 %mixed_grad.1.g_ref.refs_3_ = bf16[256,1024]{1,0:T(8,128)(2,1)} custom-call(s32[4]{0:T(128)} %get-tuple-element.52.place_ref, bf16[256,1024]{1,0:T(8,128)(2,1)} %refs_0_.4, bf16[256,1024]{1,0:T(8,128)(2,1)} %copy-done.8, bf16[256,1024]{1,0:T(8,128)(2,1)} %copy-done.7, bf16[256,1024]{1,0:T(8,128)(2,1)} %copy-done.9, bf16[4096,1024]{1,0:T(8,128)(2,1)} %w_ref.1), custom_call_target="tpu_custom_call" | custom-call | flops 214748364800 | bytes 838860800 | tf_op jit(solution)/shard_map/mixed_grad/pallas_call | solution.py:268
  47.6 12.7 %collective-permute-done.8.refs_4_ = bf16[256,1024]{1,0:T(8,128)(2,1)S(1)} collective-permute-done((bf16[256,1024]{1,0:T(8,128)(2,1)}, bf16[256,1024]{1,0:T(8,128)(2,1)S(1)}, u32[]{:S(2)}, u32[]{:S(2)}) %collective-permute-start.8) | collective-permute-done | bytes 524320 | tf_op jit(solution)/shard_map/ppermute | solution.py:26
  60.3 3.3 %collective-permute-start.9 = (bf16[256,1024]{1,0:T(8,128)(2,1)}, bf16[256,1024]{1,0:T(8,128)(2,1)S(1)}, u32[]{:S(2)}, u32[]{:S(2)}) collective-permute-start(bf16[256,1024]{1,0:T(8,128)(2,1)} %copy-done.4), channel_id=1, source_target_pairs={{0,4},{4,8},{8,12},{1,5},{5,9},{9,13},{2,6},{6,10},{10,14},{3,7},{... | collective-permute-start | bytes 1572872 | tf_op jit(solution)/shard_map/ppermute | solution.py:26
  67.1 9.1 %collective-permute-done.9.refs_5_ = bf16[256,1024]{1,0:T(8,128)(2,1)S(1)} collective-permute-done((bf16[256,1024]{1,0:T(8,128)(2,1)}, bf16[256,1024]{1,0:T(8,128)(2,1)S(1)}, u32[]{:S(2)}, u32[]{:S(2)}) %collective-permute-start.9) | collective-permute-done | bytes 524320 | tf_op jit(solution)/shard_map/ppermute | solution.py:26
  76.3 4.5 %attention_forward.1 = (bf16[256,1024]{1,0:T(8,128)(2,1)}, f32[8,256]{1,0:T(8,128)S(1)}) custom-call(s32[10]{0:T(128)S(1)} %reshape.264.use_ref, bf16[256,1024]{1,0:T(8,128)(2,1)S(1)} %copy-done, bf16[256,1024]{1,0:T(8,128)(2,1)S(1)} %copy-done.1, bf16[256,1024]{1,0:T(8,128)(2,1)} %collective-permute-done.2.refs_1_, ...), custom_call_target="tpu_custom_call" | custom-call | flops 53687091200 | bytes 419430400 | tf_op jit(solution)/shard_map/attention_forward/pallas_call | solution.py:268
  80.7 4.7 %collective-permute-done.11.refs_5_ = bf16[256,1024]{1,0:T(8,128)(2,1)S(1)} collective-permute-done((bf16[256,1024]{1,0:T(8,128)(2,1)S(1)}, bf16[256,1024]{1,0:T(8,128)(2,1)S(1)}, u32[]{:S(2)}, u32[]{:S(2)}) %collective-permute-start.11) | collective-permute-done | bytes 524320 | tf_op jit(solution)/shard_map/ppermute | solution.py:26
  85.5 2.7 %collective-permute-start.13 = (bf16[256,1024]{1,0:T(8,128)(2,1)}, bf16[256,1024]{1,0:T(8,128)(2,1)S(1)}, u32[]{:S(2)}, u32[]{:S(2)}) collective-permute-start(bf16[256,1024]{1,0:T(8,128)(2,1)} %get-tuple-element.50.m_ref.refs_0_), channel_id=1, source_target_pairs={{0,4},{4,8},{8,12},{12,0},{1,5},{5,9},{9,13},{13,1},{2,6},{6,10},{... | collective-permute-start | bytes 1572872 | tf_op jit(solution)/shard_map/ppermute | solution.py:33
  89.3 4.3 %collective-permute-start.12 = (bf16[256,1024]{1,0:T(8,128)(2,1)S(1)}, bf16[256,1024]{1,0:T(8,128)(2,1)S(1)}, u32[]{:S(2)}, u32[]{:S(2)}) collective-permute-start(bf16[256,1024]{1,0:T(8,128)(2,1)S(1)} %collective-permute-done.10), channel_id=1, source_target_pairs={{0,2},{2,0},{1,3},{3,1},{4,6},{6,4},{5,7},{7,5},{8,10},{10,8},{9,1... | collective-permute-start | bytes 1572872 | tf_op jit(solution)/shard_map/ppermute | solution.py:37
  93.6 7.3 %attention_query_grad.1 = (bf16[256,1024]{1,0:T(8,128)(2,1)}, f32[24,256]{1,0:T(8,128)S(1)}) custom-call(s32[10]{0:T(128)S(1)} %reshape.264.use_ref, bf16[256,1024]{1,0:T(8,128)(2,1)S(1)} %copy-done, bf16[256,1024]{1,0:T(8,128)(2,1)S(1)} %copy-done.3, f32[8,256]{1,0:T(8,128)S(1)} %get-tuple-element.40.lse_ref, bf16[256,1024]{1,0:T(8,128)(2,1)S(1)} %copy-done.1, ...), custom_call_target="tpu_custom_call" | custom-call | flops 80530636800 | bytes 471859200 | tf_op jit(solution)/shard_map/attention_query_grad/pallas_call | solution.py:268
  104.3 8.2 %attended_partial.1 = (bf16[2,256,1024]{2,1,0:T(8,128)(2,1)}, bf16[2,256,1024]{2,1,0:T(8,128)(2,1)}) custom-call(s32[4]{0:T(128)} %pad_add_fusion.place_ref, bf16[256,1024]{1,0:T(8,128)(2,1)} %get-tuple-element.50.m_ref.refs_0_, bf16[4096,1024]{1,0:T(8,128)(2,1)} %w_ref.1), custom_call_target="tpu_custom_call" | custom-call | tf_op jit(solution)/shard_map/attended_partial/pallas_call | solution.py:268
  112.5 9.6 %collective-permute-start.17 = (bf16[2,256,1024]{2,1,0:T(8,128)(2,1)}, bf16[2,256,1024]{2,1,0:T(8,128)(2,1)S(1)}, u32[]{:S(2)}, u32[]{:S(2)}) collective-permute-start(bf16[2,256,1024]{2,1,0:T(8,128)(2,1)} %get-tuple-element.43), channel_id=1, source_target_pairs={{0,1},{1,0},{2,3},{3,2},{4,5},{5,4},{6,7},{7,6},{8,9},{9,8},{10,11... | collective-permute-start | bytes 3145736 | tf_op jit(solution)/shard_map/ppermute | solution.py:37
  122.6 2.7 %collective-permute-done.17 = bf16[2,256,1024]{2,1,0:T(8,128)(2,1)S(1)} collective-permute-done((bf16[2,256,1024]{2,1,0:T(8,128)(2,1)}, bf16[2,256,1024]{2,1,0:T(8,128)(2,1)S(1)}, u32[]{:S(2)}, u32[]{:S(2)}) %collective-permute-start.17) | collective-permute-done | bytes 1048608 | tf_op jit(solution)/shard_map/ppermute | solution.py:37
  128.4 3.5 %collective-permute-start.21 = (bf16[256,1024]{1,0:T(8,128)(2,1)}, bf16[256,1024]{1,0:T(8,128)(2,1)S(1)}, u32[]{:S(2)}, u32[]{:S(2)}) collective-permute-start(bf16[256,1024]{1,0:T(8,128)(2,1)} %get-tuple-element.50.m_ref.refs_0_), channel_id=1, source_target_pairs={{0,8},{4,12},{8,0},{12,4},{1,9},{5,13},{9,1},{13,5},{2,10},{6,14},... | collective-permute-start | bytes 1572872 | tf_op jit(solution)/shard_map/ppermute | solution.py:33
  132.0 5.9 %attention_key_grad.1 = (bf16[256,1024]{1,0:T(8,128)(2,1)}, bf16[256,1024]{1,0:T(8,128)(2,1)}) custom-call(bf16[256,1024]{1,0:T(8,128)(2,1)S(1)} %copy-done.1, bf16[256,1024]{1,0:T(8,128)(2,1)S(1)} %copy-done.2, bf16[256,1024]{1,0:T(8,128)(2,1)S(1)} %copy-done, bf16[256,1024]{1,0:T(8,128)(2,1)} %collective-permute-done.refs_1_, ...), custom_call_target="tpu_custom_call" | custom-call | tf_op jit(solution)/shard_map/attention_key_grad/pallas_call | solution.py:268
  138.3 2.6 %collective-permute-done.18 = bf16[256,1024]{1,0:T(8,128)(2,1)S(1)} collective-permute-done((bf16[256,1024]{1,0:T(8,128)(2,1)S(1)}, bf16[256,1024]{1,0:T(8,128)(2,1)S(1)}, u32[]{:S(2)}, u32[]{:S(2)}) %collective-permute-start.18) | collective-permute-done | bytes 524320 | tf_op jit(solution)/shard_map/ppermute | solution.py:37
  141.9 13.6 %collective-permute-done.21.refs_2_ = bf16[256,1024]{1,0:T(8,128)(2,1)S(1)} collective-permute-done((bf16[256,1024]{1,0:T(8,128)(2,1)}, bf16[256,1024]{1,0:T(8,128)(2,1)S(1)}, u32[]{:S(2)}, u32[]{:S(2)}) %collective-permute-start.21) | collective-permute-done | bytes 524320 | tf_op jit(solution)/shard_map/ppermute | solution.py:33
  155.5 4.7 %weight_grad.1 = bf16[1024,1024]{1,0:T(8,128)(2,1)} custom-call(s32[4]{0:T(128)S(1)} %select_reduce_fusion.place_ref, bf16[4,256,1024]{2,1,0:T(8,128)(2,1)S(1)} %pad_maximum_fusion.c_ref, bf16[256,1024]{1,0:T(8,128)(2,1)} %get-tuple-element.50.m_ref.refs_0_, bf16[256,1024]{1,0:T(8,128)(2,1)S(1)} %collective-permute-done.13.refs_1_, ...), custom_call_target="tpu_custom_call" | custom-call | flops 2147483648 | bytes 4194304 | tf_op jit(solution)/shard_map/weight_grad/pallas_call | solution.py:268
  (61 shorter events, 20.4 us)
Async XLA Ops:
  0.6 15.1 %collective-permute-start.6 = (bf16[256,1024]{1,0:T(8,128)(2,1)}, bf16[256,1024]{1,0:T(8,128)(2,1)S(1)}, u32[]{:S(2)}, u32[]{:S(2)}) collective-permute-start(bf16[256,1024]{1,0:T(8,128)(2,1)} %refs_0_.4), channel_id=1, source_target_pairs={{0,2},{2,0},{1,3},{3,1},{4,6},{6,4},{5,7},{7,5},{8,10},{10,8},{9,1... | collective-permute-start | bytes 1572872 | tf_op jit(solution)/shard_map/ppermute | solution.py:37
  3.6 15.6 %collective-permute-start = (bf16[256,1024]{1,0:T(8,128)(2,1)}, bf16[256,1024]{1,0:T(8,128)(2,1)}, u32[]{:S(2)}, u32[]{:S(2)}) collective-permute-start(bf16[256,1024]{1,0:T(8,128)(2,1)} %refs_0_.7), channel_id=1, source_target_pairs={{4,0},{8,4},{12,8},{5,1},{9,5},{13,9},{6,2},{10,6},{14,10},{7,3},{... | collective-permute-start | bytes 1572872 | tf_op jit(solution)/shard_map/ppermute | solution.py:26
  4.9 17.2 %collective-permute-start.3 = (bf16[256,1024]{1,0:T(8,128)(2,1)}, bf16[256,1024]{1,0:T(8,128)(2,1)S(1)}, u32[]{:S(2)}, u32[]{:S(2)}) collective-permute-start(bf16[256,1024]{1,0:T(8,128)(2,1)} %v_ref.1), channel_id=1, source_target_pairs={{0,4},{4,8},{8,12},{1,5},{5,9},{9,13},{2,6},{6,10},{10,14},{3,7},{... | collective-permute-start | bytes 1572872 | tf_op jit(solution)/shard_map/ppermute | solution.py:26
  9.5 22.1 %collective-permute-start.2 = (bf16[256,1024]{1,0:T(8,128)(2,1)}, bf16[256,1024]{1,0:T(8,128)(2,1)}, u32[]{:S(2)}, u32[]{:S(2)}) collective-permute-start(bf16[256,1024]{1,0:T(8,128)(2,1)} %k_ref), channel_id=1, source_target_pairs={{0,4},{4,8},{8,12},{1,5},{5,9},{9,13},{2,6},{6,10},{10,14},{3,7},{... | collective-permute-start | bytes 1572872 | tf_op jit(solution)/shard_map/ppermute | solution.py:26
  13.8 23.1 %collective-permute-start.5 = (bf16[256,1024]{1,0:T(8,128)(2,1)}, bf16[256,1024]{1,0:T(8,128)(2,1)S(1)}, u32[]{:S(2)}, u32[]{:S(2)}) collective-permute-start(bf16[256,1024]{1,0:T(8,128)(2,1)} %refs_0_.4), channel_id=1, source_target_pairs={{0,1},{1,0},{2,3},{3,2},{4,5},{5,4},{6,7},{7,6},{8,9},{9,8},{10,11... | collective-permute-start | bytes 1572872 | tf_op jit(solution)/shard_map/ppermute | solution.py:37
  15.8 21.1 %collective-permute-start.7 = (bf16[256,1024]{1,0:T(8,128)(2,1)S(1)}, bf16[256,1024]{1,0:T(8,128)(2,1)S(1)}, u32[]{:S(2)}, u32[]{:S(2)}) collective-permute-start(bf16[256,1024]{1,0:T(8,128)(2,1)S(1)} %collective-permute-done.6.refs_2_), channel_id=1, source_target_pairs={{0,1},{1,0},{2,3},{3,2},{4,5},{5,4},{6,7},{7,6},{8,9},{9,8},{10,11... | collective-permute-start | bytes 1572872 | tf_op jit(solution)/shard_map/ppermute | solution.py:37
  19.2 26.9 %collective-permute-start.1 = (bf16[256,1024]{1,0:T(8,128)(2,1)}, bf16[256,1024]{1,0:T(8,128)(2,1)}, u32[]{:S(2)}, u32[]{:S(2)}) collective-permute-start(bf16[256,1024]{1,0:T(8,128)(2,1)} %collective-permute-done.refs_1_), channel_id=1, source_target_pairs={{4,0},{8,4},{12,8},{5,1},{9,5},{13,9},{6,2},{10,6},{14,10},{7,3},{... | collective-permute-start | bytes 1572872 | tf_op jit(solution)/shard_map/ppermute | solution.py:26
  31.6 16.0 %collective-permute-start.4 = (bf16[256,1024]{1,0:T(8,128)(2,1)}, bf16[256,1024]{1,0:T(8,128)(2,1)}, u32[]{:S(2)}, u32[]{:S(2)}) collective-permute-start(bf16[256,1024]{1,0:T(8,128)(2,1)} %collective-permute-done.2.refs_1_), channel_id=1, source_target_pairs={{0,4},{4,8},{8,12},{1,5},{5,9},{9,13},{2,6},{6,10},{10,14},{3,7},{... | collective-permute-start | bytes 1572872 | tf_op jit(solution)/shard_map/ppermute | solution.py:26
  46.1 30.2 %copy-start = (bf16[256,1024]{1,0:T(8,128)(2,1)S(1)}, bf16[256,1024]{1,0:T(8,128)(2,1)}, u32[]{:S(2)}) copy-start(bf16[256,1024]{1,0:T(8,128)(2,1)} %refs_0_.7) | copy-start | bytes 1572868
  46.1 30.2 %copy-start.1 = (bf16[256,1024]{1,0:T(8,128)(2,1)S(1)}, bf16[256,1024]{1,0:T(8,128)(2,1)}, u32[]{:S(2)}) copy-start(bf16[256,1024]{1,0:T(8,128)(2,1)} %k_ref) | copy-start | bytes 1572868
  46.2 14.1 %collective-permute-start.8 = (bf16[256,1024]{1,0:T(8,128)(2,1)}, bf16[256,1024]{1,0:T(8,128)(2,1)S(1)}, u32[]{:S(2)}, u32[]{:S(2)}) collective-permute-start(bf16[256,1024]{1,0:T(8,128)(2,1)} %mixed_grad.1.g_ref.refs_3_), channel_id=1, source_target_pairs={{4,0},{8,4},{12,8},{5,1},{9,5},{13,9},{6,2},{10,6},{14,10},{7,3},{... | collective-permute-start | bytes 1572872 | tf_op jit(solution)/shard_map/ppermute | solution.py:26
  60.3 16.0 %collective-permute-start.9 = (bf16[256,1024]{1,0:T(8,128)(2,1)}, bf16[256,1024]{1,0:T(8,128)(2,1)S(1)}, u32[]{:S(2)}, u32[]{:S(2)}) collective-permute-start(bf16[256,1024]{1,0:T(8,128)(2,1)} %copy-done.4), channel_id=1, source_target_pairs={{0,4},{4,8},{8,12},{1,5},{5,9},{9,13},{2,6},{6,10},{10,14},{3,7},{... | collective-permute-start | bytes 1572872 | tf_op jit(solution)/shard_map/ppermute | solution.py:26
  65.0 15.7 %collective-permute-start.10 = (bf16[256,1024]{1,0:T(8,128)(2,1)S(1)}, bf16[256,1024]{1,0:T(8,128)(2,1)S(1)}, u32[]{:S(2)}, u32[]{:S(2)}) collective-permute-start(bf16[256,1024]{1,0:T(8,128)(2,1)S(1)} %select_select_fusion), channel_id=1, source_target_pairs={{0,0},{1,9},{2,6},{3,15},{4,4},{5,13},{6,10},{7,3},{8,8},{9,1},{10... | collective-permute-start | bytes 1572872 | tf_op jit(solution)/shard_map/ppermute | solution.py:408
  65.8 19.6 %collective-permute-start.11 = (bf16[256,1024]{1,0:T(8,128)(2,1)S(1)}, bf16[256,1024]{1,0:T(8,128)(2,1)S(1)}, u32[]{:S(2)}, u32[]{:S(2)}) collective-permute-start(bf16[256,1024]{1,0:T(8,128)(2,1)S(1)} %collective-permute-done.8.refs_4_), channel_id=1, source_target_pairs={{4,0},{8,4},{12,8},{5,1},{9,5},{13,9},{6,2},{10,6},{14,10},{7,3},{... | collective-permute-start | bytes 1572872 | tf_op jit(solution)/shard_map/ppermute | solution.py:26
  85.5 27.0 %collective-permute-start.13 = (bf16[256,1024]{1,0:T(8,128)(2,1)}, bf16[256,1024]{1,0:T(8,128)(2,1)S(1)}, u32[]{:S(2)}, u32[]{:S(2)}) collective-permute-start(bf16[256,1024]{1,0:T(8,128)(2,1)} %get-tuple-element.50.m_ref.refs_0_), channel_id=1, source_target_pairs={{0,4},{4,8},{8,12},{12,0},{1,5},{5,9},{9,13},{13,1},{2,6},{6,10},{... | collective-permute-start | bytes 1572872 | tf_op jit(solution)/shard_map/ppermute | solution.py:33
  88.2 24.4 %collective-permute-start.14 = (bf16[256,1024]{1,0:T(8,128)(2,1)}, bf16[256,1024]{1,0:T(8,128)(2,1)S(1)}, u32[]{:S(2)}, u32[]{:S(2)}) collective-permute-start(bf16[256,1024]{1,0:T(8,128)(2,1)} %get-tuple-element.50.m_ref.refs_0_), channel_id=1, source_target_pairs={{0,12},{4,0},{8,4},{12,8},{1,13},{5,1},{9,5},{13,9},{2,14},{6,2},{... | collective-permute-start | bytes 1572872 | tf_op jit(solution)/shard_map/ppermute | solution.py:33
  89.3 23.2 %collective-permute-start.12 = (bf16[256,1024]{1,0:T(8,128)(2,1)S(1)}, bf16[256,1024]{1,0:T(8,128)(2,1)S(1)}, u32[]{:S(2)}, u32[]{:S(2)}) collective-permute-start(bf16[256,1024]{1,0:T(8,128)(2,1)S(1)} %collective-permute-done.10), channel_id=1, source_target_pairs={{0,2},{2,0},{1,3},{3,1},{4,6},{6,4},{5,7},{7,5},{8,10},{10,8},{9,1... | collective-permute-start | bytes 1572872 | tf_op jit(solution)/shard_map/ppermute | solution.py:37
  100.9 11.5 %collective-permute-start.15 = (f32[24,256]{1,0:T(8,128)S(1)}, f32[24,256]{1,0:T(8,128)S(1)}, u32[]{:S(2)}, u32[]{:S(2)}) collective-permute-start(f32[24,256]{1,0:T(8,128)S(1)} %get-tuple-element.41.refs_6_), channel_id=1, source_target_pairs={{4,0},{8,4},{12,8},{5,1},{9,5},{13,9},{6,2},{10,6},{14,10},{7,3},{... | collective-permute-start | bytes 73736 | tf_op jit(solution)/shard_map/ppermute | solution.py:26
  102.2 10.3 %collective-permute-start.16 = (f32[24,256]{1,0:T(8,128)S(1)}, f32[24,256]{1,0:T(8,128)S(1)}, u32[]{:S(2)}, u32[]{:S(2)}) collective-permute-start(f32[24,256]{1,0:T(8,128)S(1)} %get-tuple-element.41.refs_6_), channel_id=1, source_target_pairs={{8,0},{12,4},{9,1},{13,5},{10,2},{14,6},{11,3},{15,7},{24,16},{28,... | collective-permute-start | bytes 73736 | tf_op jit(solution)/shard_map/ppermute | solution.py:26
  112.5 12.8 %collective-permute-start.17 = (bf16[2,256,1024]{2,1,0:T(8,128)(2,1)}, bf16[2,256,1024]{2,1,0:T(8,128)(2,1)S(1)}, u32[]{:S(2)}, u32[]{:S(2)}) collective-permute-start(bf16[2,256,1024]{2,1,0:T(8,128)(2,1)} %get-tuple-element.43), channel_id=1, source_target_pairs={{0,1},{1,0},{2,3},{3,2},{4,5},{5,4},{6,7},{7,6},{8,9},{9,8},{10,11... | collective-permute-start | bytes 3145736 | tf_op jit(solution)/shard_map/ppermute | solution.py:37
  122.1 15.9 %collective-permute-start.19 = (bf16[256,1024]{1,0:T(8,128)(2,1)S(1)}, bf16[256,1024]{1,0:T(8,128)(2,1)S(1)}, u32[]{:S(2)}, u32[]{:S(2)}) collective-permute-start(bf16[256,1024]{1,0:T(8,128)(2,1)S(1)} %collective-permute-done.10), channel_id=1, source_target_pairs={{0,1},{1,0},{2,3},{3,2},{4,5},{5,4},{6,7},{7,6},{8,9},{9,8},{10,11... | collective-permute-start | bytes 1572872 | tf_op jit(solution)/shard_map/ppermute | solution.py:37
  122.2 15.8 %collective-permute-start.20 = (bf16[256,1024]{1,0:T(8,128)(2,1)S(1)}, bf16[256,1024]{1,0:T(8,128)(2,1)S(1)}, u32[]{:S(2)}, u32[]{:S(2)}) collective-permute-start(bf16[256,1024]{1,0:T(8,128)(2,1)S(1)} %collective-permute-done.12), channel_id=1, source_target_pairs={{0,1},{1,0},{2,3},{3,2},{4,5},{5,4},{6,7},{7,6},{8,9},{9,8},{10,11... | collective-permute-start | bytes 1572872 | tf_op jit(solution)/shard_map/ppermute | solution.py:37
  126.6 14.3 %collective-permute-start.18 = (bf16[256,1024]{1,0:T(8,128)(2,1)S(1)}, bf16[256,1024]{1,0:T(8,128)(2,1)S(1)}, u32[]{:S(2)}, u32[]{:S(2)}) collective-permute-start(bf16[256,1024]{1,0:T(8,128)(2,1)S(1)} %fusion.1), channel_id=1, source_target_pairs={{0,2},{2,0},{1,3},{3,1},{4,6},{6,4},{5,7},{7,5},{8,10},{10,8},{9,1... | collective-permute-start | bytes 1572872 | tf_op jit(solution)/shard_map/ppermute | solution.py:37
  128.4 27.2 %collective-permute-start.21 = (bf16[256,1024]{1,0:T(8,128)(2,1)}, bf16[256,1024]{1,0:T(8,128)(2,1)S(1)}, u32[]{:S(2)}, u32[]{:S(2)}) collective-permute-start(bf16[256,1024]{1,0:T(8,128)(2,1)} %get-tuple-element.50.m_ref.refs_0_), channel_id=1, source_target_pairs={{0,8},{4,12},{8,0},{12,4},{1,9},{5,13},{9,1},{13,5},{2,10},{6,14},... | collective-permute-start | bytes 1572872 | tf_op jit(solution)/shard_map/ppermute | solution.py:33
  (10 other events, 182.8 us)

commit v5 on v4

--- a/solution.py
+++ b/solution.py
@@ -85,15 +85,16 @@
 
 
 def forward_kernel(tiles, count, heads, use_ref, q_ref, *refs):
-    k_refs, v_refs = refs[:count], refs[count : 2 * count]
-    mixed_ref, lse_ref = refs[2 * count :]
+    kv_refs = refs[:count]
+    mixed_ref, lse_ref = refs[count:]
+    blocks = len(tiles)
     causal = causal_tile()
     for n, mine in enumerate(tiles):
         rows = block_rows(n)
         for j in range(heads):
             cols = head_cols(j)
-            keys = cat([k_refs[d][block_rows(b), cols] for d, b, _ in mine])
-            vals = cat([v_refs[d][block_rows(b), cols] for d, b, _ in mine])
+            keys = cat([kv_refs[d][block_rows(b), cols] for d, b, _ in mine])
+            vals = cat([kv_refs[d][block_rows(blocks + b), cols] for d, b, _ in mine])
             raw = dot_nt(keys, q_ref[rows, cols])
             parts = []
             for i, (_, _, level) in enumerate(mine):
@@ -113,15 +114,16 @@
 
 
 def query_kernel(tiles, count, heads, heads_up, use_ref, q_ref, g_ref, lse_ref, *refs):
-    k_refs, v_refs = refs[:count], refs[count : 2 * count]
-    dq_ref, stats_ref = refs[2 * count :]
+    kv_refs = refs[:count]
+    dq_ref, stats_ref = refs[count:]
+    blocks = len(tiles)
     causal = causal_tile()
     for n, mine in enumerate(tiles):
         rows = block_rows(n)
         for j in range(heads):
             cols = head_cols(j)
-            keys = cat([k_refs[d][block_rows(b), cols] for d, b, _ in mine])
-            vals = cat([v_refs[d][block_rows(b), cols] for d, b, _ in mine])
+            keys = cat([kv_refs[d][block_rows(b), cols] for d, b, _ in mine])
+            vals = cat([kv_refs[d][block_rows(blocks + b), cols] for d, b, _ in mine])
             lse = lse_ref[j : j + 1, rows]
             raw = dot_nt(keys, q_ref[rows, cols])
             prob_grad = dot_nt(vals, g_ref[rows, cols])
@@ -193,16 +195,10 @@
 
 
 class Stream:
-    def __init__(self, w_ref, held, sems, firsts, height):
+    def __init__(self, pieces, held, sems):
         self.held = held
-        self.height = height
         self.copies = [
-            pltpu.make_async_copy(
-                w_ref.at[pl.ds(pl.multiple_of(first, height), height), :],
-                held.at[i],
-                sems.at[i],
-            )
-            for i, first in enumerate(firsts)
+            pltpu.make_async_copy(piece, held.at[i], sems.at[i]) for i, piece in enumerate(pieces)
         ]
         for copy in self.copies[:2]:
             copy.start()
@@ -211,35 +207,38 @@
         self.copies[i].wait()
         if i + 2 < len(self.copies):
             self.copies[i + 2].start()
-        return self.held[i]
+        return self.held.at[i]
 
 
 def mixed_grad_kernel(count, split, place_ref, *refs):
     c_refs, w_ref, out_ref, held, sems = refs[:count], refs[count], *refs[count + 1 :]
     depth = c_refs[0].shape[1]
-    height = depth // split
-    firsts = [place_ref[i] * depth + part * height for i in range(count) for part in range(split)]
-    stream = Stream(w_ref, held, sems, firsts, height)
-    total = None
-    for i in range(count):
-        for part in range(split):
-            piece = stream.piece(i * split + part)
-            step = dot(c_refs[i][:, part * height : (part + 1) * height], piece)
+    width = out_ref.shape[1] // split
+    stream = Stream(
+        [w_ref.at[:, part * width : (part + 1) * width] for part in range(split)], held, sems
+    )
+    for part in range(split):
+        piece = stream.piece(part)
+        total = None
+        for i in range(count):
+            rows = pl.ds(pl.multiple_of(place_ref[i] * depth, depth), depth)
+            step = dot(c_refs[i][...], piece[rows, :])
             total = step if total is None else total + step
-    out_ref[...] = total.astype(BF16)
+        out_ref[:, part * width : (part + 1) * width] = total.astype(BF16)
 
 
 def partial_kernel(split, place_ref, m_ref, w_ref, keep_ref, give_ref, held, sems):
     depth = keep_ref.shape[2]
     height = depth // split
     firsts = [place_ref[i] * depth + part * height for i in range(4) for part in range(split)]
-    stream = Stream(w_ref, held, sems, firsts, height)
+    pieces = [w_ref.at[pl.ds(pl.multiple_of(first, height), height), :] for first in firsts]
+    stream = Stream(pieces, held, sems)
     outs = [(give_ref, 0), (give_ref, 1), (keep_ref, 0), (keep_ref, 1)]
     for i, (out_ref, at) in enumerate(outs):
         for part in range(split):
             piece = stream.piece(i * split + part)
             cols = slice(part * height, (part + 1) * height)
-            out_ref[at, :, cols] = dot_nt(m_ref[...], piece).astype(BF16)
+            out_ref[at, :, cols] = dot_nt(m_ref[...], piece[...]).astype(BF16)
 
 
 def weight_grad_kernel(count, place_ref, c_ref, *refs):
@@ -286,7 +285,7 @@
 
 
 VMEM_LIMIT = 20 * 1024 * 1024
-WEIGHTS = dict(mixed_grad=100.0, forward=100.0, partial=0.0, query=100.0, key=0.0)
+WEIGHTS = dict(mixed_grad=0.0, forward=100.0, partial=0.0, query=100.0, key=0.0)
 STREAM_LIMIT = 54 * 1024 * 1024
 
 
@@ -312,14 +311,14 @@
         share = out_weight.shape[0] // 4
         order = jnp.stack([places[1], places[3], places[0], places[2]])
         return kernel_call(
-            functools.partial(partial_kernel, 2),
+            functools.partial(partial_kernel, 1),
             "attended_partial",
             [order],
             [mixed_heads],
             [jax.ShapeDtypeStruct((2, rows, share), BF16)] * 2,
             estimate,
             [out_weight],
-            weight_scratch(8, share // 2, mixed_heads.shape[1]),
+            weight_scratch(4, share, mixed_heads.shape[1]),
         )
     partial_value = lax.dot_general(mixed_heads, out_weight, NT, preferred_element_type=F32)
     return [partial_value.astype(BF16)]
@@ -365,34 +364,30 @@
     use = ((block_ids[:, None] >= offsets[None]) & (level_mask == 1)).astype(jnp.int32)
     use = use.reshape(-1)
 
-    key_all = further([keys], 1)
-    value_all = further([values], 1)
+    kv_all = further([jnp.concatenate([keys, values])], 1)
     query_all = further([queries], -1)
-    first_ones = (key_all[-1], value_all[-1], query_all[-1])
     c_blocks, c_places = features_here(cotangent)
     group_count = len(c_blocks)
     part_cols = cotangent.shape[1]
     while len(query_all) < count:
         query_all = further(query_all, -1)
+    split = max(1, columns // 256)
     mixed_grad = kernel_call(
-        functools.partial(mixed_grad_kernel, group_count, 2),
+        functools.partial(mixed_grad_kernel, group_count, split),
         "mixed_grad",
         [c_places],
         c_blocks,
         like_queries,
         cost(2 * rows * columns * features, 2 * columns * features, 0, WEIGHTS["mixed_grad"]),
         [out_weight],
-        weight_scratch(2 * group_count, part_cols // 2, columns),
-    )
-    key_all = further(key_all, 1, *first_ones)
+        weight_scratch(split, features, columns // split),
+    )
+    while len(kv_all) < count:
+        kv_all = further(kv_all, 1, mixed_grad)
     grad_all = further([mixed_grad], -1, query_all[-1])
-    while len(key_all) < count:
-        key_all = further(key_all, 1)
-    relayed = (key_all[-1], grad_all[-1])
-    while len(value_all) < count:
-        value_all = further(value_all, 1, *relayed)
+    first_grad = grad_all[-1]
     while len(grad_all) < count:
-        grad_all = further(grad_all, -1, *relayed)
+        grad_all = further(grad_all, -1)
 
     h, r = lax.axis_index("head"), lax.axis_index("rep")
     n_head, n_rep = lax.axis_size("head"), lax.axis_size("rep")
@@ -405,17 +400,16 @@
     for s in range(peers):
         for q in range(group_count):
             links.append((s * group_count + q, ((s + step_of(q)) % peers) * group_count + q))
-    arrived = lax.ppermute(after(out_block, *relayed), ("seq", "head", "rep"), links)
+    arrived = lax.ppermute(after(out_block, first_grad), ("seq", "head", "rep"), links)
 
     mixed_heads, lse = kernel_call(
         functools.partial(forward_kernel, tiles, count, heads),
         "attention_forward",
         [use],
-        [after(queries, query_all[-1]), *key_all, *value_all],
+        [after(queries, query_all[-1], grad_all[-1]), *kv_all],
         [like_queries, jax.ShapeDtypeStruct((heads_up, rows), F32)],
         cost(2 * attention_flops, (2 * count + 2) * array_bytes, exps, WEIGHTS["forward"]),
     )
-    mixed_heads = after(mixed_heads, arrived, grad_all[-1])
 
     near = {}
     if peers <= 4:
@@ -425,7 +419,7 @@
         functools.partial(query_kernel, tiles, count, heads, heads_up),
         "attention_query_grad",
         [use],
-        [after(queries, mixed_heads), mixed_grad, lse, *key_all, *value_all],
+        [after(queries, mixed_heads), mixed_grad, lse, *kv_all],
         [like_queries, stats_shape],
         cost(3 * attention_flops, (2 * count + 3) * array_bytes, exps, WEIGHTS["query"]),
     )

time: 161 us -> 143 us (0.89)
  waiting for transfers between devices: 61.2 us -> 49.5 us
  starting transfers between devices: 52.8 us -> 46.1 us
    ppermute x10 -> x8, waiting for transfers between devices: 40.3 us -> 26.1 us  [shift(): lax.ppermute(value, 'seq', [(i, i + by) for i in range(peers) if 0 <= i +...]
    ppermute x8, starting transfers between devices: 19.3 us -> 5.73 us  [swap(): return lax.ppermute(value, axis, [(0, 1), (1, 0)])]
    ppermute x3, starting transfers between devices: 7.37 us -> 20.7 us  [cyclic(): lax.ppermute(value, 'seq', [(i, (i + by) % peers) for i in range(peers)])]
    ppermute x10 -> x8, starting transfers between devices: 25.4 us -> 18.9 us  [shift(): lax.ppermute(value, 'seq', [(i, i + by) for i in range(peers) if 0 <= i +...]
    ppermute x8, waiting for transfers between devices: 7.26 us -> 9.21 us  [swap(): return lax.ppermute(value, axis, [(0, 1), (1, 0)])]
  transfers between devices with their start and end apart: 22 -> 20, of which waited for: 10 -> 9; matrix products, arithmetic and copies ran while one was open for 3% -> 5% of each run, Pallas kernels for 21% -> 23%
where the time goes in v5:
time: 143 us; the launch traced here: 142 us
  waiting for transfers between devices  49.5 us (35%)
  starting transfers between devices  46.1 us (32%)
  Pallas kernels  37.8 us (26%)
  other arithmetic  5.17 us (4%)
  local copies, waits for them, and re-layouts  2.28 us (2%)
    pallas_call x6, Pallas kernels, kernel_call(): pl.pallas_call(body, in_specs=[smem] * len(scalars) + [vmem] * len(arrays...  37.8 us
    ppermute x8, waiting for transfers between devices, shift(): lax.ppermute(value, 'seq', [(i, i + by) for i in range(peers) if 0 <= i +...  26.1 us
    ppermute x3, starting transfers between devices, cyclic(): lax.ppermute(value, 'seq', [(i, (i + by) % peers) for i in range(peers)])  20.7 us
    ppermute x8, starting transfers between devices, shift(): lax.ppermute(value, 'seq', [(i, i + by) for i in range(peers) if 0 <= i +...  18.9 us
    ppermute x3, waiting for transfers between devices, cyclic(): lax.ppermute(value, 'seq', [(i, (i + by) % peers) for i in range(peers)])  14.2 us
    ppermute x8, waiting for transfers between devices, swap(): return lax.ppermute(value, axis, [(0, 1), (1, 0)])  9.21 us
    ppermute x8, starting transfers between devices, swap(): return lax.ppermute(value, axis, [(0, 1), (1, 0)])  5.73 us
  transfers between devices with their start and end apart: 20, of which 9 were waited for; matrix products, arithmetic and copies ran while one was open for 5% of the time, Pallas kernels for 23%

profile of v5, /device:TPU:0, one launch (start us, length us, event | category | flops | bytes accessed | tf_op | source)
XLA Modules:
  0.0 141.9 jit_solution(3979303020751100677)
XLA Ops:
  0.6 3.0 %collective-permute-start.3 = (bf16[256,1024]{1,0:T(8,128)(2,1)}, bf16[256,1024]{1,0:T(8,128)(2,1)}, u32[]{:S(2)}, u32[]{:S(2)}) collective-permute-start(bf16[256,1024]{1,0:T(8,128)(2,1)} %refs_0_.2), channel_id=1, source_target_pairs={{0,2},{2,0},{1,3},{3,1},{4,6},{6,4},{5,7},{7,5},{8,10},{10,8},{9,1... | collective-permute-start | bytes 1572872 | tf_op jit(solution)/shard_map/ppermute | solution.py:37
  7.1 5.5 %collective-permute-start.7 = (bf16[512,1024]{1,0:T(8,128)(2,1)S(1)}, bf16[512,1024]{1,0:T(8,128)(2,1)}, u32[]{:S(2)}, u32[]{:S(2)}) collective-permute-start(bf16[512,1024]{1,0:T(8,128)(2,1)S(1)} %constant_dynamic-update-slice_fusion.refs_0_), channel_id=1, source_target_pairs={{0,4},{4,8},{8,12},{1,5},{5,9},{9,13},{2,6},{6,10},{10,14},{3,7},{... | collective-permute-start | bytes 3145736 | tf_op jit(solution)/shard_map/ppermute | solution.py:26
  12.7 3.2 %collective-permute-done.3.refs_2_ = bf16[256,1024]{1,0:T(8,128)(2,1)} collective-permute-done((bf16[256,1024]{1,0:T(8,128)(2,1)}, bf16[256,1024]{1,0:T(8,128)(2,1)}, u32[]{:S(2)}, u32[]{:S(2)}) %collective-permute-start.3) | collective-permute-done | bytes 524320 | tf_op jit(solution)/shard_map/ppermute | solution.py:37
  15.9 3.2 %collective-permute-done.refs_1_ = bf16[256,1024]{1,0:T(8,128)(2,1)S(1)} collective-permute-done((bf16[256,1024]{1,0:T(8,128)(2,1)}, bf16[256,1024]{1,0:T(8,128)(2,1)S(1)}, u32[]{:S(2)}, u32[]{:S(2)}) %collective-permute-start) | collective-permute-done | bytes 524320 | tf_op jit(solution)/shard_map/ppermute | solution.py:26
  19.1 1.3 collective-permute-start.1
  21.0 8.9 %mixed_grad.1.g_ref.refs_3_ = bf16[256,1024]{1,0:T(8,128)(2,1)} custom-call(s32[4]{0:T(128)} %get-tuple-element.46.place_ref, bf16[256,1024]{1,0:T(8,128)(2,1)} %refs_0_.2, bf16[256,1024]{1,0:T(8,128)(2,1)} %collective-permute-done.2.refs_1_, bf16[256,1024]{1,0:T(8,128)(2,1)} %collective-permute-done.3.refs_2_, ...), custom_call_target="tpu_custom_call" | custom-call | tf_op jit(solution)/shard_map/mixed_grad/pallas_call | solution.py:267
  29.9 3.5 %collective-permute-done.1.refs_2_ = bf16[256,1024]{1,0:T(8,128)(2,1)S(1)} collective-permute-done((bf16[256,1024]{1,0:T(8,128)(2,1)S(1)}, bf16[256,1024]{1,0:T(8,128)(2,1)S(1)}, u32[]{:S(2)}, u32[]{:S(2)}) %collective-permute-start.1) | collective-permute-done | bytes 524320 | tf_op jit(solution)/shard_map/ppermute | solution.py:26
  33.5 1.3 collective-permute-start.5
  34.8 5.5 %collective-permute-start.8 = (bf16[512,1024]{1,0:T(8,128)(2,1)}, bf16[512,1024]{1,0:T(8,128)(2,1)}, u32[]{:S(2)}, u32[]{:S(2)}) collective-permute-start(bf16[512,1024]{1,0:T(8,128)(2,1)} %collective-permute-done.7.refs_1_), channel_id=1, source_target_pairs={{0,4},{4,8},{8,12},{1,5},{5,9},{9,13},{2,6},{6,10},{10,14},{3,7},{... | collective-permute-start | bytes 3145736 | tf_op jit(solution)/shard_map/ppermute | solution.py:26
  40.3 7.0 %collective-permute-done.5.refs_4_ = bf16[256,1024]{1,0:T(8,128)(2,1)S(1)} collective-permute-done((bf16[256,1024]{1,0:T(8,128)(2,1)}, bf16[256,1024]{1,0:T(8,128)(2,1)S(1)}, u32[]{:S(2)}, u32[]{:S(2)}) %collective-permute-start.5) | collective-permute-done | bytes 524320 | tf_op jit(solution)/shard_map/ppermute | solution.py:26
  50.9 10.5 %collective-permute-done.6.refs_5_ = bf16[256,1024]{1,0:T(8,128)(2,1)S(1)} collective-permute-done((bf16[256,1024]{1,0:T(8,128)(2,1)S(1)}, bf16[256,1024]{1,0:T(8,128)(2,1)S(1)}, u32[]{:S(2)}, u32[]{:S(2)}) %collective-permute-start.6) | collective-permute-done | bytes 524320 | tf_op jit(solution)/shard_map/ppermute | solution.py:26
  61.4 1.9 %collective-permute-done.8.refs_2_ = bf16[512,1024]{1,0:T(8,128)(2,1)} collective-permute-done((bf16[512,1024]{1,0:T(8,128)(2,1)}, bf16[512,1024]{1,0:T(8,128)(2,1)}, u32[]{:S(2)}, u32[]{:S(2)}) %collective-permute-start.8) | collective-permute-done | bytes 1048608 | tf_op jit(solution)/shard_map/ppermute | solution.py:26
  63.3 4.8 %attention_forward.1 = (bf16[256,1024]{1,0:T(8,128)(2,1)}, f32[8,256]{1,0:T(8,128)S(1)}) custom-call(s32[10]{0:T(128)S(1)} %reshape.264.use_ref, bf16[256,1024]{1,0:T(8,128)(2,1)S(1)} %copy-done.3, bf16[512,1024]{1,0:T(8,128)(2,1)S(1)} %copy-done.5, bf16[512,1024]{1,0:T(8,128)(2,1)} %collective-permute-done.7.refs_1_, ...), custom_call_target="tpu_custom_call" | custom-call | flops 53687091200 | bytes 419430400 | tf_op jit(solution)/shard_map/attention_forward/pallas_call | solution.py:267
  68.1 16.6 %collective-permute-start.11 = (bf16[256,1024]{1,0:T(8,128)(2,1)}, bf16[256,1024]{1,0:T(8,128)(2,1)S(1)}, u32[]{:S(2)}, u32[]{:S(2)}) collective-permute-start(bf16[256,1024]{1,0:T(8,128)(2,1)} %get-tuple-element.44.m_ref.refs_0_), channel_id=1, source_target_pairs={{0,4},{4,8},{8,12},{12,0},{1,5},{5,9},{9,13},{13,1},{2,6},{6,10},{... | collective-permute-start | bytes 1572872 | tf_op jit(solution)/shard_map/ppermute | solution.py:33
  84.7 7.6 %attention_query_grad.1 = (bf16[256,1024]{1,0:T(8,128)(2,1)}, f32[24,256]{1,0:T(8,128)S(1)}) custom-call(s32[10]{0:T(128)S(1)} %reshape.264.use_ref, bf16[256,1024]{1,0:T(8,128)(2,1)S(1)} %copy-done.3, bf16[256,1024]{1,0:T(8,128)(2,1)S(1)} %copy-done, f32[8,256]{1,0:T(8,128)S(1)} %get-tuple-element.34.lse_ref, bf16[512,1024]{1,0:T(8,128)(2,1)S(1)} %copy-done.5, ...), custom_call_target="tpu_custom_call" | custom-call | flops 80530636800 | bytes 471859200 | tf_op jit(solution)/shard_map/attention_query_grad/pallas_call | solution.py:267
  93.6 1.5 %collective-permute-start.14 = (f32[24,256]{1,0:T(8,128)S(1)}, f32[24,256]{1,0:T(8,128)S(1)}, u32[]{:S(2)}, u32[]{:S(2)}) collective-permute-start(f32[24,256]{1,0:T(8,128)S(1)} %get-tuple-element.35.refs_6_), channel_id=1, source_target_pairs={{8,0},{12,4},{9,1},{13,5},{10,2},{14,6},{11,3},{15,7},{24,16},{28,... | collective-permute-start | bytes 73736 | tf_op jit(solution)/shard_map/ppermute | solution.py:26
  95.7 7.0 %attended_partial.1 = (bf16[2,256,1024]{2,1,0:T(8,128)(2,1)}, bf16[2,256,1024]{2,1,0:T(8,128)(2,1)}) custom-call(s32[4]{0:T(128)} %pad_add_fusion.place_ref, bf16[256,1024]{1,0:T(8,128)(2,1)} %get-tuple-element.44.m_ref.refs_0_, bf16[4096,1024]{1,0:T(8,128)(2,1)} %w_ref.1), custom_call_target="tpu_custom_call" | custom-call | tf_op jit(solution)/shard_map/attended_partial/pallas_call | solution.py:267
  103.4 3.0 %collective-permute-done.15 = bf16[2,256,1024]{2,1,0:T(8,128)(2,1)S(1)} collective-permute-done((bf16[2,256,1024]{2,1,0:T(8,128)(2,1)}, bf16[2,256,1024]{2,1,0:T(8,128)(2,1)S(1)}, u32[]{:S(2)}, u32[]{:S(2)}) %collective-permute-start.15) | collective-permute-done | bytes 1048608 | tf_op jit(solution)/shard_map/ppermute | solution.py:37
  107.6 2.1 %collective-permute-start.16 = (bf16[256,1024]{1,0:T(8,128)(2,1)S(1)}, bf16[256,1024]{1,0:T(8,128)(2,1)S(1)}, u32[]{:S(2)}, u32[]{:S(2)}) collective-permute-start(bf16[256,1024]{1,0:T(8,128)(2,1)S(1)} %fusion.1), channel_id=1, source_target_pairs={{0,2},{2,0},{1,3},{3,1},{4,6},{6,4},{5,7},{7,5},{8,10},{10,8},{9,1... | collective-permute-start | bytes 1572872 | tf_op jit(solution)/shard_map/ppermute | solution.py:37
  109.7 4.1 %collective-permute-start.19 = (bf16[256,1024]{1,0:T(8,128)(2,1)}, bf16[256,1024]{1,0:T(8,128)(2,1)S(1)}, u32[]{:S(2)}, u32[]{:S(2)}) collective-permute-start(bf16[256,1024]{1,0:T(8,128)(2,1)} %get-tuple-element.44.m_ref.refs_0_), channel_id=1, source_target_pairs={{0,8},{4,12},{8,0},{12,4},{1,9},{5,13},{9,1},{13,5},{2,10},{6,14},... | collective-permute-start | bytes 1572872 | tf_op jit(solution)/shard_map/ppermute | solution.py:33
  113.9 4.7 %attention_key_grad.1 = (bf16[256,1024]{1,0:T(8,128)(2,1)}, bf16[256,1024]{1,0:T(8,128)(2,1)}) custom-call(bf16[256,1024]{1,0:T(8,128)(2,1)S(1)} %copy-done.1, bf16[256,1024]{1,0:T(8,128)(2,1)S(1)} %copy-done.2, bf16[256,1024]{1,0:T(8,128)(2,1)S(1)} %copy-done.3, bf16[256,1024]{1,0:T(8,128)(2,1)S(1)} %collective-permute-done.refs_1_, ...), custom_call_target="tpu_custom_call" | custom-call | tf_op jit(solution)/shard_map/attention_key_grad/pallas_call | solution.py:267
  118.9 3.0 %collective-permute-done.16 = bf16[256,1024]{1,0:T(8,128)(2,1)S(1)} collective-permute-done((bf16[256,1024]{1,0:T(8,128)(2,1)S(1)}, bf16[256,1024]{1,0:T(8,128)(2,1)S(1)}, u32[]{:S(2)}, u32[]{:S(2)}) %collective-permute-start.16) | collective-permute-done | bytes 524320 | tf_op jit(solution)/shard_map/ppermute | solution.py:37
  123.0 14.2 %collective-permute-done.19.refs_2_ = bf16[256,1024]{1,0:T(8,128)(2,1)S(1)} collective-permute-done((bf16[256,1024]{1,0:T(8,128)(2,1)}, bf16[256,1024]{1,0:T(8,128)(2,1)S(1)}, u32[]{:S(2)}, u32[]{:S(2)}) %collective-permute-start.19) | collective-permute-done | bytes 524320 | tf_op jit(solution)/shard_map/ppermute | solution.py:33
  137.2 4.8 %weight_grad.1 = bf16[1024,1024]{1,0:T(8,128)(2,1)} custom-call(s32[4]{0:T(128)S(1)} %select_reduce_fusion.place_ref, bf16[4,256,1024]{2,1,0:T(8,128)(2,1)S(1)} %pad_maximum_fusion.c_ref, bf16[256,1024]{1,0:T(8,128)(2,1)} %get-tuple-element.44.m_ref.refs_0_, bf16[256,1024]{1,0:T(8,128)(2,1)S(1)} %collective-permute-done.11.refs_1_, ...), custom_call_target="tpu_custom_call" | custom-call | flops 2147483648 | bytes 4194304 | tf_op jit(solution)/shard_map/weight_grad/pallas_call | solution.py:267
  (53 shorter events, 12.8 us)
Async XLA Ops:
  0.6 15.2 %collective-permute-start.3 = (bf16[256,1024]{1,0:T(8,128)(2,1)}, bf16[256,1024]{1,0:T(8,128)(2,1)}, u32[]{:S(2)}, u32[]{:S(2)}) collective-permute-start(bf16[256,1024]{1,0:T(8,128)(2,1)} %refs_0_.2), channel_id=1, source_target_pairs={{0,2},{2,0},{1,3},{3,1},{4,6},{6,4},{5,7},{7,5},{8,10},{10,8},{9,1... | collective-permute-start | bytes 1572872 | tf_op jit(solution)/shard_map/ppermute | solution.py:37
  3.6 15.5 %collective-permute-start = (bf16[256,1024]{1,0:T(8,128)(2,1)}, bf16[256,1024]{1,0:T(8,128)(2,1)S(1)}, u32[]{:S(2)}, u32[]{:S(2)}) collective-permute-start(bf16[256,1024]{1,0:T(8,128)(2,1)} %refs_0_.3), channel_id=1, source_target_pairs={{4,0},{8,4},{12,8},{5,1},{9,5},{13,9},{6,2},{10,6},{14,10},{7,3},{... | collective-permute-start | bytes 1572872 | tf_op jit(solution)/shard_map/ppermute | solution.py:26
  7.1 22.8 %copy-start.4 = (bf16[512,1024]{1,0:T(8,128)(2,1)}, bf16[512,1024]{1,0:T(8,128)(2,1)S(1)}, u32[]{:S(2)}) copy-start(bf16[512,1024]{1,0:T(8,128)(2,1)S(1)} %constant_dynamic-update-slice_fusion.refs_0_) | copy-start | bytes 3145732
  7.1 27.7 %collective-permute-start.7 = (bf16[512,1024]{1,0:T(8,128)(2,1)S(1)}, bf16[512,1024]{1,0:T(8,128)(2,1)}, u32[]{:S(2)}, u32[]{:S(2)}) collective-permute-start(bf16[512,1024]{1,0:T(8,128)(2,1)S(1)} %constant_dynamic-update-slice_fusion.refs_0_), channel_id=1, source_target_pairs={{0,4},{4,8},{8,12},{1,5},{5,9},{9,13},{2,6},{6,10},{10,14},{3,7},{... | collective-permute-start | bytes 3145736 | tf_op jit(solution)/shard_map/ppermute | solution.py:26
  12.7 8.4 %collective-permute-start.2 = (bf16[256,1024]{1,0:T(8,128)(2,1)S(1)}, bf16[256,1024]{1,0:T(8,128)(2,1)}, u32[]{:S(2)}, u32[]{:S(2)}) collective-permute-start(bf16[256,1024]{1,0:T(8,128)(2,1)S(1)} %copy-done.6), channel_id=1, source_target_pairs={{0,1},{1,0},{2,3},{3,2},{4,5},{5,4},{6,7},{7,6},{8,9},{9,8},{10,11... | collective-permute-start | bytes 1572872 | tf_op jit(solution)/shard_map/ppermute | solution.py:37
  15.9 5.1 %collective-permute-start.4 = (bf16[256,1024]{1,0:T(8,128)(2,1)}, bf16[256,1024]{1,0:T(8,128)(2,1)}, u32[]{:S(2)}, u32[]{:S(2)}) collective-permute-start(bf16[256,1024]{1,0:T(8,128)(2,1)} %collective-permute-done.3.refs_2_), channel_id=1, source_target_pairs={{0,1},{1,0},{2,3},{3,2},{4,5},{5,4},{6,7},{7,6},{8,9},{9,8},{10,11... | collective-permute-start | bytes 1572872 | tf_op jit(solution)/shard_map/ppermute | solution.py:37
  19.1 14.4 %collective-permute-start.1 = (bf16[256,1024]{1,0:T(8,128)(2,1)S(1)}, bf16[256,1024]{1,0:T(8,128)(2,1)S(1)}, u32[]{:S(2)}, u32[]{:S(2)}) collective-permute-start(bf16[256,1024]{1,0:T(8,128)(2,1)S(1)} %collective-permute-done.refs_1_), channel_id=1, source_target_pairs={{4,0},{8,4},{12,8},{5,1},{9,5},{13,9},{6,2},{10,6},{14,10},{7,3},{... | collective-permute-start | bytes 1572872 | tf_op jit(solution)/shard_map/ppermute | solution.py:26
  21.0 27.6 %copy-start.8 = (s32[2,5]{1,0:T(2,128)S(1)}, s32[2,5]{1,0:T(2,128)}, u32[]{:S(2)}) copy-start(s32[2,5]{1,0:T(2,128)} %param.10) | copy-start | bytes 124
  29.9 33.3 %copy-start.3 = (bf16[256,1024]{1,0:T(8,128)(2,1)S(1)}, bf16[256,1024]{1,0:T(8,128)(2,1)}, u32[]{:S(2)}) copy-start(bf16[256,1024]{1,0:T(8,128)(2,1)} %refs_0_.3) | copy-start | bytes 1572868
  33.5 13.8 %collective-permute-start.5 = (bf16[256,1024]{1,0:T(8,128)(2,1)}, bf16[256,1024]{1,0:T(8,128)(2,1)S(1)}, u32[]{:S(2)}, u32[]{:S(2)}) collective-permute-start(bf16[256,1024]{1,0:T(8,128)(2,1)} %mixed_grad.1.g_ref.refs_3_), channel_id=1, source_target_pairs={{4,0},{8,4},{12,8},{5,1},{9,5},{13,9},{6,2},{10,6},{14,10},{7,3},{... | collective-permute-start | bytes 1572872 | tf_op jit(solution)/shard_map/ppermute | solution.py:26
  34.8 28.5 %collective-permute-start.8 = (bf16[512,1024]{1,0:T(8,128)(2,1)}, bf16[512,1024]{1,0:T(8,128)(2,1)}, u32[]{:S(2)}, u32[]{:S(2)}) collective-permute-start(bf16[512,1024]{1,0:T(8,128)(2,1)} %collective-permute-done.7.refs_1_), channel_id=1, source_target_pairs={{0,4},{4,8},{8,12},{1,5},{5,9},{9,13},{2,6},{6,10},{10,14},{3,7},{... | collective-permute-start | bytes 3145736 | tf_op jit(solution)/shard_map/ppermute | solution.py:26
  47.3 14.1 %collective-permute-start.6 = (bf16[256,1024]{1,0:T(8,128)(2,1)S(1)}, bf16[256,1024]{1,0:T(8,128)(2,1)S(1)}, u32[]{:S(2)}, u32[]{:S(2)}) collective-permute-start(bf16[256,1024]{1,0:T(8,128)(2,1)S(1)} %collective-permute-done.5.refs_4_), channel_id=1, source_target_pairs={{4,0},{8,4},{12,8},{5,1},{9,5},{13,9},{6,2},{10,6},{14,10},{7,3},{... | collective-permute-start | bytes 1572872 | tf_op jit(solution)/shard_map/ppermute | solution.py:26
  50.0 34.6 %copy-start = (bf16[256,1024]{1,0:T(8,128)(2,1)S(1)}, bf16[256,1024]{1,0:T(8,128)(2,1)}, u32[]{:S(2)}) copy-start(bf16[256,1024]{1,0:T(8,128)(2,1)} %mixed_grad.1.g_ref.refs_3_) | copy-start | bytes 1572868
  50.0 34.6 %collective-permute-start.9 = (bf16[256,1024]{1,0:T(8,128)(2,1)S(1)}, bf16[256,1024]{1,0:T(8,128)(2,1)S(1)}, u32[]{:S(2)}, u32[]{:S(2)}) collective-permute-start(bf16[256,1024]{1,0:T(8,128)(2,1)S(1)} %select_select_fusion), channel_id=1, source_target_pairs={{0,0},{1,9},{2,6},{3,15},{4,4},{5,13},{6,10},{7,3},{8,8},{9,1},{10... | collective-permute-start | bytes 1572872 | tf_op jit(solution)/shard_map/ppermute | solution.py:403
  68.1 34.6 %collective-permute-start.11 = (bf16[256,1024]{1,0:T(8,128)(2,1)}, bf16[256,1024]{1,0:T(8,128)(2,1)S(1)}, u32[]{:S(2)}, u32[]{:S(2)}) collective-permute-start(bf16[256,1024]{1,0:T(8,128)(2,1)} %get-tuple-element.44.m_ref.refs_0_), channel_id=1, source_target_pairs={{0,4},{4,8},{8,12},{12,0},{1,5},{5,9},{9,13},{13,1},{2,6},{6,10},{... | collective-permute-start | bytes 1572872 | tf_op jit(solution)/shard_map/ppermute | solution.py:33
  84.6 18.1 %collective-permute-start.12 = (bf16[256,1024]{1,0:T(8,128)(2,1)}, bf16[256,1024]{1,0:T(8,128)(2,1)S(1)}, u32[]{:S(2)}, u32[]{:S(2)}) collective-permute-start(bf16[256,1024]{1,0:T(8,128)(2,1)} %get-tuple-element.44.m_ref.refs_0_), channel_id=1, source_target_pairs={{0,12},{4,0},{8,4},{12,8},{1,13},{5,1},{9,5},{13,9},{2,14},{6,2},{... | collective-permute-start | bytes 1572872 | tf_op jit(solution)/shard_map/ppermute | solution.py:33
  84.6 18.0 %collective-permute-start.10 = (bf16[256,1024]{1,0:T(8,128)(2,1)S(1)}, bf16[256,1024]{1,0:T(8,128)(2,1)S(1)}, u32[]{:S(2)}, u32[]{:S(2)}) collective-permute-start(bf16[256,1024]{1,0:T(8,128)(2,1)S(1)} %collective-permute-done.9), channel_id=1, source_target_pairs={{0,2},{2,0},{1,3},{3,1},{4,6},{6,4},{5,7},{7,5},{8,10},{10,8},{9,1... | collective-permute-start | bytes 1572872 | tf_op jit(solution)/shard_map/ppermute | solution.py:37
  92.3 10.3 %collective-permute-start.13 = (f32[24,256]{1,0:T(8,128)S(1)}, f32[24,256]{1,0:T(8,128)S(1)}, u32[]{:S(2)}, u32[]{:S(2)}) collective-permute-start(f32[24,256]{1,0:T(8,128)S(1)} %get-tuple-element.35.refs_6_), channel_id=1, source_target_pairs={{4,0},{8,4},{12,8},{5,1},{9,5},{13,9},{6,2},{10,6},{14,10},{7,3},{... | collective-permute-start | bytes 73736 | tf_op jit(solution)/shard_map/ppermute | solution.py:26
  93.6 9.1 %collective-permute-start.14 = (f32[24,256]{1,0:T(8,128)S(1)}, f32[24,256]{1,0:T(8,128)S(1)}, u32[]{:S(2)}, u32[]{:S(2)}) collective-permute-start(f32[24,256]{1,0:T(8,128)S(1)} %get-tuple-element.35.refs_6_), channel_id=1, source_target_pairs={{8,0},{12,4},{9,1},{13,5},{10,2},{14,6},{11,3},{15,7},{24,16},{28,... | collective-permute-start | bytes 73736 | tf_op jit(solution)/shard_map/ppermute | solution.py:26
  102.7 3.7 %collective-permute-start.15 = (bf16[2,256,1024]{2,1,0:T(8,128)(2,1)}, bf16[2,256,1024]{2,1,0:T(8,128)(2,1)S(1)}, u32[]{:S(2)}, u32[]{:S(2)}) collective-permute-start(bf16[2,256,1024]{2,1,0:T(8,128)(2,1)} %get-tuple-element.37), channel_id=1, source_target_pairs={{0,1},{1,0},{2,3},{3,2},{4,5},{5,4},{6,7},{7,6},{8,9},{9,8},{10,11... | collective-permute-start | bytes 3145736 | tf_op jit(solution)/shard_map/ppermute | solution.py:37
  102.8 15.9 %collective-permute-start.17 = (bf16[256,1024]{1,0:T(8,128)(2,1)S(1)}, bf16[256,1024]{1,0:T(8,128)(2,1)S(1)}, u32[]{:S(2)}, u32[]{:S(2)}) collective-permute-start(bf16[256,1024]{1,0:T(8,128)(2,1)S(1)} %collective-permute-done.9), channel_id=1, source_target_pairs={{0,1},{1,0},{2,3},{3,2},{4,5},{5,4},{6,7},{7,6},{8,9},{9,8},{10,11... | collective-permute-start | bytes 1572872 | tf_op jit(solution)/shard_map/ppermute | solution.py:37
  103.3 15.4 %collective-permute-start.18 = (bf16[256,1024]{1,0:T(8,128)(2,1)S(1)}, bf16[256,1024]{1,0:T(8,128)(2,1)S(1)}, u32[]{:S(2)}, u32[]{:S(2)}) collective-permute-start(bf16[256,1024]{1,0:T(8,128)(2,1)S(1)} %collective-permute-done.10), channel_id=1, source_target_pairs={{0,1},{1,0},{2,3},{3,2},{4,5},{5,4},{6,7},{7,6},{8,9},{9,8},{10,11... | collective-permute-start | bytes 1572872 | tf_op jit(solution)/shard_map/ppermute | solution.py:37
  107.6 14.3 %collective-permute-start.16 = (bf16[256,1024]{1,0:T(8,128)(2,1)S(1)}, bf16[256,1024]{1,0:T(8,128)(2,1)S(1)}, u32[]{:S(2)}, u32[]{:S(2)}) collective-permute-start(bf16[256,1024]{1,0:T(8,128)(2,1)S(1)} %fusion.1), channel_id=1, source_target_pairs={{0,2},{2,0},{1,3},{3,1},{4,6},{6,4},{5,7},{7,5},{8,10},{10,8},{9,1... | collective-permute-start | bytes 1572872 | tf_op jit(solution)/shard_map/ppermute | solution.py:37
  109.7 27.5 %collective-permute-start.19 = (bf16[256,1024]{1,0:T(8,128)(2,1)}, bf16[256,1024]{1,0:T(8,128)(2,1)S(1)}, u32[]{:S(2)}, u32[]{:S(2)}) collective-permute-start(bf16[256,1024]{1,0:T(8,128)(2,1)} %get-tuple-element.44.m_ref.refs_0_), channel_id=1, source_target_pairs={{0,8},{4,12},{8,0},{12,4},{1,9},{5,13},{9,1},{13,5},{2,10},{6,14},... | collective-permute-start | bytes 1572872 | tf_op jit(solution)/shard_map/ppermute | solution.py:33
  (5 other events, 66.2 us)

commit v6 on v5

--- a/solution.py
+++ b/solution.py
@@ -210,21 +210,16 @@
         return self.held.at[i]
 
 
-def mixed_grad_kernel(count, split, place_ref, *refs):
-    c_refs, w_ref, out_ref, held, sems = refs[:count], refs[count], *refs[count + 1 :]
+def mixed_grad_kernel(count, given, place_ref, *refs):
+    total = refs[0][...] if given else None
+    c_refs, w_ref, out_ref, held, sems = refs[given : given + count], *refs[given + count :]
     depth = c_refs[0].shape[1]
-    width = out_ref.shape[1] // split
-    stream = Stream(
-        [w_ref.at[:, part * width : (part + 1) * width] for part in range(split)], held, sems
-    )
-    for part in range(split):
-        piece = stream.piece(part)
-        total = None
-        for i in range(count):
-            rows = pl.ds(pl.multiple_of(place_ref[i] * depth, depth), depth)
-            step = dot(c_refs[i][...], piece[rows, :])
-            total = step if total is None else total + step
-        out_ref[:, part * width : (part + 1) * width] = total.astype(BF16)
+    firsts = [pl.multiple_of(place_ref[i] * depth, depth) for i in range(count)]
+    stream = Stream([w_ref.at[pl.ds(first, depth), :] for first in firsts], held, sems)
+    for i in range(count):
+        step = dot(c_refs[i][...], stream.piece(i)[...])
+        total = step if total is None else total + step
+    out_ref[...] = total.astype(out_ref.dtype)
 
 
 def partial_kernel(split, place_ref, m_ref, w_ref, keep_ref, give_ref, held, sems):
@@ -241,16 +236,17 @@
             out_ref[at, :, cols] = dot_nt(m_ref[...], piece[...]).astype(BF16)
 
 
-def weight_grad_kernel(count, place_ref, c_ref, *refs):
-    m_refs, out_ref = refs[:count], refs[count]
+def weight_grad_kernel(which, given, place_ref, *refs):
+    c_ref, m_refs, out_ref = refs[given], refs[given + 1 : -1], refs[-1]
     features = out_ref.shape[0]
     height = min(512, features)
     for first in range(0, features, height):
-        total = None
-        for p in range(count):
-            part = dot_tn(c_ref[place_ref[p], :, first : first + height], m_refs[p][...])
+        rows = slice(first, first + height)
+        total = refs[0][rows, :] if given else None
+        for p, m_ref in zip(which, m_refs):
+            part = dot_tn(c_ref[place_ref[p], :, rows], m_ref[...])
             total = part if total is None else total + part
-        out_ref[first : first + height, :] = total.astype(BF16)
+        out_ref[rows, :] = total.astype(out_ref.dtype)
 
 
 def cost(flops, bytes_accessed, exps=0, weight=1.0):
@@ -285,28 +281,35 @@
 
 
 VMEM_LIMIT = 20 * 1024 * 1024
-WEIGHTS = dict(mixed_grad=0.0, forward=100.0, partial=0.0, query=100.0, key=0.0)
+WEIGHTS = dict(mixed_grad=0.0, forward=100.0, partial=0.0, query=100.0, key=0.0, weight=0.0)
 STREAM_LIMIT = 54 * 1024 * 1024
 
 
-def features_here(value, *others, serial=False):
+def two_by_two():
+    return lax.axis_size("head") == 2 and lax.axis_size("rep") == 2
+
+
+def features_here(value):
     heads, reps = lax.axis_size("head"), lax.axis_size("rep")
-    if heads == 2 and reps == 2:
+    if two_by_two():
         h, r = lax.axis_index("head"), lax.axis_index("rep")
-        across = swap(after(value, *others), "head")
-        beside = swap(after(value, across) if serial else value, "rep")
-        corner = swap(after(across, beside) if serial else across, "rep")
-        blocks = [value, beside, across, corner]
         places = [2 * h + r, 2 * h + 1 - r, 2 * (1 - h) + r, 2 * (1 - h) + 1 - r]
-        return blocks, jnp.stack(places).astype(jnp.int32)
+        rest = swap(value, "head")
+        return [value, swap(value, "rep")], rest, jnp.stack(places).astype(jnp.int32)
+    count = heads * reps
     gathered = lax.all_gather(value, ("head", "rep"), axis=0)
-    count = heads * reps
-    return [gathered[i] for i in range(count)], jnp.arange(count, dtype=jnp.int32)
+    blocks = [gathered[i] for i in range(count)]
+    return blocks[: count // 2], blocks[count // 2 :], jnp.arange(count, dtype=jnp.int32)
+
+
+def other_features(rest, *others):
+    if two_by_two():
+        return [rest, swap(after(rest, *others), "rep")]
+    return rest
 
 
 def attended_partial(mixed_heads, out_weight, places, estimate):
-    heads, reps = lax.axis_size("head"), lax.axis_size("rep")
-    if heads == 2 and reps == 2:
+    if two_by_two():
         rows = mixed_heads.shape[0]
         share = out_weight.shape[0] // 4
         order = jnp.stack([places[1], places[3], places[0], places[2]])
@@ -366,26 +369,33 @@
 
     kv_all = further([jnp.concatenate([keys, values])], 1)
     query_all = further([queries], -1)
-    c_blocks, c_places = features_here(cotangent)
-    group_count = len(c_blocks)
+    c_blocks, c_rest, c_places = features_here(cotangent)
+    half = len(c_blocks)
     part_cols = cotangent.shape[1]
     while len(query_all) < count:
         query_all = further(query_all, -1)
-    split = max(1, columns // 256)
-    mixed_grad = kernel_call(
-        functools.partial(mixed_grad_kernel, group_count, split),
-        "mixed_grad",
-        [c_places],
-        c_blocks,
-        like_queries,
-        cost(2 * rows * columns * features, 2 * columns * features, 0, WEIGHTS["mixed_grad"]),
-        [out_weight],
-        weight_scratch(split, features, columns // split),
-    )
+    mixed_sum = []
+    for part in range(2):
+        if part:
+            c_blocks = c_blocks + other_features(c_rest, *mixed_sum)
+        mine = slice(part * half, (part + 1) * half)
+        mixed_sum = [
+            kernel_call(
+                functools.partial(mixed_grad_kernel, half, part),
+                "mixed_grad",
+                [c_places[mine]],
+                [*mixed_sum, *c_blocks[mine]],
+                jax.ShapeDtypeStruct((rows, columns), BF16 if part else F32),
+                cost(rows * columns * features, columns * features, 0, WEIGHTS["mixed_grad"] * (1 - part)),
+                [out_weight],
+                weight_scratch(half, part_cols, columns),
+            )
+        ]
+    mixed_grad = mixed_sum[0]
+    group_count = len(c_blocks)
     while len(kv_all) < count:
         kv_all = further(kv_all, 1, mixed_grad)
     grad_all = further([mixed_grad], -1, query_all[-1])
-    first_grad = grad_all[-1]
     while len(grad_all) < count:
         grad_all = further(grad_all, -1)
 
@@ -400,7 +410,7 @@
     for s in range(peers):
         for q in range(group_count):
             links.append((s * group_count + q, ((s + step_of(q)) % peers) * group_count + q))
-    arrived = lax.ppermute(after(out_block, first_grad), ("seq", "head", "rep"), links)
+    arrived = lax.ppermute(after(out_block, grad_all[-1], kv_all[-1]), ("seq", "head", "rep"), links)
 
     mixed_heads, lse = kernel_call(
         functools.partial(forward_kernel, tiles, count, heads),
@@ -427,7 +437,7 @@
     partial_products = attended_partial(
         mixed_heads, out_weight, c_places, cost(2 * rows * columns * features, 2 * rows * features, 0, WEIGHTS["partial"])
     )
-    ct_across = swap(after(arrived, mixed_heads), "head") if n_head == 2 and n_rep == 2 else arrived
+    ct_across = swap(after(arrived, mixed_heads), "head") if two_by_two() else arrived
     held = after(mixed_heads, ct_across, *near.values(), *stats_all[1:], *partial_products)
     if peers <= 4:
         mixed_all = [mixed_heads] + [
@@ -440,11 +450,11 @@
             for k in range(peers)
         ]
     attended = attended_share(partial_products, held)
-    if n_head == 2 and n_rep == 2:
-        ct_blocks = [arrived, swap(after(arrived, held), "rep"), ct_across, swap(after(ct_across, held), "rep")]
-        ct_places = c_places
+    if two_by_two():
+        ct_blocks = [arrived, swap(after(arrived, held), "rep"), *other_features(ct_across, held)]
     else:
-        ct_blocks, ct_places = features_here(arrived)
+        ct_blocks, ct_rest, _ = features_here(arrived)
+        ct_blocks = ct_blocks + ct_rest
     ct = jnp.stack(ct_blocks)
     k_grad, v_grad = kernel_call(
         functools.partial(key_kernel, tiles, count, heads, heads_up),
@@ -455,18 +465,31 @@
         cost(4 * attention_flops, (2 * count + 4) * array_bytes, exps, WEIGHTS["key"]),
     )
 
-    steps = step_of(ct_places)
+    steps = step_of(c_places)
     ct_at = jnp.sum(
         jnp.where(steps[None] == jnp.arange(peers)[:, None], jnp.arange(group_count)[None], 0), 1
     ).astype(jnp.int32)
-    weight_grad = kernel_call(
-        functools.partial(weight_grad_kernel, peers),
-        "weight_grad",
-        [ct_at],
-        [ct, after(mixed_all[0], attended, k_grad), *mixed_all[1:]],
-        jax.ShapeDtypeStruct((part_cols, columns), BF16),
-        cost(2 * part_cols * columns * rows * peers, 2 * array_bytes * peers),
-    )
+    early = sorted({0, 1, peers - 1}) if 2 < peers <= 4 else [0]
+    late = [k for k in range(peers) if k not in early]
+    weight_sum = []
+    for part, which in enumerate((early, late)):
+        if not which:
+            weight_sum = [weight_sum[0].astype(BF16)]
+            break
+        ranges = [mixed_all[k] for k in which]
+        if part:
+            ranges[0] = after(ranges[0], attended, k_grad)
+        weight_sum = [
+            kernel_call(
+                functools.partial(weight_grad_kernel, which, part),
+                "weight_grad",
+                [ct_at],
+                [*weight_sum, ct, *ranges],
+                jax.ShapeDtypeStruct((part_cols, columns), BF16 if part else F32),
+                cost(2 * part_cols * columns * rows * len(which), array_bytes * len(which), 0, WEIGHTS["weight"]),
+            )
+        ]
+    weight_grad = weight_sum[0]
     return (attended, q_grad, k_grad, v_grad, weight_grad)
 
 

time: 143 us -> 147 us (1.028)
  Pallas kernels: 37.8 us -> 40.7 us
  waiting for transfers between devices: 49.5 us -> 52.2 us
  starting transfers between devices: 46.1 us -> 44.2 us
    ppermute x3, starting transfers between devices: 20.7 us -> 10.5 us  [cyclic(): lax.ppermute(value, 'seq', [(i, (i + by) % peers) for i in range(peers)])]
    ppermute x8, waiting for transfers between devices: 26.1 us -> 34.7 us  [shift(): lax.ppermute(value, 'seq', [(i, i + by) for i in range(peers) if 0 <= i +...]
    ppermute x8, starting transfers between devices: 5.73 us -> 14.1 us  [swap(): return lax.ppermute(value, axis, [(0, 1), (1, 0)])]
    ppermute x8, waiting for transfers between devices: 9.21 us -> 3.01 us  [swap(): return lax.ppermute(value, axis, [(0, 1), (1, 0)])]
    pallas_call x6 -> x8, Pallas kernels: 37.8 us -> 40.7 us  [kernel_call(): pl.pallas_call(body, in_specs=[smem] * len(scalars) + [vmem] * len(arrays...]
  transfers between devices with their start and end apart: 20 -> 20, of which waited for: 9 -> 8; matrix products, arithmetic and copies ran while one was open for 5% -> 6% of each run, Pallas kernels for 23% -> 26%
where the time goes in v6:
time: 147 us; the launch traced here: 146 us
  waiting for transfers between devices  52.2 us (36%)
  starting transfers between devices  44.2 us (30%)
  Pallas kernels  40.7 us (28%)
  other arithmetic  5.84 us (4%)
  local copies, waits for them, and re-layouts  2.28 us (2%)
    pallas_call x8, Pallas kernels, kernel_call(): pl.pallas_call(body, in_specs=[smem] * len(scalars) + [vmem] * len(arrays...  40.7 us
    ppermute x8, waiting for transfers between devices, shift(): lax.ppermute(value, 'seq', [(i, i + by) for i in range(peers) if 0 <= i +...  34.7 us
    ppermute x8, starting transfers between devices, shift(): lax.ppermute(value, 'seq', [(i, i + by) for i in range(peers) if 0 <= i +...  18.9 us
    ppermute x3, waiting for transfers between devices, cyclic(): lax.ppermute(value, 'seq', [(i, (i + by) % peers) for i in range(peers)])  14.4 us
    ppermute x8, starting transfers between devices, swap(): return lax.ppermute(value, axis, [(0, 1), (1, 0)])  14.1 us
    ppermute x3, starting transfers between devices, cyclic(): lax.ppermute(value, 'seq', [(i, (i + by) % peers) for i in range(peers)])  10.5 us
    ppermute x8, waiting for transfers between devices, swap(): return lax.ppermute(value, axis, [(0, 1), (1, 0)])  3.01 us
  transfers between devices with their start and end apart: 20, of which 8 were waited for; matrix products, arithmetic and copies ran while one was open for 6% of the time, Pallas kernels for 26%

profile of v6, /device:TPU:0, one launch (start us, length us, event | category | flops | bytes accessed | tf_op | source)
XLA Modules:
  0.0 146.2 jit_solution(8074616572795005113)
XLA Ops:
  1.1 2.6 %collective-permute-start.3 = (bf16[256,1024]{1,0:T(8,128)(2,1)}, bf16[256,1024]{1,0:T(8,128)(2,1)}, u32[]{:S(2)}, u32[]{:S(2)}) collective-permute-start(bf16[256,1024]{1,0:T(8,128)(2,1)} %refs_0_.2), channel_id=1, source_target_pairs={{0,2},{2,0},{1,3},{3,1},{4,6},{6,4},{5,7},{7,5},{8,10},{10,8},{9,1... | collective-permute-start | bytes 1572872 | tf_op jit(solution)/shard_map/ppermute | solution.py:37
  7.2 5.5 %collective-permute-start.7 = (bf16[512,1024]{1,0:T(8,128)(2,1)S(1)}, bf16[512,1024]{1,0:T(8,128)(2,1)}, u32[]{:S(2)}, u32[]{:S(2)}) collective-permute-start(bf16[512,1024]{1,0:T(8,128)(2,1)S(1)} %constant_dynamic-update-slice_fusion.refs_0_), channel_id=1, source_target_pairs={{0,4},{4,8},{8,12},{1,5},{5,9},{9,13},{2,6},{6,10},{10,14},{3,7},{... | collective-permute-start | bytes 3145736 | tf_op jit(solution)/shard_map/ppermute | solution.py:26
  13.3 5.7 %mixed_grad.2.refs_0_ = f32[256,1024]{1,0:T(8,128)} custom-call(s32[2]{0:T(128)} %pad_add_fusion.2.place_ref, bf16[256,1024]{1,0:T(8,128)(2,1)} %refs_0_.2, bf16[256,1024]{1,0:T(8,128)(2,1)} %collective-permute-done.2.refs_1_, bf16[4096,1024]{1,0:T(8,128)(2,1)} %w_ref.1), custom_call_target="tpu_custom_call" | custom-call | tf_op jit(solution)/shard_map/mixed_grad/pallas_call | solution.py:263
  19.8 1.3 collective-permute-start.1
  21.7 5.3 %mixed_grad.3.g_ref.refs_3_ = bf16[256,1024]{1,0:T(8,128)(2,1)} custom-call(s32[2]{0:T(128)} %pad_add_fusion.1.place_ref, f32[256,1024]{1,0:T(8,128)} %mixed_grad.2.refs_0_, bf16[256,1024]{1,0:T(8,128)(2,1)} %collective-permute-done.3.refs_1_, bf16[256,1024]{1,0:T(8,128)(2,1)} %collective-permute-done.4.refs_2_, bf16[4096,1024]{1,0:T(8,128)(2,1)} %w_ref.1), custom_call_target="tpu_custom_call" | custom-call | tf_op jit(solution)/shard_map/mixed_grad/pallas_call | solution.py:263
  27.0 8.3 %collective-permute-done.1.refs_2_ = bf16[256,1024]{1,0:T(8,128)(2,1)S(1)} collective-permute-done((bf16[256,1024]{1,0:T(8,128)(2,1)S(1)}, bf16[256,1024]{1,0:T(8,128)(2,1)S(1)}, u32[]{:S(2)}, u32[]{:S(2)}) %collective-permute-start.1) | collective-permute-done | bytes 524320 | tf_op jit(solution)/shard_map/ppermute | solution.py:26
  35.3 1.3 collective-permute-start.5
  36.6 5.5 %collective-permute-start.8 = (bf16[512,1024]{1,0:T(8,128)(2,1)}, bf16[512,1024]{1,0:T(8,128)(2,1)}, u32[]{:S(2)}, u32[]{:S(2)}) collective-permute-start(bf16[512,1024]{1,0:T(8,128)(2,1)} %collective-permute-done.7.refs_1_), channel_id=1, source_target_pairs={{0,4},{4,8},{8,12},{1,5},{5,9},{9,13},{2,6},{6,10},{10,14},{3,7},{... | collective-permute-start | bytes 3145736 | tf_op jit(solution)/shard_map/ppermute | solution.py:26
  42.1 8.0 %collective-permute-done.5.refs_4_ = bf16[256,1024]{1,0:T(8,128)(2,1)S(1)} collective-permute-done((bf16[256,1024]{1,0:T(8,128)(2,1)}, bf16[256,1024]{1,0:T(8,128)(2,1)S(1)}, u32[]{:S(2)}, u32[]{:S(2)}) %collective-permute-start.5) | collective-permute-done | bytes 524320 | tf_op jit(solution)/shard_map/ppermute | solution.py:26
  50.1 1.3 collective-permute-start.6
  52.9 10.9 %collective-permute-done.6.refs_5_ = bf16[256,1024]{1,0:T(8,128)(2,1)S(1)} collective-permute-done((bf16[256,1024]{1,0:T(8,128)(2,1)S(1)}, bf16[256,1024]{1,0:T(8,128)(2,1)S(1)}, u32[]{:S(2)}, u32[]{:S(2)}) %collective-permute-start.6) | collective-permute-done | bytes 524320 | tf_op jit(solution)/shard_map/ppermute | solution.py:26
  64.5 4.8 %attention_forward.1 = (bf16[256,1024]{1,0:T(8,128)(2,1)}, f32[8,256]{1,0:T(8,128)S(1)}) custom-call(s32[10]{0:T(128)S(1)} %reshape.264.use_ref, bf16[256,1024]{1,0:T(8,128)(2,1)S(1)} %copy-done.3, bf16[512,1024]{1,0:T(8,128)(2,1)S(1)} %copy-done.5, bf16[512,1024]{1,0:T(8,128)(2,1)} %collective-permute-done.7.refs_1_, ...), custom_call_target="tpu_custom_call" | custom-call | flops 53687091200 | bytes 419430400 | tf_op jit(solution)/shard_map/attention_forward/pallas_call | solution.py:263
  69.3 2.8 %collective-permute-start.12 = (bf16[256,1024]{1,0:T(8,128)(2,1)}, bf16[256,1024]{1,0:T(8,128)(2,1)S(1)}, u32[]{:S(2)}, u32[]{:S(2)}) collective-permute-start(bf16[256,1024]{1,0:T(8,128)(2,1)} %get-tuple-element.38.m_ref.refs_1_), channel_id=1, source_target_pairs={{0,12},{4,0},{8,4},{12,8},{1,13},{5,1},{9,5},{13,9},{2,14},{6,2},{... | collective-permute-start | bytes 1572872 | tf_op jit(solution)/shard_map/ppermute | solution.py:33
  72.1 10.2 %collective-permute-start.10 = (bf16[256,1024]{1,0:T(8,128)(2,1)S(1)}, bf16[256,1024]{1,0:T(8,128)(2,1)S(1)}, u32[]{:S(2)}, u32[]{:S(2)}) collective-permute-start(bf16[256,1024]{1,0:T(8,128)(2,1)S(1)} %collective-permute-done.9), channel_id=1, source_target_pairs={{0,2},{2,0},{1,3},{3,1},{4,6},{6,4},{5,7},{7,5},{8,10},{10,8},{9,1... | collective-permute-start | bytes 1572872 | tf_op jit(solution)/shard_map/ppermute | solution.py:37
  82.3 7.7 %attention_query_grad.1 = (bf16[256,1024]{1,0:T(8,128)(2,1)}, f32[24,256]{1,0:T(8,128)S(1)}) custom-call(s32[10]{0:T(128)S(1)} %reshape.264.use_ref, bf16[256,1024]{1,0:T(8,128)(2,1)S(1)} %copy-done.3, bf16[256,1024]{1,0:T(8,128)(2,1)S(1)} %copy-done, f32[8,256]{1,0:T(8,128)S(1)} %get-tuple-element.36.lse_ref, bf16[512,1024]{1,0:T(8,128)(2,1)S(1)} %copy-done.5, ...), custom_call_target="tpu_custom_call" | custom-call | flops 80530636800 | bytes 471859200 | tf_op jit(solution)/shard_map/attention_query_grad/pallas_call | solution.py:263
  91.2 1.5 %collective-permute-start.13 = (f32[24,256]{1,0:T(8,128)S(1)}, f32[24,256]{1,0:T(8,128)S(1)}, u32[]{:S(2)}, u32[]{:S(2)}) collective-permute-start(f32[24,256]{1,0:T(8,128)S(1)} %get-tuple-element.37.refs_6_), channel_id=1, source_target_pairs={{4,0},{8,4},{12,8},{5,1},{9,5},{13,9},{6,2},{10,6},{14,10},{7,3},{... | collective-permute-start | bytes 73736 | tf_op jit(solution)/shard_map/ppermute | solution.py:26
  93.3 7.0 %attended_partial.1 = (bf16[2,256,1024]{2,1,0:T(8,128)(2,1)}, bf16[2,256,1024]{2,1,0:T(8,128)(2,1)}) custom-call(s32[4]{0:T(128)} %pad_add_fusion.place_ref, bf16[256,1024]{1,0:T(8,128)(2,1)} %get-tuple-element.38.m_ref.refs_1_, bf16[4096,1024]{1,0:T(8,128)(2,1)} %w_ref.1), custom_call_target="tpu_custom_call" | custom-call | tf_op jit(solution)/shard_map/attended_partial/pallas_call | solution.py:263
  100.3 6.5 %collective-permute-done.14.refs_8_ = f32[24,256]{1,0:T(8,128)S(1)} collective-permute-done((f32[24,256]{1,0:T(8,128)S(1)}, f32[24,256]{1,0:T(8,128)S(1)}, u32[]{:S(2)}, u32[]{:S(2)}) %collective-permute-start.14) | collective-permute-done | bytes 24608 | tf_op jit(solution)/shard_map/ppermute | solution.py:26
  107.7 3.0 %collective-permute-done.15 = bf16[2,256,1024]{2,1,0:T(8,128)(2,1)S(1)} collective-permute-done((bf16[2,256,1024]{2,1,0:T(8,128)(2,1)}, bf16[2,256,1024]{2,1,0:T(8,128)(2,1)S(1)}, u32[]{:S(2)}, u32[]{:S(2)}) %collective-permute-start.15) | collective-permute-done | bytes 1048608 | tf_op jit(solution)/shard_map/ppermute | solution.py:37
  112.1 7.7 %collective-permute-start.19 = (bf16[256,1024]{1,0:T(8,128)(2,1)}, bf16[256,1024]{1,0:T(8,128)(2,1)S(1)}, u32[]{:S(2)}, u32[]{:S(2)}) collective-permute-start(bf16[256,1024]{1,0:T(8,128)(2,1)} %get-tuple-element.38.m_ref.refs_1_), channel_id=1, source_target_pairs={{0,8},{4,12},{8,0},{12,4},{1,9},{5,13},{9,1},{13,5},{2,10},{6,14},... | collective-permute-start | bytes 1572872 | tf_op jit(solution)/shard_map/ppermute | solution.py:33
  120.0 4.7 %attention_key_grad.1 = (bf16[256,1024]{1,0:T(8,128)(2,1)}, bf16[256,1024]{1,0:T(8,128)(2,1)}) custom-call(bf16[256,1024]{1,0:T(8,128)(2,1)S(1)} %copy-done.1, bf16[256,1024]{1,0:T(8,128)(2,1)S(1)} %copy-done.2, bf16[256,1024]{1,0:T(8,128)(2,1)S(1)} %copy-done.3, bf16[256,1024]{1,0:T(8,128)(2,1)S(1)} %collective-permute-done.refs_1_, ...), custom_call_target="tpu_custom_call" | custom-call | tf_op jit(solution)/shard_map/attention_key_grad/pallas_call | solution.py:263
  125.0 3.0 %weight_grad.2.refs_0_ = f32[1024,1024]{1,0:T(8,128)S(1)} custom-call(s32[4]{0:T(128)S(1)} %select_reduce_fusion.place_ref, bf16[4,256,1024]{2,1,0:T(8,128)(2,1)S(1)} %pad_maximum_fusion.refs_0_.refs_1_, bf16[256,1024]{1,0:T(8,128)(2,1)} %get-tuple-element.38.m_ref.refs_1_, bf16[256,1024]{1,0:T(8,128)(2,1)S(1)} %collective-permute-done.11.refs_2_, ...), custom_call_target="tpu_custom_call" | custom-call | tf_op jit(solution)/shard_map/weight_grad/pallas_call | solution.py:263
  129.1 14.4 %collective-permute-done.19.refs_2_ = bf16[256,1024]{1,0:T(8,128)(2,1)S(1)} collective-permute-done((bf16[256,1024]{1,0:T(8,128)(2,1)}, bf16[256,1024]{1,0:T(8,128)(2,1)S(1)}, u32[]{:S(2)}, u32[]{:S(2)}) %collective-permute-start.19) | collective-permute-done | bytes 524320 | tf_op jit(solution)/shard_map/ppermute | solution.py:33
  143.6 2.6 %weight_grad.3 = bf16[1024,1024]{1,0:T(8,128)(2,1)} custom-call(s32[4]{0:T(128)S(1)} %select_reduce_fusion.place_ref, f32[1024,1024]{1,0:T(8,128)S(1)} %weight_grad.2.refs_0_, bf16[4,256,1024]{2,1,0:T(8,128)(2,1)S(1)} %pad_maximum_fusion.refs_0_.refs_1_, bf16[256,1024]{1,0:T(8,128)(2,1)S(1)} %collective-permute-done.19.refs_2_), custom_call_target="tpu_custom_call" | custom-call | tf_op jit(solution)/shard_map/weight_grad/pallas_call | solution.py:263
  (55 shorter events, 13.7 us)
Async XLA Ops:
  0.6 12.7 %collective-permute-start.2 = (bf16[256,1024]{1,0:T(8,128)(2,1)}, bf16[256,1024]{1,0:T(8,128)(2,1)}, u32[]{:S(2)}, u32[]{:S(2)}) collective-permute-start(bf16[256,1024]{1,0:T(8,128)(2,1)} %refs_0_.2), channel_id=1, source_target_pairs={{0,1},{1,0},{2,3},{3,2},{4,5},{5,4},{6,7},{7,6},{8,9},{9,8},{10,11... | collective-permute-start | bytes 1572872 | tf_op jit(solution)/shard_map/ppermute | solution.py:37
  1.1 17.8 %collective-permute-start.3 = (bf16[256,1024]{1,0:T(8,128)(2,1)}, bf16[256,1024]{1,0:T(8,128)(2,1)}, u32[]{:S(2)}, u32[]{:S(2)}) collective-permute-start(bf16[256,1024]{1,0:T(8,128)(2,1)} %refs_0_.2), channel_id=1, source_target_pairs={{0,2},{2,0},{1,3},{3,1},{4,6},{6,4},{5,7},{7,5},{8,10},{10,8},{9,1... | collective-permute-start | bytes 1572872 | tf_op jit(solution)/shard_map/ppermute | solution.py:37
  3.7 16.1 %collective-permute-start = (bf16[256,1024]{1,0:T(8,128)(2,1)}, bf16[256,1024]{1,0:T(8,128)(2,1)S(1)}, u32[]{:S(2)}, u32[]{:S(2)}) collective-permute-start(bf16[256,1024]{1,0:T(8,128)(2,1)} %refs_0_.3), channel_id=1, source_target_pairs={{4,0},{8,4},{12,8},{5,1},{9,5},{13,9},{6,2},{10,6},{14,10},{7,3},{... | collective-permute-start | bytes 1572872 | tf_op jit(solution)/shard_map/ppermute | solution.py:26
  7.2 29.4 %collective-permute-start.7 = (bf16[512,1024]{1,0:T(8,128)(2,1)S(1)}, bf16[512,1024]{1,0:T(8,128)(2,1)}, u32[]{:S(2)}, u32[]{:S(2)}) collective-permute-start(bf16[512,1024]{1,0:T(8,128)(2,1)S(1)} %constant_dynamic-update-slice_fusion.refs_0_), channel_id=1, source_target_pairs={{0,4},{4,8},{8,12},{1,5},{5,9},{9,13},{2,6},{6,10},{10,14},{3,7},{... | collective-permute-start | bytes 3145736 | tf_op jit(solution)/shard_map/ppermute | solution.py:26
  19.0 2.7 %collective-permute-start.4 = (bf16[256,1024]{1,0:T(8,128)(2,1)}, bf16[256,1024]{1,0:T(8,128)(2,1)}, u32[]{:S(2)}, u32[]{:S(2)}) collective-permute-start(bf16[256,1024]{1,0:T(8,128)(2,1)} %collective-permute-done.3.refs_1_), channel_id=1, source_target_pairs={{0,1},{1,0},{2,3},{3,2},{4,5},{5,4},{6,7},{7,6},{8,9},{9,8},{10,11... | collective-permute-start | bytes 1572872 | tf_op jit(solution)/shard_map/ppermute | solution.py:37
  19.8 15.5 %collective-permute-start.1 = (bf16[256,1024]{1,0:T(8,128)(2,1)S(1)}, bf16[256,1024]{1,0:T(8,128)(2,1)S(1)}, u32[]{:S(2)}, u32[]{:S(2)}) collective-permute-start(bf16[256,1024]{1,0:T(8,128)(2,1)S(1)} %collective-permute-done.refs_1_), channel_id=1, source_target_pairs={{4,0},{8,4},{12,8},{5,1},{9,5},{13,9},{6,2},{10,6},{14,10},{7,3},{... | collective-permute-start | bytes 1572872 | tf_op jit(solution)/shard_map/ppermute | solution.py:26
  21.7 29.8 %copy-start.7 = (s32[2,5]{1,0:T(2,128)S(1)}, s32[2,5]{1,0:T(2,128)}, u32[]{:S(2)}) copy-start(s32[2,5]{1,0:T(2,128)} %param.10) | copy-start | bytes 124
  27.0 37.5 %copy-start.3 = (bf16[256,1024]{1,0:T(8,128)(2,1)S(1)}, bf16[256,1024]{1,0:T(8,128)(2,1)}, u32[]{:S(2)}) copy-start(bf16[256,1024]{1,0:T(8,128)(2,1)} %refs_0_.3) | copy-start | bytes 1572868
  35.3 14.8 %collective-permute-start.5 = (bf16[256,1024]{1,0:T(8,128)(2,1)}, bf16[256,1024]{1,0:T(8,128)(2,1)S(1)}, u32[]{:S(2)}, u32[]{:S(2)}) collective-permute-start(bf16[256,1024]{1,0:T(8,128)(2,1)} %mixed_grad.3.g_ref.refs_3_), channel_id=1, source_target_pairs={{4,0},{8,4},{12,8},{5,1},{9,5},{13,9},{6,2},{10,6},{14,10},{7,3},{... | collective-permute-start | bytes 1572872 | tf_op jit(solution)/shard_map/ppermute | solution.py:26
  36.6 27.2 %collective-permute-start.8 = (bf16[512,1024]{1,0:T(8,128)(2,1)}, bf16[512,1024]{1,0:T(8,128)(2,1)}, u32[]{:S(2)}, u32[]{:S(2)}) collective-permute-start(bf16[512,1024]{1,0:T(8,128)(2,1)} %collective-permute-done.7.refs_1_), channel_id=1, source_target_pairs={{0,4},{4,8},{8,12},{1,5},{5,9},{9,13},{2,6},{6,10},{10,14},{3,7},{... | collective-permute-start | bytes 3145736 | tf_op jit(solution)/shard_map/ppermute | solution.py:26
  50.1 13.7 %collective-permute-start.6 = (bf16[256,1024]{1,0:T(8,128)(2,1)S(1)}, bf16[256,1024]{1,0:T(8,128)(2,1)S(1)}, u32[]{:S(2)}, u32[]{:S(2)}) collective-permute-start(bf16[256,1024]{1,0:T(8,128)(2,1)S(1)} %collective-permute-done.5.refs_4_), channel_id=1, source_target_pairs={{4,0},{8,4},{12,8},{5,1},{9,5},{13,9},{6,2},{10,6},{14,10},{7,3},{... | collective-permute-start | bytes 1572872 | tf_op jit(solution)/shard_map/ppermute | solution.py:26
  52.9 29.4 %copy-start = (bf16[256,1024]{1,0:T(8,128)(2,1)S(1)}, bf16[256,1024]{1,0:T(8,128)(2,1)}, u32[]{:S(2)}) copy-start(bf16[256,1024]{1,0:T(8,128)(2,1)} %mixed_grad.3.g_ref.refs_3_) | copy-start | bytes 1572868
  63.8 8.3 %collective-permute-start.9 = (bf16[256,1024]{1,0:T(8,128)(2,1)S(1)}, bf16[256,1024]{1,0:T(8,128)(2,1)S(1)}, u32[]{:S(2)}, u32[]{:S(2)}) collective-permute-start(bf16[256,1024]{1,0:T(8,128)(2,1)S(1)} %select_select_fusion), channel_id=1, source_target_pairs={{0,0},{1,9},{2,6},{3,15},{4,4},{5,13},{6,10},{7,3},{8,8},{9,1},{10... | collective-permute-start | bytes 1572872 | tf_op jit(solution)/shard_map/ppermute | solution.py:413
  69.3 37.8 %collective-permute-start.12 = (bf16[256,1024]{1,0:T(8,128)(2,1)}, bf16[256,1024]{1,0:T(8,128)(2,1)S(1)}, u32[]{:S(2)}, u32[]{:S(2)}) collective-permute-start(bf16[256,1024]{1,0:T(8,128)(2,1)} %get-tuple-element.38.m_ref.refs_1_), channel_id=1, source_target_pairs={{0,12},{4,0},{8,4},{12,8},{1,13},{5,1},{9,5},{13,9},{2,14},{6,2},{... | collective-permute-start | bytes 1572872 | tf_op jit(solution)/shard_map/ppermute | solution.py:33
  72.1 35.0 %collective-permute-start.11 = (bf16[256,1024]{1,0:T(8,128)(2,1)}, bf16[256,1024]{1,0:T(8,128)(2,1)S(1)}, u32[]{:S(2)}, u32[]{:S(2)}) collective-permute-start(bf16[256,1024]{1,0:T(8,128)(2,1)} %get-tuple-element.38.m_ref.refs_1_), channel_id=1, source_target_pairs={{0,4},{4,8},{8,12},{12,0},{1,5},{5,9},{9,13},{13,1},{2,6},{6,10},{... | collective-permute-start | bytes 1572872 | tf_op jit(solution)/shard_map/ppermute | solution.py:33
  72.1 35.0 %collective-permute-start.10 = (bf16[256,1024]{1,0:T(8,128)(2,1)S(1)}, bf16[256,1024]{1,0:T(8,128)(2,1)S(1)}, u32[]{:S(2)}, u32[]{:S(2)}) collective-permute-start(bf16[256,1024]{1,0:T(8,128)(2,1)S(1)} %collective-permute-done.9), channel_id=1, source_target_pairs={{0,2},{2,0},{1,3},{3,1},{4,6},{6,4},{5,7},{7,5},{8,10},{10,8},{9,1... | collective-permute-start | bytes 1572872 | tf_op jit(solution)/shard_map/ppermute | solution.py:37
  90.0 16.9 %collective-permute-start.14 = (f32[24,256]{1,0:T(8,128)S(1)}, f32[24,256]{1,0:T(8,128)S(1)}, u32[]{:S(2)}, u32[]{:S(2)}) collective-permute-start(f32[24,256]{1,0:T(8,128)S(1)} %get-tuple-element.37.refs_6_), channel_id=1, source_target_pairs={{8,0},{12,4},{9,1},{13,5},{10,2},{14,6},{11,3},{15,7},{24,16},{28,... | collective-permute-start | bytes 73736 | tf_op jit(solution)/shard_map/ppermute | solution.py:26
  91.2 15.8 %collective-permute-start.13 = (f32[24,256]{1,0:T(8,128)S(1)}, f32[24,256]{1,0:T(8,128)S(1)}, u32[]{:S(2)}, u32[]{:S(2)}) collective-permute-start(f32[24,256]{1,0:T(8,128)S(1)} %get-tuple-element.37.refs_6_), channel_id=1, source_target_pairs={{4,0},{8,4},{12,8},{5,1},{9,5},{13,9},{6,2},{10,6},{14,10},{7,3},{... | collective-permute-start | bytes 73736 | tf_op jit(solution)/shard_map/ppermute | solution.py:26
  93.3 26.7 %copy-start.2 = (bf16[256,1024]{1,0:T(8,128)(2,1)S(1)}, bf16[256,1024]{1,0:T(8,128)(2,1)}, u32[]{:S(2)}) copy-start(bf16[256,1024]{1,0:T(8,128)(2,1)} %v_ref.1) | copy-start | bytes 1572868
  107.1 3.7 %collective-permute-start.15 = (bf16[2,256,1024]{2,1,0:T(8,128)(2,1)}, bf16[2,256,1024]{2,1,0:T(8,128)(2,1)S(1)}, u32[]{:S(2)}, u32[]{:S(2)}) collective-permute-start(bf16[2,256,1024]{2,1,0:T(8,128)(2,1)} %get-tuple-element.39), channel_id=1, source_target_pairs={{0,1},{1,0},{2,3},{3,2},{4,5},{5,4},{6,7},{7,6},{8,9},{9,8},{10,11... | collective-permute-start | bytes 3145736 | tf_op jit(solution)/shard_map/ppermute | solution.py:37
  107.2 17.6 %collective-permute-start.17 = (bf16[256,1024]{1,0:T(8,128)(2,1)S(1)}, bf16[256,1024]{1,0:T(8,128)(2,1)S(1)}, u32[]{:S(2)}, u32[]{:S(2)}) collective-permute-start(bf16[256,1024]{1,0:T(8,128)(2,1)S(1)} %collective-permute-done.9), channel_id=1, source_target_pairs={{0,1},{1,0},{2,3},{3,2},{4,5},{5,4},{6,7},{7,6},{8,9},{9,8},{10,11... | collective-permute-start | bytes 1572872 | tf_op jit(solution)/shard_map/ppermute | solution.py:37
  107.7 17.1 %collective-permute-start.18 = (bf16[256,1024]{1,0:T(8,128)(2,1)S(1)}, bf16[256,1024]{1,0:T(8,128)(2,1)S(1)}, u32[]{:S(2)}, u32[]{:S(2)}) collective-permute-start(bf16[256,1024]{1,0:T(8,128)(2,1)S(1)} %collective-permute-done.10), channel_id=1, source_target_pairs={{0,1},{1,0},{2,3},{3,2},{4,5},{5,4},{6,7},{7,6},{8,9},{9,8},{10,11... | collective-permute-start | bytes 1572872 | tf_op jit(solution)/shard_map/ppermute | solution.py:37
  112.0 16.1 %collective-permute-start.16 = (bf16[256,1024]{1,0:T(8,128)(2,1)S(1)}, bf16[256,1024]{1,0:T(8,128)(2,1)S(1)}, u32[]{:S(2)}, u32[]{:S(2)}) collective-permute-start(bf16[256,1024]{1,0:T(8,128)(2,1)S(1)} %fusion.1), channel_id=1, source_target_pairs={{0,2},{2,0},{1,3},{3,1},{4,6},{6,4},{5,7},{7,5},{8,10},{10,8},{9,1... | collective-permute-start | bytes 1572872 | tf_op jit(solution)/shard_map/ppermute | solution.py:37
  112.1 31.4 %collective-permute-start.19 = (bf16[256,1024]{1,0:T(8,128)(2,1)}, bf16[256,1024]{1,0:T(8,128)(2,1)S(1)}, u32[]{:S(2)}, u32[]{:S(2)}) collective-permute-start(bf16[256,1024]{1,0:T(8,128)(2,1)} %get-tuple-element.38.m_ref.refs_1_), channel_id=1, source_target_pairs={{0,8},{4,12},{8,0},{12,4},{1,9},{5,13},{9,1},{13,5},{2,10},{6,14},... | collective-permute-start | bytes 1572872 | tf_op jit(solution)/shard_map/ppermute | solution.py:33
  (4 other events, 54.4 us)

commit v7 on v6

--- a/solution.py
+++ b/solution.py
@@ -281,7 +281,7 @@
 
 
 VMEM_LIMIT = 20 * 1024 * 1024
-WEIGHTS = dict(mixed_grad=0.0, forward=100.0, partial=0.0, query=100.0, key=0.0, weight=0.0)
+WEIGHTS = dict(mixed_grad=0.0, forward=100.0, partial=0.0, query=100.0, key=100.0, weight=0.0)
 STREAM_LIMIT = 54 * 1024 * 1024
 
 
@@ -327,16 +327,21 @@
     return [partial_value.astype(BF16)]
 
 
-def attended_share(partial_products, *others):
+def core_sum(partial_products):
     if len(partial_products) == 1:
-        return lax.psum_scatter(
-            partial_products[0], ("head", "rep"), scatter_dimension=1, tiled=True
-        )
+        return partial_products
     keep, give = partial_products
-    got = swap(after(give, *others), "rep")
-    across = (keep[1].astype(F32) + got[1].astype(F32)).astype(BF16)
-    across = swap(across, "head")
-    return (keep[0].astype(F32) + got[0].astype(F32) + across.astype(F32)).astype(BF16)
+    got = swap(give, "rep")
+    return [
+        keep[0].astype(F32) + got[0].astype(F32),
+        (keep[1].astype(F32) + got[1].astype(F32)).astype(BF16),
+    ]
+
+
+def chip_sum(shares, *others):
+    if len(shares) == 1:
+        return lax.psum_scatter(shares[0], ("head", "rep"), scatter_dimension=1, tiled=True)
+    return (shares[0] + swap(after(shares[1], *others), "head").astype(F32)).astype(BF16)
 
 
 def per_device(queries, keys, values, out_weight, level_mask, cotangent):
@@ -437,8 +442,8 @@
     partial_products = attended_partial(
         mixed_heads, out_weight, c_places, cost(2 * rows * columns * features, 2 * rows * features, 0, WEIGHTS["partial"])
     )
-    ct_across = swap(after(arrived, mixed_heads), "head") if two_by_two() else arrived
-    held = after(mixed_heads, ct_across, *near.values(), *stats_all[1:], *partial_products)
+    shares = core_sum(partial_products)
+    held = after(mixed_heads, arrived, *near.values(), *stats_all[1:], *shares)
     if peers <= 4:
         mixed_all = [mixed_heads] + [
             near[k] if k in near else cyclic(held, k) for k in range(1, peers)
@@ -449,13 +454,7 @@
             lax.dynamic_index_in_dim(gathered, (place - k) % peers, 0, False)
             for k in range(peers)
         ]
-    attended = attended_share(partial_products, held)
-    if two_by_two():
-        ct_blocks = [arrived, swap(after(arrived, held), "rep"), *other_features(ct_across, held)]
-    else:
-        ct_blocks, ct_rest, _ = features_here(arrived)
-        ct_blocks = ct_blocks + ct_rest
-    ct = jnp.stack(ct_blocks)
+    attended = chip_sum(shares, held)
     k_grad, v_grad = kernel_call(
         functools.partial(key_kernel, tiles, count, heads, heads_up),
         "attention_key_grad",
@@ -465,6 +464,8 @@
         cost(4 * attention_flops, (2 * count + 4) * array_bytes, exps, WEIGHTS["key"]),
     )
 
+    ct_blocks, ct_rest, _ = features_here(after(arrived, held))
+    ct = jnp.stack(ct_blocks + other_features(ct_rest, k_grad))
     steps = step_of(c_places)
     ct_at = jnp.sum(
         jnp.where(steps[None] == jnp.arange(peers)[:, None], jnp.arange(group_count)[None], 0), 1

time: 147 us -> 138 us (0.939)
  starting transfers between devices: 44.2 us -> 29.7 us
  waiting for transfers between devices: 52.2 us -> 58.4 us
  Pallas kernels: 40.7 us -> 38.4 us
  local copies, waits for them, and re-layouts: 2.28 us -> 3.88 us
    ppermute x8, waiting for transfers between devices: 3.01 us -> 16.5 us  [swap(): return lax.ppermute(value, axis, [(0, 1), (1, 0)])]
    ppermute x3, waiting for transfers between devices: 14.4 us -> 1.53 us  [cyclic(): lax.ppermute(value, 'seq', [(i, (i + by) % peers) for i in range(peers)])]
    ppermute x8, starting transfers between devices: 14.1 us -> 6.53 us  [swap(): return lax.ppermute(value, axis, [(0, 1), (1, 0)])]
    ppermute x3, starting transfers between devices: 10.5 us -> 4.57 us  [cyclic(): lax.ppermute(value, 'seq', [(i, (i + by) % peers) for i in range(peers)])]
    ppermute x8, waiting for transfers between devices: 34.7 us -> 40.4 us  [shift(): lax.ppermute(value, 'seq', [(i, i + by) for i in range(peers) if 0 <= i +...]
    pallas_call x8, Pallas kernels: 40.7 us -> 38.4 us  [kernel_call(): pl.pallas_call(body, in_specs=[smem] * len(scalars) + [vmem] * len(arrays...]
    ppermute x8, starting transfers between devices: 18.9 us -> 17.1 us  [shift(): lax.ppermute(value, 'seq', [(i, i + by) for i in range(peers) if 0 <= i +...]
    unnamed x17 -> x27, local copies, waits for them, and re-layouts: 1.12 us -> 2.72 us
  transfers between devices with their start and end apart: 20 -> 20, of which waited for: 8 -> 8; matrix products, arithmetic and copies ran while one was open for 6% -> 5% of each run, Pallas kernels for 26% -> 22%
where the time goes in v7:
time: 138 us; the launch traced here: 137 us
  waiting for transfers between devices  58.4 us (42%)
  Pallas kernels  38.4 us (28%)
  starting transfers between devices  29.7 us (22%)
  other arithmetic  5.76 us (4%)
  local copies, waits for them, and re-layouts  3.88 us (3%)
    ppermute x8, waiting for transfers between devices, shift(): lax.ppermute(value, 'seq', [(i, i + by) for i in range(peers) if 0 <= i +...  40.4 us
    pallas_call x8, Pallas kernels, kernel_call(): pl.pallas_call(body, in_specs=[smem] * len(scalars) + [vmem] * len(arrays...  38.4 us
    ppermute x8, starting transfers between devices, shift(): lax.ppermute(value, 'seq', [(i, i + by) for i in range(peers) if 0 <= i +...  17.1 us
    ppermute x8, waiting for transfers between devices, swap(): return lax.ppermute(value, axis, [(0, 1), (1, 0)])  16.5 us
    ppermute x8, starting transfers between devices, swap(): return lax.ppermute(value, axis, [(0, 1), (1, 0)])  6.53 us
    ppermute x3, starting transfers between devices, cyclic(): lax.ppermute(value, 'seq', [(i, (i + by) % peers) for i in range(peers)])  4.57 us
  transfers between devices with their start and end apart: 20, of which 8 were waited for; matrix products, arithmetic and copies ran while one was open for 5% of the time, Pallas kernels for 22%

profile of v7, /device:TPU:0, one launch (start us, length us, event | category | flops | bytes accessed | tf_op | source)
XLA Modules:
  0.0 137.2 jit_solution(21188194435101235)
XLA Ops:
  1.1 2.6 %collective-permute-start.3 = (bf16[256,1024]{1,0:T(8,128)(2,1)}, bf16[256,1024]{1,0:T(8,128)(2,1)}, u32[]{:S(2)}, u32[]{:S(2)}) collective-permute-start(bf16[256,1024]{1,0:T(8,128)(2,1)} %refs_0_.2), channel_id=1, source_target_pairs={{0,2},{2,0},{1,3},{3,1},{4,6},{6,4},{5,7},{7,5},{8,10},{10,8},{9,1... | collective-permute-start | bytes 1572872 | tf_op jit(solution)/shard_map/ppermute | solution.py:37
  7.2 4.6 %collective-permute-start.7 = (bf16[512,1024]{1,0:T(8,128)(2,1)S(1)}, bf16[512,1024]{1,0:T(8,128)(2,1)S(1)}, u32[]{:S(2)}, u32[]{:S(2)}) collective-permute-start(bf16[512,1024]{1,0:T(8,128)(2,1)S(1)} %constant_dynamic-update-slice_fusion.refs_0_), channel_id=1, source_target_pairs={{0,4},{4,8},{8,12},{1,5},{5,9},{9,13},{2,6},{6,10},{10,14},{3,7},{... | collective-permute-start | bytes 3145736 | tf_op jit(solution)/shard_map/ppermute | solution.py:26
  13.2 5.7 %mixed_grad.2.refs_0_ = f32[256,1024]{1,0:T(8,128)} custom-call(s32[2]{0:T(128)} %pad_add_fusion.2.place_ref, bf16[256,1024]{1,0:T(8,128)(2,1)} %refs_0_.2, bf16[256,1024]{1,0:T(8,128)(2,1)} %copy-done.10, bf16[4096,1024]{1,0:T(8,128)(2,1)} %w_ref.1), custom_call_target="tpu_custom_call" | custom-call | tf_op jit(solution)/shard_map/mixed_grad/pallas_call | solution.py:263
  19.8 1.3 collective-permute-start.1
  21.7 5.3 %mixed_grad.3.g_ref.refs_3_ = bf16[256,1024]{1,0:T(8,128)(2,1)} custom-call(s32[2]{0:T(128)} %pad_add_fusion.1.place_ref, f32[256,1024]{1,0:T(8,128)} %mixed_grad.2.refs_0_, bf16[256,1024]{1,0:T(8,128)(2,1)} %collective-permute-done.3.refs_1_, bf16[256,1024]{1,0:T(8,128)(2,1)} %collective-permute-done.4.refs_2_, bf16[4096,1024]{1,0:T(8,128)(2,1)} %w_ref.1), custom_call_target="tpu_custom_call" | custom-call | tf_op jit(solution)/shard_map/mixed_grad/pallas_call | solution.py:263
  27.0 8.2 %collective-permute-done.1.refs_2_ = bf16[256,1024]{1,0:T(8,128)(2,1)S(1)} collective-permute-done((bf16[256,1024]{1,0:T(8,128)(2,1)S(1)}, bf16[256,1024]{1,0:T(8,128)(2,1)S(1)}, u32[]{:S(2)}, u32[]{:S(2)}) %collective-permute-start.1) | collective-permute-done | bytes 524320 | tf_op jit(solution)/shard_map/ppermute | solution.py:26
  37.2 4.6 %collective-permute-start.8 = (bf16[512,1024]{1,0:T(8,128)(2,1)S(1)}, bf16[512,1024]{1,0:T(8,128)(2,1)S(1)}, u32[]{:S(2)}, u32[]{:S(2)}) collective-permute-start(bf16[512,1024]{1,0:T(8,128)(2,1)S(1)} %collective-permute-done.7.refs_1_), channel_id=1, source_target_pairs={{0,4},{4,8},{8,12},{1,5},{5,9},{9,13},{2,6},{6,10},{10,14},{3,7},{... | collective-permute-start | bytes 3145736 | tf_op jit(solution)/shard_map/ppermute | solution.py:26
  42.0 8.8 %collective-permute-done.5.refs_4_ = bf16[256,1024]{1,0:T(8,128)(2,1)} collective-permute-done((bf16[256,1024]{1,0:T(8,128)(2,1)}, bf16[256,1024]{1,0:T(8,128)(2,1)}, u32[]{:S(2)}, u32[]{:S(2)}) %collective-permute-start.5) | collective-permute-done | bytes 524320 | tf_op jit(solution)/shard_map/ppermute | solution.py:26
  53.9 10.7 %collective-permute-done.6.refs_5_ = bf16[256,1024]{1,0:T(8,128)(2,1)} collective-permute-done((bf16[256,1024]{1,0:T(8,128)(2,1)}, bf16[256,1024]{1,0:T(8,128)(2,1)}, u32[]{:S(2)}, u32[]{:S(2)}) %collective-permute-start.6) | collective-permute-done | bytes 524320 | tf_op jit(solution)/shard_map/ppermute | solution.py:26
  64.6 3.0 %attention_forward.1 = (bf16[256,1024]{1,0:T(8,128)(2,1)S(1)}, f32[8,256]{1,0:T(8,128)S(1)}) custom-call(s32[10]{0:T(128)S(1)} %reshape.264.use_ref, bf16[256,1024]{1,0:T(8,128)(2,1)S(1)} %copy-done.5, bf16[512,1024]{1,0:T(8,128)(2,1)S(1)} %constant_dynamic-update-slice_fusion.refs_0_, bf16[512,1024]{1,0:T(8,128)(2,1)S(1)} %collective-permute-done.7.refs_1_, ...), custom_call_target="tpu_custom_call" | custom-call | flops 53687091200 | bytes 419430400 | tf_op jit(solution)/shard_map/attention_forward/pallas_call | solution.py:263
  67.6 3.5 %collective-permute-start.12 = (bf16[256,1024]{1,0:T(8,128)(2,1)S(1)}, bf16[256,1024]{1,0:T(8,128)(2,1)S(1)}, u32[]{:S(2)}, u32[]{:S(2)}) collective-permute-start(bf16[256,1024]{1,0:T(8,128)(2,1)S(1)} %get-tuple-element.36.m_ref.refs_1_), channel_id=1, source_target_pairs={{0,12},{4,0},{8,4},{12,8},{1,13},{5,1},{9,5},{13,9},{2,14},{6,2},{... | collective-permute-start | bytes 1572872 | tf_op jit(solution)/shard_map/ppermute | solution.py:33
  71.1 1.4 %collective-permute-start.10 = (bf16[256,1024]{1,0:T(8,128)(2,1)S(1)}, bf16[256,1024]{1,0:T(8,128)(2,1)}, u32[]{:S(2)}, u32[]{:S(2)}) collective-permute-start(bf16[256,1024]{1,0:T(8,128)(2,1)S(1)} %select_select_fusion), channel_id=1, source_target_pairs={{0,0},{1,9},{2,6},{3,15},{4,4},{5,13},{6,10},{7,3},{8,8},{9,1},{10... | collective-permute-start | bytes 1572872 | tf_op jit(solution)/shard_map/ppermute | solution.py:418
  72.6 6.9 %attended_partial.1 = (bf16[2,256,1024]{2,1,0:T(8,128)(2,1)}, bf16[2,256,1024]{2,1,0:T(8,128)(2,1)}) custom-call(s32[4]{0:T(128)} %pad_add_fusion.place_ref, bf16[256,1024]{1,0:T(8,128)(2,1)} %copy-done, bf16[4096,1024]{1,0:T(8,128)(2,1)} %w_ref.1), custom_call_target="tpu_custom_call" | custom-call | tf_op jit(solution)/shard_map/attended_partial/pallas_call | solution.py:263
  79.6 6.6 %attention_query_grad.1 = (bf16[256,1024]{1,0:T(8,128)(2,1)}, f32[24,256]{1,0:T(8,128)S(1)}) custom-call(s32[10]{0:T(128)S(1)} %reshape.264.use_ref, bf16[256,1024]{1,0:T(8,128)(2,1)S(1)} %copy-done.5, bf16[256,1024]{1,0:T(8,128)(2,1)S(1)} %copy-done.2, f32[8,256]{1,0:T(8,128)S(1)} %get-tuple-element.34.lse_ref, ...), custom_call_target="tpu_custom_call" | custom-call | flops 80530636800 | bytes 471859200 | tf_op jit(solution)/shard_map/attention_query_grad/pallas_call | solution.py:263
  87.6 1.5 %collective-permute-start.13 = (f32[24,256]{1,0:T(8,128)S(1)}, f32[24,256]{1,0:T(8,128)S(1)}, u32[]{:S(2)}, u32[]{:S(2)}) collective-permute-start(f32[24,256]{1,0:T(8,128)S(1)} %get-tuple-element.35.refs_6_), channel_id=1, source_target_pairs={{4,0},{8,4},{12,8},{5,1},{9,5},{13,9},{6,2},{10,6},{14,10},{7,3},{... | collective-permute-start | bytes 73736 | tf_op jit(solution)/shard_map/ppermute | solution.py:26
  89.3 11.9 %collective-permute-done.14.refs_8_ = f32[24,256]{1,0:T(8,128)S(1)} collective-permute-done((f32[24,256]{1,0:T(8,128)S(1)}, f32[24,256]{1,0:T(8,128)S(1)}, u32[]{:S(2)}, u32[]{:S(2)}) %collective-permute-start.14) | collective-permute-done | bytes 24608 | tf_op jit(solution)/shard_map/ppermute | solution.py:26
  101.3 3.1 %collective-permute-start.17 = (bf16[256,1024]{1,0:T(8,128)(2,1)}, bf16[256,1024]{1,0:T(8,128)(2,1)S(1)}, u32[]{:S(2)}, u32[]{:S(2)}) collective-permute-start(bf16[256,1024]{1,0:T(8,128)(2,1)} %collective-permute-done.10), channel_id=1, source_target_pairs={{0,2},{2,0},{1,3},{3,1},{4,6},{6,4},{5,7},{7,5},{8,10},{10,8},{9,1... | collective-permute-start | bytes 1572872 | tf_op jit(solution)/shard_map/ppermute | solution.py:37
  105.6 6.0 %attention_key_grad.1 = (bf16[256,1024]{1,0:T(8,128)(2,1)}, bf16[256,1024]{1,0:T(8,128)(2,1)}) custom-call(bf16[256,1024]{1,0:T(8,128)(2,1)S(1)} %copy-done.3, bf16[256,1024]{1,0:T(8,128)(2,1)S(1)} %copy-done.4, bf16[256,1024]{1,0:T(8,128)(2,1)S(1)} %copy-done.5, bf16[256,1024]{1,0:T(8,128)(2,1)S(1)} %copy-done.7, bf16[256,1024]{1,0:T(8,128)(2,1)S(1)} %copy-done.9, ...), custom_call_target="tpu_custom_call" | custom-call | flops 107374182400 | bytes 524288000 | tf_op jit(solution)/shard_map/attention_key_grad/pallas_call | solution.py:263
  111.6 5.8 %collective-permute-done.17 = bf16[256,1024]{1,0:T(8,128)(2,1)S(1)} collective-permute-done((bf16[256,1024]{1,0:T(8,128)(2,1)}, bf16[256,1024]{1,0:T(8,128)(2,1)S(1)}, u32[]{:S(2)}, u32[]{:S(2)}) %collective-permute-start.17) | collective-permute-done | bytes 524320 | tf_op jit(solution)/shard_map/ppermute | solution.py:37
  117.6 10.7 %collective-permute-done.15 = bf16[256,1024]{1,0:T(8,128)(2,1)S(1)} collective-permute-done((bf16[256,1024]{1,0:T(8,128)(2,1)S(1)}, bf16[256,1024]{1,0:T(8,128)(2,1)S(1)}, u32[]{:S(2)}, u32[]{:S(2)}) %collective-permute-start.15) | collective-permute-done | bytes 524320 | tf_op jit(solution)/shard_map/ppermute | solution.py:37
  129.4 1.5 %collective-permute-done.19.refs_2_ = bf16[256,1024]{1,0:T(8,128)(2,1)S(1)} collective-permute-done((bf16[256,1024]{1,0:T(8,128)(2,1)S(1)}, bf16[256,1024]{1,0:T(8,128)(2,1)S(1)}, u32[]{:S(2)}, u32[]{:S(2)}) %collective-permute-start.19) | collective-permute-done | bytes 524320 | tf_op jit(solution)/shard_map/ppermute | solution.py:33
  130.9 1.3 pad_maximum_fusion.refs_0_.refs_1_
  132.2 2.4 %weight_grad.2.refs_0_ = f32[1024,1024]{1,0:T(8,128)S(1)} custom-call(s32[4]{0:T(128)S(1)} %select_reduce_fusion.place_ref, bf16[4,256,1024]{2,1,0:T(8,128)(2,1)S(1)} %pad_maximum_fusion.refs_0_.refs_1_, bf16[256,1024]{1,0:T(8,128)(2,1)S(1)} %copy-done.1, bf16[256,1024]{1,0:T(8,128)(2,1)S(1)} %collective-permute-done.11.refs_2_, ...), custom_call_target="tpu_custom_call" | custom-call | tf_op jit(solution)/shard_map/weight_grad/pallas_call | solution.py:263
  134.6 2.6 %weight_grad.3 = bf16[1024,1024]{1,0:T(8,128)(2,1)} custom-call(s32[4]{0:T(128)S(1)} %select_reduce_fusion.place_ref, f32[1024,1024]{1,0:T(8,128)S(1)} %weight_grad.2.refs_0_, bf16[4,256,1024]{2,1,0:T(8,128)(2,1)S(1)} %pad_maximum_fusion.refs_0_.refs_1_, bf16[256,1024]{1,0:T(8,128)(2,1)S(1)} %collective-permute-done.19.refs_2_), custom_call_target="tpu_custom_call" | custom-call | tf_op jit(solution)/shard_map/weight_grad/pallas_call | solution.py:263
  (65 shorter events, 16.2 us)
Async XLA Ops:
  0.6 11.8 %collective-permute-start.2 = (bf16[256,1024]{1,0:T(8,128)(2,1)}, bf16[256,1024]{1,0:T(8,128)(2,1)S(1)}, u32[]{:S(2)}, u32[]{:S(2)}) collective-permute-start(bf16[256,1024]{1,0:T(8,128)(2,1)} %refs_0_.2), channel_id=1, source_target_pairs={{0,1},{1,0},{2,3},{3,2},{4,5},{5,4},{6,7},{7,6},{8,9},{9,8},{10,11... | collective-permute-start | bytes 1572872 | tf_op jit(solution)/shard_map/ppermute | solution.py:37
  1.1 17.7 %collective-permute-start.3 = (bf16[256,1024]{1,0:T(8,128)(2,1)}, bf16[256,1024]{1,0:T(8,128)(2,1)}, u32[]{:S(2)}, u32[]{:S(2)}) collective-permute-start(bf16[256,1024]{1,0:T(8,128)(2,1)} %refs_0_.2), channel_id=1, source_target_pairs={{0,2},{2,0},{1,3},{3,1},{4,6},{6,4},{5,7},{7,5},{8,10},{10,8},{9,1... | collective-permute-start | bytes 1572872 | tf_op jit(solution)/shard_map/ppermute | solution.py:37
  3.7 16.1 %collective-permute-start = (bf16[256,1024]{1,0:T(8,128)(2,1)}, bf16[256,1024]{1,0:T(8,128)(2,1)S(1)}, u32[]{:S(2)}, u32[]{:S(2)}) collective-permute-start(bf16[256,1024]{1,0:T(8,128)(2,1)} %refs_0_.3), channel_id=1, source_target_pairs={{4,0},{8,4},{12,8},{5,1},{9,5},{13,9},{6,2},{10,6},{14,10},{7,3},{... | collective-permute-start | bytes 1572872 | tf_op jit(solution)/shard_map/ppermute | solution.py:26
  7.2 30.1 %collective-permute-start.7 = (bf16[512,1024]{1,0:T(8,128)(2,1)S(1)}, bf16[512,1024]{1,0:T(8,128)(2,1)S(1)}, u32[]{:S(2)}, u32[]{:S(2)}) collective-permute-start(bf16[512,1024]{1,0:T(8,128)(2,1)S(1)} %constant_dynamic-update-slice_fusion.refs_0_), channel_id=1, source_target_pairs={{0,4},{4,8},{8,12},{1,5},{5,9},{9,13},{2,6},{6,10},{10,14},{3,7},{... | collective-permute-start | bytes 3145736 | tf_op jit(solution)/shard_map/ppermute | solution.py:26
  18.9 2.8 %collective-permute-start.4 = (bf16[256,1024]{1,0:T(8,128)(2,1)}, bf16[256,1024]{1,0:T(8,128)(2,1)}, u32[]{:S(2)}, u32[]{:S(2)}) collective-permute-start(bf16[256,1024]{1,0:T(8,128)(2,1)} %collective-permute-done.3.refs_1_), channel_id=1, source_target_pairs={{0,1},{1,0},{2,3},{3,2},{4,5},{5,4},{6,7},{7,6},{8,9},{9,8},{10,11... | collective-permute-start | bytes 1572872 | tf_op jit(solution)/shard_map/ppermute | solution.py:37
  19.8 15.4 %collective-permute-start.1 = (bf16[256,1024]{1,0:T(8,128)(2,1)S(1)}, bf16[256,1024]{1,0:T(8,128)(2,1)S(1)}, u32[]{:S(2)}, u32[]{:S(2)}) collective-permute-start(bf16[256,1024]{1,0:T(8,128)(2,1)S(1)} %collective-permute-done.refs_1_), channel_id=1, source_target_pairs={{4,0},{8,4},{12,8},{5,1},{9,5},{13,9},{6,2},{10,6},{14,10},{7,3},{... | collective-permute-start | bytes 1572872 | tf_op jit(solution)/shard_map/ppermute | solution.py:26
  21.7 30.3 %copy-start.12 = (s32[2,5]{1,0:T(2,128)S(1)}, s32[2,5]{1,0:T(2,128)}, u32[]{:S(2)}) copy-start(s32[2,5]{1,0:T(2,128)} %param.10) | copy-start | bytes 124
  36.0 14.8 %collective-permute-start.5 = (bf16[256,1024]{1,0:T(8,128)(2,1)}, bf16[256,1024]{1,0:T(8,128)(2,1)}, u32[]{:S(2)}, u32[]{:S(2)}) collective-permute-start(bf16[256,1024]{1,0:T(8,128)(2,1)} %mixed_grad.3.g_ref.refs_3_), channel_id=1, source_target_pairs={{4,0},{8,4},{12,8},{5,1},{9,5},{13,9},{6,2},{10,6},{14,10},{7,3},{... | collective-permute-start | bytes 1572872 | tf_op jit(solution)/shard_map/ppermute | solution.py:26
  37.2 27.3 %collective-permute-start.8 = (bf16[512,1024]{1,0:T(8,128)(2,1)S(1)}, bf16[512,1024]{1,0:T(8,128)(2,1)S(1)}, u32[]{:S(2)}, u32[]{:S(2)}) collective-permute-start(bf16[512,1024]{1,0:T(8,128)(2,1)S(1)} %collective-permute-done.7.refs_1_), channel_id=1, source_target_pairs={{0,4},{4,8},{8,12},{1,5},{5,9},{9,13},{2,6},{6,10},{10,14},{3,7},{... | collective-permute-start | bytes 3145736 | tf_op jit(solution)/shard_map/ppermute | solution.py:26
  50.7 13.9 %collective-permute-start.6 = (bf16[256,1024]{1,0:T(8,128)(2,1)}, bf16[256,1024]{1,0:T(8,128)(2,1)}, u32[]{:S(2)}, u32[]{:S(2)}) collective-permute-start(bf16[256,1024]{1,0:T(8,128)(2,1)} %collective-permute-done.5.refs_4_), channel_id=1, source_target_pairs={{4,0},{8,4},{12,8},{5,1},{9,5},{13,9},{6,2},{10,6},{14,10},{7,3},{... | collective-permute-start | bytes 1572872 | tf_op jit(solution)/shard_map/ppermute | solution.py:26
  67.6 33.6 %collective-permute-start.12 = (bf16[256,1024]{1,0:T(8,128)(2,1)S(1)}, bf16[256,1024]{1,0:T(8,128)(2,1)S(1)}, u32[]{:S(2)}, u32[]{:S(2)}) collective-permute-start(bf16[256,1024]{1,0:T(8,128)(2,1)S(1)} %get-tuple-element.36.m_ref.refs_1_), channel_id=1, source_target_pairs={{0,12},{4,0},{8,4},{12,8},{1,13},{5,1},{9,5},{13,9},{2,14},{6,2},{... | collective-permute-start | bytes 1572872 | tf_op jit(solution)/shard_map/ppermute | solution.py:33
  71.1 30.1 %collective-permute-start.11 = (bf16[256,1024]{1,0:T(8,128)(2,1)S(1)}, bf16[256,1024]{1,0:T(8,128)(2,1)S(1)}, u32[]{:S(2)}, u32[]{:S(2)}) collective-permute-start(bf16[256,1024]{1,0:T(8,128)(2,1)S(1)} %get-tuple-element.36.m_ref.refs_1_), channel_id=1, source_target_pairs={{0,4},{4,8},{8,12},{12,0},{1,5},{5,9},{9,13},{13,1},{2,6},{6,10},{... | collective-permute-start | bytes 1572872 | tf_op jit(solution)/shard_map/ppermute | solution.py:33
  71.1 30.1 %collective-permute-start.10 = (bf16[256,1024]{1,0:T(8,128)(2,1)S(1)}, bf16[256,1024]{1,0:T(8,128)(2,1)}, u32[]{:S(2)}, u32[]{:S(2)}) collective-permute-start(bf16[256,1024]{1,0:T(8,128)(2,1)S(1)} %select_select_fusion), channel_id=1, source_target_pairs={{0,0},{1,9},{2,6},{3,15},{4,4},{5,13},{6,10},{7,3},{8,8},{9,1},{10... | collective-permute-start | bytes 1572872 | tf_op jit(solution)/shard_map/ppermute | solution.py:418
  79.5 8.1 %collective-permute-start.9 = (bf16[2,256,1024]{2,1,0:T(8,128)(2,1)}, bf16[2,256,1024]{2,1,0:T(8,128)(2,1)S(1)}, u32[]{:S(2)}, u32[]{:S(2)}) collective-permute-start(bf16[2,256,1024]{2,1,0:T(8,128)(2,1)} %get-tuple-element.31), channel_id=1, source_target_pairs={{0,1},{1,0},{2,3},{3,2},{4,5},{5,4},{6,7},{7,6},{8,9},{9,8},{10,11... | collective-permute-start | bytes 3145736 | tf_op jit(solution)/shard_map/ppermute | solution.py:37
  79.6 26.1 %copy-start.3 = (bf16[256,1024]{1,0:T(8,128)(2,1)S(1)}, bf16[256,1024]{1,0:T(8,128)(2,1)}, u32[]{:S(2)}) copy-start(bf16[256,1024]{1,0:T(8,128)(2,1)} %k_ref) | copy-start | bytes 1572868
  79.6 26.0 %copy-start.4 = (bf16[256,1024]{1,0:T(8,128)(2,1)S(1)}, bf16[256,1024]{1,0:T(8,128)(2,1)}, u32[]{:S(2)}) copy-start(bf16[256,1024]{1,0:T(8,128)(2,1)} %v_ref.1) | copy-start | bytes 1572868
  79.6 26.0 %copy-start.7 = (bf16[256,1024]{1,0:T(8,128)(2,1)S(1)}, bf16[256,1024]{1,0:T(8,128)(2,1)}, u32[]{:S(2)}) copy-start(bf16[256,1024]{1,0:T(8,128)(2,1)} %copy-done.6) | copy-start | bytes 1572868
  86.3 15.0 %collective-permute-start.14 = (f32[24,256]{1,0:T(8,128)S(1)}, f32[24,256]{1,0:T(8,128)S(1)}, u32[]{:S(2)}, u32[]{:S(2)}) collective-permute-start(f32[24,256]{1,0:T(8,128)S(1)} %get-tuple-element.35.refs_6_), channel_id=1, source_target_pairs={{8,0},{12,4},{9,1},{13,5},{10,2},{14,6},{11,3},{15,7},{24,16},{28,... | collective-permute-start | bytes 73736 | tf_op jit(solution)/shard_map/ppermute | solution.py:26
  87.6 13.7 %collective-permute-start.13 = (f32[24,256]{1,0:T(8,128)S(1)}, f32[24,256]{1,0:T(8,128)S(1)}, u32[]{:S(2)}, u32[]{:S(2)}) collective-permute-start(f32[24,256]{1,0:T(8,128)S(1)} %get-tuple-element.35.refs_6_), channel_id=1, source_target_pairs={{4,0},{8,4},{12,8},{5,1},{9,5},{13,9},{6,2},{10,6},{14,10},{7,3},{... | collective-permute-start | bytes 73736 | tf_op jit(solution)/shard_map/ppermute | solution.py:26
  101.3 16.1 %collective-permute-start.17 = (bf16[256,1024]{1,0:T(8,128)(2,1)}, bf16[256,1024]{1,0:T(8,128)(2,1)S(1)}, u32[]{:S(2)}, u32[]{:S(2)}) collective-permute-start(bf16[256,1024]{1,0:T(8,128)(2,1)} %collective-permute-done.10), channel_id=1, source_target_pairs={{0,2},{2,0},{1,3},{3,1},{4,6},{6,4},{5,7},{7,5},{8,10},{10,8},{9,1... | collective-permute-start | bytes 1572872 | tf_op jit(solution)/shard_map/ppermute | solution.py:37
  104.4 26.5 %collective-permute-start.16 = (bf16[256,1024]{1,0:T(8,128)(2,1)}, bf16[256,1024]{1,0:T(8,128)(2,1)S(1)}, u32[]{:S(2)}, u32[]{:S(2)}) collective-permute-start(bf16[256,1024]{1,0:T(8,128)(2,1)} %collective-permute-done.10), channel_id=1, source_target_pairs={{0,1},{1,0},{2,3},{3,2},{4,5},{5,4},{6,7},{7,6},{8,9},{9,8},{10,11... | collective-permute-start | bytes 1572872 | tf_op jit(solution)/shard_map/ppermute | solution.py:37
  104.4 26.5 %collective-permute-start.19 = (bf16[256,1024]{1,0:T(8,128)(2,1)S(1)}, bf16[256,1024]{1,0:T(8,128)(2,1)S(1)}, u32[]{:S(2)}, u32[]{:S(2)}) collective-permute-start(bf16[256,1024]{1,0:T(8,128)(2,1)S(1)} %copy-done.1), channel_id=1, source_target_pairs={{0,8},{4,12},{8,0},{12,4},{1,9},{5,13},{9,1},{13,5},{2,10},{6,14},... | collective-permute-start | bytes 1572872 | tf_op jit(solution)/shard_map/ppermute | solution.py:33
  105.5 22.8 %collective-permute-start.15 = (bf16[256,1024]{1,0:T(8,128)(2,1)S(1)}, bf16[256,1024]{1,0:T(8,128)(2,1)S(1)}, u32[]{:S(2)}, u32[]{:S(2)}) collective-permute-start(bf16[256,1024]{1,0:T(8,128)(2,1)S(1)} %fusion), channel_id=1, source_target_pairs={{0,2},{2,0},{1,3},{3,1},{4,6},{6,4},{5,7},{7,5},{8,10},{10,8},{9,1... | collective-permute-start | bytes 1572872 | tf_op jit(solution)/shard_map/ppermute | solution.py:37
  117.4 13.5 %collective-permute-start.18 = (bf16[256,1024]{1,0:T(8,128)(2,1)S(1)}, bf16[256,1024]{1,0:T(8,128)(2,1)S(1)}, u32[]{:S(2)}, u32[]{:S(2)}) collective-permute-start(bf16[256,1024]{1,0:T(8,128)(2,1)S(1)} %collective-permute-done.17), channel_id=1, source_target_pairs={{0,1},{1,0},{2,3},{3,2},{4,5},{5,4},{6,7},{7,6},{8,9},{9,8},{10,11... | collective-permute-start | bytes 1572872 | tf_op jit(solution)/shard_map/ppermute | solution.py:37
  (9 other events, 98.5 us)

commit v8 on v7

--- a/solution.py
+++ b/solution.py
@@ -400,9 +400,9 @@
     group_count = len(c_blocks)
     while len(kv_all) < count:
         kv_all = further(kv_all, 1, mixed_grad)
-    grad_all = further([mixed_grad], -1, query_all[-1])
+    grad_all = further([mixed_grad], -1)
     while len(grad_all) < count:
-        grad_all = further(grad_all, -1)
+        grad_all = further(grad_all, -1, query_all[-1])
 
     h, r = lax.axis_index("head"), lax.axis_index("rep")
     n_head, n_rep = lax.axis_size("head"), lax.axis_size("rep")

time: 138 us -> 139 us (level)
  waiting for transfers between devices: 58.4 us -> 62.5 us
  starting transfers between devices: 29.7 us -> 27.8 us
  local copies, waits for them, and re-layouts: 3.88 us -> 2.3 us
    ppermute x8, waiting for transfers between devices: 40.4 us -> 45 us  [shift(): lax.ppermute(value, 'seq', [(i, i + by) for i in range(peers) if 0 <= i +...]
    unnamed x27 -> x21, local copies, waits for them, and re-layouts: 2.72 us -> 1.13 us
    ppermute x3, starting transfers between devices: 4.57 us -> 3.14 us  [cyclic(): lax.ppermute(value, 'seq', [(i, (i + by) % peers) for i in range(peers)])]
where the time goes in v8:
time: 139 us; the launch traced here: 138 us
  waiting for transfers between devices  62.5 us (45%)
  Pallas kernels  38.7 us (28%)
  starting transfers between devices  27.8 us (20%)
  other arithmetic  5.76 us (4%)
  local copies, waits for them, and re-layouts  2.3 us (2%)
    ppermute x8, waiting for transfers between devices, shift(): lax.ppermute(value, 'seq', [(i, i + by) for i in range(peers) if 0 <= i +...  45 us
    pallas_call x8, Pallas kernels, kernel_call(): pl.pallas_call(body, in_specs=[smem] * len(scalars) + [vmem] * len(arrays...  38.7 us
    ppermute x8, starting transfers between devices, shift(): lax.ppermute(value, 'seq', [(i, i + by) for i in range(peers) if 0 <= i +...  16.7 us
    ppermute x8, waiting for transfers between devices, swap(): return lax.ppermute(value, axis, [(0, 1), (1, 0)])  16.3 us
    ppermute x8, starting transfers between devices, swap(): return lax.ppermute(value, axis, [(0, 1), (1, 0)])  6.51 us
    ppermute x3, starting transfers between devices, cyclic(): lax.ppermute(value, 'seq', [(i, (i + by) % peers) for i in range(peers)])  3.14 us
  transfers between devices with their start and end apart: 20, of which 8 were waited for; matrix products, arithmetic and copies ran while one was open for 5% of the time, Pallas kernels for 22%

profile of v8, /device:TPU:0, one launch (start us, length us, event | category | flops | bytes accessed | tf_op | source)
XLA Modules:
  0.0 138.1 jit_solution(16621073156048224443)
XLA Ops:
  1.2 2.6 %collective-permute-start.3 = (bf16[256,1024]{1,0:T(8,128)(2,1)}, bf16[256,1024]{1,0:T(8,128)(2,1)S(1)}, u32[]{:S(2)}, u32[]{:S(2)}) collective-permute-start(bf16[256,1024]{1,0:T(8,128)(2,1)} %refs_0_.2), channel_id=1, source_target_pairs={{0,2},{2,0},{1,3},{3,1},{4,6},{6,4},{5,7},{7,5},{8,10},{10,8},{9,1... | collective-permute-start | bytes 1572872 | tf_op jit(solution)/shard_map/ppermute | solution.py:37
  5.9 3.5 %collective-permute-start.7 = (bf16[512,1024]{1,0:T(8,128)(2,1)S(1)}, bf16[512,1024]{1,0:T(8,128)(2,1)S(1)}, u32[]{:S(2)}, u32[]{:S(2)}) collective-permute-start(bf16[512,1024]{1,0:T(8,128)(2,1)S(1)} %constant_dynamic-update-slice_fusion.refs_0_), channel_id=1, source_target_pairs={{0,4},{4,8},{8,12},{1,5},{5,9},{9,13},{2,6},{6,10},{10,14},{3,7},{... | collective-permute-start | bytes 3145736 | tf_op jit(solution)/shard_map/ppermute | solution.py:26
  11.4 5.7 %mixed_grad.2.refs_0_ = f32[256,1024]{1,0:T(8,128)} custom-call(s32[2]{0:T(128)} %pad_add_fusion.2.place_ref, bf16[256,1024]{1,0:T(8,128)(2,1)} %refs_0_.2, bf16[256,1024]{1,0:T(8,128)(2,1)} %collective-permute-done.2.refs_1_, bf16[4096,1024]{1,0:T(8,128)(2,1)} %w_ref.1), custom_call_target="tpu_custom_call" | custom-call | tf_op jit(solution)/shard_map/mixed_grad/pallas_call | solution.py:263
  17.7 7.4 %collective-permute-done.refs_1_ = bf16[256,1024]{1,0:T(8,128)(2,1)} collective-permute-done((bf16[256,1024]{1,0:T(8,128)(2,1)S(1)}, bf16[256,1024]{1,0:T(8,128)(2,1)}, u32[]{:S(2)}, u32[]{:S(2)}) %collective-permute-start) | collective-permute-done | bytes 524320 | tf_op jit(solution)/shard_map/ppermute | solution.py:26
  26.5 5.3 %mixed_grad.3.g_ref.refs_3_ = bf16[256,1024]{1,0:T(8,128)(2,1)} custom-call(s32[2]{0:T(128)} %pad_add_fusion.1.place_ref, f32[256,1024]{1,0:T(8,128)} %mixed_grad.2.refs_0_, bf16[256,1024]{1,0:T(8,128)(2,1)} %copy-done.7, bf16[256,1024]{1,0:T(8,128)(2,1)} %collective-permute-done.4.refs_2_, bf16[4096,1024]{1,0:T(8,128)(2,1)} %w_ref.1), custom_call_target="tpu_custom_call" | custom-call | tf_op jit(solution)/shard_map/mixed_grad/pallas_call | solution.py:263
  31.8 1.3 collective-permute-start.5
  33.1 5.2 %collective-permute-start.8 = (bf16[512,1024]{1,0:T(8,128)(2,1)S(1)}, bf16[512,1024]{1,0:T(8,128)(2,1)S(1)}, u32[]{:S(2)}, u32[]{:S(2)}) collective-permute-start(bf16[512,1024]{1,0:T(8,128)(2,1)S(1)} %collective-permute-done.7.refs_1_), channel_id=1, source_target_pairs={{0,4},{4,8},{8,12},{1,5},{5,9},{9,13},{2,6},{6,10},{10,14},{3,7},{... | collective-permute-start | bytes 3145736 | tf_op jit(solution)/shard_map/ppermute | solution.py:26
  38.4 3.8 %collective-permute-done.1.refs_2_ = bf16[256,1024]{1,0:T(8,128)(2,1)} collective-permute-done((bf16[256,1024]{1,0:T(8,128)(2,1)}, bf16[256,1024]{1,0:T(8,128)(2,1)}, u32[]{:S(2)}, u32[]{:S(2)}) %collective-permute-start.1) | collective-permute-done | bytes 524320 | tf_op jit(solution)/shard_map/ppermute | solution.py:26
  42.2 9.2 %collective-permute-done.5.refs_4_ = bf16[256,1024]{1,0:T(8,128)(2,1)} collective-permute-done((bf16[256,1024]{1,0:T(8,128)(2,1)}, bf16[256,1024]{1,0:T(8,128)(2,1)}, u32[]{:S(2)}, u32[]{:S(2)}) %collective-permute-start.5) | collective-permute-done | bytes 524320 | tf_op jit(solution)/shard_map/ppermute | solution.py:26
  54.6 10.9 %collective-permute-done.6.refs_5_ = bf16[256,1024]{1,0:T(8,128)(2,1)} collective-permute-done((bf16[256,1024]{1,0:T(8,128)(2,1)}, bf16[256,1024]{1,0:T(8,128)(2,1)}, u32[]{:S(2)}, u32[]{:S(2)}) %collective-permute-start.6) | collective-permute-done | bytes 524320 | tf_op jit(solution)/shard_map/ppermute | solution.py:26
  65.6 3.0 %attention_forward.1 = (bf16[256,1024]{1,0:T(8,128)(2,1)S(1)}, f32[8,256]{1,0:T(8,128)S(1)}) custom-call(s32[10]{0:T(128)S(1)} %reshape.264.use_ref, bf16[256,1024]{1,0:T(8,128)(2,1)S(1)} %copy-done.6, bf16[512,1024]{1,0:T(8,128)(2,1)S(1)} %constant_dynamic-update-slice_fusion.refs_0_, bf16[512,1024]{1,0:T(8,128)(2,1)S(1)} %collective-permute-done.7.refs_1_, ...), custom_call_target="tpu_custom_call" | custom-call | flops 53687091200 | bytes 419430400 | tf_op jit(solution)/shard_map/attention_forward/pallas_call | solution.py:263
  68.6 1.6 %collective-permute-start.12 = (bf16[256,1024]{1,0:T(8,128)(2,1)S(1)}, bf16[256,1024]{1,0:T(8,128)(2,1)S(1)}, u32[]{:S(2)}, u32[]{:S(2)}) collective-permute-start(bf16[256,1024]{1,0:T(8,128)(2,1)S(1)} %get-tuple-element.36.m_ref.refs_1_), channel_id=1, source_target_pairs={{0,12},{4,0},{8,4},{12,8},{1,13},{5,1},{9,5},{13,9},{2,14},{6,2},{... | collective-permute-start | bytes 1572872 | tf_op jit(solution)/shard_map/ppermute | solution.py:33
  70.7 1.4 %collective-permute-start.10 = (bf16[256,1024]{1,0:T(8,128)(2,1)S(1)}, bf16[256,1024]{1,0:T(8,128)(2,1)}, u32[]{:S(2)}, u32[]{:S(2)}) collective-permute-start(bf16[256,1024]{1,0:T(8,128)(2,1)S(1)} %select_select_fusion), channel_id=1, source_target_pairs={{0,0},{1,9},{2,6},{3,15},{4,4},{5,13},{6,10},{7,3},{8,8},{9,1},{10... | collective-permute-start | bytes 1572872 | tf_op jit(solution)/shard_map/ppermute | solution.py:418
  72.1 6.9 %attended_partial.1 = (bf16[2,256,1024]{2,1,0:T(8,128)(2,1)}, bf16[2,256,1024]{2,1,0:T(8,128)(2,1)}) custom-call(s32[4]{0:T(128)} %pad_add_fusion.place_ref, bf16[256,1024]{1,0:T(8,128)(2,1)} %copy-done, bf16[4096,1024]{1,0:T(8,128)(2,1)} %w_ref.1), custom_call_target="tpu_custom_call" | custom-call | tf_op jit(solution)/shard_map/attended_partial/pallas_call | solution.py:263
  79.1 6.6 %attention_query_grad.1 = (bf16[256,1024]{1,0:T(8,128)(2,1)}, f32[24,256]{1,0:T(8,128)S(1)}) custom-call(s32[10]{0:T(128)S(1)} %reshape.264.use_ref, bf16[256,1024]{1,0:T(8,128)(2,1)S(1)} %copy-done.6, bf16[256,1024]{1,0:T(8,128)(2,1)S(1)} %copy-done.2, f32[8,256]{1,0:T(8,128)S(1)} %get-tuple-element.34.lse_ref, ...), custom_call_target="tpu_custom_call" | custom-call | flops 80530636800 | bytes 471859200 | tf_op jit(solution)/shard_map/attention_query_grad/pallas_call | solution.py:263
  87.1 1.5 %collective-permute-start.13 = (f32[24,256]{1,0:T(8,128)S(1)}, f32[24,256]{1,0:T(8,128)S(1)}, u32[]{:S(2)}, u32[]{:S(2)}) collective-permute-start(f32[24,256]{1,0:T(8,128)S(1)} %get-tuple-element.35.refs_6_), channel_id=1, source_target_pairs={{4,0},{8,4},{12,8},{5,1},{9,5},{13,9},{6,2},{10,6},{14,10},{7,3},{... | collective-permute-start | bytes 73736 | tf_op jit(solution)/shard_map/ppermute | solution.py:26
  88.8 13.6 %collective-permute-done.14.refs_8_ = f32[24,256]{1,0:T(8,128)S(1)} collective-permute-done((f32[24,256]{1,0:T(8,128)S(1)}, f32[24,256]{1,0:T(8,128)S(1)}, u32[]{:S(2)}, u32[]{:S(2)}) %collective-permute-start.14) | collective-permute-done | bytes 24608 | tf_op jit(solution)/shard_map/ppermute | solution.py:26
  102.4 2.9 %collective-permute-start.17 = (bf16[256,1024]{1,0:T(8,128)(2,1)}, bf16[256,1024]{1,0:T(8,128)(2,1)S(1)}, u32[]{:S(2)}, u32[]{:S(2)}) collective-permute-start(bf16[256,1024]{1,0:T(8,128)(2,1)} %collective-permute-done.10), channel_id=1, source_target_pairs={{0,2},{2,0},{1,3},{3,1},{4,6},{6,4},{5,7},{7,5},{8,10},{10,8},{9,1... | collective-permute-start | bytes 1572872 | tf_op jit(solution)/shard_map/ppermute | solution.py:37
  106.5 6.3 %attention_key_grad.1 = (bf16[256,1024]{1,0:T(8,128)(2,1)}, bf16[256,1024]{1,0:T(8,128)(2,1)}) custom-call(bf16[256,1024]{1,0:T(8,128)(2,1)S(1)} %copy-done.3, bf16[256,1024]{1,0:T(8,128)(2,1)S(1)} %copy-done.4, bf16[256,1024]{1,0:T(8,128)(2,1)S(1)} %copy-done.6, bf16[256,1024]{1,0:T(8,128)(2,1)} %collective-permute-done.refs_1_, ...), custom_call_target="tpu_custom_call" | custom-call | flops 107374182400 | bytes 524288000 | tf_op jit(solution)/shard_map/attention_key_grad/pallas_call | solution.py:263
  112.8 5.4 %collective-permute-done.17 = bf16[256,1024]{1,0:T(8,128)(2,1)S(1)} collective-permute-done((bf16[256,1024]{1,0:T(8,128)(2,1)}, bf16[256,1024]{1,0:T(8,128)(2,1)S(1)}, u32[]{:S(2)}, u32[]{:S(2)}) %collective-permute-start.17) | collective-permute-done | bytes 524320 | tf_op jit(solution)/shard_map/ppermute | solution.py:37
  118.6 10.8 %collective-permute-done.15 = bf16[256,1024]{1,0:T(8,128)(2,1)S(1)} collective-permute-done((bf16[256,1024]{1,0:T(8,128)(2,1)S(1)}, bf16[256,1024]{1,0:T(8,128)(2,1)S(1)}, u32[]{:S(2)}, u32[]{:S(2)}) %collective-permute-start.15) | collective-permute-done | bytes 524320 | tf_op jit(solution)/shard_map/ppermute | solution.py:37
  131.8 1.3 pad_maximum_fusion.refs_0_.refs_1_
  133.1 2.4 %weight_grad.2.refs_0_ = f32[1024,1024]{1,0:T(8,128)S(1)} custom-call(s32[4]{0:T(128)S(1)} %select_reduce_fusion.place_ref, bf16[4,256,1024]{2,1,0:T(8,128)(2,1)S(1)} %pad_maximum_fusion.refs_0_.refs_1_, bf16[256,1024]{1,0:T(8,128)(2,1)S(1)} %copy-done.1, bf16[256,1024]{1,0:T(8,128)(2,1)S(1)} %collective-permute-done.11.refs_2_, ...), custom_call_target="tpu_custom_call" | custom-call | tf_op jit(solution)/shard_map/weight_grad/pallas_call | solution.py:263
  135.5 2.6 %weight_grad.3 = bf16[1024,1024]{1,0:T(8,128)(2,1)} custom-call(s32[4]{0:T(128)S(1)} %select_reduce_fusion.place_ref, f32[1024,1024]{1,0:T(8,128)S(1)} %weight_grad.2.refs_0_, bf16[4,256,1024]{2,1,0:T(8,128)(2,1)S(1)} %pad_maximum_fusion.refs_0_.refs_1_, bf16[256,1024]{1,0:T(8,128)(2,1)S(1)} %collective-permute-done.19.refs_2_), custom_call_target="tpu_custom_call" | custom-call | tf_op jit(solution)/shard_map/weight_grad/pallas_call | solution.py:263
  (59 shorter events, 15.8 us)
Async XLA Ops:
  0.6 10.7 %collective-permute-start.2 = (bf16[256,1024]{1,0:T(8,128)(2,1)}, bf16[256,1024]{1,0:T(8,128)(2,1)}, u32[]{:S(2)}, u32[]{:S(2)}) collective-permute-start(bf16[256,1024]{1,0:T(8,128)(2,1)} %refs_0_.2), channel_id=1, source_target_pairs={{0,1},{1,0},{2,3},{3,2},{4,5},{5,4},{6,7},{7,6},{8,9},{9,8},{10,11... | collective-permute-start | bytes 1572872 | tf_op jit(solution)/shard_map/ppermute | solution.py:37
  1.2 15.9 %collective-permute-start.3 = (bf16[256,1024]{1,0:T(8,128)(2,1)}, bf16[256,1024]{1,0:T(8,128)(2,1)S(1)}, u32[]{:S(2)}, u32[]{:S(2)}) collective-permute-start(bf16[256,1024]{1,0:T(8,128)(2,1)} %refs_0_.2), channel_id=1, source_target_pairs={{0,2},{2,0},{1,3},{3,1},{4,6},{6,4},{5,7},{7,5},{8,10},{10,8},{9,1... | collective-permute-start | bytes 1572872 | tf_op jit(solution)/shard_map/ppermute | solution.py:37
  5.9 27.2 %collective-permute-start.7 = (bf16[512,1024]{1,0:T(8,128)(2,1)S(1)}, bf16[512,1024]{1,0:T(8,128)(2,1)S(1)}, u32[]{:S(2)}, u32[]{:S(2)}) collective-permute-start(bf16[512,1024]{1,0:T(8,128)(2,1)S(1)} %constant_dynamic-update-slice_fusion.refs_0_), channel_id=1, source_target_pairs={{0,4},{4,8},{8,12},{1,5},{5,9},{9,13},{2,6},{6,10},{10,14},{3,7},{... | collective-permute-start | bytes 3145736 | tf_op jit(solution)/shard_map/ppermute | solution.py:26
  9.5 15.7 %collective-permute-start = (bf16[256,1024]{1,0:T(8,128)(2,1)S(1)}, bf16[256,1024]{1,0:T(8,128)(2,1)}, u32[]{:S(2)}, u32[]{:S(2)}) collective-permute-start(bf16[256,1024]{1,0:T(8,128)(2,1)S(1)} %copy-done.5), channel_id=1, source_target_pairs={{4,0},{8,4},{12,8},{5,1},{9,5},{13,9},{6,2},{10,6},{14,10},{7,3},{... | collective-permute-start | bytes 1572872 | tf_op jit(solution)/shard_map/ppermute | solution.py:26
  17.1 9.4 %collective-permute-start.4 = (bf16[256,1024]{1,0:T(8,128)(2,1)S(1)}, bf16[256,1024]{1,0:T(8,128)(2,1)}, u32[]{:S(2)}, u32[]{:S(2)}) collective-permute-start(bf16[256,1024]{1,0:T(8,128)(2,1)S(1)} %collective-permute-done.3.refs_1_), channel_id=1, source_target_pairs={{0,1},{1,0},{2,3},{3,2},{4,5},{5,4},{6,7},{7,6},{8,9},{9,8},{10,11... | collective-permute-start | bytes 1572872 | tf_op jit(solution)/shard_map/ppermute | solution.py:37
  17.7 35.0 %copy-start.9 = (s32[2,5]{1,0:T(2,128)S(1)}, s32[2,5]{1,0:T(2,128)}, u32[]{:S(2)}) copy-start(s32[2,5]{1,0:T(2,128)} %param.10) | copy-start | bytes 124
  25.2 17.1 %collective-permute-start.1 = (bf16[256,1024]{1,0:T(8,128)(2,1)}, bf16[256,1024]{1,0:T(8,128)(2,1)}, u32[]{:S(2)}, u32[]{:S(2)}) collective-permute-start(bf16[256,1024]{1,0:T(8,128)(2,1)} %collective-permute-done.refs_1_), channel_id=1, source_target_pairs={{4,0},{8,4},{12,8},{5,1},{9,5},{13,9},{6,2},{10,6},{14,10},{7,3},{... | collective-permute-start | bytes 1572872 | tf_op jit(solution)/shard_map/ppermute | solution.py:26
  31.8 19.7 %collective-permute-start.5 = (bf16[256,1024]{1,0:T(8,128)(2,1)}, bf16[256,1024]{1,0:T(8,128)(2,1)}, u32[]{:S(2)}, u32[]{:S(2)}) collective-permute-start(bf16[256,1024]{1,0:T(8,128)(2,1)} %mixed_grad.3.g_ref.refs_3_), channel_id=1, source_target_pairs={{4,0},{8,4},{12,8},{5,1},{9,5},{13,9},{6,2},{10,6},{14,10},{7,3},{... | collective-permute-start | bytes 1572872 | tf_op jit(solution)/shard_map/ppermute | solution.py:26
  33.1 32.5 %collective-permute-start.8 = (bf16[512,1024]{1,0:T(8,128)(2,1)S(1)}, bf16[512,1024]{1,0:T(8,128)(2,1)S(1)}, u32[]{:S(2)}, u32[]{:S(2)}) collective-permute-start(bf16[512,1024]{1,0:T(8,128)(2,1)S(1)} %collective-permute-done.7.refs_1_), channel_id=1, source_target_pairs={{0,4},{4,8},{8,12},{1,5},{5,9},{9,13},{2,6},{6,10},{10,14},{3,7},{... | collective-permute-start | bytes 3145736 | tf_op jit(solution)/shard_map/ppermute | solution.py:26
  51.4 14.1 %collective-permute-start.6 = (bf16[256,1024]{1,0:T(8,128)(2,1)}, bf16[256,1024]{1,0:T(8,128)(2,1)}, u32[]{:S(2)}, u32[]{:S(2)}) collective-permute-start(bf16[256,1024]{1,0:T(8,128)(2,1)} %collective-permute-done.5.refs_4_), channel_id=1, source_target_pairs={{4,0},{8,4},{12,8},{5,1},{9,5},{13,9},{6,2},{10,6},{14,10},{7,3},{... | collective-permute-start | bytes 1572872 | tf_op jit(solution)/shard_map/ppermute | solution.py:26
  68.6 33.8 %collective-permute-start.12 = (bf16[256,1024]{1,0:T(8,128)(2,1)S(1)}, bf16[256,1024]{1,0:T(8,128)(2,1)S(1)}, u32[]{:S(2)}, u32[]{:S(2)}) collective-permute-start(bf16[256,1024]{1,0:T(8,128)(2,1)S(1)} %get-tuple-element.36.m_ref.refs_1_), channel_id=1, source_target_pairs={{0,12},{4,0},{8,4},{12,8},{1,13},{5,1},{9,5},{13,9},{2,14},{6,2},{... | collective-permute-start | bytes 1572872 | tf_op jit(solution)/shard_map/ppermute | solution.py:33
  70.1 32.2 %collective-permute-start.11 = (bf16[256,1024]{1,0:T(8,128)(2,1)S(1)}, bf16[256,1024]{1,0:T(8,128)(2,1)S(1)}, u32[]{:S(2)}, u32[]{:S(2)}) collective-permute-start(bf16[256,1024]{1,0:T(8,128)(2,1)S(1)} %get-tuple-element.36.m_ref.refs_1_), channel_id=1, source_target_pairs={{0,4},{4,8},{8,12},{12,0},{1,5},{5,9},{9,13},{13,1},{2,6},{6,10},{... | collective-permute-start | bytes 1572872 | tf_op jit(solution)/shard_map/ppermute | solution.py:33
  70.7 31.7 %collective-permute-start.10 = (bf16[256,1024]{1,0:T(8,128)(2,1)S(1)}, bf16[256,1024]{1,0:T(8,128)(2,1)}, u32[]{:S(2)}, u32[]{:S(2)}) collective-permute-start(bf16[256,1024]{1,0:T(8,128)(2,1)S(1)} %select_select_fusion), channel_id=1, source_target_pairs={{0,0},{1,9},{2,6},{3,15},{4,4},{5,13},{6,10},{7,3},{8,8},{9,1},{10... | collective-permute-start | bytes 1572872 | tf_op jit(solution)/shard_map/ppermute | solution.py:418
  79.0 8.1 %collective-permute-start.9 = (bf16[2,256,1024]{2,1,0:T(8,128)(2,1)}, bf16[2,256,1024]{2,1,0:T(8,128)(2,1)S(1)}, u32[]{:S(2)}, u32[]{:S(2)}) collective-permute-start(bf16[2,256,1024]{2,1,0:T(8,128)(2,1)} %get-tuple-element.31), channel_id=1, source_target_pairs={{0,1},{1,0},{2,3},{3,2},{4,5},{5,4},{6,7},{7,6},{8,9},{9,8},{10,11... | collective-permute-start | bytes 3145736 | tf_op jit(solution)/shard_map/ppermute | solution.py:37
  79.1 26.2 %copy-start.1 = (bf16[256,1024]{1,0:T(8,128)(2,1)S(1)}, bf16[256,1024]{1,0:T(8,128)(2,1)}, u32[]{:S(2)}) copy-start(bf16[256,1024]{1,0:T(8,128)(2,1)} %copy-done) | copy-start | bytes 1572868
  79.1 27.4 %copy-start.3 = (bf16[256,1024]{1,0:T(8,128)(2,1)S(1)}, bf16[256,1024]{1,0:T(8,128)(2,1)}, u32[]{:S(2)}) copy-start(bf16[256,1024]{1,0:T(8,128)(2,1)} %k_ref) | copy-start | bytes 1572868
  79.1 27.4 %copy-start.4 = (bf16[256,1024]{1,0:T(8,128)(2,1)S(1)}, bf16[256,1024]{1,0:T(8,128)(2,1)}, u32[]{:S(2)}) copy-start(bf16[256,1024]{1,0:T(8,128)(2,1)} %v_ref.1) | copy-start | bytes 1572868
  85.8 16.6 %collective-permute-start.14 = (f32[24,256]{1,0:T(8,128)S(1)}, f32[24,256]{1,0:T(8,128)S(1)}, u32[]{:S(2)}, u32[]{:S(2)}) collective-permute-start(f32[24,256]{1,0:T(8,128)S(1)} %get-tuple-element.35.refs_6_), channel_id=1, source_target_pairs={{8,0},{12,4},{9,1},{13,5},{10,2},{14,6},{11,3},{15,7},{24,16},{28,... | collective-permute-start | bytes 73736 | tf_op jit(solution)/shard_map/ppermute | solution.py:26
  87.1 15.3 %collective-permute-start.13 = (f32[24,256]{1,0:T(8,128)S(1)}, f32[24,256]{1,0:T(8,128)S(1)}, u32[]{:S(2)}, u32[]{:S(2)}) collective-permute-start(f32[24,256]{1,0:T(8,128)S(1)} %get-tuple-element.35.refs_6_), channel_id=1, source_target_pairs={{4,0},{8,4},{12,8},{5,1},{9,5},{13,9},{6,2},{10,6},{14,10},{7,3},{... | collective-permute-start | bytes 73736 | tf_op jit(solution)/shard_map/ppermute | solution.py:26
  102.4 15.8 %collective-permute-start.17 = (bf16[256,1024]{1,0:T(8,128)(2,1)}, bf16[256,1024]{1,0:T(8,128)(2,1)S(1)}, u32[]{:S(2)}, u32[]{:S(2)}) collective-permute-start(bf16[256,1024]{1,0:T(8,128)(2,1)} %collective-permute-done.10), channel_id=1, source_target_pairs={{0,2},{2,0},{1,3},{3,1},{4,6},{6,4},{5,7},{7,5},{8,10},{10,8},{9,1... | collective-permute-start | bytes 1572872 | tf_op jit(solution)/shard_map/ppermute | solution.py:37
  105.3 26.5 %collective-permute-start.16 = (bf16[256,1024]{1,0:T(8,128)(2,1)}, bf16[256,1024]{1,0:T(8,128)(2,1)S(1)}, u32[]{:S(2)}, u32[]{:S(2)}) collective-permute-start(bf16[256,1024]{1,0:T(8,128)(2,1)} %collective-permute-done.10), channel_id=1, source_target_pairs={{0,1},{1,0},{2,3},{3,2},{4,5},{5,4},{6,7},{7,6},{8,9},{9,8},{10,11... | collective-permute-start | bytes 1572872 | tf_op jit(solution)/shard_map/ppermute | solution.py:37
  105.3 26.5 %collective-permute-start.19 = (bf16[256,1024]{1,0:T(8,128)(2,1)S(1)}, bf16[256,1024]{1,0:T(8,128)(2,1)S(1)}, u32[]{:S(2)}, u32[]{:S(2)}) collective-permute-start(bf16[256,1024]{1,0:T(8,128)(2,1)S(1)} %copy-done.1), channel_id=1, source_target_pairs={{0,8},{4,12},{8,0},{12,4},{1,9},{5,13},{9,1},{13,5},{2,10},{6,14},... | collective-permute-start | bytes 1572872 | tf_op jit(solution)/shard_map/ppermute | solution.py:33
  106.4 23.1 %collective-permute-start.15 = (bf16[256,1024]{1,0:T(8,128)(2,1)S(1)}, bf16[256,1024]{1,0:T(8,128)(2,1)S(1)}, u32[]{:S(2)}, u32[]{:S(2)}) collective-permute-start(bf16[256,1024]{1,0:T(8,128)(2,1)S(1)} %fusion), channel_id=1, source_target_pairs={{0,2},{2,0},{1,3},{3,1},{4,6},{6,4},{5,7},{7,5},{8,10},{10,8},{9,1... | collective-permute-start | bytes 1572872 | tf_op jit(solution)/shard_map/ppermute | solution.py:37
  118.2 13.6 %collective-permute-start.18 = (bf16[256,1024]{1,0:T(8,128)(2,1)S(1)}, bf16[256,1024]{1,0:T(8,128)(2,1)S(1)}, u32[]{:S(2)}, u32[]{:S(2)}) collective-permute-start(bf16[256,1024]{1,0:T(8,128)(2,1)S(1)} %collective-permute-done.17), channel_id=1, source_target_pairs={{0,1},{1,0},{2,3},{3,2},{4,5},{5,4},{6,7},{7,6},{8,9},{9,8},{10,11... | collective-permute-start | bytes 1572872 | tf_op jit(solution)/shard_map/ppermute | solution.py:37
  (6 other events, 54.5 us)

commit v9 on v8

--- a/solution.py
+++ b/solution.py
@@ -281,7 +281,7 @@
 
 
 VMEM_LIMIT = 20 * 1024 * 1024
-WEIGHTS = dict(mixed_grad=0.0, forward=100.0, partial=0.0, query=100.0, key=100.0, weight=0.0)
+WEIGHTS = dict(mixed_grad=0.0, forward=0.0, partial=0.0, query=100.0, key=100.0, weight=0.0)
 STREAM_LIMIT = 54 * 1024 * 1024
 
 
@@ -377,12 +377,10 @@
     c_blocks, c_rest, c_places = features_here(cotangent)
     half = len(c_blocks)
     part_cols = cotangent.shape[1]
-    while len(query_all) < count:
-        query_all = further(query_all, -1)
     mixed_sum = []
     for part in range(2):
         if part:
-            c_blocks = c_blocks + other_features(c_rest, *mixed_sum)
+            c_blocks = c_blocks + other_features(c_rest, *mixed_sum, query_all[1])
         mine = slice(part * half, (part + 1) * half)
         mixed_sum = [
             kernel_call(
@@ -401,8 +399,10 @@
     while len(kv_all) < count:
         kv_all = further(kv_all, 1, mixed_grad)
     grad_all = further([mixed_grad], -1)
+    while len(query_all) < count:
+        query_all = further(query_all, -1, mixed_grad)
     while len(grad_all) < count:
-        grad_all = further(grad_all, -1, query_all[-1])
+        grad_all = further(grad_all, -1)
 
     h, r = lax.axis_index("head"), lax.axis_index("rep")
     n_head, n_rep = lax.axis_size("head"), lax.axis_size("rep")
@@ -415,13 +415,13 @@
     for s in range(peers):
         for q in range(group_count):
             links.append((s * group_count + q, ((s + step_of(q)) % peers) * group_count + q))
-    arrived = lax.ppermute(after(out_block, grad_all[-1], kv_all[-1]), ("seq", "head", "rep"), links)
+    arrived = lax.ppermute(after(out_block, grad_all[1], kv_all[-1]), ("seq", "head", "rep"), links)
 
     mixed_heads, lse = kernel_call(
         functools.partial(forward_kernel, tiles, count, heads),
         "attention_forward",
         [use],
-        [after(queries, query_all[-1], grad_all[-1]), *kv_all],
+        [queries, *kv_all],
         [like_queries, jax.ShapeDtypeStruct((heads_up, rows), F32)],
         cost(2 * attention_flops, (2 * count + 2) * array_bytes, exps, WEIGHTS["forward"]),
     )
@@ -440,7 +440,7 @@
     )
     stats_all = [stats] + [shift(stats, -d) for d in distances[1:]]
     partial_products = attended_partial(
-        mixed_heads, out_weight, c_places, cost(2 * rows * columns * features, 2 * rows * features, 0, WEIGHTS["partial"])
+        after(mixed_heads, query_all[-1], grad_all[-1]), out_weight, c_places, cost(2 * rows * columns * features, 2 * rows * features, 0, WEIGHTS["partial"])
     )
     shares = core_sum(partial_products)
     held = after(mixed_heads, arrived, *near.values(), *stats_all[1:], *shares)

time: 139 us -> 136 us (0.978)
  waiting for transfers between devices: 62.5 us -> 50.8 us
  starting transfers between devices: 27.8 us -> 36.2 us
    ppermute x8, waiting for transfers between devices: 45 us -> 31.8 us  [shift(): lax.ppermute(value, 'seq', [(i, i + by) for i in range(peers) if 0 <= i +...]
    ppermute x1, starting transfers between devices: 1.44 us -> 5.36 us  [per_device(): lax.ppermute(after(out_block, grad_all[1], kv_all[-1]), ('seq', 'head', '...]
    ppermute x3, starting transfers between devices: 3.14 us -> 5.55 us  [cyclic(): lax.ppermute(value, 'seq', [(i, (i + by) % peers) for i in range(peers)])]
    ppermute x8, starting transfers between devices: 6.51 us -> 8.28 us  [swap(): return lax.ppermute(value, axis, [(0, 1), (1, 0)])]
    ppermute x8, waiting for transfers between devices: 16.3 us -> 17.7 us  [swap(): return lax.ppermute(value, axis, [(0, 1), (1, 0)])]
  transfers between devices with their start and end apart: 20 -> 20, of which waited for: 8 -> 9; matrix products, arithmetic and copies ran while one was open for 5% -> 6% of each run, Pallas kernels for 22% -> 25%
where the time goes in v9:
time: 136 us; the launch traced here: 135 us
  waiting for transfers between devices  50.8 us (37%)
  Pallas kernels  38.6 us (28%)
  starting transfers between devices  36.2 us (27%)
  other arithmetic  6.7 us (5%)
  local copies, waits for them, and re-layouts  2.3 us (2%)
    pallas_call x8, Pallas kernels, kernel_call(): pl.pallas_call(body, in_specs=[smem] * len(scalars) + [vmem] * len(arrays...  38.6 us
    ppermute x8, waiting for transfers between devices, shift(): lax.ppermute(value, 'seq', [(i, i + by) for i in range(peers) if 0 <= i +...  31.8 us
    ppermute x8, waiting for transfers between devices, swap(): return lax.ppermute(value, axis, [(0, 1), (1, 0)])  17.7 us
    ppermute x8, starting transfers between devices, shift(): lax.ppermute(value, 'seq', [(i, i + by) for i in range(peers) if 0 <= i +...  17 us
    ppermute x8, starting transfers between devices, swap(): return lax.ppermute(value, axis, [(0, 1), (1, 0)])  8.28 us
    ppermute x3, starting transfers between devices, cyclic(): lax.ppermute(value, 'seq', [(i, (i + by) % peers) for i in range(peers)])  5.55 us
    ppermute x1, starting transfers between devices, per_device(): lax.ppermute(after(out_block, grad_all[1], kv_all[-1]), ('seq', 'head', '...  5.36 us
  transfers between devices with their start and end apart: 20, of which 9 were waited for; matrix products, arithmetic and copies ran while one was open for 6% of the time, Pallas kernels for 25%

profile of v9, /device:TPU:0, one launch (start us, length us, event | category | flops | bytes accessed | tf_op | source)
XLA Modules:
  0.0 135.5 jit_solution(4911645647376735201)
XLA Ops:
  1.1 2.6 %collective-permute-start.2 = (bf16[256,1024]{1,0:T(8,128)(2,1)}, bf16[256,1024]{1,0:T(8,128)(2,1)S(1)}, u32[]{:S(2)}, u32[]{:S(2)}) collective-permute-start(bf16[256,1024]{1,0:T(8,128)(2,1)} %refs_0_.2), channel_id=1, source_target_pairs={{0,2},{2,0},{1,3},{3,1},{4,6},{6,4},{5,7},{7,5},{8,10},{10,8},{9,1... | collective-permute-start | bytes 1572872 | tf_op jit(solution)/shard_map/ppermute | solution.py:37
  7.2 4.6 %collective-permute-start = (bf16[512,1024]{1,0:T(8,128)(2,1)S(1)}, bf16[512,1024]{1,0:T(8,128)(2,1)S(1)}, u32[]{:S(2)}, u32[]{:S(2)}) collective-permute-start(bf16[512,1024]{1,0:T(8,128)(2,1)S(1)} %constant_dynamic-update-slice_fusion.refs_0_), channel_id=1, source_target_pairs={{0,4},{4,8},{8,12},{1,5},{5,9},{9,13},{2,6},{6,10},{10,14},{3,7},{... | collective-permute-start | bytes 3145736 | tf_op jit(solution)/shard_map/ppermute | solution.py:26
  12.4 5.7 %mixed_grad.2.refs_0_ = f32[256,1024]{1,0:T(8,128)} custom-call(s32[2]{0:T(128)} %pad_add_fusion.2.place_ref, bf16[256,1024]{1,0:T(8,128)(2,1)} %refs_0_.2, bf16[256,1024]{1,0:T(8,128)(2,1)} %collective-permute-done.1.refs_1_, bf16[4096,1024]{1,0:T(8,128)(2,1)} %w_ref.1), custom_call_target="tpu_custom_call" | custom-call | tf_op jit(solution)/shard_map/mixed_grad/pallas_call | solution.py:263
  18.1 1.7 %collective-permute-done.3.refs_1_ = bf16[256,1024]{1,0:T(8,128)(2,1)S(1)} collective-permute-done((bf16[256,1024]{1,0:T(8,128)(2,1)}, bf16[256,1024]{1,0:T(8,128)(2,1)S(1)}, u32[]{:S(2)}, u32[]{:S(2)}) %collective-permute-start.3) | collective-permute-done | bytes 524320 | tf_op jit(solution)/shard_map/ppermute | solution.py:26
  21.9 5.3 %mixed_grad.3.g_ref.refs_3_ = bf16[256,1024]{1,0:T(8,128)(2,1)} custom-call(s32[2]{0:T(128)} %pad_add_fusion.1.place_ref, f32[256,1024]{1,0:T(8,128)} %mixed_grad.2.refs_0_, bf16[256,1024]{1,0:T(8,128)(2,1)} %copy-done.8, bf16[256,1024]{1,0:T(8,128)(2,1)} %collective-permute-done.4.refs_2_, bf16[4096,1024]{1,0:T(8,128)(2,1)} %w_ref.1), custom_call_target="tpu_custom_call" | custom-call | tf_op jit(solution)/shard_map/mixed_grad/pallas_call | solution.py:263
  28.5 5.7 %collective-permute-done.refs_1_ = bf16[512,1024]{1,0:T(8,128)(2,1)S(1)} collective-permute-done((bf16[512,1024]{1,0:T(8,128)(2,1)S(1)}, bf16[512,1024]{1,0:T(8,128)(2,1)S(1)}, u32[]{:S(2)}, u32[]{:S(2)}) %collective-permute-start) | collective-permute-done | bytes 1048608 | tf_op jit(solution)/shard_map/ppermute | solution.py:26
  34.2 4.4 %collective-permute-start.5 = (bf16[512,1024]{1,0:T(8,128)(2,1)S(1)}, bf16[512,1024]{1,0:T(8,128)(2,1)S(1)}, u32[]{:S(2)}, u32[]{:S(2)}) collective-permute-start(bf16[512,1024]{1,0:T(8,128)(2,1)S(1)} %collective-permute-done.refs_1_), channel_id=1, source_target_pairs={{0,4},{4,8},{8,12},{1,5},{5,9},{9,13},{2,6},{6,10},{10,14},{3,7},{... | collective-permute-start | bytes 3145736 | tf_op jit(solution)/shard_map/ppermute | solution.py:26
  40.0 4.2 %collective-permute-done.7.refs_4_ = bf16[256,1024]{1,0:T(8,128)(2,1)} collective-permute-done((bf16[256,1024]{1,0:T(8,128)(2,1)}, bf16[256,1024]{1,0:T(8,128)(2,1)}, u32[]{:S(2)}, u32[]{:S(2)}) %collective-permute-start.7) | collective-permute-done | bytes 524320 | tf_op jit(solution)/shard_map/ppermute | solution.py:26
  46.2 1.9 %select_select_fusion = bf16[256,1024]{1,0:T(8,128)(2,1)} fusion(bf16[256,1024]{1,0:T(8,128)(2,1)} %collective-permute-done.4.refs_2_, bf16[256,1024]{1,0:T(8,128)(2,1)} %copy-done.8, bf16[256,1024]{1,0:T(8,128)(2,1)} %collective-permute-done.1.refs_1_, bf16[256,1024]{1,0:T(8,128)(2,1)} %refs_0_.2, pred[]{:T(512)S(6)} %eq.33, pred[]{:T(512)S(6)} %eq.32, ...), kind=kLoop, calls=%fused_computation.5 | loop fusion | flops 786432 | bytes 2621443 | tf_op jit(solution)/shard_map/jit(_where)/select_n | solution.py:413
  48.2 12.1 %collective-permute-done.5.refs_2_ = bf16[512,1024]{1,0:T(8,128)(2,1)S(1)} collective-permute-done((bf16[512,1024]{1,0:T(8,128)(2,1)S(1)}, bf16[512,1024]{1,0:T(8,128)(2,1)S(1)}, u32[]{:S(2)}, u32[]{:S(2)}) %collective-permute-start.5) | collective-permute-done | bytes 1048608 | tf_op jit(solution)/shard_map/ppermute | solution.py:26
  60.2 3.0 %attention_forward.1 = (bf16[256,1024]{1,0:T(8,128)(2,1)S(1)}, f32[8,256]{1,0:T(8,128)S(1)}) custom-call(s32[10]{0:T(128)S(1)} %reshape.264.use_ref, bf16[256,1024]{1,0:T(8,128)(2,1)S(1)} %copy-done.5, bf16[512,1024]{1,0:T(8,128)(2,1)S(1)} %constant_dynamic-update-slice_fusion.refs_0_, bf16[512,1024]{1,0:T(8,128)(2,1)S(1)} %collective-permute-done.refs_1_, ...), custom_call_target="tpu_custom_call" | custom-call | tf_op jit(solution)/shard_map/attention_forward/pallas_call | solution.py:263
  63.3 4.5 %collective-permute-start.12 = (bf16[256,1024]{1,0:T(8,128)(2,1)S(1)}, bf16[256,1024]{1,0:T(8,128)(2,1)S(1)}, u32[]{:S(2)}, u32[]{:S(2)}) collective-permute-start(bf16[256,1024]{1,0:T(8,128)(2,1)S(1)} %get-tuple-element.36.m_ref.refs_1_), channel_id=1, source_target_pairs={{0,12},{4,0},{8,4},{12,8},{1,13},{5,1},{9,5},{13,9},{2,14},{6,2},{... | collective-permute-start | bytes 1572872 | tf_op jit(solution)/shard_map/ppermute | solution.py:33
  67.7 5.4 %collective-permute-start.10 = (bf16[256,1024]{1,0:T(8,128)(2,1)}, bf16[256,1024]{1,0:T(8,128)(2,1)}, u32[]{:S(2)}, u32[]{:S(2)}) collective-permute-start(bf16[256,1024]{1,0:T(8,128)(2,1)} %select_select_fusion), channel_id=1, source_target_pairs={{0,0},{1,9},{2,6},{3,15},{4,4},{5,13},{6,10},{7,3},{8,8},{9,1},{10... | collective-permute-start | bytes 1572872 | tf_op jit(solution)/shard_map/ppermute | solution.py:418
  73.1 6.9 %attended_partial.1 = (bf16[2,256,1024]{2,1,0:T(8,128)(2,1)}, bf16[2,256,1024]{2,1,0:T(8,128)(2,1)}) custom-call(s32[4]{0:T(128)} %pad_add_fusion.place_ref, bf16[256,1024]{1,0:T(8,128)(2,1)} %copy-done, bf16[4096,1024]{1,0:T(8,128)(2,1)} %w_ref.1), custom_call_target="tpu_custom_call" | custom-call | tf_op jit(solution)/shard_map/attended_partial/pallas_call | solution.py:263
  80.2 6.6 %attention_query_grad.1 = (bf16[256,1024]{1,0:T(8,128)(2,1)}, f32[24,256]{1,0:T(8,128)S(1)}) custom-call(s32[10]{0:T(128)S(1)} %reshape.264.use_ref, bf16[256,1024]{1,0:T(8,128)(2,1)S(1)} %copy-done.5, bf16[256,1024]{1,0:T(8,128)(2,1)S(1)} %copy-done.2, f32[8,256]{1,0:T(8,128)S(1)} %get-tuple-element.34.lse_ref, ...), custom_call_target="tpu_custom_call" | custom-call | flops 80530636800 | bytes 471859200 | tf_op jit(solution)/shard_map/attention_query_grad/pallas_call | solution.py:263
  88.1 1.5 %collective-permute-start.13 = (f32[24,256]{1,0:T(8,128)S(1)}, f32[24,256]{1,0:T(8,128)S(1)}, u32[]{:S(2)}, u32[]{:S(2)}) collective-permute-start(f32[24,256]{1,0:T(8,128)S(1)} %get-tuple-element.35.refs_6_), channel_id=1, source_target_pairs={{4,0},{8,4},{12,8},{5,1},{9,5},{13,9},{6,2},{10,6},{14,10},{7,3},{... | collective-permute-start | bytes 73736 | tf_op jit(solution)/shard_map/ppermute | solution.py:26
  89.8 8.2 %collective-permute-done.14.refs_8_ = f32[24,256]{1,0:T(8,128)S(1)} collective-permute-done((f32[24,256]{1,0:T(8,128)S(1)}, f32[24,256]{1,0:T(8,128)S(1)}, u32[]{:S(2)}, u32[]{:S(2)}) %collective-permute-start.14) | collective-permute-done | bytes 24608 | tf_op jit(solution)/shard_map/ppermute | solution.py:26
  98.0 4.7 %collective-permute-start.17 = (bf16[256,1024]{1,0:T(8,128)(2,1)}, bf16[256,1024]{1,0:T(8,128)(2,1)S(1)}, u32[]{:S(2)}, u32[]{:S(2)}) collective-permute-start(bf16[256,1024]{1,0:T(8,128)(2,1)} %collective-permute-done.10), channel_id=1, source_target_pairs={{0,2},{2,0},{1,3},{3,1},{4,6},{6,4},{5,7},{7,5},{8,10},{10,8},{9,1... | collective-permute-start | bytes 1572872 | tf_op jit(solution)/shard_map/ppermute | solution.py:37
  103.9 6.1 %attention_key_grad.1 = (bf16[256,1024]{1,0:T(8,128)(2,1)}, bf16[256,1024]{1,0:T(8,128)(2,1)}) custom-call(bf16[256,1024]{1,0:T(8,128)(2,1)S(1)} %copy-done.3, bf16[256,1024]{1,0:T(8,128)(2,1)S(1)} %copy-done.4, bf16[256,1024]{1,0:T(8,128)(2,1)S(1)} %copy-done.5, bf16[256,1024]{1,0:T(8,128)(2,1)S(1)} %copy-done.7, ...), custom_call_target="tpu_custom_call" | custom-call | flops 107374182400 | bytes 524288000 | tf_op jit(solution)/shard_map/attention_key_grad/pallas_call | solution.py:263
  110.1 5.6 %collective-permute-done.17 = bf16[256,1024]{1,0:T(8,128)(2,1)S(1)} collective-permute-done((bf16[256,1024]{1,0:T(8,128)(2,1)}, bf16[256,1024]{1,0:T(8,128)(2,1)S(1)}, u32[]{:S(2)}, u32[]{:S(2)}) %collective-permute-start.17) | collective-permute-done | bytes 524320 | tf_op jit(solution)/shard_map/ppermute | solution.py:37
  116.0 10.8 %collective-permute-done.15 = bf16[256,1024]{1,0:T(8,128)(2,1)S(1)} collective-permute-done((bf16[256,1024]{1,0:T(8,128)(2,1)S(1)}, bf16[256,1024]{1,0:T(8,128)(2,1)S(1)}, u32[]{:S(2)}, u32[]{:S(2)}) %collective-permute-start.15) | collective-permute-done | bytes 524320 | tf_op jit(solution)/shard_map/ppermute | solution.py:37
  129.2 1.3 pad_maximum_fusion.refs_0_.refs_1_
  130.5 2.4 %weight_grad.2.refs_0_ = f32[1024,1024]{1,0:T(8,128)S(1)} custom-call(s32[4]{0:T(128)S(1)} %select_reduce_fusion.place_ref, bf16[4,256,1024]{2,1,0:T(8,128)(2,1)S(1)} %pad_maximum_fusion.refs_0_.refs_1_, bf16[256,1024]{1,0:T(8,128)(2,1)S(1)} %copy-done.1, bf16[256,1024]{1,0:T(8,128)(2,1)S(1)} %collective-permute-done.11.refs_2_, ...), custom_call_target="tpu_custom_call" | custom-call | tf_op jit(solution)/shard_map/weight_grad/pallas_call | solution.py:263
  132.9 2.6 %weight_grad.3 = bf16[1024,1024]{1,0:T(8,128)(2,1)} custom-call(s32[4]{0:T(128)S(1)} %select_reduce_fusion.place_ref, f32[1024,1024]{1,0:T(8,128)S(1)} %weight_grad.2.refs_0_, bf16[4,256,1024]{2,1,0:T(8,128)(2,1)S(1)} %pad_maximum_fusion.refs_0_.refs_1_, bf16[256,1024]{1,0:T(8,128)(2,1)S(1)} %collective-permute-done.19.refs_2_), custom_call_target="tpu_custom_call" | custom-call | tf_op jit(solution)/shard_map/weight_grad/pallas_call | solution.py:263
  (61 shorter events, 16.8 us)
Async XLA Ops:
  0.6 11.8 %collective-permute-start.1 = (bf16[256,1024]{1,0:T(8,128)(2,1)}, bf16[256,1024]{1,0:T(8,128)(2,1)}, u32[]{:S(2)}, u32[]{:S(2)}) collective-permute-start(bf16[256,1024]{1,0:T(8,128)(2,1)} %refs_0_.2), channel_id=1, source_target_pairs={{0,1},{1,0},{2,3},{3,2},{4,5},{5,4},{6,7},{7,6},{8,9},{9,8},{10,11... | collective-permute-start | bytes 1572872 | tf_op jit(solution)/shard_map/ppermute | solution.py:37
  1.1 18.7 %collective-permute-start.2 = (bf16[256,1024]{1,0:T(8,128)(2,1)}, bf16[256,1024]{1,0:T(8,128)(2,1)S(1)}, u32[]{:S(2)}, u32[]{:S(2)}) collective-permute-start(bf16[256,1024]{1,0:T(8,128)(2,1)} %refs_0_.2), channel_id=1, source_target_pairs={{0,2},{2,0},{1,3},{3,1},{4,6},{6,4},{5,7},{7,5},{8,10},{10,8},{9,1... | collective-permute-start | bytes 1572872 | tf_op jit(solution)/shard_map/ppermute | solution.py:37
  3.7 16.1 %collective-permute-start.3 = (bf16[256,1024]{1,0:T(8,128)(2,1)}, bf16[256,1024]{1,0:T(8,128)(2,1)S(1)}, u32[]{:S(2)}, u32[]{:S(2)}) collective-permute-start(bf16[256,1024]{1,0:T(8,128)(2,1)} %refs_0_.3), channel_id=1, source_target_pairs={{4,0},{8,4},{12,8},{5,1},{9,5},{13,9},{6,2},{10,6},{14,10},{7,3},{... | collective-permute-start | bytes 1572872 | tf_op jit(solution)/shard_map/ppermute | solution.py:26
  7.2 27.0 %collective-permute-start = (bf16[512,1024]{1,0:T(8,128)(2,1)S(1)}, bf16[512,1024]{1,0:T(8,128)(2,1)S(1)}, u32[]{:S(2)}, u32[]{:S(2)}) collective-permute-start(bf16[512,1024]{1,0:T(8,128)(2,1)S(1)} %constant_dynamic-update-slice_fusion.refs_0_), channel_id=1, source_target_pairs={{0,4},{4,8},{8,12},{1,5},{5,9},{9,13},{2,6},{6,10},{10,14},{3,7},{... | collective-permute-start | bytes 3145736 | tf_op jit(solution)/shard_map/ppermute | solution.py:26
  19.8 2.1 %collective-permute-start.4 = (bf16[256,1024]{1,0:T(8,128)(2,1)S(1)}, bf16[256,1024]{1,0:T(8,128)(2,1)}, u32[]{:S(2)}, u32[]{:S(2)}) collective-permute-start(bf16[256,1024]{1,0:T(8,128)(2,1)S(1)} %collective-permute-done.2.refs_1_), channel_id=1, source_target_pairs={{0,1},{1,0},{2,3},{3,2},{4,5},{5,4},{6,7},{7,6},{8,9},{9,8},{10,11... | collective-permute-start | bytes 1572872 | tf_op jit(solution)/shard_map/ppermute | solution.py:37
  20.6 24.9 %copy-start.10 = (s32[2,5]{1,0:T(2,128)S(1)}, s32[2,5]{1,0:T(2,128)}, u32[]{:S(2)}) copy-start(s32[2,5]{1,0:T(2,128)} %param.10) | copy-start | bytes 124
  27.2 17.0 %collective-permute-start.7 = (bf16[256,1024]{1,0:T(8,128)(2,1)}, bf16[256,1024]{1,0:T(8,128)(2,1)}, u32[]{:S(2)}, u32[]{:S(2)}) collective-permute-start(bf16[256,1024]{1,0:T(8,128)(2,1)} %mixed_grad.3.g_ref.refs_3_), channel_id=1, source_target_pairs={{4,0},{8,4},{12,8},{5,1},{9,5},{13,9},{6,2},{10,6},{14,10},{7,3},{... | collective-permute-start | bytes 1572872 | tf_op jit(solution)/shard_map/ppermute | solution.py:26
  34.2 26.1 %collective-permute-start.5 = (bf16[512,1024]{1,0:T(8,128)(2,1)S(1)}, bf16[512,1024]{1,0:T(8,128)(2,1)S(1)}, u32[]{:S(2)}, u32[]{:S(2)}) collective-permute-start(bf16[512,1024]{1,0:T(8,128)(2,1)S(1)} %collective-permute-done.refs_1_), channel_id=1, source_target_pairs={{0,4},{4,8},{8,12},{1,5},{5,9},{9,13},{2,6},{6,10},{10,14},{3,7},{... | collective-permute-start | bytes 3145736 | tf_op jit(solution)/shard_map/ppermute | solution.py:26
  38.7 29.0 %collective-permute-start.6 = (bf16[256,1024]{1,0:T(8,128)(2,1)}, bf16[256,1024]{1,0:T(8,128)(2,1)}, u32[]{:S(2)}, u32[]{:S(2)}) collective-permute-start(bf16[256,1024]{1,0:T(8,128)(2,1)} %copy-done.6), channel_id=1, source_target_pairs={{4,0},{8,4},{12,8},{5,1},{9,5},{13,9},{6,2},{10,6},{14,10},{7,3},{... | collective-permute-start | bytes 1572872 | tf_op jit(solution)/shard_map/ppermute | solution.py:26
  44.2 23.6 %collective-permute-start.8 = (bf16[256,1024]{1,0:T(8,128)(2,1)}, bf16[256,1024]{1,0:T(8,128)(2,1)}, u32[]{:S(2)}, u32[]{:S(2)}) collective-permute-start(bf16[256,1024]{1,0:T(8,128)(2,1)} %collective-permute-done.7.refs_4_), channel_id=1, source_target_pairs={{4,0},{8,4},{12,8},{5,1},{9,5},{13,9},{6,2},{10,6},{14,10},{7,3},{... | collective-permute-start | bytes 1572872 | tf_op jit(solution)/shard_map/ppermute | solution.py:26
  63.3 34.8 %collective-permute-start.12 = (bf16[256,1024]{1,0:T(8,128)(2,1)S(1)}, bf16[256,1024]{1,0:T(8,128)(2,1)S(1)}, u32[]{:S(2)}, u32[]{:S(2)}) collective-permute-start(bf16[256,1024]{1,0:T(8,128)(2,1)S(1)} %get-tuple-element.36.m_ref.refs_1_), channel_id=1, source_target_pairs={{0,12},{4,0},{8,4},{12,8},{1,13},{5,1},{9,5},{13,9},{2,14},{6,2},{... | collective-permute-start | bytes 1572872 | tf_op jit(solution)/shard_map/ppermute | solution.py:33
  67.7 30.3 %collective-permute-start.11 = (bf16[256,1024]{1,0:T(8,128)(2,1)S(1)}, bf16[256,1024]{1,0:T(8,128)(2,1)S(1)}, u32[]{:S(2)}, u32[]{:S(2)}) collective-permute-start(bf16[256,1024]{1,0:T(8,128)(2,1)S(1)} %get-tuple-element.36.m_ref.refs_1_), channel_id=1, source_target_pairs={{0,4},{4,8},{8,12},{12,0},{1,5},{5,9},{9,13},{13,1},{2,6},{6,10},{... | collective-permute-start | bytes 1572872 | tf_op jit(solution)/shard_map/ppermute | solution.py:33
  67.7 30.3 %collective-permute-start.10 = (bf16[256,1024]{1,0:T(8,128)(2,1)}, bf16[256,1024]{1,0:T(8,128)(2,1)}, u32[]{:S(2)}, u32[]{:S(2)}) collective-permute-start(bf16[256,1024]{1,0:T(8,128)(2,1)} %select_select_fusion), channel_id=1, source_target_pairs={{0,0},{1,9},{2,6},{3,15},{4,4},{5,13},{6,10},{7,3},{8,8},{9,1},{10... | collective-permute-start | bytes 1572872 | tf_op jit(solution)/shard_map/ppermute | solution.py:418
  80.0 8.1 %collective-permute-start.9 = (bf16[2,256,1024]{2,1,0:T(8,128)(2,1)}, bf16[2,256,1024]{2,1,0:T(8,128)(2,1)S(1)}, u32[]{:S(2)}, u32[]{:S(2)}) collective-permute-start(bf16[2,256,1024]{2,1,0:T(8,128)(2,1)} %get-tuple-element.31), channel_id=1, source_target_pairs={{0,1},{1,0},{2,3},{3,2},{4,5},{5,4},{6,7},{7,6},{8,9},{9,8},{10,11... | collective-permute-start | bytes 3145736 | tf_op jit(solution)/shard_map/ppermute | solution.py:37
  80.1 23.8 %copy-start.3 = (bf16[256,1024]{1,0:T(8,128)(2,1)S(1)}, bf16[256,1024]{1,0:T(8,128)(2,1)}, u32[]{:S(2)}) copy-start(bf16[256,1024]{1,0:T(8,128)(2,1)} %k_ref) | copy-start | bytes 1572868
  80.1 23.8 %copy-start.4 = (bf16[256,1024]{1,0:T(8,128)(2,1)S(1)}, bf16[256,1024]{1,0:T(8,128)(2,1)}, u32[]{:S(2)}) copy-start(bf16[256,1024]{1,0:T(8,128)(2,1)} %v_ref.1) | copy-start | bytes 1572868
  80.1 23.8 %copy-start.7 = (bf16[256,1024]{1,0:T(8,128)(2,1)S(1)}, bf16[256,1024]{1,0:T(8,128)(2,1)}, u32[]{:S(2)}) copy-start(bf16[256,1024]{1,0:T(8,128)(2,1)} %copy-done.6) | copy-start | bytes 1572868
  86.8 11.2 %collective-permute-start.14 = (f32[24,256]{1,0:T(8,128)S(1)}, f32[24,256]{1,0:T(8,128)S(1)}, u32[]{:S(2)}, u32[]{:S(2)}) collective-permute-start(f32[24,256]{1,0:T(8,128)S(1)} %get-tuple-element.35.refs_6_), channel_id=1, source_target_pairs={{8,0},{12,4},{9,1},{13,5},{10,2},{14,6},{11,3},{15,7},{24,16},{28,... | collective-permute-start | bytes 73736 | tf_op jit(solution)/shard_map/ppermute | solution.py:26
  88.1 9.9 %collective-permute-start.13 = (f32[24,256]{1,0:T(8,128)S(1)}, f32[24,256]{1,0:T(8,128)S(1)}, u32[]{:S(2)}, u32[]{:S(2)}) collective-permute-start(f32[24,256]{1,0:T(8,128)S(1)} %get-tuple-element.35.refs_6_), channel_id=1, source_target_pairs={{4,0},{8,4},{12,8},{5,1},{9,5},{13,9},{6,2},{10,6},{14,10},{7,3},{... | collective-permute-start | bytes 73736 | tf_op jit(solution)/shard_map/ppermute | solution.py:26
  98.0 17.6 %collective-permute-start.17 = (bf16[256,1024]{1,0:T(8,128)(2,1)}, bf16[256,1024]{1,0:T(8,128)(2,1)S(1)}, u32[]{:S(2)}, u32[]{:S(2)}) collective-permute-start(bf16[256,1024]{1,0:T(8,128)(2,1)} %collective-permute-done.10), channel_id=1, source_target_pairs={{0,2},{2,0},{1,3},{3,1},{4,6},{6,4},{5,7},{7,5},{8,10},{10,8},{9,1... | collective-permute-start | bytes 1572872 | tf_op jit(solution)/shard_map/ppermute | solution.py:37
  102.7 26.5 %collective-permute-start.16 = (bf16[256,1024]{1,0:T(8,128)(2,1)}, bf16[256,1024]{1,0:T(8,128)(2,1)S(1)}, u32[]{:S(2)}, u32[]{:S(2)}) collective-permute-start(bf16[256,1024]{1,0:T(8,128)(2,1)} %collective-permute-done.10), channel_id=1, source_target_pairs={{0,1},{1,0},{2,3},{3,2},{4,5},{5,4},{6,7},{7,6},{8,9},{9,8},{10,11... | collective-permute-start | bytes 1572872 | tf_op jit(solution)/shard_map/ppermute | solution.py:37
  102.7 26.5 %collective-permute-start.19 = (bf16[256,1024]{1,0:T(8,128)(2,1)S(1)}, bf16[256,1024]{1,0:T(8,128)(2,1)S(1)}, u32[]{:S(2)}, u32[]{:S(2)}) collective-permute-start(bf16[256,1024]{1,0:T(8,128)(2,1)S(1)} %copy-done.1), channel_id=1, source_target_pairs={{0,8},{4,12},{8,0},{12,4},{1,9},{5,13},{9,1},{13,5},{2,10},{6,14},... | collective-permute-start | bytes 1572872 | tf_op jit(solution)/shard_map/ppermute | solution.py:33
  103.8 23.1 %collective-permute-start.15 = (bf16[256,1024]{1,0:T(8,128)(2,1)S(1)}, bf16[256,1024]{1,0:T(8,128)(2,1)S(1)}, u32[]{:S(2)}, u32[]{:S(2)}) collective-permute-start(bf16[256,1024]{1,0:T(8,128)(2,1)S(1)} %fusion), channel_id=1, source_target_pairs={{0,2},{2,0},{1,3},{3,1},{4,6},{6,4},{5,7},{7,5},{8,10},{10,8},{9,1... | collective-permute-start | bytes 1572872 | tf_op jit(solution)/shard_map/ppermute | solution.py:37
  115.6 13.6 %collective-permute-start.18 = (bf16[256,1024]{1,0:T(8,128)(2,1)S(1)}, bf16[256,1024]{1,0:T(8,128)(2,1)S(1)}, u32[]{:S(2)}, u32[]{:S(2)}) collective-permute-start(bf16[256,1024]{1,0:T(8,128)(2,1)S(1)} %collective-permute-done.17), channel_id=1, source_target_pairs={{0,1},{1,0},{2,3},{3,2},{4,5},{5,4},{6,7},{7,6},{8,9},{9,8},{10,11... | collective-permute-start | bytes 1572872 | tf_op jit(solution)/shard_map/ppermute | solution.py:37
  (7 other events, 82.9 us)

commit v10 on v9

--- a/solution.py
+++ b/solution.py
@@ -243,8 +243,10 @@
     for first in range(0, features, height):
         rows = slice(first, first + height)
         total = refs[0][rows, :] if given else None
-        for p, m_ref in zip(which, m_refs):
-            part = dot_tn(c_ref[place_ref[p], :, rows], m_ref[...])
+        fold = len(m_refs) // len(which)
+        for i, p in enumerate(which):
+            mixed = functools.reduce(jnp.add, [m[...] for m in m_refs[i * fold : (i + 1) * fold]])
+            part = dot_tn(c_ref[place_ref[p], :, rows], mixed)
             total = part if total is None else total + part
         out_ref[rows, :] = total.astype(out_ref.dtype)
 
@@ -281,7 +283,7 @@
 
 
 VMEM_LIMIT = 20 * 1024 * 1024
-WEIGHTS = dict(mixed_grad=0.0, forward=0.0, partial=0.0, query=100.0, key=100.0, weight=0.0)
+WEIGHTS = dict(mixed_grad=0.0, forward=0.0, partial=100.0, query=100.0, key=100.0, weight=0.0)
 STREAM_LIMIT = 54 * 1024 * 1024
 
 
@@ -338,10 +340,10 @@
     ]
 
 
-def chip_sum(shares, *others):
+def chip_sum(shares):
     if len(shares) == 1:
         return lax.psum_scatter(shares[0], ("head", "rep"), scatter_dimension=1, tiled=True)
-    return (shares[0] + swap(after(shares[1], *others), "head").astype(F32)).astype(BF16)
+    return (shares[0] + swap(shares[1], "head").astype(F32)).astype(BF16)
 
 
 def per_device(queries, keys, values, out_weight, level_mask, cotangent):
@@ -434,27 +436,31 @@
         functools.partial(query_kernel, tiles, count, heads, heads_up),
         "attention_query_grad",
         [use],
-        [after(queries, mixed_heads), mixed_grad, lse, *kv_all],
+        [after(queries, mixed_heads, query_all[-1], grad_all[-1]), mixed_grad, lse, *kv_all],
         [like_queries, stats_shape],
         cost(3 * attention_flops, (2 * count + 3) * array_bytes, exps, WEIGHTS["query"]),
     )
-    stats_all = [stats] + [shift(stats, -d) for d in distances[1:]]
+    stats_all = further([stats], -1)
     partial_products = attended_partial(
         after(mixed_heads, query_all[-1], grad_all[-1]), out_weight, c_places, cost(2 * rows * columns * features, 2 * rows * features, 0, WEIGHTS["partial"])
     )
     shares = core_sum(partial_products)
-    held = after(mixed_heads, arrived, *near.values(), *stats_all[1:], *shares)
+    attended = chip_sum(shares)
+    held = after(mixed_heads, arrived, *near.values(), *stats_all[1:], attended)
+    while len(stats_all) < count:
+        stats_all = further(stats_all, -1, held)
     if peers <= 4:
-        mixed_all = [mixed_heads] + [
-            near[k] if k in near else cyclic(held, k) for k in range(1, peers)
-        ]
+        mixed_all = [[mixed_heads]] + [[near[k]] if k in near else [] for k in range(1, peers)]
+        if peers == 4:
+            up = lax.ppermute(after(near[1], held), "seq", [(1, 2), (2, 3)])
+            down = lax.ppermute(after(near[3], held), "seq", [(1, 0), (2, 1)])
+            mixed_all[2] = [up, down]
     else:
         gathered = lax.all_gather(mixed_heads, "seq", axis=0)
         mixed_all = [
-            lax.dynamic_index_in_dim(gathered, (place - k) % peers, 0, False)
+            [lax.dynamic_index_in_dim(gathered, (place - k) % peers, 0, False)]
             for k in range(peers)
         ]
-    attended = chip_sum(shares, held)
     k_grad, v_grad = kernel_call(
         functools.partial(key_kernel, tiles, count, heads, heads_up),
         "attention_key_grad",
@@ -464,8 +470,15 @@
         cost(4 * attention_flops, (2 * count + 4) * array_bytes, exps, WEIGHTS["key"]),
     )
 
-    ct_blocks, ct_rest, _ = features_here(after(arrived, held))
-    ct = jnp.stack(ct_blocks + other_features(ct_rest, k_grad))
+    if two_by_two():
+        ct_across = swap(after(arrived, held), "head")
+        far = [value for values in mixed_all for value in values]
+        beside = swap(after(arrived, ct_across, *far), "rep")
+        ct_blocks = [arrived, beside, *other_features(ct_across, *far, k_grad)]
+    else:
+        ct_blocks, ct_rest, _ = features_here(arrived)
+        ct_blocks = ct_blocks + ct_rest
+    ct = jnp.stack(ct_blocks)
     steps = step_of(c_places)
     ct_at = jnp.sum(
         jnp.where(steps[None] == jnp.arange(peers)[:, None], jnp.arange(group_count)[None], 0), 1
@@ -477,9 +490,9 @@
         if not which:
             weight_sum = [weight_sum[0].astype(BF16)]
             break
-        ranges = [mixed_all[k] for k in which]
+        ranges = [value for k in which for value in mixed_all[k]]
         if part:
-            ranges[0] = after(ranges[0], attended, k_grad)
+            ranges[0] = after(ranges[0], k_grad)
         weight_sum = [
             kernel_call(
                 functools.partial(weight_grad_kernel, which, part),

time: 136 us -> 141 us (1.037)
  starting transfers between devices: 36.2 us -> 40.7 us
  local copies, waits for them, and re-layouts: 2.3 us -> 4.12 us
  waiting for transfers between devices: 50.8 us -> 49.1 us
    ppermute x8, starting transfers between devices: 8.28 us -> 17.1 us  [swap(): return lax.ppermute(value, axis, [(0, 1), (1, 0)])]
    ppermute x8, waiting for transfers between devices: 17.7 us -> 9.77 us  [swap(): return lax.ppermute(value, axis, [(0, 1), (1, 0)])]
    ppermute x0 -> x2, waiting for transfers between devices: none -> 5.02 us  [the longest x1 5.02 us: per_device(): down = lax.ppermute(after(near[3], held), 'seq', [(1, 0), (2, 1)])]
    ppermute x1, starting transfers between devices: 5.36 us -> 0.86 us  [per_device(): lax.ppermute(after(out_block, grad_all[1], kv_all[-1]), ('seq', 'head', '...]
    ppermute x0 -> x2, starting transfers between devices: none -> 1.97 us  [the longest x1 1.29 us: per_device(): down = lax.ppermute(after(near[3], held), 'seq', [(1, 0), (2, 1)])]
    ppermute x8, waiting for transfers between devices: 31.8 us -> 33.7 us  [shift(): lax.ppermute(value, 'seq', [(i, i + by) for i in range(peers) if 0 <= i +...]
    unnamed x23 -> x25, local copies, waits for them, and re-layouts: 1.14 us -> 2.95 us
    ppermute x3 -> x2, starting transfers between devices: 5.55 us -> 3.85 us  [cyclic(): lax.ppermute(value, 'seq', [(i, (i + by) % peers) for i in range(peers)])]
  transfers between devices with their start and end apart: 20 -> 21, of which waited for: 9 -> 13; matrix products, arithmetic and copies ran while one was open for 6% -> 6% of each run, Pallas kernels for 25% -> 19%
where the time goes in v10:
time: 141 us
  waiting for transfers between devices  49.1 us (35%)
  starting transfers between devices  40.7 us (29%)
  Pallas kernels  38.6 us (27%)
  other arithmetic  7.1 us (5%)
  local copies, waits for them, and re-layouts  4.12 us (3%)
    pallas_call x8, Pallas kernels, kernel_call(): pl.pallas_call(body, in_specs=[smem] * len(scalars) + [vmem] * len(arrays...  38.6 us
    ppermute x8, waiting for transfers between devices, shift(): lax.ppermute(value, 'seq', [(i, i + by) for i in range(peers) if 0 <= i +...  33.7 us
    ppermute x8, starting transfers between devices, swap(): return lax.ppermute(value, axis, [(0, 1), (1, 0)])  17.1 us
    ppermute x8, starting transfers between devices, shift(): lax.ppermute(value, 'seq', [(i, i + by) for i in range(peers) if 0 <= i +...  16.9 us
    ppermute x8, waiting for transfers between devices, swap(): return lax.ppermute(value, axis, [(0, 1), (1, 0)])  9.77 us
    ppermute x1, waiting for transfers between devices, per_device(): down = lax.ppermute(after(near[3], held), 'seq', [(1, 0), (2, 1)])  5.02 us
    ppermute x2, starting transfers between devices, cyclic(): lax.ppermute(value, 'seq', [(i, (i + by) % peers) for i in range(peers)])  3.85 us
    unnamed x25, local copies, waits for them, and re-layouts  2.95 us
  transfers between devices with their start and end apart: 21, of which 13 were waited for; matrix products, arithmetic and copies ran while one was open for 6% of the time, Pallas kernels for 19%

profile of v10, /device:TPU:0, one launch (start us, length us, event | category | flops | bytes accessed | tf_op | source)
XLA Modules:
  0.0 140.6 jit_solution(9020816815956132543)
XLA Ops:
  1.1 2.6 %collective-permute-start.2 = (bf16[256,1024]{1,0:T(8,128)(2,1)}, bf16[256,1024]{1,0:T(8,128)(2,1)S(1)}, u32[]{:S(2)}, u32[]{:S(2)}) collective-permute-start(bf16[256,1024]{1,0:T(8,128)(2,1)} %refs_0_.2), channel_id=1, source_target_pairs={{0,2},{2,0},{1,3},{3,1},{4,6},{6,4},{5,7},{7,5},{8,10},{10,8},{9,1... | collective-permute-start | bytes 1572872 | tf_op jit(solution)/shard_map/ppermute | solution.py:37
  7.2 4.6 %collective-permute-start = (bf16[512,1024]{1,0:T(8,128)(2,1)S(1)}, bf16[512,1024]{1,0:T(8,128)(2,1)S(1)}, u32[]{:S(2)}, u32[]{:S(2)}) collective-permute-start(bf16[512,1024]{1,0:T(8,128)(2,1)S(1)} %constant_dynamic-update-slice_fusion.refs_0_), channel_id=1, source_target_pairs={{0,4},{4,8},{8,12},{1,5},{5,9},{9,13},{2,6},{6,10},{10,14},{3,7},{... | collective-permute-start | bytes 3145736 | tf_op jit(solution)/shard_map/ppermute | solution.py:26
  12.4 5.7 %mixed_grad.2.refs_0_ = f32[256,1024]{1,0:T(8,128)} custom-call(s32[2]{0:T(128)} %pad_add_fusion.2.place_ref, bf16[256,1024]{1,0:T(8,128)(2,1)} %refs_0_.2, bf16[256,1024]{1,0:T(8,128)(2,1)} %collective-permute-done.1.refs_1_, bf16[4096,1024]{1,0:T(8,128)(2,1)} %w_ref.1), custom_call_target="tpu_custom_call" | custom-call | tf_op jit(solution)/shard_map/mixed_grad/pallas_call | solution.py:265
  18.1 1.7 %collective-permute-done.3.refs_1_ = bf16[256,1024]{1,0:T(8,128)(2,1)S(1)} collective-permute-done((bf16[256,1024]{1,0:T(8,128)(2,1)}, bf16[256,1024]{1,0:T(8,128)(2,1)S(1)}, u32[]{:S(2)}, u32[]{:S(2)}) %collective-permute-start.3) | collective-permute-done | bytes 524320 | tf_op jit(solution)/shard_map/ppermute | solution.py:26
  21.9 5.3 %mixed_grad.3.g_ref.refs_3_ = bf16[256,1024]{1,0:T(8,128)(2,1)} custom-call(s32[2]{0:T(128)} %pad_add_fusion.1.place_ref, f32[256,1024]{1,0:T(8,128)} %mixed_grad.2.refs_0_, bf16[256,1024]{1,0:T(8,128)(2,1)} %copy-done.9, bf16[256,1024]{1,0:T(8,128)(2,1)} %collective-permute-done.4.refs_2_, bf16[4096,1024]{1,0:T(8,128)(2,1)} %w_ref.1), custom_call_target="tpu_custom_call" | custom-call | tf_op jit(solution)/shard_map/mixed_grad/pallas_call | solution.py:265
  28.5 5.7 %collective-permute-done.refs_1_ = bf16[512,1024]{1,0:T(8,128)(2,1)S(1)} collective-permute-done((bf16[512,1024]{1,0:T(8,128)(2,1)S(1)}, bf16[512,1024]{1,0:T(8,128)(2,1)S(1)}, u32[]{:S(2)}, u32[]{:S(2)}) %collective-permute-start) | collective-permute-done | bytes 1048608 | tf_op jit(solution)/shard_map/ppermute | solution.py:26
  34.2 4.4 %collective-permute-start.5 = (bf16[512,1024]{1,0:T(8,128)(2,1)S(1)}, bf16[512,1024]{1,0:T(8,128)(2,1)S(1)}, u32[]{:S(2)}, u32[]{:S(2)}) collective-permute-start(bf16[512,1024]{1,0:T(8,128)(2,1)S(1)} %collective-permute-done.refs_1_), channel_id=1, source_target_pairs={{0,4},{4,8},{8,12},{1,5},{5,9},{9,13},{2,6},{6,10},{10,14},{3,7},{... | collective-permute-start | bytes 3145736 | tf_op jit(solution)/shard_map/ppermute | solution.py:26
  39.9 4.3 %collective-permute-done.7.refs_4_ = bf16[256,1024]{1,0:T(8,128)(2,1)} collective-permute-done((bf16[256,1024]{1,0:T(8,128)(2,1)}, bf16[256,1024]{1,0:T(8,128)(2,1)}, u32[]{:S(2)}, u32[]{:S(2)}) %collective-permute-start.7) | collective-permute-done | bytes 524320 | tf_op jit(solution)/shard_map/ppermute | solution.py:26
  46.3 14.0 %collective-permute-done.5.refs_2_ = bf16[512,1024]{1,0:T(8,128)(2,1)S(1)} collective-permute-done((bf16[512,1024]{1,0:T(8,128)(2,1)S(1)}, bf16[512,1024]{1,0:T(8,128)(2,1)S(1)}, u32[]{:S(2)}, u32[]{:S(2)}) %collective-permute-start.5) | collective-permute-done | bytes 1048608 | tf_op jit(solution)/shard_map/ppermute | solution.py:26
  61.3 3.0 %attention_forward.1 = (bf16[256,1024]{1,0:T(8,128)(2,1)S(1)}, f32[8,256]{1,0:T(8,128)S(1)}) custom-call(s32[10]{0:T(128)S(1)} %reshape.264.use_ref, bf16[256,1024]{1,0:T(8,128)(2,1)S(1)} %copy-done.5, bf16[512,1024]{1,0:T(8,128)(2,1)S(1)} %constant_dynamic-update-slice_fusion.refs_0_, bf16[512,1024]{1,0:T(8,128)(2,1)S(1)} %collective-permute-done.refs_1_, ...), custom_call_target="tpu_custom_call" | custom-call | tf_op jit(solution)/shard_map/attention_forward/pallas_call | solution.py:265
  65.9 6.9 %attended_partial.1 = (bf16[2,256,1024]{2,1,0:T(8,128)(2,1)}, bf16[2,256,1024]{2,1,0:T(8,128)(2,1)}) custom-call(s32[4]{0:T(128)} %pad_add_fusion.place_ref, bf16[256,1024]{1,0:T(8,128)(2,1)} %copy-done.1, bf16[4096,1024]{1,0:T(8,128)(2,1)} %w_ref.1), custom_call_target="tpu_custom_call" | custom-call | flops 214748364800 | bytes 209715200 | tf_op jit(solution)/shard_map/attended_partial/pallas_call | solution.py:265
  74.2 3.9 %collective-permute-start.13 = (bf16[256,1024]{1,0:T(8,128)(2,1)S(1)}, bf16[256,1024]{1,0:T(8,128)(2,1)S(1)}, u32[]{:S(2)}, u32[]{:S(2)}) collective-permute-start(bf16[256,1024]{1,0:T(8,128)(2,1)S(1)} %copy-done.2), channel_id=1, source_target_pairs={{0,12},{4,0},{8,4},{12,8},{1,13},{5,1},{9,5},{13,9},{2,14},{6,2},{... | collective-permute-start | bytes 1572872 | tf_op jit(solution)/shard_map/ppermute | solution.py:33
  80.2 1.9 %collective-permute-start.10 = (bf16[256,1024]{1,0:T(8,128)(2,1)S(1)}, bf16[256,1024]{1,0:T(8,128)(2,1)S(1)}, u32[]{:S(2)}, u32[]{:S(2)}) collective-permute-start(bf16[256,1024]{1,0:T(8,128)(2,1)S(1)} %fusion.1), channel_id=1, source_target_pairs={{0,2},{2,0},{1,3},{3,1},{4,6},{6,4},{5,7},{7,5},{8,10},{10,8},{9,1... | collective-permute-start | bytes 1572872 | tf_op jit(solution)/shard_map/ppermute | solution.py:37
  82.1 6.6 %attention_query_grad.1 = (bf16[256,1024]{1,0:T(8,128)(2,1)}, f32[24,256]{1,0:T(8,128)S(1)}) custom-call(s32[10]{0:T(128)S(1)} %reshape.264.use_ref, bf16[256,1024]{1,0:T(8,128)(2,1)S(1)} %copy-done.6, bf16[256,1024]{1,0:T(8,128)(2,1)S(1)} %copy-done, f32[8,256]{1,0:T(8,128)S(1)} %get-tuple-element.36.lse_ref, ...), custom_call_target="tpu_custom_call" | custom-call | flops 80530636800 | bytes 471859200 | tf_op jit(solution)/shard_map/attention_query_grad/pallas_call | solution.py:265
  88.8 1.4 %collective-permute-start.14 = (f32[24,256]{1,0:T(8,128)S(1)}, f32[24,256]{1,0:T(8,128)S(1)}, u32[]{:S(2)}, u32[]{:S(2)}) collective-permute-start(f32[24,256]{1,0:T(8,128)S(1)} %get-tuple-element.39.refs_6_), channel_id=1, source_target_pairs={{4,0},{8,4},{12,8},{5,1},{9,5},{13,9},{6,2},{10,6},{14,10},{7,3},{... | collective-permute-start | bytes 73736 | tf_op jit(solution)/shard_map/ppermute | solution.py:26
  90.2 2.5 %collective-permute-done.10 = bf16[256,1024]{1,0:T(8,128)(2,1)S(1)} collective-permute-done((bf16[256,1024]{1,0:T(8,128)(2,1)S(1)}, bf16[256,1024]{1,0:T(8,128)(2,1)S(1)}, u32[]{:S(2)}, u32[]{:S(2)}) %collective-permute-start.10) | collective-permute-done | bytes 524320 | tf_op jit(solution)/shard_map/ppermute | solution.py:37
  92.8 2.1 %fusion = bf16[256,1024]{1,0:T(8,128)(2,1)} fusion(bf16[256,1024]{1,0:T(8,128)(2,1)S(1)} %collective-permute-done.10, bf16[2,256,1024]{2,1,0:T(8,128)(2,1)} %collective-permute-done.9, bf16[2,256,1024]{2,1,0:T(8,128)(2,1)S(1)} %copy-done.10), kind=kLoop, calls=%fused_computation.2 | loop fusion | flops 1572864 | bytes 2097152 | tf_op jit(solution)/shard_map/convert_element_type | solution.py:346
  94.9 7.3 %collective-permute-done.14.refs_7_ = f32[24,256]{1,0:T(8,128)S(1)} collective-permute-done((f32[24,256]{1,0:T(8,128)S(1)}, f32[24,256]{1,0:T(8,128)S(1)}, u32[]{:S(2)}, u32[]{:S(2)}) %collective-permute-start.14) | collective-permute-done | bytes 24608 | tf_op jit(solution)/shard_map/ppermute | solution.py:26
  104.0 11.5 %collective-permute-start.16 = (bf16[256,1024]{1,0:T(8,128)(2,1)S(1)}, bf16[256,1024]{1,0:T(8,128)(2,1)S(1)}, u32[]{:S(2)}, u32[]{:S(2)}) collective-permute-start(bf16[256,1024]{1,0:T(8,128)(2,1)S(1)} %collective-permute-done.11), channel_id=1, source_target_pairs={{0,2},{2,0},{1,3},{3,1},{4,6},{6,4},{5,7},{7,5},{8,10},{10,8},{9,1... | collective-permute-start | bytes 1572872 | tf_op jit(solution)/shard_map/ppermute | solution.py:37
  117.5 6.1 %attention_key_grad.1 = (bf16[256,1024]{1,0:T(8,128)(2,1)}, bf16[256,1024]{1,0:T(8,128)(2,1)}) custom-call(bf16[256,1024]{1,0:T(8,128)(2,1)S(1)} %copy-done.3, bf16[256,1024]{1,0:T(8,128)(2,1)S(1)} %copy-done.4, bf16[256,1024]{1,0:T(8,128)(2,1)S(1)} %copy-done.6, bf16[256,1024]{1,0:T(8,128)(2,1)S(1)} %copy-done.8, ...), custom_call_target="tpu_custom_call" | custom-call | flops 107374182400 | bytes 524288000 | tf_op jit(solution)/shard_map/attention_key_grad/pallas_call | solution.py:265
  123.7 4.0 %collective-permute-done.16 = bf16[256,1024]{1,0:T(8,128)(2,1)S(1)} collective-permute-done((bf16[256,1024]{1,0:T(8,128)(2,1)S(1)}, bf16[256,1024]{1,0:T(8,128)(2,1)S(1)}, u32[]{:S(2)}, u32[]{:S(2)}) %collective-permute-start.16) | collective-permute-done | bytes 524320 | tf_op jit(solution)/shard_map/ppermute | solution.py:37
  127.6 5.0 %collective-permute-done.18.refs_3_ = bf16[256,1024]{1,0:T(8,128)(2,1)S(1)} collective-permute-done((bf16[256,1024]{1,0:T(8,128)(2,1)S(1)}, bf16[256,1024]{1,0:T(8,128)(2,1)S(1)}, u32[]{:S(2)}, u32[]{:S(2)}) %collective-permute-start.18) | collective-permute-done | bytes 524320 | tf_op jit(solution)/shard_map/ppermute | solution.py:456
  135.6 2.4 %weight_grad.2.refs_0_ = f32[1024,1024]{1,0:T(8,128)S(1)} custom-call(s32[4]{0:T(128)S(1)} %select_reduce_fusion.place_ref, bf16[4,256,1024]{2,1,0:T(8,128)(2,1)S(1)} %pad_maximum_fusion.refs_0_.refs_1_, bf16[256,1024]{1,0:T(8,128)(2,1)S(1)} %copy-done.2, bf16[256,1024]{1,0:T(8,128)(2,1)S(1)} %collective-permute-done.12.refs_2_, ...), custom_call_target="tpu_custom_call" | custom-call | tf_op jit(solution)/shard_map/weight_grad/pallas_call | solution.py:265
  138.0 2.7 %weight_grad.3 = bf16[1024,1024]{1,0:T(8,128)(2,1)} custom-call(s32[4]{0:T(128)S(1)} %select_reduce_fusion.place_ref, f32[1024,1024]{1,0:T(8,128)S(1)} %weight_grad.2.refs_0_, bf16[4,256,1024]{2,1,0:T(8,128)(2,1)S(1)} %pad_maximum_fusion.refs_0_.refs_1_, bf16[256,1024]{1,0:T(8,128)(2,1)S(1)} %collective-permute-done.17.refs_2_, ...), custom_call_target="tpu_custom_call" | custom-call | tf_op jit(solution)/shard_map/weight_grad/pallas_call | solution.py:265
  (65 shorter events, 24.2 us)
Async XLA Ops:
  0.6 11.8 %collective-permute-start.1 = (bf16[256,1024]{1,0:T(8,128)(2,1)}, bf16[256,1024]{1,0:T(8,128)(2,1)}, u32[]{:S(2)}, u32[]{:S(2)}) collective-permute-start(bf16[256,1024]{1,0:T(8,128)(2,1)} %refs_0_.2), channel_id=1, source_target_pairs={{0,1},{1,0},{2,3},{3,2},{4,5},{5,4},{6,7},{7,6},{8,9},{9,8},{10,11... | collective-permute-start | bytes 1572872 | tf_op jit(solution)/shard_map/ppermute | solution.py:37
  1.1 18.7 %collective-permute-start.2 = (bf16[256,1024]{1,0:T(8,128)(2,1)}, bf16[256,1024]{1,0:T(8,128)(2,1)S(1)}, u32[]{:S(2)}, u32[]{:S(2)}) collective-permute-start(bf16[256,1024]{1,0:T(8,128)(2,1)} %refs_0_.2), channel_id=1, source_target_pairs={{0,2},{2,0},{1,3},{3,1},{4,6},{6,4},{5,7},{7,5},{8,10},{10,8},{9,1... | collective-permute-start | bytes 1572872 | tf_op jit(solution)/shard_map/ppermute | solution.py:37
  3.7 16.1 %collective-permute-start.3 = (bf16[256,1024]{1,0:T(8,128)(2,1)}, bf16[256,1024]{1,0:T(8,128)(2,1)S(1)}, u32[]{:S(2)}, u32[]{:S(2)}) collective-permute-start(bf16[256,1024]{1,0:T(8,128)(2,1)} %refs_0_.3), channel_id=1, source_target_pairs={{4,0},{8,4},{12,8},{5,1},{9,5},{13,9},{6,2},{10,6},{14,10},{7,3},{... | collective-permute-start | bytes 1572872 | tf_op jit(solution)/shard_map/ppermute | solution.py:26
  7.2 27.0 %collective-permute-start = (bf16[512,1024]{1,0:T(8,128)(2,1)S(1)}, bf16[512,1024]{1,0:T(8,128)(2,1)S(1)}, u32[]{:S(2)}, u32[]{:S(2)}) collective-permute-start(bf16[512,1024]{1,0:T(8,128)(2,1)S(1)} %constant_dynamic-update-slice_fusion.refs_0_), channel_id=1, source_target_pairs={{0,4},{4,8},{8,12},{1,5},{5,9},{9,13},{2,6},{6,10},{10,14},{3,7},{... | collective-permute-start | bytes 3145736 | tf_op jit(solution)/shard_map/ppermute | solution.py:26
  19.8 2.1 %collective-permute-start.4 = (bf16[256,1024]{1,0:T(8,128)(2,1)S(1)}, bf16[256,1024]{1,0:T(8,128)(2,1)}, u32[]{:S(2)}, u32[]{:S(2)}) collective-permute-start(bf16[256,1024]{1,0:T(8,128)(2,1)S(1)} %collective-permute-done.2.refs_1_), channel_id=1, source_target_pairs={{0,1},{1,0},{2,3},{3,2},{4,5},{5,4},{6,7},{7,6},{8,9},{9,8},{10,11... | collective-permute-start | bytes 1572872 | tf_op jit(solution)/shard_map/ppermute | solution.py:37
  27.2 17.0 %collective-permute-start.7 = (bf16[256,1024]{1,0:T(8,128)(2,1)}, bf16[256,1024]{1,0:T(8,128)(2,1)}, u32[]{:S(2)}, u32[]{:S(2)}) collective-permute-start(bf16[256,1024]{1,0:T(8,128)(2,1)} %mixed_grad.3.g_ref.refs_3_), channel_id=1, source_target_pairs={{4,0},{8,4},{12,8},{5,1},{9,5},{13,9},{6,2},{10,6},{14,10},{7,3},{... | collective-permute-start | bytes 1572872 | tf_op jit(solution)/shard_map/ppermute | solution.py:26
  34.2 26.1 %collective-permute-start.5 = (bf16[512,1024]{1,0:T(8,128)(2,1)S(1)}, bf16[512,1024]{1,0:T(8,128)(2,1)S(1)}, u32[]{:S(2)}, u32[]{:S(2)}) collective-permute-start(bf16[512,1024]{1,0:T(8,128)(2,1)S(1)} %collective-permute-done.refs_1_), channel_id=1, source_target_pairs={{0,4},{4,8},{8,12},{1,5},{5,9},{9,13},{2,6},{6,10},{10,14},{3,7},{... | collective-permute-start | bytes 3145736 | tf_op jit(solution)/shard_map/ppermute | solution.py:26
  38.6 26.4 %collective-permute-start.6 = (bf16[256,1024]{1,0:T(8,128)(2,1)}, bf16[256,1024]{1,0:T(8,128)(2,1)}, u32[]{:S(2)}, u32[]{:S(2)}) collective-permute-start(bf16[256,1024]{1,0:T(8,128)(2,1)} %copy-done.7), channel_id=1, source_target_pairs={{4,0},{8,4},{12,8},{5,1},{9,5},{13,9},{6,2},{10,6},{14,10},{7,3},{... | collective-permute-start | bytes 1572872 | tf_op jit(solution)/shard_map/ppermute | solution.py:26
  44.2 21.7 %collective-permute-start.8 = (bf16[256,1024]{1,0:T(8,128)(2,1)}, bf16[256,1024]{1,0:T(8,128)(2,1)}, u32[]{:S(2)}, u32[]{:S(2)}) collective-permute-start(bf16[256,1024]{1,0:T(8,128)(2,1)} %collective-permute-done.7.refs_4_), channel_id=1, source_target_pairs={{4,0},{8,4},{12,8},{5,1},{9,5},{13,9},{6,2},{10,6},{14,10},{7,3},{... | collective-permute-start | bytes 1572872 | tf_op jit(solution)/shard_map/ppermute | solution.py:26
  72.7 6.2 %collective-permute-start.9 = (bf16[2,256,1024]{2,1,0:T(8,128)(2,1)}, bf16[2,256,1024]{2,1,0:T(8,128)(2,1)}, u32[]{:S(2)}, u32[]{:S(2)}) collective-permute-start(bf16[2,256,1024]{2,1,0:T(8,128)(2,1)} %get-tuple-element.34), channel_id=1, source_target_pairs={{0,1},{1,0},{2,3},{3,2},{4,5},{5,4},{6,7},{7,6},{8,9},{9,8},{10,11... | collective-permute-start | bytes 3145736 | tf_op jit(solution)/shard_map/ppermute | solution.py:37
  74.2 27.9 %collective-permute-start.13 = (bf16[256,1024]{1,0:T(8,128)(2,1)S(1)}, bf16[256,1024]{1,0:T(8,128)(2,1)S(1)}, u32[]{:S(2)}, u32[]{:S(2)}) collective-permute-start(bf16[256,1024]{1,0:T(8,128)(2,1)S(1)} %copy-done.2), channel_id=1, source_target_pairs={{0,12},{4,0},{8,4},{12,8},{1,13},{5,1},{9,5},{13,9},{2,14},{6,2},{... | collective-permute-start | bytes 1572872 | tf_op jit(solution)/shard_map/ppermute | solution.py:33
  78.1 24.6 %collective-permute-start.12 = (bf16[256,1024]{1,0:T(8,128)(2,1)S(1)}, bf16[256,1024]{1,0:T(8,128)(2,1)S(1)}, u32[]{:S(2)}, u32[]{:S(2)}) collective-permute-start(bf16[256,1024]{1,0:T(8,128)(2,1)S(1)} %copy-done.2), channel_id=1, source_target_pairs={{0,4},{4,8},{8,12},{12,0},{1,5},{5,9},{9,13},{13,1},{2,6},{6,10},{... | collective-permute-start | bytes 1572872 | tf_op jit(solution)/shard_map/ppermute | solution.py:33
  78.1 24.6 %collective-permute-start.11 = (bf16[256,1024]{1,0:T(8,128)(2,1)S(1)}, bf16[256,1024]{1,0:T(8,128)(2,1)S(1)}, u32[]{:S(2)}, u32[]{:S(2)}) collective-permute-start(bf16[256,1024]{1,0:T(8,128)(2,1)S(1)} %select_select_fusion), channel_id=1, source_target_pairs={{0,0},{1,9},{2,6},{3,15},{4,4},{5,13},{6,10},{7,3},{8,8},{9,1},{10... | collective-permute-start | bytes 1572872 | tf_op jit(solution)/shard_map/ppermute | solution.py:420
  80.2 12.5 %collective-permute-start.10 = (bf16[256,1024]{1,0:T(8,128)(2,1)S(1)}, bf16[256,1024]{1,0:T(8,128)(2,1)S(1)}, u32[]{:S(2)}, u32[]{:S(2)}) collective-permute-start(bf16[256,1024]{1,0:T(8,128)(2,1)S(1)} %fusion.1), channel_id=1, source_target_pairs={{0,2},{2,0},{1,3},{3,1},{4,6},{6,4},{5,7},{7,5},{8,10},{10,8},{9,1... | collective-permute-start | bytes 1572872 | tf_op jit(solution)/shard_map/ppermute | solution.py:37
  88.8 28.7 %copy-start.3 = (bf16[256,1024]{1,0:T(8,128)(2,1)S(1)}, bf16[256,1024]{1,0:T(8,128)(2,1)}, u32[]{:S(2)}) copy-start(bf16[256,1024]{1,0:T(8,128)(2,1)} %k_ref) | copy-start | bytes 1572868
  88.8 28.7 %copy-start.4 = (bf16[256,1024]{1,0:T(8,128)(2,1)S(1)}, bf16[256,1024]{1,0:T(8,128)(2,1)}, u32[]{:S(2)}) copy-start(bf16[256,1024]{1,0:T(8,128)(2,1)} %v_ref.1) | copy-start | bytes 1572868
  88.8 28.8 %copy-start.8 = (bf16[256,1024]{1,0:T(8,128)(2,1)S(1)}, bf16[256,1024]{1,0:T(8,128)(2,1)}, u32[]{:S(2)}) copy-start(bf16[256,1024]{1,0:T(8,128)(2,1)} %copy-done.7) | copy-start | bytes 1572868
  88.8 13.4 %collective-permute-start.14 = (f32[24,256]{1,0:T(8,128)S(1)}, f32[24,256]{1,0:T(8,128)S(1)}, u32[]{:S(2)}, u32[]{:S(2)}) collective-permute-start(f32[24,256]{1,0:T(8,128)S(1)} %get-tuple-element.39.refs_6_), channel_id=1, source_target_pairs={{4,0},{8,4},{12,8},{5,1},{9,5},{13,9},{6,2},{10,6},{14,10},{7,3},{... | collective-permute-start | bytes 73736 | tf_op jit(solution)/shard_map/ppermute | solution.py:26
  102.7 14.8 %collective-permute-start.15 = (f32[24,256]{1,0:T(8,128)S(1)}, f32[24,256]{1,0:T(8,128)S(1)}, u32[]{:S(2)}, u32[]{:S(2)}) collective-permute-start(f32[24,256]{1,0:T(8,128)S(1)} %collective-permute-done.14.refs_7_), channel_id=1, source_target_pairs={{4,0},{8,4},{12,8},{5,1},{9,5},{13,9},{6,2},{10,6},{14,10},{7,3},{... | collective-permute-start | bytes 73736 | tf_op jit(solution)/shard_map/ppermute | solution.py:26
  104.0 23.6 %collective-permute-start.16 = (bf16[256,1024]{1,0:T(8,128)(2,1)S(1)}, bf16[256,1024]{1,0:T(8,128)(2,1)S(1)}, u32[]{:S(2)}, u32[]{:S(2)}) collective-permute-start(bf16[256,1024]{1,0:T(8,128)(2,1)S(1)} %collective-permute-done.11), channel_id=1, source_target_pairs={{0,2},{2,0},{1,3},{3,1},{4,6},{6,4},{5,7},{7,5},{8,10},{10,8},{9,1... | collective-permute-start | bytes 1572872 | tf_op jit(solution)/shard_map/ppermute | solution.py:37
  115.5 12.1 %collective-permute-start.17 = (bf16[256,1024]{1,0:T(8,128)(2,1)S(1)}, bf16[256,1024]{1,0:T(8,128)(2,1)S(1)}, u32[]{:S(2)}, u32[]{:S(2)}) collective-permute-start(bf16[256,1024]{1,0:T(8,128)(2,1)S(1)} %collective-permute-done.12.refs_2_), channel_id=1, source_target_pairs={{4,8},{8,12},{5,9},{9,13},{6,10},{10,14},{7,11},{11,15},{20,24},{2... | collective-permute-start | bytes 1572872 | tf_op jit(solution)/shard_map/ppermute | solution.py:455
  116.2 16.5 %collective-permute-start.18 = (bf16[256,1024]{1,0:T(8,128)(2,1)S(1)}, bf16[256,1024]{1,0:T(8,128)(2,1)S(1)}, u32[]{:S(2)}, u32[]{:S(2)}) collective-permute-start(bf16[256,1024]{1,0:T(8,128)(2,1)S(1)} %collective-permute-done.13.refs_3_), channel_id=1, source_target_pairs={{4,0},{8,4},{5,1},{9,5},{6,2},{10,6},{7,3},{11,7},{20,16},{24,20},... | collective-permute-start | bytes 1572872 | tf_op jit(solution)/shard_map/ppermute | solution.py:456
  132.7 1.9 %collective-permute-start.19 = (bf16[256,1024]{1,0:T(8,128)(2,1)S(1)}, bf16[256,1024]{1,0:T(8,128)(2,1)S(1)}, u32[]{:S(2)}, u32[]{:S(2)}) collective-permute-start(bf16[256,1024]{1,0:T(8,128)(2,1)S(1)} %collective-permute-done.11), channel_id=1, source_target_pairs={{0,1},{1,0},{2,3},{3,2},{4,5},{5,4},{6,7},{7,6},{8,9},{9,8},{10,11... | collective-permute-start | bytes 1572872 | tf_op jit(solution)/shard_map/ppermute | solution.py:37
  132.7 2.7 %collective-permute-start.20 = (bf16[256,1024]{1,0:T(8,128)(2,1)S(1)}, bf16[256,1024]{1,0:T(8,128)(2,1)S(1)}, u32[]{:S(2)}, u32[]{:S(2)}) collective-permute-start(bf16[256,1024]{1,0:T(8,128)(2,1)S(1)} %collective-permute-done.16), channel_id=1, source_target_pairs={{0,1},{1,0},{2,3},{3,2},{4,5},{5,4},{6,7},{7,6},{8,9},{9,8},{10,11... | collective-permute-start | bytes 1572872 | tf_op jit(solution)/shard_map/ppermute | solution.py:37
  (9 other events, 62.2 us)

commit v11 on v10

--- a/solution.py
+++ b/solution.py
@@ -283,7 +283,7 @@
 
 
 VMEM_LIMIT = 20 * 1024 * 1024
-WEIGHTS = dict(mixed_grad=0.0, forward=0.0, partial=100.0, query=100.0, key=100.0, weight=0.0)
+WEIGHTS = dict(mixed_grad=0.0, forward=0.0, partial=0.0, query=100.0, key=100.0, weight=0.0)
 STREAM_LIMIT = 54 * 1024 * 1024
 
 
@@ -340,10 +340,10 @@
     ]
 
 
-def chip_sum(shares):
+def chip_sum(shares, *others):
     if len(shares) == 1:
         return lax.psum_scatter(shares[0], ("head", "rep"), scatter_dimension=1, tiled=True)
-    return (shares[0] + swap(shares[1], "head").astype(F32)).astype(BF16)
+    return (shares[0] + swap(after(shares[1], *others), "head").astype(F32)).astype(BF16)
 
 
 def per_device(queries, keys, values, out_weight, level_mask, cotangent):
@@ -436,19 +436,17 @@
         functools.partial(query_kernel, tiles, count, heads, heads_up),
         "attention_query_grad",
         [use],
-        [after(queries, mixed_heads, query_all[-1], grad_all[-1]), mixed_grad, lse, *kv_all],
+        [after(queries, mixed_heads), mixed_grad, lse, *kv_all],
         [like_queries, stats_shape],
         cost(3 * attention_flops, (2 * count + 3) * array_bytes, exps, WEIGHTS["query"]),
     )
-    stats_all = further([stats], -1)
+    stats_all = [stats] + [shift(stats, -d) for d in distances[1:]]
     partial_products = attended_partial(
         after(mixed_heads, query_all[-1], grad_all[-1]), out_weight, c_places, cost(2 * rows * columns * features, 2 * rows * features, 0, WEIGHTS["partial"])
     )
     shares = core_sum(partial_products)
-    attended = chip_sum(shares)
-    held = after(mixed_heads, arrived, *near.values(), *stats_all[1:], attended)
-    while len(stats_all) < count:
-        stats_all = further(stats_all, -1, held)
+    ct_across = swap(after(arrived, *partial_products), "head") if two_by_two() else arrived
+    held = after(mixed_heads, ct_across, *near.values(), *stats_all[1:], *shares)
     if peers <= 4:
         mixed_all = [[mixed_heads]] + [[near[k]] if k in near else [] for k in range(1, peers)]
         if peers == 4:
@@ -461,6 +459,7 @@
             [lax.dynamic_index_in_dim(gathered, (place - k) % peers, 0, False)]
             for k in range(peers)
         ]
+    attended = chip_sum(shares, held)
     k_grad, v_grad = kernel_call(
         functools.partial(key_kernel, tiles, count, heads, heads_up),
         "attention_key_grad",
@@ -471,10 +470,7 @@
     )
 
     if two_by_two():
-        ct_across = swap(after(arrived, held), "head")
-        far = [value for values in mixed_all for value in values]
-        beside = swap(after(arrived, ct_across, *far), "rep")
-        ct_blocks = [arrived, beside, *other_features(ct_across, *far, k_grad)]
+        ct_blocks = [arrived, swap(after(arrived, held), "rep"), *other_features(ct_across, held)]
     else:
         ct_blocks, ct_rest, _ = features_here(arrived)
         ct_blocks = ct_blocks + ct_rest
@@ -492,7 +488,7 @@
             break
         ranges = [value for k in which for value in mixed_all[k]]
         if part:
-            ranges[0] = after(ranges[0], k_grad)
+            ranges[0] = after(ranges[0], k_grad, attended)
         weight_sum = [
             kernel_call(
                 functools.partial(weight_grad_kernel, which, part),

time: 141 us -> 134 us (0.950)
  waiting for transfers between devices: 49.1 us -> 40.5 us
  starting transfers between devices: 40.7 us -> 42.9 us
    ppermute x8, waiting for transfers between devices: 9.77 us -> 4.72 us  [swap(): return lax.ppermute(value, axis, [(0, 1), (1, 0)])]
    ppermute x1, waiting for transfers between devices: 5.02 us -> 0.17 us  [per_device(): down = lax.ppermute(after(near[3], held), 'seq', [(1, 0), (2, 1)])]
    ppermute x1, starting transfers between devices: 0.86 us -> 5.37 us  [per_device(): lax.ppermute(after(out_block, grad_all[1], kv_all[-1]), ('seq', 'head', '...]
    ppermute x8, starting transfers between devices: 17.1 us -> 14 us  [swap(): return lax.ppermute(value, axis, [(0, 1), (1, 0)])]
    ppermute x8, waiting for transfers between devices: 33.7 us -> 35.6 us  [shift(): lax.ppermute(value, 'seq', [(i, i + by) for i in range(peers) if 0 <= i +...]
  transfers between devices with their start and end apart: 21 -> 21, of which waited for: 13 -> 9; matrix products, arithmetic and copies ran while one was open for 6% -> 7% of each run, Pallas kernels for 19% -> 27%
where the time goes in v11:
time: 134 us; the launch traced here: 133 us
  starting transfers between devices  42.9 us (32%)
  waiting for transfers between devices  40.5 us (30%)
  Pallas kernels  38.6 us (29%)
  other arithmetic  6.82 us (5%)
  local copies, waits for them, and re-layouts  3.34 us (2%)
    pallas_call x8, Pallas kernels, kernel_call(): pl.pallas_call(body, in_specs=[smem] * len(scalars) + [vmem] * len(arrays...  38.6 us
    ppermute x8, waiting for transfers between devices, shift(): lax.ppermute(value, 'seq', [(i, i + by) for i in range(peers) if 0 <= i +...  35.6 us
    ppermute x8, starting transfers between devices, shift(): lax.ppermute(value, 'seq', [(i, i + by) for i in range(peers) if 0 <= i +...  16.8 us
    ppermute x8, starting transfers between devices, swap(): return lax.ppermute(value, axis, [(0, 1), (1, 0)])  14 us
    ppermute x1, starting transfers between devices, per_device(): lax.ppermute(after(out_block, grad_all[1], kv_all[-1]), ('seq', 'head', '...  5.37 us
    ppermute x8, waiting for transfers between devices, swap(): return lax.ppermute(value, axis, [(0, 1), (1, 0)])  4.72 us
    ppermute x2, starting transfers between devices, cyclic(): lax.ppermute(value, 'seq', [(i, (i + by) % peers) for i in range(peers)])  4.59 us
  transfers between devices with their start and end apart: 21, of which 9 were waited for; matrix products, arithmetic and copies ran while one was open for 7% of the time, Pallas kernels for 27%

profile of v11, /device:TPU:0, one launch (start us, length us, event | category | flops | bytes accessed | tf_op | source)
XLA Modules:
  0.0 133.2 jit_solution(1635347039521868619)
XLA Ops:
  1.1 2.6 %collective-permute-start.2 = (bf16[256,1024]{1,0:T(8,128)(2,1)}, bf16[256,1024]{1,0:T(8,128)(2,1)S(1)}, u32[]{:S(2)}, u32[]{:S(2)}) collective-permute-start(bf16[256,1024]{1,0:T(8,128)(2,1)} %refs_0_.2), channel_id=1, source_target_pairs={{0,2},{2,0},{1,3},{3,1},{4,6},{6,4},{5,7},{7,5},{8,10},{10,8},{9,1... | collective-permute-start | bytes 1572872 | tf_op jit(solution)/shard_map/ppermute | solution.py:37
  7.2 4.6 %collective-permute-start = (bf16[512,1024]{1,0:T(8,128)(2,1)S(1)}, bf16[512,1024]{1,0:T(8,128)(2,1)S(1)}, u32[]{:S(2)}, u32[]{:S(2)}) collective-permute-start(bf16[512,1024]{1,0:T(8,128)(2,1)S(1)} %constant_dynamic-update-slice_fusion.refs_0_), channel_id=1, source_target_pairs={{0,4},{4,8},{8,12},{1,5},{5,9},{9,13},{2,6},{6,10},{10,14},{3,7},{... | collective-permute-start | bytes 3145736 | tf_op jit(solution)/shard_map/ppermute | solution.py:26
  12.4 5.7 %mixed_grad.2.refs_0_ = f32[256,1024]{1,0:T(8,128)} custom-call(s32[2]{0:T(128)} %pad_add_fusion.2.place_ref, bf16[256,1024]{1,0:T(8,128)(2,1)} %refs_0_.2, bf16[256,1024]{1,0:T(8,128)(2,1)} %collective-permute-done.1.refs_1_, bf16[4096,1024]{1,0:T(8,128)(2,1)} %w_ref.1), custom_call_target="tpu_custom_call" | custom-call | tf_op jit(solution)/shard_map/mixed_grad/pallas_call | solution.py:265
  18.1 1.7 %collective-permute-done.3.refs_1_ = bf16[256,1024]{1,0:T(8,128)(2,1)S(1)} collective-permute-done((bf16[256,1024]{1,0:T(8,128)(2,1)}, bf16[256,1024]{1,0:T(8,128)(2,1)S(1)}, u32[]{:S(2)}, u32[]{:S(2)}) %collective-permute-start.3) | collective-permute-done | bytes 524320 | tf_op jit(solution)/shard_map/ppermute | solution.py:26
  21.9 5.3 %mixed_grad.3.g_ref.refs_3_ = bf16[256,1024]{1,0:T(8,128)(2,1)} custom-call(s32[2]{0:T(128)} %pad_add_fusion.1.place_ref, f32[256,1024]{1,0:T(8,128)} %mixed_grad.2.refs_0_, bf16[256,1024]{1,0:T(8,128)(2,1)} %copy-done.9, bf16[256,1024]{1,0:T(8,128)(2,1)} %collective-permute-done.4.refs_2_, bf16[4096,1024]{1,0:T(8,128)(2,1)} %w_ref.1), custom_call_target="tpu_custom_call" | custom-call | tf_op jit(solution)/shard_map/mixed_grad/pallas_call | solution.py:265
  27.2 7.0 %collective-permute-done.refs_1_ = bf16[512,1024]{1,0:T(8,128)(2,1)S(1)} collective-permute-done((bf16[512,1024]{1,0:T(8,128)(2,1)S(1)}, bf16[512,1024]{1,0:T(8,128)(2,1)S(1)}, u32[]{:S(2)}, u32[]{:S(2)}) %collective-permute-start) | collective-permute-done | bytes 1048608 | tf_op jit(solution)/shard_map/ppermute | solution.py:26
  34.2 4.4 %collective-permute-start.5 = (bf16[512,1024]{1,0:T(8,128)(2,1)S(1)}, bf16[512,1024]{1,0:T(8,128)(2,1)S(1)}, u32[]{:S(2)}, u32[]{:S(2)}) collective-permute-start(bf16[512,1024]{1,0:T(8,128)(2,1)S(1)} %collective-permute-done.refs_1_), channel_id=1, source_target_pairs={{0,4},{4,8},{8,12},{1,5},{5,9},{9,13},{2,6},{6,10},{10,14},{3,7},{... | collective-permute-start | bytes 3145736 | tf_op jit(solution)/shard_map/ppermute | solution.py:26
  41.3 2.0 %select_select_fusion = bf16[256,1024]{1,0:T(8,128)(2,1)} fusion(bf16[256,1024]{1,0:T(8,128)(2,1)} %collective-permute-done.4.refs_2_, bf16[256,1024]{1,0:T(8,128)(2,1)} %copy-done.9, bf16[256,1024]{1,0:T(8,128)(2,1)} %collective-permute-done.1.refs_1_, bf16[256,1024]{1,0:T(8,128)(2,1)} %refs_0_.2, pred[]{:T(512)S(6)} %eq.33, pred[]{:T(512)S(6)} %eq.32, ...), kind=kLoop, calls=%fused_computation.5 | loop fusion | flops 786432 | bytes 2621443 | tf_op jit(solution)/shard_map/jit(_where)/select_n | solution.py:415
  43.3 12.4 %collective-permute-done.7.refs_4_ = bf16[256,1024]{1,0:T(8,128)(2,1)} collective-permute-done((bf16[256,1024]{1,0:T(8,128)(2,1)}, bf16[256,1024]{1,0:T(8,128)(2,1)}, u32[]{:S(2)}, u32[]{:S(2)}) %collective-permute-start.7) | collective-permute-done | bytes 524320 | tf_op jit(solution)/shard_map/ppermute | solution.py:26
  57.0 3.2 %collective-permute-done.5.refs_2_ = bf16[512,1024]{1,0:T(8,128)(2,1)S(1)} collective-permute-done((bf16[512,1024]{1,0:T(8,128)(2,1)S(1)}, bf16[512,1024]{1,0:T(8,128)(2,1)S(1)}, u32[]{:S(2)}, u32[]{:S(2)}) %collective-permute-start.5) | collective-permute-done | bytes 1048608 | tf_op jit(solution)/shard_map/ppermute | solution.py:26
  60.1 5.4 %collective-permute-start.10 = (bf16[256,1024]{1,0:T(8,128)(2,1)}, bf16[256,1024]{1,0:T(8,128)(2,1)}, u32[]{:S(2)}, u32[]{:S(2)}) collective-permute-start(bf16[256,1024]{1,0:T(8,128)(2,1)} %select_select_fusion), channel_id=1, source_target_pairs={{0,0},{1,9},{2,6},{3,15},{4,4},{5,13},{6,10},{7,3},{8,8},{9,1},{10... | collective-permute-start | bytes 1572872 | tf_op jit(solution)/shard_map/ppermute | solution.py:420
  67.5 3.0 %attention_forward.1 = (bf16[256,1024]{1,0:T(8,128)(2,1)S(1)}, f32[8,256]{1,0:T(8,128)S(1)}) custom-call(s32[10]{0:T(128)S(1)} %reshape.264.use_ref, bf16[256,1024]{1,0:T(8,128)(2,1)S(1)} %copy-done.5, bf16[512,1024]{1,0:T(8,128)(2,1)S(1)} %constant_dynamic-update-slice_fusion.refs_0_, bf16[512,1024]{1,0:T(8,128)(2,1)S(1)} %collective-permute-done.refs_1_, ...), custom_call_target="tpu_custom_call" | custom-call | tf_op jit(solution)/shard_map/attention_forward/pallas_call | solution.py:265
  70.5 4.6 %collective-permute-start.13 = (bf16[256,1024]{1,0:T(8,128)(2,1)S(1)}, bf16[256,1024]{1,0:T(8,128)(2,1)S(1)}, u32[]{:S(2)}, u32[]{:S(2)}) collective-permute-start(bf16[256,1024]{1,0:T(8,128)(2,1)S(1)} %get-tuple-element.40.m_ref.refs_1_), channel_id=1, source_target_pairs={{0,12},{4,0},{8,4},{12,8},{1,13},{5,1},{9,5},{13,9},{2,14},{6,2},{... | collective-permute-start | bytes 1572872 | tf_op jit(solution)/shard_map/ppermute | solution.py:33
  75.1 4.6 %collective-permute-done.8.refs_5_ = bf16[256,1024]{1,0:T(8,128)(2,1)} collective-permute-done((bf16[256,1024]{1,0:T(8,128)(2,1)}, bf16[256,1024]{1,0:T(8,128)(2,1)}, u32[]{:S(2)}, u32[]{:S(2)}) %collective-permute-start.8) | collective-permute-done | bytes 524320 | tf_op jit(solution)/shard_map/ppermute | solution.py:26
  79.7 6.9 %attended_partial.1 = (bf16[2,256,1024]{2,1,0:T(8,128)(2,1)}, bf16[2,256,1024]{2,1,0:T(8,128)(2,1)}) custom-call(s32[4]{0:T(128)} %pad_add_fusion.place_ref, bf16[256,1024]{1,0:T(8,128)(2,1)} %copy-done, bf16[4096,1024]{1,0:T(8,128)(2,1)} %w_ref.1), custom_call_target="tpu_custom_call" | custom-call | tf_op jit(solution)/shard_map/attended_partial/pallas_call | solution.py:265
  86.7 5.2 %collective-permute-start.11 = (bf16[256,1024]{1,0:T(8,128)(2,1)}, bf16[256,1024]{1,0:T(8,128)(2,1)S(1)}, u32[]{:S(2)}, u32[]{:S(2)}) collective-permute-start(bf16[256,1024]{1,0:T(8,128)(2,1)} %collective-permute-done.10), channel_id=1, source_target_pairs={{0,2},{2,0},{1,3},{3,1},{4,6},{6,4},{5,7},{7,5},{8,10},{10,8},{9,1... | collective-permute-start | bytes 1572872 | tf_op jit(solution)/shard_map/ppermute | solution.py:37
  92.0 6.6 %attention_query_grad.1 = (bf16[256,1024]{1,0:T(8,128)(2,1)}, f32[24,256]{1,0:T(8,128)S(1)}) custom-call(s32[10]{0:T(128)S(1)} %reshape.264.use_ref, bf16[256,1024]{1,0:T(8,128)(2,1)S(1)} %copy-done.6, bf16[256,1024]{1,0:T(8,128)(2,1)S(1)} %copy-done.2, f32[8,256]{1,0:T(8,128)S(1)} %get-tuple-element.38.lse_ref, ...), custom_call_target="tpu_custom_call" | custom-call | flops 80530636800 | bytes 471859200 | tf_op jit(solution)/shard_map/attention_query_grad/pallas_call | solution.py:265
  101.4 6.7 %collective-permute-done.15.refs_8_ = f32[24,256]{1,0:T(8,128)S(1)} collective-permute-done((f32[24,256]{1,0:T(8,128)S(1)}, f32[24,256]{1,0:T(8,128)S(1)}, u32[]{:S(2)}, u32[]{:S(2)}) %collective-permute-start.15) | collective-permute-done | bytes 24608 | tf_op jit(solution)/shard_map/ppermute | solution.py:26
  108.2 5.0 %collective-permute-start.16 = (bf16[256,1024]{1,0:T(8,128)(2,1)S(1)}, bf16[256,1024]{1,0:T(8,128)(2,1)S(1)}, u32[]{:S(2)}, u32[]{:S(2)}) collective-permute-start(bf16[256,1024]{1,0:T(8,128)(2,1)S(1)} %fusion), channel_id=1, source_target_pairs={{0,2},{2,0},{1,3},{3,1},{4,6},{6,4},{5,7},{7,5},{8,10},{10,8},{9,1... | collective-permute-start | bytes 1572872 | tf_op jit(solution)/shard_map/ppermute | solution.py:37
  114.4 1.5 %collective-permute-start.20 = (bf16[256,1024]{1,0:T(8,128)(2,1)S(1)}, bf16[256,1024]{1,0:T(8,128)(2,1)S(1)}, u32[]{:S(2)}, u32[]{:S(2)}) collective-permute-start(bf16[256,1024]{1,0:T(8,128)(2,1)S(1)} %collective-permute-done.13.refs_3_), channel_id=1, source_target_pairs={{4,0},{8,4},{5,1},{9,5},{6,2},{10,6},{7,3},{11,7},{20,16},{24,20},... | collective-permute-start | bytes 1572872 | tf_op jit(solution)/shard_map/ppermute | solution.py:454
  115.9 6.1 %attention_key_grad.1 = (bf16[256,1024]{1,0:T(8,128)(2,1)}, bf16[256,1024]{1,0:T(8,128)(2,1)}) custom-call(bf16[256,1024]{1,0:T(8,128)(2,1)S(1)} %copy-done.3, bf16[256,1024]{1,0:T(8,128)(2,1)S(1)} %copy-done.4, bf16[256,1024]{1,0:T(8,128)(2,1)S(1)} %copy-done.6, bf16[256,1024]{1,0:T(8,128)(2,1)S(1)} %copy-done.8, ...), custom_call_target="tpu_custom_call" | custom-call | flops 107374182400 | bytes 524288000 | tf_op jit(solution)/shard_map/attention_key_grad/pallas_call | solution.py:265
  122.0 3.5 %collective-permute-done.16 = bf16[256,1024]{1,0:T(8,128)(2,1)S(1)} collective-permute-done((bf16[256,1024]{1,0:T(8,128)(2,1)S(1)}, bf16[256,1024]{1,0:T(8,128)(2,1)S(1)}, u32[]{:S(2)}, u32[]{:S(2)}) %collective-permute-start.16) | collective-permute-done | bytes 524320 | tf_op jit(solution)/shard_map/ppermute | solution.py:37
  127.9 2.4 %weight_grad.2.refs_0_ = f32[1024,1024]{1,0:T(8,128)S(1)} custom-call(s32[4]{0:T(128)S(1)} %select_reduce_fusion.place_ref, bf16[4,256,1024]{2,1,0:T(8,128)(2,1)S(1)} %pad_maximum_fusion.refs_0_.refs_1_, bf16[256,1024]{1,0:T(8,128)(2,1)S(1)} %copy-done.1, bf16[256,1024]{1,0:T(8,128)(2,1)S(1)} %collective-permute-done.12.refs_2_, ...), custom_call_target="tpu_custom_call" | custom-call | tf_op jit(solution)/shard_map/weight_grad/pallas_call | solution.py:265
  130.5 2.7 %weight_grad.3 = bf16[1024,1024]{1,0:T(8,128)(2,1)} custom-call(s32[4]{0:T(128)S(1)} %select_reduce_fusion.place_ref, f32[1024,1024]{1,0:T(8,128)S(1)} %weight_grad.2.refs_0_, bf16[4,256,1024]{2,1,0:T(8,128)(2,1)S(1)} %pad_maximum_fusion.refs_0_.refs_1_, bf16[256,1024]{1,0:T(8,128)(2,1)S(1)} %collective-permute-done.19.refs_2_, ...), custom_call_target="tpu_custom_call" | custom-call | tf_op jit(solution)/shard_map/weight_grad/pallas_call | solution.py:265
  (65 shorter events, 19.2 us)
Async XLA Ops:
  0.6 11.8 %collective-permute-start.1 = (bf16[256,1024]{1,0:T(8,128)(2,1)}, bf16[256,1024]{1,0:T(8,128)(2,1)}, u32[]{:S(2)}, u32[]{:S(2)}) collective-permute-start(bf16[256,1024]{1,0:T(8,128)(2,1)} %refs_0_.2), channel_id=1, source_target_pairs={{0,1},{1,0},{2,3},{3,2},{4,5},{5,4},{6,7},{7,6},{8,9},{9,8},{10,11... | collective-permute-start | bytes 1572872 | tf_op jit(solution)/shard_map/ppermute | solution.py:37
  1.1 18.7 %collective-permute-start.2 = (bf16[256,1024]{1,0:T(8,128)(2,1)}, bf16[256,1024]{1,0:T(8,128)(2,1)S(1)}, u32[]{:S(2)}, u32[]{:S(2)}) collective-permute-start(bf16[256,1024]{1,0:T(8,128)(2,1)} %refs_0_.2), channel_id=1, source_target_pairs={{0,2},{2,0},{1,3},{3,1},{4,6},{6,4},{5,7},{7,5},{8,10},{10,8},{9,1... | collective-permute-start | bytes 1572872 | tf_op jit(solution)/shard_map/ppermute | solution.py:37
  3.7 16.1 %collective-permute-start.3 = (bf16[256,1024]{1,0:T(8,128)(2,1)}, bf16[256,1024]{1,0:T(8,128)(2,1)S(1)}, u32[]{:S(2)}, u32[]{:S(2)}) collective-permute-start(bf16[256,1024]{1,0:T(8,128)(2,1)} %refs_0_.3), channel_id=1, source_target_pairs={{4,0},{8,4},{12,8},{5,1},{9,5},{13,9},{6,2},{10,6},{14,10},{7,3},{... | collective-permute-start | bytes 1572872 | tf_op jit(solution)/shard_map/ppermute | solution.py:26
  7.2 27.0 %collective-permute-start = (bf16[512,1024]{1,0:T(8,128)(2,1)S(1)}, bf16[512,1024]{1,0:T(8,128)(2,1)S(1)}, u32[]{:S(2)}, u32[]{:S(2)}) collective-permute-start(bf16[512,1024]{1,0:T(8,128)(2,1)S(1)} %constant_dynamic-update-slice_fusion.refs_0_), channel_id=1, source_target_pairs={{0,4},{4,8},{8,12},{1,5},{5,9},{9,13},{2,6},{6,10},{10,14},{3,7},{... | collective-permute-start | bytes 3145736 | tf_op jit(solution)/shard_map/ppermute | solution.py:26
  19.8 2.1 %collective-permute-start.4 = (bf16[256,1024]{1,0:T(8,128)(2,1)S(1)}, bf16[256,1024]{1,0:T(8,128)(2,1)}, u32[]{:S(2)}, u32[]{:S(2)}) collective-permute-start(bf16[256,1024]{1,0:T(8,128)(2,1)S(1)} %collective-permute-done.2.refs_1_), channel_id=1, source_target_pairs={{0,1},{1,0},{2,3},{3,2},{4,5},{5,4},{6,7},{7,6},{8,9},{9,8},{10,11... | collective-permute-start | bytes 1572872 | tf_op jit(solution)/shard_map/ppermute | solution.py:37
  27.2 38.3 %copy-start.11 = (s32[2,5]{1,0:T(2,128)S(1)}, s32[2,5]{1,0:T(2,128)}, u32[]{:S(2)}) copy-start(s32[2,5]{1,0:T(2,128)} %param.10) | copy-start | bytes 124
  34.2 26.0 %collective-permute-start.5 = (bf16[512,1024]{1,0:T(8,128)(2,1)S(1)}, bf16[512,1024]{1,0:T(8,128)(2,1)S(1)}, u32[]{:S(2)}, u32[]{:S(2)}) collective-permute-start(bf16[512,1024]{1,0:T(8,128)(2,1)S(1)} %collective-permute-done.refs_1_), channel_id=1, source_target_pairs={{0,4},{4,8},{8,12},{1,5},{5,9},{9,13},{2,6},{6,10},{10,14},{3,7},{... | collective-permute-start | bytes 3145736 | tf_op jit(solution)/shard_map/ppermute | solution.py:26
  38.6 17.1 %collective-permute-start.7 = (bf16[256,1024]{1,0:T(8,128)(2,1)}, bf16[256,1024]{1,0:T(8,128)(2,1)}, u32[]{:S(2)}, u32[]{:S(2)}) collective-permute-start(bf16[256,1024]{1,0:T(8,128)(2,1)} %mixed_grad.3.g_ref.refs_3_), channel_id=1, source_target_pairs={{4,0},{8,4},{12,8},{5,1},{9,5},{13,9},{6,2},{10,6},{14,10},{7,3},{... | collective-permute-start | bytes 1572872 | tf_op jit(solution)/shard_map/ppermute | solution.py:26
  40.0 35.1 %collective-permute-start.6 = (bf16[256,1024]{1,0:T(8,128)(2,1)}, bf16[256,1024]{1,0:T(8,128)(2,1)}, u32[]{:S(2)}, u32[]{:S(2)}) collective-permute-start(bf16[256,1024]{1,0:T(8,128)(2,1)} %copy-done.7), channel_id=1, source_target_pairs={{4,0},{8,4},{12,8},{5,1},{9,5},{13,9},{6,2},{10,6},{14,10},{7,3},{... | collective-permute-start | bytes 1572872 | tf_op jit(solution)/shard_map/ppermute | solution.py:26
  55.7 24.0 %collective-permute-start.8 = (bf16[256,1024]{1,0:T(8,128)(2,1)}, bf16[256,1024]{1,0:T(8,128)(2,1)}, u32[]{:S(2)}, u32[]{:S(2)}) collective-permute-start(bf16[256,1024]{1,0:T(8,128)(2,1)} %collective-permute-done.7.refs_4_), channel_id=1, source_target_pairs={{4,0},{8,4},{12,8},{5,1},{9,5},{13,9},{6,2},{10,6},{14,10},{7,3},{... | collective-permute-start | bytes 1572872 | tf_op jit(solution)/shard_map/ppermute | solution.py:26
  60.1 26.6 %collective-permute-start.10 = (bf16[256,1024]{1,0:T(8,128)(2,1)}, bf16[256,1024]{1,0:T(8,128)(2,1)}, u32[]{:S(2)}, u32[]{:S(2)}) collective-permute-start(bf16[256,1024]{1,0:T(8,128)(2,1)} %select_select_fusion), channel_id=1, source_target_pairs={{0,0},{1,9},{2,6},{3,15},{4,4},{5,13},{6,10},{7,3},{8,8},{9,1},{10... | collective-permute-start | bytes 1572872 | tf_op jit(solution)/shard_map/ppermute | solution.py:420
  70.5 37.6 %collective-permute-start.13 = (bf16[256,1024]{1,0:T(8,128)(2,1)S(1)}, bf16[256,1024]{1,0:T(8,128)(2,1)S(1)}, u32[]{:S(2)}, u32[]{:S(2)}) collective-permute-start(bf16[256,1024]{1,0:T(8,128)(2,1)S(1)} %get-tuple-element.40.m_ref.refs_1_), channel_id=1, source_target_pairs={{0,12},{4,0},{8,4},{12,8},{1,13},{5,1},{9,5},{13,9},{2,14},{6,2},{... | collective-permute-start | bytes 1572872 | tf_op jit(solution)/shard_map/ppermute | solution.py:33
  75.1 33.1 %collective-permute-start.12 = (bf16[256,1024]{1,0:T(8,128)(2,1)S(1)}, bf16[256,1024]{1,0:T(8,128)(2,1)S(1)}, u32[]{:S(2)}, u32[]{:S(2)}) collective-permute-start(bf16[256,1024]{1,0:T(8,128)(2,1)S(1)} %get-tuple-element.40.m_ref.refs_1_), channel_id=1, source_target_pairs={{0,4},{4,8},{8,12},{12,0},{1,5},{5,9},{9,13},{13,1},{2,6},{6,10},{... | collective-permute-start | bytes 1572872 | tf_op jit(solution)/shard_map/ppermute | solution.py:33
  86.6 13.3 %collective-permute-start.9 = (bf16[2,256,1024]{2,1,0:T(8,128)(2,1)}, bf16[2,256,1024]{2,1,0:T(8,128)(2,1)S(1)}, u32[]{:S(2)}, u32[]{:S(2)}) collective-permute-start(bf16[2,256,1024]{2,1,0:T(8,128)(2,1)} %get-tuple-element.34), channel_id=1, source_target_pairs={{0,1},{1,0},{2,3},{3,2},{4,5},{5,4},{6,7},{7,6},{8,9},{9,8},{10,11... | collective-permute-start | bytes 3145736 | tf_op jit(solution)/shard_map/ppermute | solution.py:37
  86.7 21.5 %collective-permute-start.11 = (bf16[256,1024]{1,0:T(8,128)(2,1)}, bf16[256,1024]{1,0:T(8,128)(2,1)S(1)}, u32[]{:S(2)}, u32[]{:S(2)}) collective-permute-start(bf16[256,1024]{1,0:T(8,128)(2,1)} %collective-permute-done.10), channel_id=1, source_target_pairs={{0,2},{2,0},{1,3},{3,1},{4,6},{6,4},{5,7},{7,5},{8,10},{10,8},{9,1... | collective-permute-start | bytes 1572872 | tf_op jit(solution)/shard_map/ppermute | solution.py:37
  91.9 24.0 %copy-start.4 = (bf16[256,1024]{1,0:T(8,128)(2,1)S(1)}, bf16[256,1024]{1,0:T(8,128)(2,1)}, u32[]{:S(2)}) copy-start(bf16[256,1024]{1,0:T(8,128)(2,1)} %v_ref.1) | copy-start | bytes 1572868
  92.0 24.0 %copy-start.8 = (bf16[256,1024]{1,0:T(8,128)(2,1)S(1)}, bf16[256,1024]{1,0:T(8,128)(2,1)}, u32[]{:S(2)}) copy-start(bf16[256,1024]{1,0:T(8,128)(2,1)} %copy-done.7) | copy-start | bytes 1572868
  98.6 9.5 %collective-permute-start.15 = (f32[24,256]{1,0:T(8,128)S(1)}, f32[24,256]{1,0:T(8,128)S(1)}, u32[]{:S(2)}, u32[]{:S(2)}) collective-permute-start(f32[24,256]{1,0:T(8,128)S(1)} %get-tuple-element.39.refs_6_), channel_id=1, source_target_pairs={{8,0},{12,4},{9,1},{13,5},{10,2},{14,6},{11,3},{15,7},{24,16},{28,... | collective-permute-start | bytes 73736 | tf_op jit(solution)/shard_map/ppermute | solution.py:26
  99.9 8.2 %collective-permute-start.14 = (f32[24,256]{1,0:T(8,128)S(1)}, f32[24,256]{1,0:T(8,128)S(1)}, u32[]{:S(2)}, u32[]{:S(2)}) collective-permute-start(f32[24,256]{1,0:T(8,128)S(1)} %get-tuple-element.39.refs_6_), channel_id=1, source_target_pairs={{4,0},{8,4},{12,8},{5,1},{9,5},{13,9},{6,2},{10,6},{14,10},{7,3},{... | collective-permute-start | bytes 73736 | tf_op jit(solution)/shard_map/ppermute | solution.py:26
  108.2 17.3 %collective-permute-start.16 = (bf16[256,1024]{1,0:T(8,128)(2,1)S(1)}, bf16[256,1024]{1,0:T(8,128)(2,1)S(1)}, u32[]{:S(2)}, u32[]{:S(2)}) collective-permute-start(bf16[256,1024]{1,0:T(8,128)(2,1)S(1)} %fusion), channel_id=1, source_target_pairs={{0,2},{2,0},{1,3},{3,1},{4,6},{6,4},{5,7},{7,5},{8,10},{10,8},{9,1... | collective-permute-start | bytes 1572872 | tf_op jit(solution)/shard_map/ppermute | solution.py:37
  113.2 13.4 %collective-permute-start.17 = (bf16[256,1024]{1,0:T(8,128)(2,1)}, bf16[256,1024]{1,0:T(8,128)(2,1)S(1)}, u32[]{:S(2)}, u32[]{:S(2)}) collective-permute-start(bf16[256,1024]{1,0:T(8,128)(2,1)} %collective-permute-done.10), channel_id=1, source_target_pairs={{0,1},{1,0},{2,3},{3,2},{4,5},{5,4},{6,7},{7,6},{8,9},{9,8},{10,11... | collective-permute-start | bytes 1572872 | tf_op jit(solution)/shard_map/ppermute | solution.py:37
  113.2 13.4 %collective-permute-start.18 = (bf16[256,1024]{1,0:T(8,128)(2,1)S(1)}, bf16[256,1024]{1,0:T(8,128)(2,1)S(1)}, u32[]{:S(2)}, u32[]{:S(2)}) collective-permute-start(bf16[256,1024]{1,0:T(8,128)(2,1)S(1)} %collective-permute-done.11), channel_id=1, source_target_pairs={{0,1},{1,0},{2,3},{3,2},{4,5},{5,4},{6,7},{7,6},{8,9},{9,8},{10,11... | collective-permute-start | bytes 1572872 | tf_op jit(solution)/shard_map/ppermute | solution.py:37
  113.7 12.9 %collective-permute-start.19 = (bf16[256,1024]{1,0:T(8,128)(2,1)S(1)}, bf16[256,1024]{1,0:T(8,128)(2,1)S(1)}, u32[]{:S(2)}, u32[]{:S(2)}) collective-permute-start(bf16[256,1024]{1,0:T(8,128)(2,1)S(1)} %collective-permute-done.12.refs_2_), channel_id=1, source_target_pairs={{4,8},{8,12},{5,9},{9,13},{6,10},{10,14},{7,11},{11,15},{20,24},{2... | collective-permute-start | bytes 1572872 | tf_op jit(solution)/shard_map/ppermute | solution.py:453
  114.4 16.1 %collective-permute-start.20 = (bf16[256,1024]{1,0:T(8,128)(2,1)S(1)}, bf16[256,1024]{1,0:T(8,128)(2,1)S(1)}, u32[]{:S(2)}, u32[]{:S(2)}) collective-permute-start(bf16[256,1024]{1,0:T(8,128)(2,1)S(1)} %collective-permute-done.13.refs_3_), channel_id=1, source_target_pairs={{4,0},{8,4},{5,1},{9,5},{6,2},{10,6},{7,3},{11,7},{20,16},{24,20},... | collective-permute-start | bytes 1572872 | tf_op jit(solution)/shard_map/ppermute | solution.py:454
  (9 other events, 97.3 us)

commit v12 on v11

--- a/solution.py
+++ b/solution.py
@@ -417,7 +417,7 @@
     for s in range(peers):
         for q in range(group_count):
             links.append((s * group_count + q, ((s + step_of(q)) % peers) * group_count + q))
-    arrived = lax.ppermute(after(out_block, grad_all[1], kv_all[-1]), ("seq", "head", "rep"), links)
+    arrived = lax.ppermute(after(out_block, grad_all[1]), ("seq", "head", "rep"), links)
 
     mixed_heads, lse = kernel_call(
         functools.partial(forward_kernel, tiles, count, heads),

time: 134 us -> 129 us (0.963)
  waiting for transfers between devices: 40.5 us -> 32.6 us
  starting transfers between devices: 42.9 us -> 45.9 us
    ppermute x2, starting transfers between devices: 4.59 us -> 15.6 us  [cyclic(): lax.ppermute(value, 'seq', [(i, (i + by) % peers) for i in range(peers)])]
    ppermute x8, waiting for transfers between devices: 35.6 us -> 25 us  [shift(): lax.ppermute(value, 'seq', [(i, i + by) for i in range(peers) if 0 <= i +...]
    ppermute x8, starting transfers between devices: 14 us -> 5.97 us  [swap(): return lax.ppermute(value, axis, [(0, 1), (1, 0)])]
    ppermute x1, waiting for transfers between devices: 0.17 us -> 3.41 us  [per_device(): down = lax.ppermute(after(near[3], held), 'seq', [(1, 0), (2, 1)])]
  transfers between devices with their start and end apart: 21 -> 21, of which waited for: 9 -> 9; matrix products, arithmetic and copies ran while one was open for 7% -> 7% of each run, Pallas kernels for 27% -> 28%
where the time goes in v12:
time: 129 us; the launch traced here: 128 us
  starting transfers between devices  45.9 us (36%)
  Pallas kernels  38.6 us (30%)
  waiting for transfers between devices  32.6 us (25%)
  other arithmetic  6.83 us (5%)
  local copies, waits for them, and re-layouts  3.33 us (3%)
    pallas_call x8, Pallas kernels, kernel_call(): pl.pallas_call(body, in_specs=[smem] * len(scalars) + [vmem] * len(arrays...  38.6 us
    ppermute x8, waiting for transfers between devices, shift(): lax.ppermute(value, 'seq', [(i, i + by) for i in range(peers) if 0 <= i +...  25 us
    ppermute x8, starting transfers between devices, shift(): lax.ppermute(value, 'seq', [(i, i + by) for i in range(peers) if 0 <= i +...  16.8 us
    ppermute x2, starting transfers between devices, cyclic(): lax.ppermute(value, 'seq', [(i, (i + by) % peers) for i in range(peers)])  15.6 us
    ppermute x8, starting transfers between devices, swap(): return lax.ppermute(value, axis, [(0, 1), (1, 0)])  5.97 us
    ppermute x1, starting transfers between devices, per_device(): lax.ppermute(after(out_block, grad_all[1]), ('seq', 'head', 'rep'), links)  5.35 us
    ppermute x8, waiting for transfers between devices, swap(): return lax.ppermute(value, axis, [(0, 1), (1, 0)])  4.17 us
    ppermute x1, waiting for transfers between devices, per_device(): down = lax.ppermute(after(near[3], held), 'seq', [(1, 0), (2, 1)])  3.41 us
  transfers between devices with their start and end apart: 21, of which 9 were waited for; matrix products, arithmetic and copies ran while one was open for 7% of the time, Pallas kernels for 28%

profile of v12, /device:TPU:0, one launch (start us, length us, event | category | flops | bytes accessed | tf_op | source)
XLA Modules:
  0.0 128.2 jit_solution(1330978842808017111)
XLA Ops:
  1.1 2.6 %collective-permute-start.2 = (bf16[256,1024]{1,0:T(8,128)(2,1)}, bf16[256,1024]{1,0:T(8,128)(2,1)S(1)}, u32[]{:S(2)}, u32[]{:S(2)}) collective-permute-start(bf16[256,1024]{1,0:T(8,128)(2,1)} %refs_0_.2), channel_id=1, source_target_pairs={{0,2},{2,0},{1,3},{3,1},{4,6},{6,4},{5,7},{7,5},{8,10},{10,8},{9,1... | collective-permute-start | bytes 1572872 | tf_op jit(solution)/shard_map/ppermute | solution.py:37
  7.2 4.6 %collective-permute-start = (bf16[512,1024]{1,0:T(8,128)(2,1)S(1)}, bf16[512,1024]{1,0:T(8,128)(2,1)S(1)}, u32[]{:S(2)}, u32[]{:S(2)}) collective-permute-start(bf16[512,1024]{1,0:T(8,128)(2,1)S(1)} %constant_dynamic-update-slice_fusion.refs_0_), channel_id=1, source_target_pairs={{0,4},{4,8},{8,12},{1,5},{5,9},{9,13},{2,6},{6,10},{10,14},{3,7},{... | collective-permute-start | bytes 3145736 | tf_op jit(solution)/shard_map/ppermute | solution.py:26
  12.4 5.7 %mixed_grad.2.refs_0_ = f32[256,1024]{1,0:T(8,128)} custom-call(s32[2]{0:T(128)} %pad_add_fusion.2.place_ref, bf16[256,1024]{1,0:T(8,128)(2,1)} %refs_0_.2, bf16[256,1024]{1,0:T(8,128)(2,1)} %collective-permute-done.1.refs_1_, bf16[4096,1024]{1,0:T(8,128)(2,1)} %w_ref.1), custom_call_target="tpu_custom_call" | custom-call | tf_op jit(solution)/shard_map/mixed_grad/pallas_call | solution.py:265
  18.1 1.7 %collective-permute-done.3.refs_1_ = bf16[256,1024]{1,0:T(8,128)(2,1)S(1)} collective-permute-done((bf16[256,1024]{1,0:T(8,128)(2,1)}, bf16[256,1024]{1,0:T(8,128)(2,1)S(1)}, u32[]{:S(2)}, u32[]{:S(2)}) %collective-permute-start.3) | collective-permute-done | bytes 524320 | tf_op jit(solution)/shard_map/ppermute | solution.py:26
  21.9 5.3 %mixed_grad.3.g_ref.refs_3_ = bf16[256,1024]{1,0:T(8,128)(2,1)} custom-call(s32[2]{0:T(128)} %pad_add_fusion.1.place_ref, f32[256,1024]{1,0:T(8,128)} %mixed_grad.2.refs_0_, bf16[256,1024]{1,0:T(8,128)(2,1)} %copy-done.8, bf16[256,1024]{1,0:T(8,128)(2,1)} %collective-permute-done.4.refs_2_, bf16[4096,1024]{1,0:T(8,128)(2,1)} %w_ref.1), custom_call_target="tpu_custom_call" | custom-call | tf_op jit(solution)/shard_map/mixed_grad/pallas_call | solution.py:265
  28.6 5.6 %collective-permute-done.refs_1_ = bf16[512,1024]{1,0:T(8,128)(2,1)S(1)} collective-permute-done((bf16[512,1024]{1,0:T(8,128)(2,1)S(1)}, bf16[512,1024]{1,0:T(8,128)(2,1)S(1)}, u32[]{:S(2)}, u32[]{:S(2)}) %collective-permute-start) | collective-permute-done | bytes 1048608 | tf_op jit(solution)/shard_map/ppermute | solution.py:26
  34.2 4.4 %collective-permute-start.5 = (bf16[512,1024]{1,0:T(8,128)(2,1)S(1)}, bf16[512,1024]{1,0:T(8,128)(2,1)S(1)}, u32[]{:S(2)}, u32[]{:S(2)}) collective-permute-start(bf16[512,1024]{1,0:T(8,128)(2,1)S(1)} %collective-permute-done.refs_1_), channel_id=1, source_target_pairs={{0,4},{4,8},{8,12},{1,5},{5,9},{9,13},{2,6},{6,10},{10,14},{3,7},{... | collective-permute-start | bytes 3145736 | tf_op jit(solution)/shard_map/ppermute | solution.py:26
  40.0 2.0 %select_select_fusion = bf16[256,1024]{1,0:T(8,128)(2,1)} fusion(bf16[256,1024]{1,0:T(8,128)(2,1)} %collective-permute-done.4.refs_2_, bf16[256,1024]{1,0:T(8,128)(2,1)} %copy-done.8, bf16[256,1024]{1,0:T(8,128)(2,1)} %collective-permute-done.1.refs_1_, bf16[256,1024]{1,0:T(8,128)(2,1)} %refs_0_.2, pred[]{:T(512)S(6)} %eq.33, pred[]{:T(512)S(6)} %eq.32, ...), kind=kLoop, calls=%fused_computation.5 | loop fusion | flops 786432 | bytes 2621443 | tf_op jit(solution)/shard_map/jit(_where)/select_n | solution.py:415
  41.9 2.3 %collective-permute-done.7.refs_4_ = bf16[256,1024]{1,0:T(8,128)(2,1)} collective-permute-done((bf16[256,1024]{1,0:T(8,128)(2,1)}, bf16[256,1024]{1,0:T(8,128)(2,1)}, u32[]{:S(2)}, u32[]{:S(2)}) %collective-permute-start.7) | collective-permute-done | bytes 524320 | tf_op jit(solution)/shard_map/ppermute | solution.py:26
  44.2 5.3 %collective-permute-start.10 = (bf16[256,1024]{1,0:T(8,128)(2,1)}, bf16[256,1024]{1,0:T(8,128)(2,1)}, u32[]{:S(2)}, u32[]{:S(2)}) collective-permute-start(bf16[256,1024]{1,0:T(8,128)(2,1)} %select_select_fusion), channel_id=1, source_target_pairs={{0,0},{1,9},{2,6},{3,15},{4,4},{5,13},{6,10},{7,3},{8,8},{9,1},{10... | collective-permute-start | bytes 1572872 | tf_op jit(solution)/shard_map/ppermute | solution.py:420
  51.9 10.3 %collective-permute-done.5.refs_2_ = bf16[512,1024]{1,0:T(8,128)(2,1)S(1)} collective-permute-done((bf16[512,1024]{1,0:T(8,128)(2,1)S(1)}, bf16[512,1024]{1,0:T(8,128)(2,1)S(1)}, u32[]{:S(2)}, u32[]{:S(2)}) %collective-permute-start.5) | collective-permute-done | bytes 1048608 | tf_op jit(solution)/shard_map/ppermute | solution.py:26
  63.2 3.0 %attention_forward.1 = (bf16[256,1024]{1,0:T(8,128)(2,1)S(1)}, f32[8,256]{1,0:T(8,128)S(1)}) custom-call(s32[10]{0:T(128)S(1)} %reshape.264.use_ref, bf16[256,1024]{1,0:T(8,128)(2,1)S(1)} %copy-done.5, bf16[512,1024]{1,0:T(8,128)(2,1)S(1)} %constant_dynamic-update-slice_fusion.refs_0_, bf16[512,1024]{1,0:T(8,128)(2,1)S(1)} %collective-permute-done.refs_1_, ...), custom_call_target="tpu_custom_call" | custom-call | tf_op jit(solution)/shard_map/attention_forward/pallas_call | solution.py:265
  66.2 3.2 %collective-permute-start.13 = (bf16[256,1024]{1,0:T(8,128)(2,1)S(1)}, bf16[256,1024]{1,0:T(8,128)(2,1)S(1)}, u32[]{:S(2)}, u32[]{:S(2)}) collective-permute-start(bf16[256,1024]{1,0:T(8,128)(2,1)S(1)} %get-tuple-element.40.m_ref.refs_1_), channel_id=1, source_target_pairs={{0,12},{4,0},{8,4},{12,8},{1,13},{5,1},{9,5},{13,9},{2,14},{6,2},{... | collective-permute-start | bytes 1572872 | tf_op jit(solution)/shard_map/ppermute | solution.py:33
  69.4 12.4 %collective-permute-start.12 = (bf16[256,1024]{1,0:T(8,128)(2,1)S(1)}, bf16[256,1024]{1,0:T(8,128)(2,1)S(1)}, u32[]{:S(2)}, u32[]{:S(2)}) collective-permute-start(bf16[256,1024]{1,0:T(8,128)(2,1)S(1)} %get-tuple-element.40.m_ref.refs_1_), channel_id=1, source_target_pairs={{0,4},{4,8},{8,12},{12,0},{1,5},{5,9},{9,13},{13,1},{2,6},{6,10},{... | collective-permute-start | bytes 1572872 | tf_op jit(solution)/shard_map/ppermute | solution.py:33
  81.8 6.9 %attended_partial.1 = (bf16[2,256,1024]{2,1,0:T(8,128)(2,1)}, bf16[2,256,1024]{2,1,0:T(8,128)(2,1)}) custom-call(s32[4]{0:T(128)} %pad_add_fusion.place_ref, bf16[256,1024]{1,0:T(8,128)(2,1)} %copy-done, bf16[4096,1024]{1,0:T(8,128)(2,1)} %w_ref.1), custom_call_target="tpu_custom_call" | custom-call | tf_op jit(solution)/shard_map/attended_partial/pallas_call | solution.py:265
  89.0 6.6 %attention_query_grad.1 = (bf16[256,1024]{1,0:T(8,128)(2,1)}, f32[24,256]{1,0:T(8,128)S(1)}) custom-call(s32[10]{0:T(128)S(1)} %reshape.264.use_ref, bf16[256,1024]{1,0:T(8,128)(2,1)S(1)} %copy-done.5, bf16[256,1024]{1,0:T(8,128)(2,1)S(1)} %copy-done.2, f32[8,256]{1,0:T(8,128)S(1)} %get-tuple-element.38.lse_ref, ...), custom_call_target="tpu_custom_call" | custom-call | flops 80530636800 | bytes 471859200 | tf_op jit(solution)/shard_map/attention_query_grad/pallas_call | solution.py:265
  98.4 4.4 %collective-permute-done.15.refs_8_ = f32[24,256]{1,0:T(8,128)S(1)} collective-permute-done((f32[24,256]{1,0:T(8,128)S(1)}, f32[24,256]{1,0:T(8,128)S(1)}, u32[]{:S(2)}, u32[]{:S(2)}) %collective-permute-start.15) | collective-permute-done | bytes 24608 | tf_op jit(solution)/shard_map/ppermute | solution.py:26
  103.6 2.0 %collective-permute-start.16 = (bf16[256,1024]{1,0:T(8,128)(2,1)S(1)}, bf16[256,1024]{1,0:T(8,128)(2,1)S(1)}, u32[]{:S(2)}, u32[]{:S(2)}) collective-permute-start(bf16[256,1024]{1,0:T(8,128)(2,1)S(1)} %fusion), channel_id=1, source_target_pairs={{0,2},{2,0},{1,3},{3,1},{4,6},{6,4},{5,7},{7,5},{8,10},{10,8},{9,1... | collective-permute-start | bytes 1572872 | tf_op jit(solution)/shard_map/ppermute | solution.py:37
  106.8 1.5 %collective-permute-start.20 = (bf16[256,1024]{1,0:T(8,128)(2,1)S(1)}, bf16[256,1024]{1,0:T(8,128)(2,1)S(1)}, u32[]{:S(2)}, u32[]{:S(2)}) collective-permute-start(bf16[256,1024]{1,0:T(8,128)(2,1)S(1)} %collective-permute-done.13.refs_3_), channel_id=1, source_target_pairs={{4,0},{8,4},{5,1},{9,5},{6,2},{10,6},{7,3},{11,7},{20,16},{24,20},... | collective-permute-start | bytes 1572872 | tf_op jit(solution)/shard_map/ppermute | solution.py:454
  108.3 6.1 %attention_key_grad.1 = (bf16[256,1024]{1,0:T(8,128)(2,1)}, bf16[256,1024]{1,0:T(8,128)(2,1)}) custom-call(bf16[256,1024]{1,0:T(8,128)(2,1)S(1)} %copy-done.3, bf16[256,1024]{1,0:T(8,128)(2,1)S(1)} %copy-done.4, bf16[256,1024]{1,0:T(8,128)(2,1)S(1)} %copy-done.5, bf16[256,1024]{1,0:T(8,128)(2,1)S(1)} %copy-done.7, ...), custom_call_target="tpu_custom_call" | custom-call | flops 107374182400 | bytes 524288000 | tf_op jit(solution)/shard_map/attention_key_grad/pallas_call | solution.py:265
  114.4 2.9 %collective-permute-done.16 = bf16[256,1024]{1,0:T(8,128)(2,1)S(1)} collective-permute-done((bf16[256,1024]{1,0:T(8,128)(2,1)S(1)}, bf16[256,1024]{1,0:T(8,128)(2,1)S(1)}, u32[]{:S(2)}, u32[]{:S(2)}) %collective-permute-start.16) | collective-permute-done | bytes 524320 | tf_op jit(solution)/shard_map/ppermute | solution.py:37
  119.7 2.4 %weight_grad.2.refs_0_ = f32[1024,1024]{1,0:T(8,128)S(1)} custom-call(s32[4]{0:T(128)S(1)} %select_reduce_fusion.place_ref, bf16[4,256,1024]{2,1,0:T(8,128)(2,1)S(1)} %pad_maximum_fusion.refs_0_.refs_1_, bf16[256,1024]{1,0:T(8,128)(2,1)S(1)} %copy-done.1, bf16[256,1024]{1,0:T(8,128)(2,1)S(1)} %collective-permute-done.12.refs_2_, ...), custom_call_target="tpu_custom_call" | custom-call | tf_op jit(solution)/shard_map/weight_grad/pallas_call | solution.py:265
  122.1 3.4 %collective-permute-done.20.refs_3_ = bf16[256,1024]{1,0:T(8,128)(2,1)S(1)} collective-permute-done((bf16[256,1024]{1,0:T(8,128)(2,1)S(1)}, bf16[256,1024]{1,0:T(8,128)(2,1)S(1)}, u32[]{:S(2)}, u32[]{:S(2)}) %collective-permute-start.20) | collective-permute-done | bytes 524320 | tf_op jit(solution)/shard_map/ppermute | solution.py:454
  125.5 2.7 %weight_grad.3 = bf16[1024,1024]{1,0:T(8,128)(2,1)} custom-call(s32[4]{0:T(128)S(1)} %select_reduce_fusion.place_ref, f32[1024,1024]{1,0:T(8,128)S(1)} %weight_grad.2.refs_0_, bf16[4,256,1024]{2,1,0:T(8,128)(2,1)S(1)} %pad_maximum_fusion.refs_0_.refs_1_, bf16[256,1024]{1,0:T(8,128)(2,1)S(1)} %collective-permute-done.19.refs_2_, ...), custom_call_target="tpu_custom_call" | custom-call | tf_op jit(solution)/shard_map/weight_grad/pallas_call | solution.py:265
  (63 shorter events, 20.0 us)
Async XLA Ops:
  0.6 11.8 %collective-permute-start.1 = (bf16[256,1024]{1,0:T(8,128)(2,1)}, bf16[256,1024]{1,0:T(8,128)(2,1)}, u32[]{:S(2)}, u32[]{:S(2)}) collective-permute-start(bf16[256,1024]{1,0:T(8,128)(2,1)} %refs_0_.2), channel_id=1, source_target_pairs={{0,1},{1,0},{2,3},{3,2},{4,5},{5,4},{6,7},{7,6},{8,9},{9,8},{10,11... | collective-permute-start | bytes 1572872 | tf_op jit(solution)/shard_map/ppermute | solution.py:37
  1.1 18.7 %collective-permute-start.2 = (bf16[256,1024]{1,0:T(8,128)(2,1)}, bf16[256,1024]{1,0:T(8,128)(2,1)S(1)}, u32[]{:S(2)}, u32[]{:S(2)}) collective-permute-start(bf16[256,1024]{1,0:T(8,128)(2,1)} %refs_0_.2), channel_id=1, source_target_pairs={{0,2},{2,0},{1,3},{3,1},{4,6},{6,4},{5,7},{7,5},{8,10},{10,8},{9,1... | collective-permute-start | bytes 1572872 | tf_op jit(solution)/shard_map/ppermute | solution.py:37
  3.7 16.1 %collective-permute-start.3 = (bf16[256,1024]{1,0:T(8,128)(2,1)}, bf16[256,1024]{1,0:T(8,128)(2,1)S(1)}, u32[]{:S(2)}, u32[]{:S(2)}) collective-permute-start(bf16[256,1024]{1,0:T(8,128)(2,1)} %refs_0_.3), channel_id=1, source_target_pairs={{4,0},{8,4},{12,8},{5,1},{9,5},{13,9},{6,2},{10,6},{14,10},{7,3},{... | collective-permute-start | bytes 1572872 | tf_op jit(solution)/shard_map/ppermute | solution.py:26
  7.2 27.0 %collective-permute-start = (bf16[512,1024]{1,0:T(8,128)(2,1)S(1)}, bf16[512,1024]{1,0:T(8,128)(2,1)S(1)}, u32[]{:S(2)}, u32[]{:S(2)}) collective-permute-start(bf16[512,1024]{1,0:T(8,128)(2,1)S(1)} %constant_dynamic-update-slice_fusion.refs_0_), channel_id=1, source_target_pairs={{0,4},{4,8},{8,12},{1,5},{5,9},{9,13},{2,6},{6,10},{10,14},{3,7},{... | collective-permute-start | bytes 3145736 | tf_op jit(solution)/shard_map/ppermute | solution.py:26
  19.8 2.1 %collective-permute-start.4 = (bf16[256,1024]{1,0:T(8,128)(2,1)S(1)}, bf16[256,1024]{1,0:T(8,128)(2,1)}, u32[]{:S(2)}, u32[]{:S(2)}) collective-permute-start(bf16[256,1024]{1,0:T(8,128)(2,1)S(1)} %collective-permute-done.2.refs_1_), channel_id=1, source_target_pairs={{0,1},{1,0},{2,3},{3,2},{4,5},{5,4},{6,7},{7,6},{8,9},{9,8},{10,11... | collective-permute-start | bytes 1572872 | tf_op jit(solution)/shard_map/ppermute | solution.py:37
  27.2 23.6 %copy-start.10 = (s32[2,5]{1,0:T(2,128)S(1)}, s32[2,5]{1,0:T(2,128)}, u32[]{:S(2)}) copy-start(s32[2,5]{1,0:T(2,128)} %param.10) | copy-start | bytes 124
  27.2 17.0 %collective-permute-start.7 = (bf16[256,1024]{1,0:T(8,128)(2,1)}, bf16[256,1024]{1,0:T(8,128)(2,1)}, u32[]{:S(2)}, u32[]{:S(2)}) collective-permute-start(bf16[256,1024]{1,0:T(8,128)(2,1)} %mixed_grad.3.g_ref.refs_3_), channel_id=1, source_target_pairs={{4,0},{8,4},{12,8},{5,1},{9,5},{13,9},{6,2},{10,6},{14,10},{7,3},{... | collective-permute-start | bytes 1572872 | tf_op jit(solution)/shard_map/ppermute | solution.py:26
  34.2 28.0 %collective-permute-start.5 = (bf16[512,1024]{1,0:T(8,128)(2,1)S(1)}, bf16[512,1024]{1,0:T(8,128)(2,1)S(1)}, u32[]{:S(2)}, u32[]{:S(2)}) collective-permute-start(bf16[512,1024]{1,0:T(8,128)(2,1)S(1)} %collective-permute-done.refs_1_), channel_id=1, source_target_pairs={{0,4},{4,8},{8,12},{1,5},{5,9},{9,13},{2,6},{6,10},{10,14},{3,7},{... | collective-permute-start | bytes 3145736 | tf_op jit(solution)/shard_map/ppermute | solution.py:26
  38.7 43.1 %collective-permute-start.6 = (bf16[256,1024]{1,0:T(8,128)(2,1)}, bf16[256,1024]{1,0:T(8,128)(2,1)}, u32[]{:S(2)}, u32[]{:S(2)}) collective-permute-start(bf16[256,1024]{1,0:T(8,128)(2,1)} %copy-done.6), channel_id=1, source_target_pairs={{4,0},{8,4},{12,8},{5,1},{9,5},{13,9},{6,2},{10,6},{14,10},{7,3},{... | collective-permute-start | bytes 1572872 | tf_op jit(solution)/shard_map/ppermute | solution.py:26
  44.2 44.6 %collective-permute-start.10 = (bf16[256,1024]{1,0:T(8,128)(2,1)}, bf16[256,1024]{1,0:T(8,128)(2,1)}, u32[]{:S(2)}, u32[]{:S(2)}) collective-permute-start(bf16[256,1024]{1,0:T(8,128)(2,1)} %select_select_fusion), channel_id=1, source_target_pairs={{0,0},{1,9},{2,6},{3,15},{4,4},{5,13},{6,10},{7,3},{8,8},{9,1},{10... | collective-permute-start | bytes 1572872 | tf_op jit(solution)/shard_map/ppermute | solution.py:420
  49.5 32.2 %collective-permute-start.8 = (bf16[256,1024]{1,0:T(8,128)(2,1)}, bf16[256,1024]{1,0:T(8,128)(2,1)}, u32[]{:S(2)}, u32[]{:S(2)}) collective-permute-start(bf16[256,1024]{1,0:T(8,128)(2,1)} %collective-permute-done.7.refs_4_), channel_id=1, source_target_pairs={{4,0},{8,4},{12,8},{5,1},{9,5},{13,9},{6,2},{10,6},{14,10},{7,3},{... | collective-permute-start | bytes 1572872 | tf_op jit(solution)/shard_map/ppermute | solution.py:26
  66.2 22.8 %copy-start.2 = (bf16[256,1024]{1,0:T(8,128)(2,1)S(1)}, bf16[256,1024]{1,0:T(8,128)(2,1)}, u32[]{:S(2)}) copy-start(bf16[256,1024]{1,0:T(8,128)(2,1)} %mixed_grad.3.g_ref.refs_3_) | copy-start | bytes 1572868
  66.2 37.3 %collective-permute-start.13 = (bf16[256,1024]{1,0:T(8,128)(2,1)S(1)}, bf16[256,1024]{1,0:T(8,128)(2,1)S(1)}, u32[]{:S(2)}, u32[]{:S(2)}) collective-permute-start(bf16[256,1024]{1,0:T(8,128)(2,1)S(1)} %get-tuple-element.40.m_ref.refs_1_), channel_id=1, source_target_pairs={{0,12},{4,0},{8,4},{12,8},{1,13},{5,1},{9,5},{13,9},{2,14},{6,2},{... | collective-permute-start | bytes 1572872 | tf_op jit(solution)/shard_map/ppermute | solution.py:33
  69.4 34.2 %collective-permute-start.12 = (bf16[256,1024]{1,0:T(8,128)(2,1)S(1)}, bf16[256,1024]{1,0:T(8,128)(2,1)S(1)}, u32[]{:S(2)}, u32[]{:S(2)}) collective-permute-start(bf16[256,1024]{1,0:T(8,128)(2,1)S(1)} %get-tuple-element.40.m_ref.refs_1_), channel_id=1, source_target_pairs={{0,4},{4,8},{8,12},{12,0},{1,5},{5,9},{9,13},{13,1},{2,6},{6,10},{... | collective-permute-start | bytes 1572872 | tf_op jit(solution)/shard_map/ppermute | solution.py:33
  88.7 8.2 %collective-permute-start.9 = (bf16[2,256,1024]{2,1,0:T(8,128)(2,1)}, bf16[2,256,1024]{2,1,0:T(8,128)(2,1)S(1)}, u32[]{:S(2)}, u32[]{:S(2)}) collective-permute-start(bf16[2,256,1024]{2,1,0:T(8,128)(2,1)} %get-tuple-element.34), channel_id=1, source_target_pairs={{0,1},{1,0},{2,3},{3,2},{4,5},{5,4},{6,7},{7,6},{8,9},{9,8},{10,11... | collective-permute-start | bytes 3145736 | tf_op jit(solution)/shard_map/ppermute | solution.py:37
  88.8 14.8 %collective-permute-start.11 = (bf16[256,1024]{1,0:T(8,128)(2,1)}, bf16[256,1024]{1,0:T(8,128)(2,1)S(1)}, u32[]{:S(2)}, u32[]{:S(2)}) collective-permute-start(bf16[256,1024]{1,0:T(8,128)(2,1)} %collective-permute-done.10), channel_id=1, source_target_pairs={{0,2},{2,0},{1,3},{3,1},{4,6},{6,4},{5,7},{7,5},{8,10},{10,8},{9,1... | collective-permute-start | bytes 1572872 | tf_op jit(solution)/shard_map/ppermute | solution.py:37
  89.0 19.4 %copy-start.7 = (bf16[256,1024]{1,0:T(8,128)(2,1)S(1)}, bf16[256,1024]{1,0:T(8,128)(2,1)}, u32[]{:S(2)}) copy-start(bf16[256,1024]{1,0:T(8,128)(2,1)} %copy-done.6) | copy-start | bytes 1572868
  95.6 7.2 %collective-permute-start.15 = (f32[24,256]{1,0:T(8,128)S(1)}, f32[24,256]{1,0:T(8,128)S(1)}, u32[]{:S(2)}, u32[]{:S(2)}) collective-permute-start(f32[24,256]{1,0:T(8,128)S(1)} %get-tuple-element.39.refs_6_), channel_id=1, source_target_pairs={{8,0},{12,4},{9,1},{13,5},{10,2},{14,6},{11,3},{15,7},{24,16},{28,... | collective-permute-start | bytes 73736 | tf_op jit(solution)/shard_map/ppermute | solution.py:26
  96.9 6.6 %collective-permute-start.14 = (f32[24,256]{1,0:T(8,128)S(1)}, f32[24,256]{1,0:T(8,128)S(1)}, u32[]{:S(2)}, u32[]{:S(2)}) collective-permute-start(f32[24,256]{1,0:T(8,128)S(1)} %get-tuple-element.39.refs_6_), channel_id=1, source_target_pairs={{4,0},{8,4},{12,8},{5,1},{9,5},{13,9},{6,2},{10,6},{14,10},{7,3},{... | collective-permute-start | bytes 73736 | tf_op jit(solution)/shard_map/ppermute | solution.py:26
  103.6 13.7 %collective-permute-start.16 = (bf16[256,1024]{1,0:T(8,128)(2,1)S(1)}, bf16[256,1024]{1,0:T(8,128)(2,1)S(1)}, u32[]{:S(2)}, u32[]{:S(2)}) collective-permute-start(bf16[256,1024]{1,0:T(8,128)(2,1)S(1)} %fusion), channel_id=1, source_target_pairs={{0,2},{2,0},{1,3},{3,1},{4,6},{6,4},{5,7},{7,5},{8,10},{10,8},{9,1... | collective-permute-start | bytes 1572872 | tf_op jit(solution)/shard_map/ppermute | solution.py:37
  105.6 12.8 %collective-permute-start.17 = (bf16[256,1024]{1,0:T(8,128)(2,1)}, bf16[256,1024]{1,0:T(8,128)(2,1)S(1)}, u32[]{:S(2)}, u32[]{:S(2)}) collective-permute-start(bf16[256,1024]{1,0:T(8,128)(2,1)} %collective-permute-done.10), channel_id=1, source_target_pairs={{0,1},{1,0},{2,3},{3,2},{4,5},{5,4},{6,7},{7,6},{8,9},{9,8},{10,11... | collective-permute-start | bytes 1572872 | tf_op jit(solution)/shard_map/ppermute | solution.py:37
  105.6 12.8 %collective-permute-start.18 = (bf16[256,1024]{1,0:T(8,128)(2,1)S(1)}, bf16[256,1024]{1,0:T(8,128)(2,1)S(1)}, u32[]{:S(2)}, u32[]{:S(2)}) collective-permute-start(bf16[256,1024]{1,0:T(8,128)(2,1)S(1)} %collective-permute-done.11), channel_id=1, source_target_pairs={{0,1},{1,0},{2,3},{3,2},{4,5},{5,4},{6,7},{7,6},{8,9},{9,8},{10,11... | collective-permute-start | bytes 1572872 | tf_op jit(solution)/shard_map/ppermute | solution.py:37
  106.1 12.2 %collective-permute-start.19 = (bf16[256,1024]{1,0:T(8,128)(2,1)S(1)}, bf16[256,1024]{1,0:T(8,128)(2,1)S(1)}, u32[]{:S(2)}, u32[]{:S(2)}) collective-permute-start(bf16[256,1024]{1,0:T(8,128)(2,1)S(1)} %collective-permute-done.12.refs_2_), channel_id=1, source_target_pairs={{4,8},{8,12},{5,9},{9,13},{6,10},{10,14},{7,11},{11,15},{20,24},{2... | collective-permute-start | bytes 1572872 | tf_op jit(solution)/shard_map/ppermute | solution.py:453
  106.8 18.7 %collective-permute-start.20 = (bf16[256,1024]{1,0:T(8,128)(2,1)S(1)}, bf16[256,1024]{1,0:T(8,128)(2,1)S(1)}, u32[]{:S(2)}, u32[]{:S(2)}) collective-permute-start(bf16[256,1024]{1,0:T(8,128)(2,1)S(1)} %collective-permute-done.13.refs_3_), channel_id=1, source_target_pairs={{4,0},{8,4},{5,1},{9,5},{6,2},{10,6},{7,3},{11,7},{20,16},{24,20},... | collective-permute-start | bytes 1572872 | tf_op jit(solution)/shard_map/ppermute | solution.py:454
  (8 other events, 75.5 us)
